TPU v7x, 256 devices: a whole 4x4x8 slice. The times are simulated.
256 devices in a mesh: ha: 8 (over x, y_lo), wa: 32 (over z, y_hi, core).
Axes of the slice: x: 4, y: 4 (y_hi: 2, y_lo: 2; y = y_hi * 2 + y_lo), z: 8, core: 2. Of those that a mesh axis runs over, the one named last changes fastest.
Arguments:
- tokens: bfloat16 [4, 64, 256, 1536], P(None, 'ha', 'wa'), may hold values from -6 to 6
- shift: float32 [1536], replicated, may hold values from -3 to 3
- scale: float32 [1536], replicated, may hold values from -3 to 3
- gate: float32 [1536], replicated, may hold values from -4 to 4
- qkv_weight: bfloat16 [1536, 4608], P('wa'), may hold values from -0.17860863 to 0.17860863
- out_weight: bfloat16 [1536, 1536], P('wa'), may hold values from -0.15625 to 0.15625
- q_gain: float32 [128], replicated, may hold values from 1.4 to 6.5
- k_gain: float32 [128], replicated, may hold values from 1.4 to 6.5
Outputs:
- update: bfloat16 [4, 64, 256, 1536], P(None, 'ha', 'wa')
All inputs are finite; a program needn't handle non-finite values.
Results may differ from a plain program's by a relative error of at most 0.009.
The roundings to bfloat16 on the way count: a program that leaves them out, or rounds other values in their place, can miss the bound.
Values may be sent and summed in bfloat16 or wider, within the bound.
No kernel may reach another device: no remote copies, remote signals or barrier semaphores. Data moves between devices by JAX's collectives and lax.ppermute only.
A program may use at most 128 MiB of HBM per device.

v0:
```python
import jax
import jax.numpy as jnp
from jax import lax
from jax.sharding import PartitionSpec as P

HEADS = 12
HD = 128
TILE_T = 4


def padded(x, sides, width):
    for axis, dim in sides:
        peers, length = (lax.axis_size(axis), x.shape[dim])
        up = [(i, (i + 1) % peers) for i in range(peers - 1)]
        down = [(j, i) for i, j in up]
        last = lax.slice_in_dim(x, length - width, length, axis=dim)
        initial = lax.slice_in_dim(x, 0, width, axis=dim)
        before = lax.ppermute(last, axis, up)
        after = lax.ppermute(initial, axis, down)
        x = jnp.concatenate([before, x, after], axis=dim)
    return x


def add_rows(left, piece):
    return jnp.dot(left, piece, preferred_element_type=jnp.float32)


def per_head_norm(raw, gain):
    return (raw * lax.rsqrt(jnp.mean(raw * raw, axis=-1, keepdims=True) + 1e-06) * gain).astype(
        jnp.bfloat16
    )


def shards(tokens, shift, scale, gate, qkv_weight, out_weight, q_gain, k_gain):
    frame_list, tile_h, tile_w, width = tokens.shape
    count = frame_list * tile_h * tile_w
    inner = HEADS * HD
    groups = frame_list // TILE_T
    tall = lax.axis_size("ha")
    wide = lax.axis_size("wa")
    flat = tokens.reshape(count, width).astype(jnp.float32)
    mean = jnp.mean(flat, axis=-1, keepdims=True)
    centred = flat - mean
    var = jnp.mean(centred * centred, axis=-1, keepdims=True)
    normed = centred / jnp.sqrt(var + 1e-06)
    modulated = (normed * (1.0 + scale) + shift).astype(jnp.bfloat16)
    projected = add_rows(modulated, lax.all_gather(qkv_weight, "wa", axis=0, tiled=True))
    query = per_head_norm(projected[:, :inner].reshape(count, HEADS, HD), q_gain)
    key = per_head_norm(projected[:, inner : 2 * inner].reshape(count, HEADS, HD), k_gain)
    value = projected[:, 2 * inner :].astype(jnp.bfloat16)
    both = jnp.concatenate(
        [
            key.reshape(frame_list, tile_h, tile_w, inner),
            value.reshape(frame_list, tile_h, tile_w, inner),
        ],
        axis=-1,
    )
    window = padded(both, (("ha", 1), ("wa", 2)), tile_h)
    rows = lax.axis_index("ha") * tile_h - tile_h + jnp.arange(3 * tile_h, dtype=jnp.int32)
    cols = lax.axis_index("wa") * tile_w - tile_w + jnp.arange(3 * tile_w, dtype=jnp.int32)
    rows_ok = (rows >= 0) & (rows < tile_h * tall)
    cols_ok = (cols >= 0) & (cols < tile_w * wide)
    valid = jnp.broadcast_to(
        rows_ok[:, None] & cols_ok[None, :], (TILE_T, 3 * tile_h, 3 * tile_w)
    ).reshape(-1)
    window = window.reshape(groups, -1, 2 * inner)
    keys = window[:, :, :inner].reshape(groups, -1, HEADS, HD)
    values = window[:, :, inner:].reshape(groups, -1, HEADS, HD)
    queries = query.reshape(groups, -1, HEADS, HD)
    inv_root = 1.0 / jnp.sqrt(jnp.float32(HD))

    def one_head(head):
        query_head_rows = lax.dynamic_index_in_dim(queries, head, 2, keepdims=False)
        key_head_rows = lax.dynamic_index_in_dim(keys, head, 2, keepdims=False)
        value_head_rows = lax.dynamic_index_in_dim(values, head, 2, keepdims=False)
        scores = (
            jnp.einsum(
                "nur,ncr->nuc", query_head_rows, key_head_rows, preferred_element_type=jnp.float32
            )
            * inv_root
        )
        scores = jnp.where(valid[None, None, :], scores, -jnp.inf)
        top = jnp.max(scores, axis=-1, keepdims=True)
        expo = jnp.exp(scores - top)
        total = jnp.sum(expo, axis=-1, keepdims=True)
        probability_rows = expo.astype(jnp.bfloat16)
        summed_output = jnp.einsum(
            "ypi,yif->ypf", probability_rows, value_head_rows, preferred_element_type=jnp.float32
        )
        return summed_output / total

    per_head = lax.map(one_head, jnp.arange(HEADS, dtype=jnp.int32))
    attended = jnp.transpose(per_head, (1, 2, 0, 3)).reshape(count, inner).astype(jnp.bfloat16)
    output = add_rows(attended, lax.all_gather(out_weight, "wa", axis=0, tiled=True))
    return (gate * output).astype(jnp.bfloat16).reshape(frame_list, tile_h, tile_w, width)


def solution(mesh):
    return jax.shard_map(
        shards,
        mesh=mesh,
        in_specs=(P(None, "ha", "wa", None), P(), P(), P(), P("wa", None), P("wa", None), P(), P()),
        out_specs=P(None, "ha", "wa", None),
        check_vma=False,
    )
```

profile of v0, /device:TPU:1, one launch (start us, length us, event | category | flops | bytes accessed | tf_op | source)
XLA Modules:
  0.0 473.5 jit_solution(12902752711311697447)
XLA Ops:
  6.5 0.7 all-gather.3.cloned.1.call-update
  7.3 1.3 convert_reduce_fusion
  8.7 1.5 multiply_reduce_fusion
  10.3 0.7 broadcast_add_fusion
  11.0 1.0 fusion.26
  12.1 127.1 %all-gather.3.cloned.1.call-done = bf16[1536,4608]{1,0:T(8,128)(2,1)} async-done(((bf16[48,4608]{1,0:T(8,128)(2,1)}), bf16[1536,4608]{1,0:T(8,128)(2,1)}) %all-gather.3.cloned.1.call-update) | async-done | bytes 14155792 | tf_op jit(solution)/shard_map/all_gather | solution.py:47
  139.2 7.0 %fusion.29 = f32[256,4608]{1,0:T(8,128)S(1)} fusion(bf16[256,1536]{1,0:T(8,128)(2,1)S(1)} %fusion.26, bf16[1536,4608]{1,0:T(8,128)(2,1)} %all-gather.3.cloned.1.call-done), kind=kOutput, calls=%fused_computation.47 | convolution fusion | flops 3623878656 | bytes 19660800 | tf_op jit(solution)/shard_map/dot_general | solution.py:25
  146.2 2.5 slice_multiply_fusion
  148.8 1.6 copy.11
  150.4 1.5 reduce_sum.48
  152.1 0.6 mul.110
  152.7 1.4 mul.111
  154.1 2.2 multiply_convert_fusion
  156.5 1.3 collective-permute-start.1
  157.8 4.1 collective-permute-start
  161.9 32.2 %collective-permute-done.1 = bf16[4,8,8,3072]{3,2,1,0:T(8,128)(2,1)S(1)} collective-permute-done((bf16[4,8,8,3072]{3,2,1,0:T(8,128)(2,1)S(1)}, bf16[4,8,8,3072]{3,2,1,0:T(8,128)(2,1)S(1)}, u32[]{:S(2)}, u32[]{:S(2)}) %collective-permute-start.1) | collective-permute-done | bytes 1572896 | tf_op jit(solution)/shard_map/ppermute | solution.py:19
  194.1 33.3 %collective-permute-done = bf16[4,8,8,3072]{3,2,1,0:T(8,128)(2,1)S(1)} collective-permute-done((bf16[4,8,8,3072]{3,2,1,0:T(8,128)(2,1)S(1)}, bf16[4,8,8,3072]{3,2,1,0:T(8,128)(2,1)S(1)}, u32[]{:S(2)}, u32[]{:S(2)}) %collective-permute-start) | collective-permute-done | bytes 1572896 | tf_op jit(solution)/shard_map/ppermute | solution.py:18
  227.4 2.7 pad_maximum_fusion.1
  230.1 2.4 collective-permute-start.3
  232.5 4.7 collective-permute-start.2
  237.3 3.0 copy.9
  240.4 3.0 copy.10
  243.4 1.5 reduce_sum.47
  244.9 2.7 multiply_convert_fusion.1
  247.7 41.3 %collective-permute-done.3 = bf16[4,24,8,3072]{3,2,1,0:T(8,128)(2,1)} collective-permute-done((bf16[4,24,8,3072]{3,2,1,0:T(8,128)(2,1)}, bf16[4,24,8,3072]{3,2,1,0:T(8,128)(2,1)}, u32[]{:S(2)}, u32[]{:S(2)}) %collective-permute-start.3) | collective-permute-done | bytes 4718624 | tf_op jit(solution)/shard_map/ppermute | solution.py:19
  288.9 62.5 %collective-permute-done.2 = bf16[4,24,8,3072]{3,2,1,0:T(8,128)(2,1)} collective-permute-done((bf16[4,24,8,3072]{3,2,1,0:T(8,128)(2,1)}, bf16[4,24,8,3072]{3,2,1,0:T(8,128)(2,1)}, u32[]{:S(2)}, u32[]{:S(2)}) %collective-permute-start.2) | collective-permute-done | bytes 4718624 | tf_op jit(solution)/shard_map/ppermute | solution.py:18
  351.4 6.8 %pad_maximum_fusion = bf16[4,24,24,3072]{3,2,1,0:T(8,128)(2,1)S(1)} fusion(bf16[4,24,8,3072]{3,2,1,0:T(8,128)(2,1)} %collective-permute-done.3, bf16[4,8,8,3072]{3,2,1,0:T(8,128)(2,1)S(1)} %collective-permute-done.1, bf16[4,8,8,1536]{3,2,1,0:T(8,128)(2,1)S(1)} %bitcast.62, bf16[4,8,8,1536]{3,2,1,0:T(8,128)(2,1)S(1)} %multiply_convert_fusion, ...), kind=kLoop, calls=%fused_computation.19 | loop fusion | flops 84934656 | bytes 28311552 | tf_op jit(solution)/shard_map/concatenate | solution.py:20
  358.2 5.5 %fusion.28 = (bf16[1,2304,1536]{2,1,0:T(8,128)(2,1)}, bf16[1,2304,1536]{2,1,0:T(8,128)(2,1)}) fusion(bf16[1,2304,3072]{2,1,0:T(8,128)(2,1)S(1)} %bitcast.57), kind=kLoop, calls=%fused_computation.46 | loop fusion | bytes 28311552 | tf_op jit(solution)/shard_map/slice | solution.py:68
  363.6 9.7 %copy.24 = bf16[1,2304,1536]{1,2,0:T(8,128)(2,1)} copy(bf16[1,2304,1536]{2,1,0:T(8,128)(2,1)} %get-tuple-element.84) | data formatting | bytes 14155776
  373.3 9.9 %copy.25 = bf16[1,2304,1536]{1,2,0:T(8,128)(2,1)} copy(bf16[1,2304,1536]{2,1,0:T(8,128)(2,1)} %get-tuple-element.83) | data formatting | bytes 14155776
  383.3 78.7 %while.11 = (s32[]{:T(128)}, bf16[12,1,256,128]{2,3,0,1:T(8,128)(2,1)S(1)}, s32[12]{0:T(128)S(1)}, bf16[1,256,12,128]{1,3,2,0:T(8,128)(2,1)}, bf16[1,2304,12,128...) while((s32[]{:T(128)}, ...), condition=%wide.region_7.8_spmd.clone, body=%wide.region_4.7_spmd.clone.sunk | while | flops 306183680 | bytes 8666851 | solution.py:92
  383.3 0.6 dynamic_slice.42
  386.0 1.7 fusion.41
  388.1 1.6 fusion.43
  389.9 0.6 dynamic_slice.42
  392.5 1.7 fusion.41
  394.7 1.6 fusion.43
  396.4 0.6 dynamic_slice.42
  399.1 1.7 fusion.41
  401.2 1.6 fusion.43
  403.0 0.6 dynamic_slice.42
  405.6 1.7 fusion.41
  407.8 1.6 fusion.43
  409.6 0.6 dynamic_slice.42
  412.2 1.7 fusion.41
  414.4 1.6 fusion.43
  416.1 0.6 dynamic_slice.42
  418.8 1.7 fusion.41
  420.9 1.6 fusion.43
  422.7 0.6 dynamic_slice.42
  425.3 1.7 fusion.41
  427.5 1.6 fusion.43
  429.2 0.6 dynamic_slice.42
  431.9 1.7 fusion.41
  434.0 1.6 fusion.43
  438.4 1.7 fusion.41
  440.6 1.6 fusion.43
  445.0 1.7 fusion.41
  447.2 1.6 fusion.43
  451.6 1.7 fusion.41
  453.7 1.6 fusion.43
  458.1 1.7 fusion.41
  460.3 1.6 fusion.43
  462.1 4.6 fusion.22
  (98 shorter events, 11.5 us)
Async XLA Ops:
  6.5 3.8 copy-start
  6.5 4.5 copy-start.2
  6.5 132.7 %all-gather.3.cloned.1.call-start = ((), (), s32[]{:S(2)}) async-start(), calls=%async_computation | async-start | bytes 14598144 | tf_op jit(solution)/shard_map/all_gather | solution.py:47
  7.3 454.8 %all-gather.5.cloned.1.call-start = ((), (), s32[]{:S(2)}) async-start(), calls=%async_computation.1 | async-start | bytes 4866048 | tf_op jit(solution)/shard_map/all_gather | solution.py:94
  156.5 37.6 %collective-permute-start.1 = (bf16[4,8,8,3072]{3,2,1,0:T(8,128)(2,1)S(1)}, bf16[4,8,8,3072]{3,2,1,0:T(8,128)(2,1)S(1)}, u32[]{:S(2)}, u32[]{:S(2)}) collective-permute-start(bf16[4,8,8,3072]{3,2,1,0:T(8,128)(2,1)S(1)} %pad_maximum_fusion.2), channel_id=1, source_target_pairs={{32,0},{64,32},{96,64},{128,96},{160,128},{192,160},{224,192},{33,... | collective-permute-start | bytes 4718600 | tf_op jit(solution)/shard_map/ppermute | solution.py:19
  157.8 69.6 %collective-permute-start = (bf16[4,8,8,3072]{3,2,1,0:T(8,128)(2,1)S(1)}, bf16[4,8,8,3072]{3,2,1,0:T(8,128)(2,1)S(1)}, u32[]{:S(2)}, u32[]{:S(2)}) collective-permute-start(bf16[4,8,8,3072]{3,2,1,0:T(8,128)(2,1)S(1)} %pad_maximum_fusion.2), channel_id=1, source_target_pairs={{0,32},{32,64},{64,96},{96,128},{128,160},{160,192},{192,224},{1,3... | collective-permute-start | bytes 4718600 | tf_op jit(solution)/shard_map/ppermute | solution.py:18
  227.4 2.7 copy-start.3
  230.1 58.8 %collective-permute-start.3 = (bf16[4,24,8,3072]{3,2,1,0:T(8,128)(2,1)}, bf16[4,24,8,3072]{3,2,1,0:T(8,128)(2,1)}, u32[]{:S(2)}, u32[]{:S(2)}) collective-permute-start(bf16[4,24,8,3072]{3,2,1,0:T(8,128)(2,1)} %pad_maximum_fusion.1), channel_id=1, source_target_pairs={{1,0},{2,1},{3,2},{4,3},{5,4},{6,5},{7,6},{8,7},{9,8},{10,9},{11,1... | collective-permute-start | bytes 14155784 | tf_op jit(solution)/shard_map/ppermute | solution.py:19
  232.5 118.9 %collective-permute-start.2 = (bf16[4,24,8,3072]{3,2,1,0:T(8,128)(2,1)}, bf16[4,24,8,3072]{3,2,1,0:T(8,128)(2,1)}, u32[]{:S(2)}, u32[]{:S(2)}) collective-permute-start(bf16[4,24,8,3072]{3,2,1,0:T(8,128)(2,1)} %pad_maximum_fusion.1), channel_id=1, source_target_pairs={{0,1},{1,2},{2,3},{3,4},{4,5},{5,6},{6,7},{7,8},{8,9},{9,10},{10,1... | collective-permute-start | bytes 14155784 | tf_op jit(solution)/shard_map/ppermute | solution.py:18
  240.4 4.6 copy-start.5
  244.9 106.5 %copy-start.4 = (bf16[4,8,8,3072]{3,2,1,0:T(8,128)(2,1)S(1)}, bf16[4,8,8,3072]{3,2,1,0:T(8,128)(2,1)}, u32[]{:S(2)}) copy-start(bf16[4,8,8,3072]{3,2,1,0:T(8,128)(2,1)} %copy-done.3) | copy-start | bytes 4718596
  373.3 10.0 %copy-start.6 = (bf16[12,1,256,128]{2,3,0,1:T(8,128)(2,1)S(1)}, bf16[12,1,256,128]{2,3,0,1:T(8,128)(2,1)}, u32[]{:S(2)}) copy-start(bf16[12,1,256,128]{2,3,0,1:T(8,128)(2,1)} %custom-call) | copy-start | bytes 2359300
  383.3 78.8 %copy-start.7 = (f32[1536]{0:T(1024)S(1)}, f32[1536]{0:T(1024)}, u32[]{:S(2)}) copy-start(f32[1536]{0:T(1024)} %param.13) | copy-start | bytes 18436
  462.1 4.6 copy-start.1
Sparse Core Ops, SparseCore 0:
  10.1 129.0 all-gather.2
  237.3 134.2 all-gather.4
where the time goes:
time: 477 us; the launch traced here: 474 us
  waiting for transfers between devices  297 us (62%)
  matrix products  51.1 us (11%)
  local copies, waits for them, and re-layouts  44.9 us (9%)
  other arithmetic  30.5 us (6%)
  loops' own time  23.9 us (5%)
  between operations  13.6 us (3%)
  starting transfers between devices  12.5 us (3%)
    all_gather x1, waiting for transfers between devices, shards(): lax.all_gather(qkv_weight, 'wa', axis=0, tiled=True)  127 us
    ppermute x2, waiting for transfers between devices, padded(): before = lax.ppermute(last, axis, up)  95.7 us
    ppermute x2, waiting for transfers between devices, padded(): after = lax.ppermute(initial, axis, down)  73.5 us
    another operation x1, loops' own time, shards(): per_head = lax.map(one_head, jnp.arange(HEADS, dtype=jnp.int32))  23.9 us
    dot_general x12, matrix products, one_head(): jnp.einsum('nur,ncr->nuc', query_head_rows, key_head_rows, preferred_elem...  20.4 us
    unnamed x18, local copies, waits for them, and re-layouts  19.7 us
    dot_general x12, matrix products, one_head(): jnp.einsum('ypi,yif->ypf', probability_rows, value_head_rows, preferred_e...  19.1 us
    dot_general x2, matrix products, add_rows(): return jnp.dot(left, piece, preferred_element_type=jnp.float32)  11.7 us
  transfers between devices with their start and end apart: 6, of which 5 were waited for; matrix products, arithmetic and copies ran while one was open for 22% of the time, Pallas kernels for 0%

commit v1 on v0

v1 whole, which is shorter than its diff:
```python
import functools

import jax
import jax.numpy as jnp
from jax import lax
from jax.experimental import pallas as pl
from jax.experimental.pallas import tpu as pltpu
from jax.sharding import Mesh
from jax.sharding import PartitionSpec as P

HEADS = 12
HD = 128
TILE_T = 4
EPS = 1e-06
HALF = 3 * HD
AXES = ("x", "l", "z", "u", "c")
SIZES = (4, 2, 8, 2, 2)
FAR = 1e30
BF = jnp.bfloat16
F32 = jnp.float32


def hops(move):
    pairs = []
    for x in range(4):
        for l in range(2):
            for z in range(8):
                for u in range(2):
                    for c in range(2):
                        h, s = (x * 2 + l, (z * 2 + u) * 2 + c)
                        h2, s2 = move(h, s)
                        pairs.append((h * 32 + s, h2 % 8 * 32 + s2 % 32))
    return pairs


def across(s):
    return s + 1 if s % 2 else s - 1


def flip_y(h, s):
    return (h ^ 1, s ^ 2)


SIBLING = hops(lambda h, s: (h, s ^ 1))
H_UP = hops(lambda h, s: (h + 1, s))
H_DOWN = hops(lambda h, s: (h - 1, s))
SIDE = hops(lambda h, s: (h, across(s)))
SIDE_UP = hops(lambda h, s: (h + 1, across(s)))
SIDE_DOWN = hops(lambda h, s: (h - 1, across(s)))
Y_FLIP = hops(flip_y)
X_UP = hops(lambda h, s: (h + 2, s))
X_DOWN = hops(lambda h, s: (h - 2, s))


def send(x, pairs):
    return lax.ppermute(x, AXES, pairs)


def cost(flops, nbytes, trans=0):
    return pl.CostEstimate(flops=int(flops), bytes_accessed=int(nbytes), transcendentals=int(trans))


def modulate_kernel(x_ref, scale_ref, shift_ref, o_ref):
    x = x_ref[...].astype(F32)
    mean = jnp.mean(x, axis=-1, keepdims=True)
    centred = x - mean
    var = jnp.mean(centred * centred, axis=-1, keepdims=True)
    normed = centred * lax.rsqrt(var + EPS)
    o_ref[...] = (normed * (1.0 + scale_ref[...]) + shift_ref[...]).astype(BF)


def modulate(x, scale, shift):
    rows, width = x.shape
    step = 64
    return pl.pallas_call(
        modulate_kernel,
        out_shape=jax.ShapeDtypeStruct((rows, width), BF),
        grid=(rows // step,),
        in_specs=[
            pl.BlockSpec((step, width), lambda i: (i, 0)),
            pl.BlockSpec((1, width), lambda i: (0, 0)),
            pl.BlockSpec((1, width), lambda i: (0, 0)),
        ],
        out_specs=pl.BlockSpec((step, width), lambda i: (i, 0)),
        cost_estimate=cost(rows * width * 8, rows * width * 4),
        name="modulate",
    )(x, scale.reshape(1, -1), shift.reshape(1, -1))


def head_norm(raw, gain):
    return (raw * lax.rsqrt(jnp.mean(raw * raw, axis=-1, keepdims=True) + EPS) * gain).astype(BF)


def kv_kernel(n, *refs):
    tiles = refs[:n]
    wk_ref, wv_ref, gain_ref, k_ref, v_ref, buf, sem = refs[n:]
    i = pl.program_id(0)

    def fetch(j, slot):
        for t in range(n):

            @pl.when(j == t)
            def _():
                pltpu.make_async_copy(tiles[t], buf.at[slot], sem.at[slot]).start()

    @pl.when(i == 0)
    def _():
        fetch(i, 0)

    slot = lax.rem(i, 2)

    @pl.when(i + 1 < n)
    def _():
        fetch(i + 1, 1 - slot)

    pltpu.make_async_copy(tiles[0], buf.at[slot], sem.at[slot]).wait()
    x = buf[slot]
    raw = jnp.dot(x, wk_ref[...], preferred_element_type=F32)
    for h in range(3):
        k_ref[h] = head_norm(raw[:, h * HD : (h + 1) * HD], gain_ref[...])
    raw = jnp.dot(x, wv_ref[...], preferred_element_type=F32)
    for h in range(3):
        v_ref[h] = raw[:, h * HD : (h + 1) * HD].astype(BF)


def keys_values(tiles, wk, wv, gain):
    n = len(tiles)
    rows, width = tiles[0].shape
    return pl.pallas_call(
        functools.partial(kv_kernel, n),
        out_shape=[jax.ShapeDtypeStruct((3, n * rows, HD), BF)] * 2,
        grid=(n,),
        in_specs=[pl.BlockSpec(memory_space=pl.ANY)] * n
        + [
            pl.BlockSpec((width, HALF), lambda i: (0, 0)),
            pl.BlockSpec((width, HALF), lambda i: (0, 0)),
            pl.BlockSpec((1, HD), lambda i: (0, 0)),
        ],
        out_specs=[pl.BlockSpec((3, rows, HD), lambda i: (0, i, 0))] * 2,
        scratch_shapes=[pltpu.VMEM((2, rows, width), BF), pltpu.SemaphoreType.DMA((2,))],
        compiler_params=pltpu.CompilerParams(vmem_limit_bytes=24 << 20),
        cost_estimate=cost(2 * n * rows * width * 2 * HALF, n * rows * (width + 2 * HALF) * 2),
        name="keys_values",
    )(*tiles, wk, wv, gain)


def query_kernel(x0_ref, x1_ref, w_ref, gain_ref, o_ref):
    for t, x_ref in enumerate((x0_ref, x1_ref)):
        raw = jnp.dot(x_ref[...], w_ref[...], preferred_element_type=F32)
        for h in range(3):
            o_ref[t, h] = head_norm(raw[:, h * HD : (h + 1) * HD], gain_ref[...])


def queries(x0, x1, wq, gain):
    rows, width = x0.shape
    return pl.pallas_call(
        query_kernel,
        out_shape=jax.ShapeDtypeStruct((2, 3, rows, HD), BF),
        in_specs=[pl.BlockSpec(memory_space=pltpu.VMEM)] * 4,
        out_specs=pl.BlockSpec(memory_space=pltpu.VMEM),
        compiler_params=pltpu.CompilerParams(vmem_limit_bytes=16 << 20),
        cost_estimate=cost(4 * rows * width * HALF, rows * (2 * width + 2 * HALF) * 2 + width * HALF * 2),
        name="queries",
    )(x0, x1, wq, gain)


def attend_kernel(far_ref, q_ref, k_ref, v_ref, o_ref):
    tile = pl.program_id(1)
    rows = q_ref.shape[2]
    q = q_ref[0, 0]
    factor = 1.4426950408889634 / jnp.sqrt(F32(HD))
    base = tile * 3
    scores, top = ([], None)
    for j in range(9):
        at = pl.multiple_of((base + j) * rows, rows)
        k = k_ref[0, pl.ds(at, rows), :]
        s = lax.dot_general(q, k, (((1,), (1,)), ((), ())), preferred_element_type=F32)
        scores.append(s)
        most = jnp.max(s, axis=-1, keepdims=True) - far_ref[base + j]
        top = most if top is None else jnp.maximum(top, most)
    total = jnp.zeros((rows, 1), F32)
    acc = jnp.zeros((rows, HD), F32)
    for j in range(9):
        at = pl.multiple_of((base + j) * rows, rows)
        expo = jnp.exp2((scores[j] - (top + far_ref[base + j])) * factor)
        total += jnp.sum(expo, axis=-1, keepdims=True)
        acc += jnp.dot(expo.astype(BF), v_ref[0, pl.ds(at, rows), :], preferred_element_type=F32)
    o_ref[0] = (acc / total).astype(BF)


def attend(far, q, k, v):
    rows = q.shape[2]
    keys = k.shape[1]
    window = 9 * rows
    return pl.pallas_call(
        attend_kernel,
        out_shape=jax.ShapeDtypeStruct((2, rows, HALF), BF),
        grid_spec=pltpu.PrefetchScalarGridSpec(
            num_scalar_prefetch=1,
            grid=(3, 2),
            in_specs=[
                pl.BlockSpec((1, 1, rows, HD), lambda h, t, far: (t, h, 0, 0)),
                pl.BlockSpec((1, keys, HD), lambda h, t, far: (h, 0, 0)),
                pl.BlockSpec((1, keys, HD), lambda h, t, far: (h, 0, 0)),
            ],
            out_specs=pl.BlockSpec((1, rows, HD), lambda h, t, far: (t, 0, h)),
        ),
        compiler_params=pltpu.CompilerParams(vmem_limit_bytes=32 << 20),
        cost_estimate=cost(6 * rows * window * HD * 4, 6 * keys * HD * 2 * 2, 6 * rows * window),
        name="attend",
    )(far, q, k, v)


def project_kernel(at_ref, a0, a1, a2, a3, w0, w1, w2, w3, gate_ref, o_ref, left):
    for j, a in enumerate((a0, a1, a2, a3)):
        left[:, pl.ds(pl.multiple_of(at_ref[j] * HALF, HD), HALF)] = a[...]
    for j, w in enumerate((w0, w1, w2, w3)):
        cols = pl.ds(pl.multiple_of(at_ref[j] * HALF, HD), HALF)
        out = jnp.dot(left[...], w[...], preferred_element_type=F32)
        o_ref[:, cols] = (gate_ref[:, cols] * out).astype(BF)


def project(at, attended, pieces, gate):
    rows = attended[0].shape[0]
    width = pieces[0].shape[0]
    vmem = pl.BlockSpec(memory_space=pltpu.VMEM)
    return pl.pallas_call(
        project_kernel,
        out_shape=jax.ShapeDtypeStruct((rows, 4 * HALF), BF),
        in_specs=[pl.BlockSpec(memory_space=pltpu.SMEM)] + [vmem] * 9,
        out_specs=vmem,
        scratch_shapes=[pltpu.VMEM((rows, width), BF)],
        compiler_params=pltpu.CompilerParams(vmem_limit_bytes=24 << 20),
        cost_estimate=cost(2 * rows * width * 4 * HALF, width * 4 * HALF * 2 + rows * width * 4),
        name="project",
    )(at, *attended, *pieces, gate.reshape(1, -1))


def shards(tokens, shift, scale, gate, qkv_weight, out_weight, q_gain, k_gain):
    frames, tile_h, tile_w, width = tokens.shape
    count = frames * tile_h * tile_w
    x, l, z, u, c = (lax.axis_index(a) for a in AXES)
    parity = lax.rem(x, 2)
    h = x * 2 + l
    w = z * 2 + u

    parts = [qkv_weight[:, width : 2 * width], qkv_weight[:, 2 * width :], qkv_weight[:, :width], out_weight]
    mine = jnp.concatenate(
        [lax.dynamic_slice_in_dim(m, (c * 2 + parity) * HALF, HALF, 1) for m in parts], axis=1
    )
    theirs = jnp.concatenate(
        [lax.dynamic_slice_in_dim(m, ((1 - c) * 2 + parity) * HALF, HALF, 1) for m in parts], axis=1
    )
    other = send(theirs, SIBLING)
    pair = jnp.where(c == 0, jnp.concatenate([mine, other]), jnp.concatenate([other, mine]))
    other = send(pair, Y_FLIP)
    quad = jnp.where(u == 0, jnp.concatenate([pair, other]), jnp.concatenate([other, pair]))
    wk, wv, wq, wo = (
        lax.all_gather(quad[:, i * HALF : (i + 1) * HALF], "z", axis=0, tiled=True) for i in range(4)
    )
    wk2, wv2 = send(wk, X_DOWN), send(wv, X_UP)
    wq2, wo2 = send(wq, X_DOWN), send(wo, X_UP)
    wo3, wo4 = send(wo, SIBLING), send(wo2, SIBLING)

    own = modulate(tokens.reshape(count, width), scale, shift)
    below, above = send(own, H_UP), send(own, H_DOWN)
    side, side_below, side_above = send(own, SIDE), send(own, SIDE_UP), send(own, SIDE_DOWN)
    outer = [side_below, side, side_above]
    inner = [below, own, above]
    inner2 = [send(t, SIBLING) for t in inner]
    outer2 = [send(t, SIBLING) for t in outer]
    tiles = outer + inner + inner2 + outer2

    col_ok = [jnp.where(c == 0, w > 0, w < 15), True, True, jnp.where(c == 0, w < 15, w > 0)]
    row_ok = [h > 0, True, h < 7]
    far = jnp.stack([jnp.where(jnp.logical_and(a, b), 0.0, FAR).astype(F32) for a in col_ok for b in row_ok])

    q_gain, k_gain = q_gain.reshape(1, HD), k_gain.reshape(1, HD)
    k, v = keys_values(tiles, wk, wv, k_gain)
    q = queries(own, inner2[1], wq, q_gain)
    first = attend(far, q, k, v)
    first2 = send(first[1], SIBLING)
    k, v = keys_values(tiles, wk2, wv2, k_gain)
    q = queries(own, inner2[1], wq2, q_gain)
    second = attend(far, q, k, v)
    second2 = send(second[1], SIBLING)

    at = jnp.stack([c * 2 + parity, c * 2 + 1 - parity, (1 - c) * 2 + parity, (1 - c) * 2 + 1 - parity])
    out = project(at.astype(jnp.int32), [first[0], second[0], first2, second2], [wo, wo2, wo3, wo4], gate)
    return out.reshape(frames, tile_h, tile_w, width)


def solution(mesh):
    fine = Mesh(mesh.devices.reshape(SIZES), AXES)
    tile = P(None, ("x", "l"), ("z", "u", "c"), None)
    rows = P(("z", "u", "c"), None)
    return jax.shard_map(
        shards,
        mesh=fine,
        in_specs=(tile, P(), P(), P(), rows, rows, P(), P()),
        out_specs=tile,
        check_vma=False,
    )
```

time: 477 us -> 253 us (0.53)
  waiting for transfers between devices: 297 us -> 141 us
  Pallas kernels: 0 us -> 53.9 us
  matrix products: 51.1 us -> 0 us
  other arithmetic: 30.5 us -> 0.25 us
  local copies, waits for them, and re-layouts: 44.9 us -> 16.2 us
  loops' own time: 23.9 us -> 0 us
  starting transfers between devices: 12.5 us -> 27.4 us
    ppermute x4 -> x21, waiting for transfers between devices: 169 us -> 59.1 us  [send(): return lax.ppermute(x, AXES, pairs)]
    pallas_call x0 -> x8, Pallas kernels: none -> 53.9 us  [the longest x2 28.2 us: keys_values(): pl.pallas_call(functools.partial(kv_kernel, n), out_shape=[jax.ShapeDtype...]
    dot_general x26 -> x0, matrix products: 51.1 us -> none  [the longest x12 20.4 us: one_head(): jnp.einsum('nur,ncr->nuc', query_head_rows, key_head_rows, preferred_elem...]
    all_gather x2 -> x4, waiting for transfers between devices: 127 us -> 80.7 us  [shards(): lax.all_gather(quad[:, i * HALF:(i + 1) * HALF], 'z', axis=0, tiled=True)]
    another operation x1 -> x0, loops' own time: 23.9 us -> none  [shards(): per_head = lax.map(one_head, jnp.arange(HEADS, dtype=jnp.int32))]
    ppermute x4 -> x21, starting transfers between devices: 12.4 us -> 27.3 us  [send(): return lax.ppermute(x, AXES, pairs)]
    reduce_sum x16 -> x0, other arithmetic: 11.6 us -> none  [the longest x12 5.71 us: one_head(): total = jnp.sum(expo, axis=-1, keepdims=True)]
    concatenate x3 -> x1, other arithmetic: 9.7 us -> 0.02 us  [shards(): jnp.concatenate([lax.dynamic_slice_in_dim(m, ((1 - c) * 2 + parity) * HAL...]
  transfers between devices with their start and end apart: 6 -> 25, of which waited for: 5 -> 10; matrix products, arithmetic and copies ran while one was open for 22% -> 1% of each run, Pallas kernels for 0% -> 19%
where the time goes in v1:
time: 253 us; the launch traced here: 252 us
  waiting for transfers between devices  141 us (56%)
  Pallas kernels  53.9 us (21%)
  starting transfers between devices  27.4 us (11%)
  local copies, waits for them, and re-layouts  16.2 us (6%)
  between operations  13.4 us (5%)
    all_gather x4, waiting for transfers between devices, shards(): lax.all_gather(quad[:, i * HALF:(i + 1) * HALF], 'z', axis=0, tiled=True)  80.7 us
    ppermute x21, waiting for transfers between devices, send(): return lax.ppermute(x, AXES, pairs)  59.1 us
    pallas_call x2, Pallas kernels, keys_values(): pl.pallas_call(functools.partial(kv_kernel, n), out_shape=[jax.ShapeDtype...  28.2 us
    ppermute x21, starting transfers between devices, send(): return lax.ppermute(x, AXES, pairs)  27.3 us
    pallas_call x2, Pallas kernels, attend(): pl.pallas_call(attend_kernel, out_shape=jax.ShapeDtypeStruct((2, rows, HA...  15.1 us
    unnamed x46, local copies, waits for them, and re-layouts  11.4 us
  transfers between devices with their start and end apart: 25, of which 10 were waited for; matrix products, arithmetic and copies ran while one was open for 1% of the time, Pallas kernels for 19%

profile of v1, /device:TPU:1, one launch (start us, length us, event | category | flops | bytes accessed | tf_op | source)
XLA Modules:
  0.0 252.4 jit_solution(10799894008350286543)
XLA Ops:
  6.5 1.1 fusion.1
  7.6 0.8 constant_dynamic-slice_fusion.4
  8.5 3.3 %collective-permute-start.1 = (bf16[48,1536]{1,0:T(8,128)(2,1)S(1)}, bf16[48,1536]{1,0:T(8,128)(2,1)S(1)}, u32[]{:S(2)}, u32[]{:S(2)}) collective-permute-start(bf16[48,1536]{1,0:T(8,128)(2,1)S(1)} %pad_maximum_fusion), channel_id=1, source_target_pairs={{0,1},{1,0},{2,3},{3,2},{4,5},{5,4},{6,7},{7,6},{8,9},{9,8},{10,11... | collective-permute-start | bytes 442376 | tf_op jit(solution)/shard_map/ppermute | solution.py:56
  11.8 1.0 collective-permute-done.1
  12.8 0.1 maximum_select_fusion.1
  12.9 1.1 collective-permute-start.2
  14.0 8.4 %collective-permute-done.2 = bf16[96,1536]{1,0:T(8,128)(2,1)S(1)} collective-permute-done((bf16[96,1536]{1,0:T(8,128)(2,1)S(1)}, bf16[96,1536]{1,0:T(8,128)(2,1)S(1)}, u32[]{:S(2)}, u32[]{:S(2)}) %collective-permute-start.2) | collective-permute-done | bytes 294944 | tf_op jit(solution)/shard_map/ppermute | solution.py:56
  22.4 0.1 maximum_select_fusion
  22.5 0.8 fusion
  23.4 0.0 all-gather.5.cloned.1.call-update
  23.4 0.0 all-gather.11.cloned.1.call-start
  23.4 0.7 all-gather.11.cloned.1.call-update
  24.1 0.0 all-gather.7.cloned.1.call-start
  24.2 0.7 all-gather.7.cloned.1.call-update
  24.9 0.0 all-gather.9.cloned.1.call-start
  24.9 0.6 reshape.22.scale_ref
  25.5 0.6 reshape.23.shift_ref
  26.1 3.7 %modulate.1.x0_ref.refs_4_ = bf16[256,1536]{1,0:T(8,128)(2,1)} custom-call(bf16[256,1536]{1,0:T(8,128)(2,1)} %bitcast.28, f32[1,1536]{1,0:T(1,128)} %reshape.22.scale_ref, f32[1,1536]{1,0:T(1,128)} %reshape.23.shift_ref), custom_call_target="tpu_custom_call" | custom-call | flops 3145728 | bytes 1572864 | tf_op jit(solution)/shard_map/modulate/pallas_call | solution.py:75
  29.9 1.2 collective-permute-start
  31.1 0.1 collective-permute-start.6
  31.2 3.6 %collective-permute-start.7 = (bf16[256,1536]{1,0:T(8,128)(2,1)}, bf16[256,1536]{1,0:T(8,128)(2,1)S(1)}, u32[]{:S(2)}, u32[]{:S(2)}) collective-permute-start(bf16[256,1536]{1,0:T(8,128)(2,1)} %modulate.1.x0_ref.refs_4_), channel_id=1, source_target_pairs={{0,224},{1,225},{2,226},{3,227},{4,228},{5,229},{6,230},{7,231},{8... | collective-permute-start | bytes 2359304 | tf_op jit(solution)/shard_map/ppermute | solution.py:56
  34.7 1.1 collective-permute-start.4
  35.8 4.5 %collective-permute-start.5 = (bf16[256,1536]{1,0:T(8,128)(2,1)}, bf16[256,1536]{1,0:T(8,128)(2,1)}, u32[]{:S(2)}, u32[]{:S(2)}) collective-permute-start(bf16[256,1536]{1,0:T(8,128)(2,1)} %modulate.1.x0_ref.refs_4_), channel_id=1, source_target_pairs={{0,255},{1,226},{2,225},{3,228},{4,227},{5,230},{6,229},{7,232},{8... | collective-permute-start | bytes 2359304 | tf_op jit(solution)/shard_map/ppermute | solution.py:56
  40.3 33.7 %collective-permute-done.6.refs_3_ = bf16[256,1536]{1,0:T(8,128)(2,1)S(1)} collective-permute-done((bf16[256,1536]{1,0:T(8,128)(2,1)}, bf16[256,1536]{1,0:T(8,128)(2,1)S(1)}, u32[]{:S(2)}, u32[]{:S(2)}) %collective-permute-start.6) | collective-permute-done | bytes 786464 | tf_op jit(solution)/shard_map/ppermute | solution.py:56
  73.9 0.8 collective-permute-start.8
  74.7 1.0 copy-done.7
  75.7 0.4 collective-permute-done.7.refs_5_
  76.0 1.1 collective-permute-start.9
  77.1 0.9 copy-done.10
  78.0 8.2 %collective-permute-done.3.refs_0_ = bf16[256,1536]{1,0:T(8,128)(2,1)S(1)} collective-permute-done((bf16[256,1536]{1,0:T(8,128)(2,1)}, bf16[256,1536]{1,0:T(8,128)(2,1)S(1)}, u32[]{:S(2)}, u32[]{:S(2)}) %collective-permute-start.3) | collective-permute-done | bytes 786464 | tf_op jit(solution)/shard_map/ppermute | solution.py:56
  86.2 0.9 copy-done.13
  87.1 6.2 %collective-permute-done.4.refs_1_ = bf16[256,1536]{1,0:T(8,128)(2,1)} collective-permute-done((bf16[256,1536]{1,0:T(8,128)(2,1)}, bf16[256,1536]{1,0:T(8,128)(2,1)}, u32[]{:S(2)}, u32[]{:S(2)}) %collective-permute-start.4) | collective-permute-done | bytes 786464 | tf_op jit(solution)/shard_map/ppermute | solution.py:56
  93.3 0.5 collective-permute-start.12
  93.8 0.9 copy-done.16
  94.7 0.3 collective-permute-start.13
  95.0 5.7 %all-gather.11.cloned.1.call-done.w0 = bf16[1536,384]{1,0:T(8,128)(2,1)} async-done(((bf16[192,384]{1,0:T(8,128)(2,1)}), bf16[1536,384]{1,0:T(8,128)(2,1)}) %all-gather.11.cloned.1.call-update) | async-done | bytes 1179664 | tf_op jit(solution)/shard_map/all_gather | solution.py:259
  100.7 1.2 collective-permute-start.18
  101.9 0.1 stack.59.far_ref
  102.0 38.2 %all-gather.7.cloned.1.call-done.refs_12_ = bf16[1536,384]{1,0:T(8,128)(2,1)} async-done(((bf16[192,384]{1,0:T(8,128)(2,1)}), bf16[1536,384]{1,0:T(8,128)(2,1)}) %all-gather.7.cloned.1.call-update) | async-done | bytes 1179664 | tf_op jit(solution)/shard_map/all_gather | solution.py:259
  140.2 2.1 collective-permute-start.14
  142.3 36.8 %all-gather.9.cloned.1.call-done.refs_13_ = bf16[1536,384]{1,0:T(8,128)(2,1)} async-done(((bf16[192,384]{1,0:T(8,128)(2,1)}), bf16[1536,384]{1,0:T(8,128)(2,1)}) %all-gather.9.cloned.1.call-update) | async-done | bytes 1179664 | tf_op jit(solution)/shard_map/all_gather | solution.py:259
  179.1 1.2 collective-permute-start.15
  180.3 1.1 copy-done
  181.5 1.3 copy-done.2
  182.7 1.1 queries.2.q_ref
  183.9 0.4 copy-done.5
  184.2 0.4 copy-done.6
  184.6 1.1 copy-done.8
  185.7 1.1 copy-done.11
  186.9 1.1 copy-done.14
  188.0 1.1 copy-done.17
  189.1 13.5 %keys_values.2 = (bf16[3,3072,128]{2,1,0:T(8,128)(2,1)S(1)}, bf16[3,3072,128]{2,1,0:T(8,128)(2,1)S(1)}) custom-call(bf16[256,1536]{1,0:T(8,128)(2,1)S(1)} %copy-done.14, bf16[256,1536]{1,0:T(8,128)(2,1)} %collective-permute-done.4.refs_1_, bf16[256,1536]{1,0:T(8,128)(2,1)} %collective-permute-done.5.refs_2_, bf16[256,1536]{1,0:T(8,128)(2,1)S(1)} %copy-done.8, ...), custom_call_target="tpu_custom_call" | custom-call | flops 7247757312 | bytes 14155776 | tf_op jit(solution)/shard_map/keys_values/pallas_call | solution.py:129
  202.6 7.5 %attend.2 = bf16[2,256,384]{2,1,0:T(8,128)(2,1)S(1)} custom-call(f32[12]{0:T(128)S(1)} %stack.59.far_ref, bf16[2,3,256,128]{3,2,1,0:T(8,128)(2,1)S(1)} %queries.2.q_ref, bf16[3,3072,128]{2,1,0:T(8,128)(2,1)S(1)} %get-tuple-element.9.k_ref, bf16[3,3072,128]{2,1,0:T(8,128)(2,1)S(1)} %get-tuple-element.10.v_ref), custom_call_target="tpu_custom_call" | custom-call | flops 1811939328 | bytes 9437184 | tf_op jit(solution)/shard_map/attend/pallas_call | solution.py:195
  210.2 0.7 slice_bitcast_fusion.1
  210.9 4.6 %collective-permute-start.16 = (bf16[256,384]{1,0:T(8,128)(2,1)}, bf16[256,384]{1,0:T(8,128)(2,1)S(1)}, u32[]{:S(2)}, u32[]{:S(2)}) collective-permute-start(bf16[256,384]{1,0:T(8,128)(2,1)} %get-tuple-element.22), channel_id=1, source_target_pairs={{0,1},{1,0},{2,3},{3,2},{4,5},{5,4},{6,7},{7,6},{8,9},{9,8},{10,11... | collective-permute-start | bytes 589832 | tf_op jit(solution)/shard_map/ppermute | solution.py:56
  215.6 0.1 collective-permute-start.19
  215.7 0.4 collective-permute-start.20
  216.1 1.1 queries.3.q_ref
  217.2 14.7 %keys_values.3 = (bf16[3,3072,128]{2,1,0:T(8,128)(2,1)S(1)}, bf16[3,3072,128]{2,1,0:T(8,128)(2,1)S(1)}) custom-call(bf16[256,1536]{1,0:T(8,128)(2,1)S(1)} %copy-done.15, bf16[256,1536]{1,0:T(8,128)(2,1)} %collective-permute-done.4.refs_1_, bf16[256,1536]{1,0:T(8,128)(2,1)} %collective-permute-done.5.refs_2_, bf16[256,1536]{1,0:T(8,128)(2,1)S(1)} %copy-done.9, ...), custom_call_target="tpu_custom_call" | custom-call | flops 7247757312 | bytes 14155776 | tf_op jit(solution)/shard_map/keys_values/pallas_call | solution.py:129
  232.0 7.5 %attend.3 = bf16[2,256,384]{2,1,0:T(8,128)(2,1)S(1)} custom-call(f32[12]{0:T(128)S(1)} %stack.59.far_ref, bf16[2,3,256,128]{3,2,1,0:T(8,128)(2,1)S(1)} %queries.3.q_ref, bf16[3,3072,128]{2,1,0:T(8,128)(2,1)S(1)} %get-tuple-element.11.k_ref, bf16[3,3072,128]{2,1,0:T(8,128)(2,1)S(1)} %get-tuple-element.12.v_ref), custom_call_target="tpu_custom_call" | custom-call | flops 1811939328 | bytes 9437184 | tf_op jit(solution)/shard_map/attend/pallas_call | solution.py:195
  239.6 0.2 collective-permute-start.17
  239.8 0.1 pad_add_fusion.at_ref
  239.9 1.2 collective-permute-done.17.a3
  241.1 4.7 %project.1 = bf16[256,1536]{1,0:T(8,128)(2,1)} custom-call(s32[4]{0:T(128)S(1)} %pad_add_fusion.at_ref, bf16[256,384]{1,0:T(8,128)(2,1)S(1)} %get-tuple-element.23.a0, bf16[256,384]{1,0:T(8,128)(2,1)S(1)} %get-tuple-element.21.a1, bf16[256,384]{1,0:T(8,128)(2,1)S(1)} %collective-permute-done.16.a2, bf16[256,384]{1,0:T(8,128)(2,1)S(1)} %collective-permute-done.17.a3, ...), custom_call_target="tpu_custom_call" | custom-call | flops 1207959552 | bytes 6291456 | tf_op jit(solution)/shard_map/project/pallas_call | solution.py:227
  (58 shorter events, 0.2 us)
Async XLA Ops:
  6.5 88.2 %all-gather.5.cloned.1.call-start = ((), (), s32[]{:S(2)}) async-start(), calls=%async_computation | async-start | bytes 1327104 | tf_op jit(solution)/shard_map/all_gather | solution.py:259
  8.5 4.3 %collective-permute-start.1 = (bf16[48,1536]{1,0:T(8,128)(2,1)S(1)}, bf16[48,1536]{1,0:T(8,128)(2,1)S(1)}, u32[]{:S(2)}, u32[]{:S(2)}) collective-permute-start(bf16[48,1536]{1,0:T(8,128)(2,1)S(1)} %pad_maximum_fusion), channel_id=1, source_target_pairs={{0,1},{1,0},{2,3},{3,2},{4,5},{5,4},{6,7},{7,6},{8,9},{9,8},{10,11... | collective-permute-start | bytes 442376 | tf_op jit(solution)/shard_map/ppermute | solution.py:56
  12.9 9.5 %collective-permute-start.2 = (bf16[96,1536]{1,0:T(8,128)(2,1)S(1)}, bf16[96,1536]{1,0:T(8,128)(2,1)S(1)}, u32[]{:S(2)}, u32[]{:S(2)}) collective-permute-start(bf16[96,1536]{1,0:T(8,128)(2,1)S(1)} %maximum_select_fusion.1), channel_id=1, source_target_pairs={{0,34},{1,35},{2,32},{3,33},{4,38},{5,39},{6,36},{7,37},{8,42},{9,... | collective-permute-start | bytes 884744 | tf_op jit(solution)/shard_map/ppermute | solution.py:56
  14.0 10.9 %copy-start.20 = (f32[1536]{0:T(1024)S(1)}, f32[1536]{0:T(1024)}, u32[]{:S(2)}) copy-start(f32[1536]{0:T(1024)} %param.10) | copy-start | bytes 18436
  14.0 11.5 %copy-start.21 = (f32[1536]{0:T(1024)S(1)}, f32[1536]{0:T(1024)}, u32[]{:S(2)}) copy-start(f32[1536]{0:T(1024)} %param.9) | copy-start | bytes 18436
  23.4 157.0 %copy-start.4 = (f32[128]{0:T(128)S(1)}, f32[128]{0:T(128)}, u32[]{:S(2)}) copy-start(f32[128]{0:T(128)} %param.14) | copy-start | bytes 1540
  23.4 77.3 %all-gather.11.cloned.1.call-start = ((), (), s32[]{:S(2)}) async-start(), calls=%async_computation.3 | async-start | bytes 1327104 | tf_op jit(solution)/shard_map/all_gather | solution.py:259
  24.1 116.1 %all-gather.7.cloned.1.call-start = ((), (), s32[]{:S(2)}) async-start(), calls=%async_computation.1 | async-start | bytes 1327104 | tf_op jit(solution)/shard_map/all_gather | solution.py:259
  24.9 154.3 %all-gather.9.cloned.1.call-start = ((), (), s32[]{:S(2)}) async-start(), calls=%async_computation.2 | async-start | bytes 1327104 | tf_op jit(solution)/shard_map/all_gather | solution.py:259
  29.9 5.9 %collective-permute-start = (bf16[256,1536]{1,0:T(8,128)(2,1)}, bf16[256,1536]{1,0:T(8,128)(2,1)S(1)}, u32[]{:S(2)}, u32[]{:S(2)}) collective-permute-start(bf16[256,1536]{1,0:T(8,128)(2,1)} %modulate.1.x0_ref.refs_4_), channel_id=1, source_target_pairs={{0,1},{1,0},{2,3},{3,2},{4,5},{5,4},{6,7},{7,6},{8,9},{9,8},{10,11... | collective-permute-start | bytes 2359304 | tf_op jit(solution)/shard_map/ppermute | solution.py:56
  31.1 42.9 %collective-permute-start.6 = (bf16[256,1536]{1,0:T(8,128)(2,1)}, bf16[256,1536]{1,0:T(8,128)(2,1)S(1)}, u32[]{:S(2)}, u32[]{:S(2)}) collective-permute-start(bf16[256,1536]{1,0:T(8,128)(2,1)} %modulate.1.x0_ref.refs_4_), channel_id=1, source_target_pairs={{0,32},{1,33},{2,34},{3,35},{4,36},{5,37},{6,38},{7,39},{8,40},{9,... | collective-permute-start | bytes 2359304 | tf_op jit(solution)/shard_map/ppermute | solution.py:56
  31.2 44.8 %collective-permute-start.7 = (bf16[256,1536]{1,0:T(8,128)(2,1)}, bf16[256,1536]{1,0:T(8,128)(2,1)S(1)}, u32[]{:S(2)}, u32[]{:S(2)}) collective-permute-start(bf16[256,1536]{1,0:T(8,128)(2,1)} %modulate.1.x0_ref.refs_4_), channel_id=1, source_target_pairs={{0,224},{1,225},{2,226},{3,227},{4,228},{5,229},{6,230},{7,231},{8... | collective-permute-start | bytes 2359304 | tf_op jit(solution)/shard_map/ppermute | solution.py:56
  34.7 51.4 %collective-permute-start.3 = (bf16[256,1536]{1,0:T(8,128)(2,1)}, bf16[256,1536]{1,0:T(8,128)(2,1)S(1)}, u32[]{:S(2)}, u32[]{:S(2)}) collective-permute-start(bf16[256,1536]{1,0:T(8,128)(2,1)} %modulate.1.x0_ref.refs_4_), channel_id=1, source_target_pairs={{0,63},{1,34},{2,33},{3,36},{4,35},{5,38},{6,37},{7,40},{8,39},{9,... | collective-permute-start | bytes 2359304 | tf_op jit(solution)/shard_map/ppermute | solution.py:56
  34.7 58.5 %collective-permute-start.4 = (bf16[256,1536]{1,0:T(8,128)(2,1)}, bf16[256,1536]{1,0:T(8,128)(2,1)}, u32[]{:S(2)}, u32[]{:S(2)}) collective-permute-start(bf16[256,1536]{1,0:T(8,128)(2,1)} %modulate.1.x0_ref.refs_4_), channel_id=1, source_target_pairs={{0,31},{1,2},{2,1},{3,4},{4,3},{5,6},{6,5},{7,8},{8,7},{9,10},{10,... | collective-permute-start | bytes 2359304 | tf_op jit(solution)/shard_map/ppermute | solution.py:56
  35.8 57.5 %collective-permute-start.5 = (bf16[256,1536]{1,0:T(8,128)(2,1)}, bf16[256,1536]{1,0:T(8,128)(2,1)}, u32[]{:S(2)}, u32[]{:S(2)}) collective-permute-start(bf16[256,1536]{1,0:T(8,128)(2,1)} %modulate.1.x0_ref.refs_4_), channel_id=1, source_target_pairs={{0,255},{1,226},{2,225},{3,228},{4,227},{5,230},{6,229},{7,232},{8... | collective-permute-start | bytes 2359304 | tf_op jit(solution)/shard_map/ppermute | solution.py:56
  73.9 19.8 %collective-permute-start.8 = (bf16[256,1536]{1,0:T(8,128)(2,1)S(1)}, bf16[256,1536]{1,0:T(8,128)(2,1)S(1)}, u32[]{:S(2)}, u32[]{:S(2)}) collective-permute-start(bf16[256,1536]{1,0:T(8,128)(2,1)S(1)} %collective-permute-done.6.refs_3_), channel_id=1, source_target_pairs={{0,1},{1,0},{2,3},{3,2},{4,5},{5,4},{6,7},{7,6},{8,9},{9,8},{10,11... | collective-permute-start | bytes 2359304 | tf_op jit(solution)/shard_map/ppermute | solution.py:56
  74.7 1.0 copy-start.7
  76.0 19.0 %collective-permute-start.9 = (bf16[256,1536]{1,0:T(8,128)(2,1)S(1)}, bf16[256,1536]{1,0:T(8,128)(2,1)}, u32[]{:S(2)}, u32[]{:S(2)}) collective-permute-start(bf16[256,1536]{1,0:T(8,128)(2,1)S(1)} %collective-permute-done.7.refs_5_), channel_id=1, source_target_pairs={{0,1},{1,0},{2,3},{3,2},{4,5},{5,4},{6,7},{7,6},{8,9},{9,8},{10,11... | collective-permute-start | bytes 2359304 | tf_op jit(solution)/shard_map/ppermute | solution.py:56
  77.1 0.9 copy-start.10
  86.2 15.9 %collective-permute-start.10 = (bf16[256,1536]{1,0:T(8,128)(2,1)S(1)}, bf16[256,1536]{1,0:T(8,128)(2,1)}, u32[]{:S(2)}, u32[]{:S(2)}) collective-permute-start(bf16[256,1536]{1,0:T(8,128)(2,1)S(1)} %collective-permute-done.3.refs_0_), channel_id=1, source_target_pairs={{0,1},{1,0},{2,3},{3,2},{4,5},{5,4},{6,7},{7,6},{8,9},{9,8},{10,11... | collective-permute-start | bytes 2359304 | tf_op jit(solution)/shard_map/ppermute | solution.py:56
  86.2 0.9 copy-start.13
  93.3 49.1 %collective-permute-start.11 = (bf16[256,1536]{1,0:T(8,128)(2,1)}, bf16[256,1536]{1,0:T(8,128)(2,1)}, u32[]{:S(2)}, u32[]{:S(2)}) collective-permute-start(bf16[256,1536]{1,0:T(8,128)(2,1)} %collective-permute-done.4.refs_1_), channel_id=1, source_target_pairs={{0,1},{1,0},{2,3},{3,2},{4,5},{5,4},{6,7},{7,6},{8,9},{9,8},{10,11... | collective-permute-start | bytes 2359304 | tf_op jit(solution)/shard_map/ppermute | solution.py:56
  93.3 90.6 %collective-permute-start.12 = (bf16[256,1536]{1,0:T(8,128)(2,1)}, bf16[256,1536]{1,0:T(8,128)(2,1)}, u32[]{:S(2)}, u32[]{:S(2)}) collective-permute-start(bf16[256,1536]{1,0:T(8,128)(2,1)} %collective-permute-done.5.refs_2_), channel_id=1, source_target_pairs={{0,1},{1,0},{2,3},{3,2},{4,5},{5,4},{6,7},{7,6},{8,9},{9,8},{10,11... | collective-permute-start | bytes 2359304 | tf_op jit(solution)/shard_map/ppermute | solution.py:56
  93.8 0.9 copy-start.16
  94.7 120.9 %collective-permute-start.13 = (bf16[1536,384]{1,0:T(8,128)(2,1)}, bf16[1536,384]{1,0:T(8,128)(2,1)S(1)}, u32[]{:S(2)}, u32[]{:S(2)}) collective-permute-start(bf16[1536,384]{1,0:T(8,128)(2,1)} %all-gather.5.cloned.1.call-done.w_ref), channel_id=1, source_target_pairs={{0,192},{1,193},{2,194},{3,195},{4,196},{5,197},{6,198},{7,199},{8... | collective-permute-start | bytes 3538952 | tf_op jit(solution)/shard_map/ppermute | solution.py:56
  100.7 115.0 %collective-permute-start.18 = (bf16[1536,384]{1,0:T(8,128)(2,1)}, bf16[1536,384]{1,0:T(8,128)(2,1)}, u32[]{:S(2)}, u32[]{:S(2)}) collective-permute-start(bf16[1536,384]{1,0:T(8,128)(2,1)} %all-gather.11.cloned.1.call-done.w0), channel_id=1, source_target_pairs={{0,64},{1,65},{2,66},{3,67},{4,68},{5,69},{6,70},{7,71},{8,72},{9,... | collective-permute-start | bytes 3538952 | tf_op jit(solution)/shard_map/ppermute | solution.py:56
  140.2 76.9 %collective-permute-start.14 = (bf16[1536,384]{1,0:T(8,128)(2,1)}, bf16[1536,384]{1,0:T(8,128)(2,1)}, u32[]{:S(2)}, u32[]{:S(2)}) collective-permute-start(bf16[1536,384]{1,0:T(8,128)(2,1)} %all-gather.7.cloned.1.call-done.refs_12_), channel_id=1, source_target_pairs={{0,192},{1,193},{2,194},{3,195},{4,196},{5,197},{6,198},{7,199},{8... | collective-permute-start | bytes 3538952 | tf_op jit(solution)/shard_map/ppermute | solution.py:56
  179.1 38.0 %collective-permute-start.15 = (bf16[1536,384]{1,0:T(8,128)(2,1)}, bf16[1536,384]{1,0:T(8,128)(2,1)S(1)}, u32[]{:S(2)}, u32[]{:S(2)}) collective-permute-start(bf16[1536,384]{1,0:T(8,128)(2,1)} %all-gather.9.cloned.1.call-done.refs_13_), channel_id=1, source_target_pairs={{0,64},{1,65},{2,66},{3,67},{4,68},{5,69},{6,70},{7,71},{8,72},{9,... | collective-permute-start | bytes 3538952 | tf_op jit(solution)/shard_map/ppermute | solution.py:56
  180.3 1.1 copy-start
  181.5 1.3 copy-start.2
  182.7 1.1 copy-start.1
  182.7 1.5 copy-start.5
  182.7 1.9 copy-start.6
  182.7 1.9 copy-start.19
  184.6 1.1 copy-start.8
  185.7 1.1 copy-start.11
  186.9 1.1 copy-start.14
  188.0 1.1 copy-start.17
  202.6 12.9 %copy-start.3 = (bf16[1536,384]{1,0:T(8,128)(2,1)S(1)}, bf16[1536,384]{1,0:T(8,128)(2,1)}, u32[]{:S(2)}) copy-start(bf16[1536,384]{1,0:T(8,128)(2,1)} %all-gather.11.cloned.1.call-done.w0) | copy-start | bytes 3538948
  210.9 6.3 %copy-start.9 = (bf16[256,1536]{1,0:T(8,128)(2,1)S(1)}, bf16[256,1536]{1,0:T(8,128)(2,1)}, u32[]{:S(2)}) copy-start(bf16[256,1536]{1,0:T(8,128)(2,1)} %copy-done.7) | copy-start | bytes 2359300
  210.9 6.3 %copy-start.12 = (bf16[256,1536]{1,0:T(8,128)(2,1)S(1)}, bf16[256,1536]{1,0:T(8,128)(2,1)}, u32[]{:S(2)}) copy-start(bf16[256,1536]{1,0:T(8,128)(2,1)} %copy-done.10) | copy-start | bytes 2359300
  210.9 6.3 %copy-start.15 = (bf16[256,1536]{1,0:T(8,128)(2,1)S(1)}, bf16[256,1536]{1,0:T(8,128)(2,1)}, u32[]{:S(2)}) copy-start(bf16[256,1536]{1,0:T(8,128)(2,1)} %copy-done.13) | copy-start | bytes 2359300
  210.9 6.3 %copy-start.18 = (bf16[256,1536]{1,0:T(8,128)(2,1)S(1)}, bf16[256,1536]{1,0:T(8,128)(2,1)}, u32[]{:S(2)}) copy-start(bf16[256,1536]{1,0:T(8,128)(2,1)} %copy-done.16) | copy-start | bytes 2359300
  210.9 29.0 %collective-permute-start.16 = (bf16[256,384]{1,0:T(8,128)(2,1)}, bf16[256,384]{1,0:T(8,128)(2,1)S(1)}, u32[]{:S(2)}, u32[]{:S(2)}) collective-permute-start(bf16[256,384]{1,0:T(8,128)(2,1)} %get-tuple-element.22), channel_id=1, source_target_pairs={{0,1},{1,0},{2,3},{3,2},{4,5},{5,4},{6,7},{7,6},{8,9},{9,8},{10,11... | collective-permute-start | bytes 589832 | tf_op jit(solution)/shard_map/ppermute | solution.py:56
  215.6 24.3 %collective-permute-start.19 = (bf16[1536,384]{1,0:T(8,128)(2,1)S(1)}, bf16[1536,384]{1,0:T(8,128)(2,1)}, u32[]{:S(2)}, u32[]{:S(2)}) collective-permute-start(bf16[1536,384]{1,0:T(8,128)(2,1)S(1)} %copy-done.3), channel_id=1, source_target_pairs={{0,1},{1,0},{2,3},{3,2},{4,5},{5,4},{6,7},{7,6},{8,9},{9,8},{10,11... | collective-permute-start | bytes 3538952 | tf_op jit(solution)/shard_map/ppermute | solution.py:56
  215.7 25.4 %collective-permute-start.20 = (bf16[1536,384]{1,0:T(8,128)(2,1)}, bf16[1536,384]{1,0:T(8,128)(2,1)}, u32[]{:S(2)}, u32[]{:S(2)}) collective-permute-start(bf16[1536,384]{1,0:T(8,128)(2,1)} %collective-permute-done.18.w1), channel_id=1, source_target_pairs={{0,1},{1,0},{2,3},{3,2},{4,5},{5,4},{6,7},{7,6},{8,9},{9,8},{10,11... | collective-permute-start | bytes 3538952 | tf_op jit(solution)/shard_map/ppermute | solution.py:56
  232.0 7.8 %copy-start.22 = (f32[1536]{0:T(1024)S(1)}, f32[1536]{0:T(1024)}, u32[]{:S(2)}) copy-start(f32[1536]{0:T(1024)} %param.11) | copy-start | bytes 18436
  239.6 1.5 collective-permute-start.17
Sparse Core Ops, SparseCore 0:
  23.5 38.1 all-gather.4
  63.4 37.2 all-gather.10
  102.5 37.6 all-gather.6
  141.9 37.2 all-gather.8

commit v2 on v1

--- a/solution.py
+++ b/solution.py
@@ -91,10 +91,16 @@
     return (raw * lax.rsqrt(jnp.mean(raw * raw, axis=-1, keepdims=True) + EPS) * gain).astype(BF)
 
 
-def kv_kernel(n, *refs):
-    tiles = refs[:n]
-    wk_ref, wv_ref, gain_ref, k_ref, v_ref, buf, sem = refs[n:]
+def qkv_kernel(n, m, mine, at_ref, *refs):
+    tiles, blocks = (refs[:n], refs[n : n + m])
+    qg_ref, kg_ref, q_ref, k_ref, v_ref, buf, weight, sem, wsem = refs[n + m :]
     i = pl.program_id(0)
+    deep = weight.shape[0] // m
+
+    def copies():
+        for j, block in enumerate(blocks):
+            rows = pl.ds(pl.multiple_of(at_ref[j] * deep, deep), deep)
+            yield pltpu.make_async_copy(block, weight.at[rows], wsem.at[j])
 
     def fetch(j, slot):
         for t in range(n):
@@ -105,7 +111,11 @@
 
     @pl.when(i == 0)
     def _():
+        for copy in copies():
+            copy.start()
         fetch(i, 0)
+        for copy in copies():
+            copy.wait()
 
     slot = lax.rem(i, 2)
 
@@ -115,53 +125,45 @@
 
     pltpu.make_async_copy(tiles[0], buf.at[slot], sem.at[slot]).wait()
     x = buf[slot]
-    raw = jnp.dot(x, wk_ref[...], preferred_element_type=F32)
+    raw = jnp.dot(x, weight[:, : 2 * HALF], preferred_element_type=F32)
     for h in range(3):
-        k_ref[h] = head_norm(raw[:, h * HD : (h + 1) * HD], gain_ref[...])
-    raw = jnp.dot(x, wv_ref[...], preferred_element_type=F32)
-    for h in range(3):
-        v_ref[h] = raw[:, h * HD : (h + 1) * HD].astype(BF)
-
-
-def keys_values(tiles, wk, wv, gain):
-    n = len(tiles)
+        k_ref[h] = head_norm(raw[:, h * HD : (h + 1) * HD], kg_ref[...])
+        v_ref[h] = raw[:, HALF + h * HD : HALF + (h + 1) * HD].astype(BF)
+
+    @pl.when(jnp.logical_or(i == mine[0], i == mine[1]))
+    def _():
+        t = jnp.where(i == mine[0], 0, 1)
+        raw = jnp.dot(buf[slot], weight[:, 2 * HALF :], preferred_element_type=F32)
+        for h in range(3):
+            q_ref[t, h] = head_norm(raw[:, h * HD : (h + 1) * HD], qg_ref[...])
+
+
+def project_in(at, tiles, blocks, q_gain, k_gain, mine):
+    n, m = (len(tiles), len(blocks))
     rows, width = tiles[0].shape
+    hbm = pl.BlockSpec(memory_space=pltpu.HBM)
     return pl.pallas_call(
-        functools.partial(kv_kernel, n),
-        out_shape=[jax.ShapeDtypeStruct((3, n * rows, HD), BF)] * 2,
+        functools.partial(qkv_kernel, n, m, mine),
+        out_shape=[jax.ShapeDtypeStruct((2, 3, rows, HD), BF)]
+        + [jax.ShapeDtypeStruct((3, n * rows, HD), BF)] * 2,
         grid=(n,),
-        in_specs=[pl.BlockSpec(memory_space=pl.ANY)] * n
-        + [
-            pl.BlockSpec((width, HALF), lambda i: (0, 0)),
-            pl.BlockSpec((width, HALF), lambda i: (0, 0)),
-            pl.BlockSpec((1, HD), lambda i: (0, 0)),
+        in_specs=[pl.BlockSpec(memory_space=pltpu.SMEM)]
+        + [hbm] * (n + m)
+        + [pl.BlockSpec((1, HD), lambda i: (0, 0))] * 2,
+        out_specs=[pl.BlockSpec((2, 3, rows, HD), lambda i: (0, 0, 0, 0))]
+        + [pl.BlockSpec((3, rows, HD), lambda i: (0, i, 0))] * 2,
+        scratch_shapes=[
+            pltpu.VMEM((2, rows, width), BF),
+            pltpu.VMEM((width, 3 * HALF), BF),
+            pltpu.SemaphoreType.DMA((2,)),
+            pltpu.SemaphoreType.DMA((m,)),
         ],
-        out_specs=[pl.BlockSpec((3, rows, HD), lambda i: (0, i, 0))] * 2,
-        scratch_shapes=[pltpu.VMEM((2, rows, width), BF), pltpu.SemaphoreType.DMA((2,))],
-        compiler_params=pltpu.CompilerParams(vmem_limit_bytes=24 << 20),
-        cost_estimate=cost(2 * n * rows * width * 2 * HALF, n * rows * (width + 2 * HALF) * 2),
-        name="keys_values",
-    )(*tiles, wk, wv, gain)
-
-
-def query_kernel(x0_ref, x1_ref, w_ref, gain_ref, o_ref):
-    for t, x_ref in enumerate((x0_ref, x1_ref)):
-        raw = jnp.dot(x_ref[...], w_ref[...], preferred_element_type=F32)
-        for h in range(3):
-            o_ref[t, h] = head_norm(raw[:, h * HD : (h + 1) * HD], gain_ref[...])
-
-
-def queries(x0, x1, wq, gain):
-    rows, width = x0.shape
-    return pl.pallas_call(
-        query_kernel,
-        out_shape=jax.ShapeDtypeStruct((2, 3, rows, HD), BF),
-        in_specs=[pl.BlockSpec(memory_space=pltpu.VMEM)] * 4,
-        out_specs=pl.BlockSpec(memory_space=pltpu.VMEM),
-        compiler_params=pltpu.CompilerParams(vmem_limit_bytes=16 << 20),
-        cost_estimate=cost(4 * rows * width * HALF, rows * (2 * width + 2 * HALF) * 2 + width * HALF * 2),
-        name="queries",
-    )(x0, x1, wq, gain)
+        compiler_params=pltpu.CompilerParams(vmem_limit_bytes=20 << 20),
+        cost_estimate=cost(
+            2 * (n * 2 + 2) * rows * width * HALF, (n * rows * (width + 2 * HALF) + width * 3 * HALF) * 2
+        ),
+        name="project_in",
+    )(at, *tiles, *blocks, q_gain, k_gain)
 
 
 def attend_kernel(far_ref, q_ref, k_ref, v_ref, o_ref):
@@ -205,35 +207,36 @@
             ],
             out_specs=pl.BlockSpec((1, rows, HD), lambda h, t, far: (t, 0, h)),
         ),
-        compiler_params=pltpu.CompilerParams(vmem_limit_bytes=32 << 20),
+        compiler_params=pltpu.CompilerParams(vmem_limit_bytes=20 << 20),
         cost_estimate=cost(6 * rows * window * HD * 4, 6 * keys * HD * 2 * 2, 6 * rows * window),
         name="attend",
     )(far, q, k, v)
 
 
-def project_kernel(at_ref, a0, a1, a2, a3, w0, w1, w2, w3, gate_ref, o_ref, left):
+def project_kernel(c_ref, at_ref, a0, a1, a2, a3, w0, w1, gate_ref, o_ref, left):
     for j, a in enumerate((a0, a1, a2, a3)):
         left[:, pl.ds(pl.multiple_of(at_ref[j] * HALF, HD), HALF)] = a[...]
-    for j, w in enumerate((w0, w1, w2, w3)):
-        cols = pl.ds(pl.multiple_of(at_ref[j] * HALF, HD), HALF)
+    for j, w in enumerate((w0, w1)):
+        side = c_ref[0] if j == 0 else 1 - c_ref[0]
+        cols = pl.ds(pl.multiple_of(side * 2 * HALF, HD), 2 * HALF)
         out = jnp.dot(left[...], w[...], preferred_element_type=F32)
         o_ref[:, cols] = (gate_ref[:, cols] * out).astype(BF)
 
 
-def project(at, attended, pieces, gate):
+def project_out(c, at, attended, pieces, gate):
     rows = attended[0].shape[0]
     width = pieces[0].shape[0]
     vmem = pl.BlockSpec(memory_space=pltpu.VMEM)
     return pl.pallas_call(
         project_kernel,
         out_shape=jax.ShapeDtypeStruct((rows, 4 * HALF), BF),
-        in_specs=[pl.BlockSpec(memory_space=pltpu.SMEM)] + [vmem] * 9,
+        in_specs=[pl.BlockSpec(memory_space=pltpu.SMEM)] * 2 + [vmem] * 7,
         out_specs=vmem,
         scratch_shapes=[pltpu.VMEM((rows, width), BF)],
         compiler_params=pltpu.CompilerParams(vmem_limit_bytes=24 << 20),
         cost_estimate=cost(2 * rows * width * 4 * HALF, width * 4 * HALF * 2 + rows * width * 4),
-        name="project",
-    )(at, *attended, *pieces, gate.reshape(1, -1))
+        name="project_out",
+    )(c, at, *attended, *pieces, gate.reshape(1, -1))
 
 
 def shards(tokens, shift, scale, gate, qkv_weight, out_weight, q_gain, k_gain):
@@ -244,25 +247,23 @@
     h = x * 2 + l
     w = z * 2 + u
 
-    parts = [qkv_weight[:, width : 2 * width], qkv_weight[:, 2 * width :], qkv_weight[:, :width], out_weight]
-    mine = jnp.concatenate(
-        [lax.dynamic_slice_in_dim(m, (c * 2 + parity) * HALF, HALF, 1) for m in parts], axis=1
-    )
-    theirs = jnp.concatenate(
-        [lax.dynamic_slice_in_dim(m, ((1 - c) * 2 + parity) * HALF, HALF, 1) for m in parts], axis=1
-    )
-    other = send(theirs, SIBLING)
+    def columns(core):
+        at = (core * 2 + parity) * HALF
+        parts = [lax.dynamic_slice_in_dim(qkv_weight, i * width + at, HALF, 1) for i in (1, 2, 0)]
+        parts.append(lax.dynamic_slice_in_dim(out_weight, core * 2 * HALF, 2 * HALF, 1))
+        return jnp.concatenate(parts, axis=1)
+
+    mine, other = columns(c), send(columns(1 - c), SIBLING)
     pair = jnp.where(c == 0, jnp.concatenate([mine, other]), jnp.concatenate([other, mine]))
     other = send(pair, Y_FLIP)
+    flat, pair = lax.optimization_barrier((tokens.reshape(count, width), pair))
+    own = modulate(flat, scale, shift)
+    own, other = lax.optimization_barrier((own, other))
     quad = jnp.where(u == 0, jnp.concatenate([pair, other]), jnp.concatenate([other, pair]))
-    wk, wv, wq, wo = (
-        lax.all_gather(quad[:, i * HALF : (i + 1) * HALF], "z", axis=0, tiled=True) for i in range(4)
-    )
-    wk2, wv2 = send(wk, X_DOWN), send(wv, X_UP)
-    wq2, wo2 = send(wq, X_DOWN), send(wo, X_UP)
-    wo3, wo4 = send(wo, SIBLING), send(wo2, SIBLING)
-
-    own = modulate(tokens.reshape(count, width), scale, shift)
+    w_in = lax.all_gather(quad[:, : 3 * HALF], "z", axis=0, tiled=True)
+    w_out = lax.all_gather(quad[:, 3 * HALF :], "z", axis=0, tiled=True)
+    w_in2 = [send(w_in[: width // 2], X_DOWN), send(w_in[width // 2 :], X_UP)]
+
     below, above = send(own, H_UP), send(own, H_DOWN)
     side, side_below, side_above = send(own, SIDE), send(own, SIDE_UP), send(own, SIDE_DOWN)
     outer = [side_below, side, side_above]
@@ -275,18 +276,19 @@
     row_ok = [h > 0, True, h < 7]
     far = jnp.stack([jnp.where(jnp.logical_and(a, b), 0.0, FAR).astype(F32) for a in col_ok for b in row_ok])
 
-    q_gain, k_gain = q_gain.reshape(1, HD), k_gain.reshape(1, HD)
-    k, v = keys_values(tiles, wk, wv, k_gain)
-    q = queries(own, inner2[1], wq, q_gain)
+    gains = (q_gain.reshape(1, HD), k_gain.reshape(1, HD))
+    q, k, v = project_in(jnp.arange(1, dtype=jnp.int32), tiles, [w_in], *gains, (4, 7))
     first = attend(far, q, k, v)
     first2 = send(first[1], SIBLING)
-    k, v = keys_values(tiles, wk2, wv2, k_gain)
-    q = queries(own, inner2[1], wq2, q_gain)
+    q, k, v = project_in(jnp.arange(2, dtype=jnp.int32), tiles, w_in2, *gains, (4, 7))
+    q, w_out = lax.optimization_barrier((q, w_out))
+    w_out2 = send(w_out, SIBLING)
     second = attend(far, q, k, v)
     second2 = send(second[1], SIBLING)
 
     at = jnp.stack([c * 2 + parity, c * 2 + 1 - parity, (1 - c) * 2 + parity, (1 - c) * 2 + 1 - parity])
-    out = project(at.astype(jnp.int32), [first[0], second[0], first2, second2], [wo, wo2, wo3, wo4], gate)
+    attended = [first[0], second[0], first2, second2]
+    out = project_out(c.reshape(1), at.astype(jnp.int32), attended, [w_out, w_out2], gate)
     return out.reshape(frames, tile_h, tile_w, width)
 
 

time: 253 us -> 224 us (0.89)
  waiting for transfers between devices: 141 us -> 98.9 us
  local copies, waits for them, and re-layouts: 16.2 us -> 34.7 us
  starting transfers between devices: 27.4 us -> 23.7 us
    all_gather x4 -> x2, waiting for transfers between devices: 80.7 us -> 56.2 us  [the longest x1 56.2 us: shards(): w_in = lax.all_gather(quad[:, :3 * HALF], 'z', axis=0, tiled=True)]
    ppermute x21 -> x18, waiting for transfers between devices: 59.1 us -> 42.7 us  [send(): return lax.ppermute(x, AXES, pairs)]
    unnamed x46 -> x74, local copies, waits for them, and re-layouts: 11.4 us -> 27.6 us
    ppermute x21 -> x18, starting transfers between devices: 27.3 us -> 23.6 us  [send(): return lax.ppermute(x, AXES, pairs)]
    pallas_call x5 -> x3, Pallas kernels: 35.1 us -> 33 us  [the longest x2 29 us: project_in(): pl.pallas_call(functools.partial(qkv_kernel, n, m, mine), out_shape=[jax....]
  transfers between devices with their start and end apart: 25 -> 20, of which waited for: 10 -> 9; matrix products, arithmetic and copies ran while one was open for 1% -> 2% of each run, Pallas kernels for 19% -> 21%
where the time goes in v2:
time: 224 us; the launch traced here: 223 us
  waiting for transfers between devices  98.9 us (44%)
  Pallas kernels  51.6 us (23%)
  local copies, waits for them, and re-layouts  34.7 us (15%)
  starting transfers between devices  23.7 us (11%)
  between operations  13.7 us (6%)
    all_gather x1, waiting for transfers between devices, shards(): w_in = lax.all_gather(quad[:, :3 * HALF], 'z', axis=0, tiled=True)  56.2 us
    ppermute x18, waiting for transfers between devices, send(): return lax.ppermute(x, AXES, pairs)  42.7 us
    pallas_call x2, Pallas kernels, project_in(): pl.pallas_call(functools.partial(qkv_kernel, n, m, mine), out_shape=[jax....  29 us
    unnamed x74, local copies, waits for them, and re-layouts  27.6 us
    ppermute x18, starting transfers between devices, send(): return lax.ppermute(x, AXES, pairs)  23.6 us
    pallas_call x2, Pallas kernels, attend(): pl.pallas_call(attend_kernel, out_shape=jax.ShapeDtypeStruct((2, rows, HA...  14.9 us
  transfers between devices with their start and end apart: 20, of which 9 were waited for; matrix products, arithmetic and copies ran while one was open for 2% of the time, Pallas kernels for 21%

profile of v2, /device:TPU:1, one launch (start us, length us, event | category | flops | bytes accessed | tf_op | source)
XLA Modules:
  0.0 222.8 jit_solution(12170696756386408382)
XLA Ops:
  6.5 1.0 constant_dynamic-slice_fusion.4
  7.5 0.9 constant_dynamic-slice_fusion.7
  8.4 3.3 %collective-permute-start = (bf16[48,1920]{1,0:T(8,128)(2,1)S(1)}, bf16[48,1920]{1,0:T(8,128)(2,1)S(1)}, u32[]{:S(2)}, u32[]{:S(2)}) collective-permute-start(bf16[48,1920]{1,0:T(8,128)(2,1)S(1)} %pad_maximum_fusion), channel_id=1, source_target_pairs={{0,1},{1,0},{2,3},{3,2},{4,5},{5,4},{6,7},{7,6},{8,9},{9,8},{10,11... | collective-permute-start | bytes 552968 | tf_op jit(solution)/shard_map/ppermute | solution.py:56
  11.8 1.1 collective-permute-done
  12.9 1.1 collective-permute-start.1
  14.0 0.6 reshape.26.scale_ref
  14.6 0.6 reshape.27.shift_ref
  15.2 3.7 %modulate.1.refs_4_ = bf16[256,1536]{1,0:T(8,128)(2,1)} custom-call(bf16[256,1536]{1,0:T(8,128)(2,1)} %bitcast.29, f32[1,1536]{1,0:T(1,128)} %reshape.26.scale_ref, f32[1,1536]{1,0:T(1,128)} %reshape.27.shift_ref), custom_call_target="tpu_custom_call" | custom-call | flops 3145728 | bytes 1572864 | tf_op jit(solution)/shard_map/modulate/pallas_call | solution.py:75
  18.9 5.1 %collective-permute-done.1 = bf16[96,1920]{1,0:T(8,128)(2,1)S(1)} collective-permute-done((bf16[96,1920]{1,0:T(8,128)(2,1)S(1)}, bf16[96,1920]{1,0:T(8,128)(2,1)S(1)}, u32[]{:S(2)}, u32[]{:S(2)}) %collective-permute-start.1) | collective-permute-done | bytes 368672 | tf_op jit(solution)/shard_map/ppermute | solution.py:56
  24.0 0.1 maximum_select_fusion
  24.1 0.8 slice.32
  25.0 0.7 slice.36
  25.8 2.2 collective-permute-start.2
  28.0 3.4 %collective-permute-start.4 = (bf16[256,1536]{1,0:T(8,128)(2,1)S(1)}, bf16[256,1536]{1,0:T(8,128)(2,1)S(1)}, u32[]{:S(2)}, u32[]{:S(2)}) collective-permute-start(bf16[256,1536]{1,0:T(8,128)(2,1)S(1)} %copy-done.2), channel_id=1, source_target_pairs={{0,255},{1,226},{2,225},{3,228},{4,227},{5,230},{6,229},{7,232},{8... | collective-permute-start | bytes 2359304 | tf_op jit(solution)/shard_map/ppermute | solution.py:56
  31.4 3.6 %collective-permute-start.6 = (bf16[256,1536]{1,0:T(8,128)(2,1)S(1)}, bf16[256,1536]{1,0:T(8,128)(2,1)}, u32[]{:S(2)}, u32[]{:S(2)}) collective-permute-start(bf16[256,1536]{1,0:T(8,128)(2,1)S(1)} %copy-done.2), channel_id=1, source_target_pairs={{0,224},{1,225},{2,226},{3,227},{4,228},{5,229},{6,230},{7,231},{8... | collective-permute-start | bytes 2359304 | tf_op jit(solution)/shard_map/ppermute | solution.py:56
  35.0 56.2 %all-gather.3.cloned.1.call-done.refs_12_ = bf16[1536,1152]{1,0:T(8,128)(2,1)} async-done(((bf16[192,1152]{1,0:T(8,128)(2,1)}), bf16[1536,1152]{1,0:T(8,128)(2,1)}) %all-gather.3.cloned.1.call-update) | async-done | bytes 3538960 | tf_op jit(solution)/shard_map/all_gather | solution.py:263
  91.1 2.3 %fusion = (bf16[768,1152]{1,0:T(8,128)(2,1)S(1)}, bf16[768,1152]{1,0:T(8,128)(2,1)S(1)}) fusion(bf16[1536,1152]{1,0:T(8,128)(2,1)} %all-gather.3.cloned.1.call-done.refs_12_), kind=kLoop, calls=%fused_computation.16 | loop fusion | bytes 7077888 | tf_op jit(solution)/shard_map/slice | solution.py:265
  93.4 5.4 %collective-permute-start.13 = (bf16[768,1152]{1,0:T(8,128)(2,1)S(1)}, bf16[768,1152]{1,0:T(8,128)(2,1)S(1)}, u32[]{:S(2)}, u32[]{:S(2)}) collective-permute-start(bf16[768,1152]{1,0:T(8,128)(2,1)S(1)} %get-tuple-element.30), channel_id=1, source_target_pairs={{0,192},{1,193},{2,194},{3,195},{4,196},{5,197},{6,198},{7,199},{8... | collective-permute-start | bytes 5308424 | tf_op jit(solution)/shard_map/ppermute | solution.py:56
  98.8 0.8 collective-permute-start.8
  99.7 0.1 collective-permute-start.7
  99.8 0.4 collective-permute-start.9
  100.2 1.4 collective-permute-done.8.refs_7_
  101.6 0.4 collective-permute-start.10
  102.0 0.9 copy-done.5
  102.9 0.4 collective-permute-start.11
  103.3 0.9 copy-done.8
  104.2 0.2 collective-permute-start.12
  104.4 0.9 copy-done.11
  105.3 0.8 collective-permute-done.11.refs_10_
  106.1 1.1 collective-permute-done.12.refs_11_
  107.2 29.1 %collective-permute-done.13.refs_12_ = bf16[768,1152]{1,0:T(8,128)(2,1)S(1)} collective-permute-done((bf16[768,1152]{1,0:T(8,128)(2,1)S(1)}, bf16[768,1152]{1,0:T(8,128)(2,1)S(1)}, u32[]{:S(2)}, u32[]{:S(2)}) %collective-permute-start.13) | collective-permute-done | bytes 1769504 | tf_op jit(solution)/shard_map/ppermute | solution.py:56
  136.3 3.1 %collective-permute-done.14.refs_13_ = bf16[768,1152]{1,0:T(8,128)(2,1)S(1)} collective-permute-done((bf16[768,1152]{1,0:T(8,128)(2,1)S(1)}, bf16[768,1152]{1,0:T(8,128)(2,1)S(1)}, u32[]{:S(2)}, u32[]{:S(2)}) %collective-permute-start.14) | collective-permute-done | bytes 1769504 | tf_op jit(solution)/shard_map/ppermute | solution.py:56
  139.4 1.1 copy-done.3
  140.6 1.1 copy-done.6
  141.7 1.1 copy-done.9
  142.8 1.1 copy-done.12
  144.0 15.0 %project_in.3 = (bf16[2,3,256,128]{3,2,1,0:T(8,128)(2,1)S(1)}, bf16[3,3072,128]{2,1,0:T(8,128)(2,1)S(1)}, bf16[3,3072,128]{2,1,0:T(8,128)(2,1)S(1)}) custom-call(s32[2]{0:T(128)S(1)} %iota.3.at_ref, bf16[256,1536]{1,0:T(8,128)(2,1)S(1)} %copy-done.6, bf16[256,1536]{1,0:T(8,128)(2,1)S(1)} %copy-done.9, bf16[256,1536]{1,0:T(8,128)(2,1)S(1)} %copy-done.12, ...), custom_call_target="tpu_custom_call" | custom-call | flops 7851737088 | bytes 17694720 | tf_op jit(solution)/shard_map/project_in/pallas_call | solution.py:145
  159.0 0.9 copy-done.14
  159.9 0.9 copy-done.16
  160.8 0.9 copy-done.18
  161.7 0.9 copy-done.20
  162.6 0.9 copy-done.22
  163.5 0.9 copy-done.24
  164.4 1.4 copy-done.28
  165.8 1.5 copy-done.30
  167.3 0.7 copy-done.32
  168.1 1.6 collective-permute-start.17
  169.8 1.1 copy-done.4
  170.9 1.1 copy-done.7
  172.1 1.1 copy-done.10
  173.2 1.1 copy-done.13
  174.3 1.1 copy-done.15
  175.5 1.1 copy-done.17
  176.6 1.1 copy-done.19
  177.7 1.1 copy-done.21
  178.9 1.1 copy-done.23
  180.0 1.1 copy-done.25
  181.1 14.0 %project_in.2 = (bf16[2,3,256,128]{3,2,1,0:T(8,128)(2,1)S(1)}, bf16[3,3072,128]{2,1,0:T(8,128)(2,1)S(1)}, bf16[3,3072,128]{2,1,0:T(8,128)(2,1)S(1)}) custom-call(s32[1]{0:T(128)} %constant.51.clone.1.at_ref, bf16[256,1536]{1,0:T(8,128)(2,1)S(1)} %copy-done.7, bf16[256,1536]{1,0:T(8,128)(2,1)S(1)} %copy-done.10, bf16[256,1536]{1,0:T(8,128)(2,1)S(1)} %copy-done.13, ...), custom_call_target="tpu_custom_call" | custom-call | flops 7851737088 | bytes 17694720 | tf_op jit(solution)/shard_map/project_in/pallas_call | solution.py:145
  195.2 7.4 %attend.2 = bf16[2,256,384]{2,1,0:T(8,128)(2,1)S(1)} custom-call(f32[12]{0:T(128)S(1)} %stack.59.far_ref, bf16[2,3,256,128]{3,2,1,0:T(8,128)(2,1)S(1)} %get-tuple-element.21.q_ref, bf16[3,3072,128]{2,1,0:T(8,128)(2,1)S(1)} %get-tuple-element.22.k_ref, bf16[3,3072,128]{2,1,0:T(8,128)(2,1)S(1)} %get-tuple-element.23.v_ref), custom_call_target="tpu_custom_call" | custom-call | flops 1811939328 | bytes 9437184 | tf_op jit(solution)/shard_map/attend/pallas_call | solution.py:197
  202.7 0.1 collective-permute-start.15
  202.9 7.4 %attend.3 = bf16[2,256,384]{2,1,0:T(8,128)(2,1)S(1)} custom-call(f32[12]{0:T(128)S(1)} %stack.59.far_ref, bf16[2,3,256,128]{3,2,1,0:T(8,128)(2,1)S(1)} %copy-done.33, bf16[3,3072,128]{2,1,0:T(8,128)(2,1)S(1)} %copy-done.29, bf16[3,3072,128]{2,1,0:T(8,128)(2,1)S(1)} %copy-done.31), custom_call_target="tpu_custom_call" | custom-call | flops 1811939328 | bytes 9437184 | tf_op jit(solution)/shard_map/attend/pallas_call | solution.py:197
  210.4 0.6 collective-permute-start.16
  211.0 1.0 collective-permute-done.16.a3
  212.0 4.0 %project_out.1 = bf16[256,1536]{1,0:T(8,128)(2,1)} custom-call(s32[1]{0:T(128)} %bitcast.c_ref, s32[4]{0:T(128)S(1)} %pad_add_fusion.at_ref, bf16[256,384]{1,0:T(8,128)(2,1)S(1)} %get-tuple-element.40.a0, bf16[256,384]{1,0:T(8,128)(2,1)S(1)} %get-tuple-element.38.a1, bf16[256,384]{1,0:T(8,128)(2,1)S(1)} %collective-permute-done.15.a2, ...), custom_call_target="tpu_custom_call" | custom-call | flops 1207959552 | bytes 6291456 | tf_op jit(solution)/shard_map/project_out/pallas_call | solution.py:230
  (74 shorter events, 0.6 us)
Async XLA Ops:
  6.5 7.4 %copy-start.34 = (f32[1536]{0:T(1024)S(1)}, f32[1536]{0:T(1024)}, u32[]{:S(2)}) copy-start(f32[1536]{0:T(1024)} %param.10) | copy-start | bytes 18436
  6.5 8.0 %copy-start.35 = (f32[1536]{0:T(1024)S(1)}, f32[1536]{0:T(1024)}, u32[]{:S(2)}) copy-start(f32[1536]{0:T(1024)} %param.9) | copy-start | bytes 18436
  6.5 84.6 %all-gather.3.cloned.1.call-start = ((), (), s32[]{:S(2)}) async-start(), calls=%async_computation | async-start | bytes 3981312 | tf_op jit(solution)/shard_map/all_gather | solution.py:263
  8.4 4.4 %collective-permute-start = (bf16[48,1920]{1,0:T(8,128)(2,1)S(1)}, bf16[48,1920]{1,0:T(8,128)(2,1)S(1)}, u32[]{:S(2)}, u32[]{:S(2)}) collective-permute-start(bf16[48,1920]{1,0:T(8,128)(2,1)S(1)} %pad_maximum_fusion), channel_id=1, source_target_pairs={{0,1},{1,0},{2,3},{3,2},{4,5},{5,4},{6,7},{7,6},{8,9},{9,8},{10,11... | collective-permute-start | bytes 552968 | tf_op jit(solution)/shard_map/ppermute | solution.py:56
  12.9 11.1 %collective-permute-start.1 = (bf16[96,1920]{1,0:T(8,128)(2,1)S(1)}, bf16[96,1920]{1,0:T(8,128)(2,1)S(1)}, u32[]{:S(2)}, u32[]{:S(2)}) collective-permute-start(bf16[96,1920]{1,0:T(8,128)(2,1)S(1)} %maximum_select_fusion.1), channel_id=1, source_target_pairs={{0,34},{1,35},{2,32},{3,33},{4,38},{5,39},{6,36},{7,37},{8,42},{9,... | collective-permute-start | bytes 1105928 | tf_op jit(solution)/shard_map/ppermute | solution.py:56
  18.9 6.9 %copy-start.2 = (bf16[256,1536]{1,0:T(8,128)(2,1)S(1)}, bf16[256,1536]{1,0:T(8,128)(2,1)}, u32[]{:S(2)}) copy-start(bf16[256,1536]{1,0:T(8,128)(2,1)} %modulate.1.refs_4_) | copy-start | bytes 2359300
  24.9 143.1 %all-gather.5.cloned.1.call-start = ((), (), s32[]{:S(2)}) async-start(), calls=%async_computation.1 | async-start | bytes 2654208 | tf_op jit(solution)/shard_map/all_gather | solution.py:264
  25.8 113.7 %copy-start.26 = (f32[128]{0:T(128)S(1)}, f32[128]{0:T(128)}, u32[]{:S(2)}) copy-start(f32[128]{0:T(128)} %param.14) | copy-start | bytes 1540
  25.8 113.7 %copy-start.27 = (f32[128]{0:T(128)S(1)}, f32[128]{0:T(128)}, u32[]{:S(2)}) copy-start(f32[128]{0:T(128)} %param.15) | copy-start | bytes 1540
  25.8 67.6 %collective-permute-start.2 = (bf16[256,1536]{1,0:T(8,128)(2,1)S(1)}, bf16[256,1536]{1,0:T(8,128)(2,1)S(1)}, u32[]{:S(2)}, u32[]{:S(2)}) collective-permute-start(bf16[256,1536]{1,0:T(8,128)(2,1)S(1)} %copy-done.2), channel_id=1, source_target_pairs={{0,63},{1,34},{2,33},{3,36},{4,35},{5,38},{6,37},{7,40},{8,39},{9,... | collective-permute-start | bytes 2359304 | tf_op jit(solution)/shard_map/ppermute | solution.py:56
  27.9 70.9 %collective-permute-start.3 = (bf16[256,1536]{1,0:T(8,128)(2,1)S(1)}, bf16[256,1536]{1,0:T(8,128)(2,1)S(1)}, u32[]{:S(2)}, u32[]{:S(2)}) collective-permute-start(bf16[256,1536]{1,0:T(8,128)(2,1)S(1)} %copy-done.2), channel_id=1, source_target_pairs={{0,31},{1,2},{2,1},{3,4},{4,3},{5,6},{6,5},{7,8},{8,7},{9,10},{10,... | collective-permute-start | bytes 2359304 | tf_op jit(solution)/shard_map/ppermute | solution.py:56
  28.0 70.9 %collective-permute-start.4 = (bf16[256,1536]{1,0:T(8,128)(2,1)S(1)}, bf16[256,1536]{1,0:T(8,128)(2,1)S(1)}, u32[]{:S(2)}, u32[]{:S(2)}) collective-permute-start(bf16[256,1536]{1,0:T(8,128)(2,1)S(1)} %copy-done.2), channel_id=1, source_target_pairs={{0,255},{1,226},{2,225},{3,228},{4,227},{5,230},{6,229},{7,232},{8... | collective-permute-start | bytes 2359304 | tf_op jit(solution)/shard_map/ppermute | solution.py:56
  31.4 68.3 %collective-permute-start.5 = (bf16[256,1536]{1,0:T(8,128)(2,1)S(1)}, bf16[256,1536]{1,0:T(8,128)(2,1)}, u32[]{:S(2)}, u32[]{:S(2)}) collective-permute-start(bf16[256,1536]{1,0:T(8,128)(2,1)S(1)} %copy-done.2), channel_id=1, source_target_pairs={{0,32},{1,33},{2,34},{3,35},{4,36},{5,37},{6,38},{7,39},{8,40},{9,... | collective-permute-start | bytes 2359304 | tf_op jit(solution)/shard_map/ppermute | solution.py:56
  31.4 68.4 %collective-permute-start.6 = (bf16[256,1536]{1,0:T(8,128)(2,1)S(1)}, bf16[256,1536]{1,0:T(8,128)(2,1)}, u32[]{:S(2)}, u32[]{:S(2)}) collective-permute-start(bf16[256,1536]{1,0:T(8,128)(2,1)S(1)} %copy-done.2), channel_id=1, source_target_pairs={{0,224},{1,225},{2,226},{3,227},{4,228},{5,229},{6,230},{7,231},{8... | collective-permute-start | bytes 2359304 | tf_op jit(solution)/shard_map/ppermute | solution.py:56
  93.4 42.9 %collective-permute-start.13 = (bf16[768,1152]{1,0:T(8,128)(2,1)S(1)}, bf16[768,1152]{1,0:T(8,128)(2,1)S(1)}, u32[]{:S(2)}, u32[]{:S(2)}) collective-permute-start(bf16[768,1152]{1,0:T(8,128)(2,1)S(1)} %get-tuple-element.30), channel_id=1, source_target_pairs={{0,192},{1,193},{2,194},{3,195},{4,196},{5,197},{6,198},{7,199},{8... | collective-permute-start | bytes 5308424 | tf_op jit(solution)/shard_map/ppermute | solution.py:56
  98.8 40.6 %collective-permute-start.14 = (bf16[768,1152]{1,0:T(8,128)(2,1)S(1)}, bf16[768,1152]{1,0:T(8,128)(2,1)S(1)}, u32[]{:S(2)}, u32[]{:S(2)}) collective-permute-start(bf16[768,1152]{1,0:T(8,128)(2,1)S(1)} %get-tuple-element.29), channel_id=1, source_target_pairs={{0,64},{1,65},{2,66},{3,67},{4,68},{5,69},{6,70},{7,71},{8,72},{9,... | collective-permute-start | bytes 5308424 | tf_op jit(solution)/shard_map/ppermute | solution.py:56
  98.8 2.8 %collective-permute-start.8 = (bf16[256,1536]{1,0:T(8,128)(2,1)S(1)}, bf16[256,1536]{1,0:T(8,128)(2,1)S(1)}, u32[]{:S(2)}, u32[]{:S(2)}) collective-permute-start(bf16[256,1536]{1,0:T(8,128)(2,1)S(1)} %copy-done.2), channel_id=1, source_target_pairs={{0,1},{1,0},{2,3},{3,2},{4,5},{5,4},{6,7},{7,6},{8,9},{9,8},{10,11... | collective-permute-start | bytes 2359304 | tf_op jit(solution)/shard_map/ppermute | solution.py:56
  99.7 3.2 %collective-permute-start.7 = (bf16[256,1536]{1,0:T(8,128)(2,1)}, bf16[256,1536]{1,0:T(8,128)(2,1)S(1)}, u32[]{:S(2)}, u32[]{:S(2)}) collective-permute-start(bf16[256,1536]{1,0:T(8,128)(2,1)} %collective-permute-done.5.refs_3_), channel_id=1, source_target_pairs={{0,1},{1,0},{2,3},{3,2},{4,5},{5,4},{6,7},{7,6},{8,9},{9,8},{10,11... | collective-permute-start | bytes 2359304 | tf_op jit(solution)/shard_map/ppermute | solution.py:56
  99.8 4.4 %collective-permute-start.9 = (bf16[256,1536]{1,0:T(8,128)(2,1)}, bf16[256,1536]{1,0:T(8,128)(2,1)S(1)}, u32[]{:S(2)}, u32[]{:S(2)}) collective-permute-start(bf16[256,1536]{1,0:T(8,128)(2,1)} %collective-permute-done.6.refs_5_), channel_id=1, source_target_pairs={{0,1},{1,0},{2,3},{3,2},{4,5},{5,4},{6,7},{7,6},{8,9},{9,8},{10,11... | collective-permute-start | bytes 2359304 | tf_op jit(solution)/shard_map/ppermute | solution.py:56
  101.6 3.7 %collective-permute-start.10 = (bf16[256,1536]{1,0:T(8,128)(2,1)S(1)}, bf16[256,1536]{1,0:T(8,128)(2,1)S(1)}, u32[]{:S(2)}, u32[]{:S(2)}) collective-permute-start(bf16[256,1536]{1,0:T(8,128)(2,1)S(1)} %collective-permute-done.2.refs_0_), channel_id=1, source_target_pairs={{0,1},{1,0},{2,3},{3,2},{4,5},{5,4},{6,7},{7,6},{8,9},{9,8},{10,11... | collective-permute-start | bytes 2359304 | tf_op jit(solution)/shard_map/ppermute | solution.py:56
  102.0 0.9 copy-start.5
  102.9 3.2 %collective-permute-start.11 = (bf16[256,1536]{1,0:T(8,128)(2,1)S(1)}, bf16[256,1536]{1,0:T(8,128)(2,1)S(1)}, u32[]{:S(2)}, u32[]{:S(2)}) collective-permute-start(bf16[256,1536]{1,0:T(8,128)(2,1)S(1)} %collective-permute-done.3.refs_1_), channel_id=1, source_target_pairs={{0,1},{1,0},{2,3},{3,2},{4,5},{5,4},{6,7},{7,6},{8,9},{9,8},{10,11... | collective-permute-start | bytes 2359304 | tf_op jit(solution)/shard_map/ppermute | solution.py:56
  103.3 0.9 copy-start.8
  104.2 3.0 %collective-permute-start.12 = (bf16[256,1536]{1,0:T(8,128)(2,1)S(1)}, bf16[256,1536]{1,0:T(8,128)(2,1)S(1)}, u32[]{:S(2)}, u32[]{:S(2)}) collective-permute-start(bf16[256,1536]{1,0:T(8,128)(2,1)S(1)} %collective-permute-done.4.refs_2_), channel_id=1, source_target_pairs={{0,1},{1,0},{2,3},{3,2},{4,5},{5,4},{6,7},{7,6},{8,9},{9,8},{10,11... | collective-permute-start | bytes 2359304 | tf_op jit(solution)/shard_map/ppermute | solution.py:56
  104.4 0.9 copy-start.11
  139.4 1.1 copy-start.3
  140.6 1.1 copy-start.6
  141.7 1.1 copy-start.9
  142.8 1.1 copy-start.12
  144.0 25.8 %copy-start = (bf16[1536,1152]{1,0:T(8,128)(2,1)S(1)}, bf16[1536,1152]{1,0:T(8,128)(2,1)}, u32[]{:S(2)}) copy-start(bf16[1536,1152]{1,0:T(8,128)(2,1)} %all-gather.3.cloned.1.call-done.refs_12_) | copy-start | bytes 10616836
  159.0 0.9 copy-start.14
  159.9 0.9 copy-start.16
  160.8 0.9 copy-start.18
  161.7 0.9 copy-start.20
  162.6 0.9 copy-start.22
  163.5 0.9 copy-start.24
  164.4 1.4 copy-start.28
  165.8 1.5 copy-start.30
  167.3 0.7 copy-start.32
  168.1 43.9 %collective-permute-start.17 = (bf16[1536,768]{1,0:T(8,128)(2,1)}, bf16[1536,768]{1,0:T(8,128)(2,1)}, u32[]{:S(2)}, u32[]{:S(2)}) collective-permute-start(bf16[1536,768]{1,0:T(8,128)(2,1)} %all-gather.5.cloned.1.call-done.w0), channel_id=1, source_target_pairs={{0,1},{1,0},{2,3},{3,2},{4,5},{5,4},{6,7},{7,6},{8,9},{9,8},{10,11... | collective-permute-start | bytes 7077896 | tf_op jit(solution)/shard_map/ppermute | solution.py:56
  169.8 1.1 copy-start.4
  170.9 1.1 copy-start.7
  172.1 1.1 copy-start.10
  173.2 1.1 copy-start.13
  174.3 1.1 copy-start.15
  175.5 1.1 copy-start.17
  176.6 1.1 copy-start.19
  177.7 1.1 copy-start.21
  178.9 1.1 copy-start.23
  180.0 1.1 copy-start.25
  195.2 7.6 %copy-start.29 = (bf16[3,3072,128]{2,1,0:T(8,128)(2,1)S(1)}, bf16[3,3072,128]{2,1,0:T(8,128)(2,1)}, u32[]{:S(2)}) copy-start(bf16[3,3072,128]{2,1,0:T(8,128)(2,1)} %copy-done.28) | copy-start | bytes 7077892
  195.2 7.6 %copy-start.31 = (bf16[3,3072,128]{2,1,0:T(8,128)(2,1)S(1)}, bf16[3,3072,128]{2,1,0:T(8,128)(2,1)}, u32[]{:S(2)}) copy-start(bf16[3,3072,128]{2,1,0:T(8,128)(2,1)} %copy-done.30) | copy-start | bytes 7077892
  195.2 7.6 %copy-start.33 = (bf16[2,3,256,128]{3,2,1,0:T(8,128)(2,1)S(1)}, bf16[2,3,256,128]{3,2,1,0:T(8,128)(2,1)}, u32[]{:S(2)}) copy-start(bf16[2,3,256,128]{3,2,1,0:T(8,128)(2,1)} %copy-done.32) | copy-start | bytes 1179652
  202.7 8.3 %collective-permute-start.15 = (bf16[256,384]{1,0:T(8,128)(2,1)S(1)}, bf16[256,384]{1,0:T(8,128)(2,1)S(1)}, u32[]{:S(2)}, u32[]{:S(2)}) collective-permute-start(bf16[256,384]{1,0:T(8,128)(2,1)S(1)} %get-tuple-element.39), channel_id=1, source_target_pairs={{0,1},{1,0},{2,3},{3,2},{4,5},{5,4},{6,7},{7,6},{8,9},{9,8},{10,11... | collective-permute-start | bytes 589832 | tf_op jit(solution)/shard_map/ppermute | solution.py:56
  202.8 8.1 %copy-start.36 = (f32[1536]{0:T(1024)S(1)}, f32[1536]{0:T(1024)}, u32[]{:S(2)}) copy-start(f32[1536]{0:T(1024)} %param.11) | copy-start | bytes 18436
  202.8 9.1 %copy-start.1 = (bf16[1536,768]{1,0:T(8,128)(2,1)S(1)}, bf16[1536,768]{1,0:T(8,128)(2,1)}, u32[]{:S(2)}) copy-start(bf16[1536,768]{1,0:T(8,128)(2,1)} %all-gather.5.cloned.1.call-done.w0) | copy-start | bytes 7077892
  210.4 1.6 collective-permute-start.16
Sparse Core Ops, SparseCore 0:
  25.1 66.0 all-gather.2
  92.9 39.2 all-gather.4

commit v3 on v2

--- a/solution.py
+++ b/solution.py
@@ -91,79 +91,87 @@
     return (raw * lax.rsqrt(jnp.mean(raw * raw, axis=-1, keepdims=True) + EPS) * gain).astype(BF)
 
 
-def qkv_kernel(n, m, mine, at_ref, *refs):
+def qkv_kernel(n, m, order_ref, at_ref, *refs):
     tiles, blocks = (refs[:n], refs[n : n + m])
     qg_ref, kg_ref, q_ref, k_ref, v_ref, buf, weight, sem, wsem = refs[n + m :]
     i = pl.program_id(0)
     deep = weight.shape[0] // m
+    rows = buf.shape[1] // 2
 
     def copies():
         for j, block in enumerate(blocks):
-            rows = pl.ds(pl.multiple_of(at_ref[j] * deep, deep), deep)
-            yield pltpu.make_async_copy(block, weight.at[rows], wsem.at[j])
-
-    def fetch(j, slot):
-        for t in range(n):
-
-            @pl.when(j == t)
-            def _():
-                pltpu.make_async_copy(tiles[t], buf.at[slot], sem.at[slot]).start()
+            to = pl.ds(pl.multiple_of(at_ref[j] * deep, deep), deep)
+            yield pltpu.make_async_copy(block, weight.at[to], wsem.at[j])
+
+    def fetch(step, slot):
+        for part in range(2):
+            which = order_ref[step * 2 + part]
+            for t in range(n):
+
+                @pl.when(which == t)
+                def _():
+                    to = buf.at[slot, pl.ds(part * rows, rows)]
+                    pltpu.make_async_copy(tiles[t], to, sem.at[slot, part]).start()
 
     @pl.when(i == 0)
     def _():
+        fetch(i, 0)
         for copy in copies():
             copy.start()
-        fetch(i, 0)
         for copy in copies():
             copy.wait()
 
     slot = lax.rem(i, 2)
 
-    @pl.when(i + 1 < n)
+    @pl.when(i + 1 < n // 2)
     def _():
         fetch(i + 1, 1 - slot)
 
-    pltpu.make_async_copy(tiles[0], buf.at[slot], sem.at[slot]).wait()
+    for part in range(2):
+        to = buf.at[slot, pl.ds(part * rows, rows)]
+        pltpu.make_async_copy(tiles[0], to, sem.at[slot, part]).wait()
     x = buf[slot]
     raw = jnp.dot(x, weight[:, : 2 * HALF], preferred_element_type=F32)
     for h in range(3):
         k_ref[h] = head_norm(raw[:, h * HD : (h + 1) * HD], kg_ref[...])
         v_ref[h] = raw[:, HALF + h * HD : HALF + (h + 1) * HD].astype(BF)
 
-    @pl.when(jnp.logical_or(i == mine[0], i == mine[1]))
-    def _():
-        t = jnp.where(i == mine[0], 0, 1)
-        raw = jnp.dot(buf[slot], weight[:, 2 * HALF :], preferred_element_type=F32)
-        for h in range(3):
-            q_ref[t, h] = head_norm(raw[:, h * HD : (h + 1) * HD], qg_ref[...])
-
-
-def project_in(at, tiles, blocks, q_gain, k_gain, mine):
+    for t, slots in enumerate((4, 7)):
+
+        @pl.when(i == slots // 2)
+        def _():
+            x = buf[slot, pl.ds(slots % 2 * rows, rows)]
+            raw = jnp.dot(x, weight[:, 2 * HALF :], preferred_element_type=F32)
+            for h in range(3):
+                q_ref[t, h] = head_norm(raw[:, h * HD : (h + 1) * HD], qg_ref[...])
+
+
+def project_in(order, at, tiles, blocks, q_gain, k_gain):
     n, m = (len(tiles), len(blocks))
     rows, width = tiles[0].shape
     hbm = pl.BlockSpec(memory_space=pltpu.HBM)
     return pl.pallas_call(
-        functools.partial(qkv_kernel, n, m, mine),
+        functools.partial(qkv_kernel, n, m),
         out_shape=[jax.ShapeDtypeStruct((2, 3, rows, HD), BF)]
         + [jax.ShapeDtypeStruct((3, n * rows, HD), BF)] * 2,
-        grid=(n,),
-        in_specs=[pl.BlockSpec(memory_space=pltpu.SMEM)]
+        grid=(n // 2,),
+        in_specs=[pl.BlockSpec(memory_space=pltpu.SMEM)] * 2
         + [hbm] * (n + m)
         + [pl.BlockSpec((1, HD), lambda i: (0, 0))] * 2,
         out_specs=[pl.BlockSpec((2, 3, rows, HD), lambda i: (0, 0, 0, 0))]
-        + [pl.BlockSpec((3, rows, HD), lambda i: (0, i, 0))] * 2,
+        + [pl.BlockSpec((3, 2 * rows, HD), lambda i: (0, i, 0))] * 2,
         scratch_shapes=[
-            pltpu.VMEM((2, rows, width), BF),
+            pltpu.VMEM((2, 2 * rows, width), BF),
             pltpu.VMEM((width, 3 * HALF), BF),
-            pltpu.SemaphoreType.DMA((2,)),
+            pltpu.SemaphoreType.DMA((2, 2)),
             pltpu.SemaphoreType.DMA((m,)),
         ],
-        compiler_params=pltpu.CompilerParams(vmem_limit_bytes=20 << 20),
+        compiler_params=pltpu.CompilerParams(vmem_limit_bytes=60 << 20),
         cost_estimate=cost(
             2 * (n * 2 + 2) * rows * width * HALF, (n * rows * (width + 2 * HALF) + width * 3 * HALF) * 2
         ),
         name="project_in",
-    )(at, *tiles, *blocks, q_gain, k_gain)
+    )(order, at, *tiles, *blocks, q_gain, k_gain)
 
 
 def attend_kernel(far_ref, q_ref, k_ref, v_ref, o_ref):
@@ -207,7 +215,7 @@
             ],
             out_specs=pl.BlockSpec((1, rows, HD), lambda h, t, far: (t, 0, h)),
         ),
-        compiler_params=pltpu.CompilerParams(vmem_limit_bytes=20 << 20),
+        compiler_params=pltpu.CompilerParams(vmem_limit_bytes=60 << 20),
         cost_estimate=cost(6 * rows * window * HD * 4, 6 * keys * HD * 2 * 2, 6 * rows * window),
         name="attend",
     )(far, q, k, v)
@@ -233,7 +241,7 @@
         in_specs=[pl.BlockSpec(memory_space=pltpu.SMEM)] * 2 + [vmem] * 7,
         out_specs=vmem,
         scratch_shapes=[pltpu.VMEM((rows, width), BF)],
-        compiler_params=pltpu.CompilerParams(vmem_limit_bytes=24 << 20),
+        compiler_params=pltpu.CompilerParams(vmem_limit_bytes=16 << 20),
         cost_estimate=cost(2 * rows * width * 4 * HALF, width * 4 * HALF * 2 + rows * width * 4),
         name="project_out",
     )(c, at, *attended, *pieces, gate.reshape(1, -1))
@@ -277,10 +285,12 @@
     far = jnp.stack([jnp.where(jnp.logical_and(a, b), 0.0, FAR).astype(F32) for a in col_ok for b in row_ok])
 
     gains = (q_gain.reshape(1, HD), k_gain.reshape(1, HD))
-    q, k, v = project_in(jnp.arange(1, dtype=jnp.int32), tiles, [w_in], *gains, (4, 7))
+    order = jnp.arange(12, dtype=jnp.int32)
+    q, k, v = project_in(order, jnp.arange(1, dtype=jnp.int32), tiles, [w_in], *gains)
     first = attend(far, q, k, v)
     first2 = send(first[1], SIBLING)
-    q, k, v = project_in(jnp.arange(2, dtype=jnp.int32), tiles, w_in2, *gains, (4, 7))
+    first, *w_in2 = lax.optimization_barrier((first, *w_in2))
+    q, k, v = project_in(order, jnp.arange(2, dtype=jnp.int32), tiles, w_in2, *gains)
     q, w_out = lax.optimization_barrier((q, w_out))
     w_out2 = send(w_out, SIBLING)
     second = attend(far, q, k, v)

time: 224 us -> 184 us (0.82)
  waiting for transfers between devices: 98.9 us -> 62.4 us
  local copies, waits for them, and re-layouts: 34.7 us -> 10.3 us
  starting transfers between devices: 23.7 us -> 38.4 us
  Pallas kernels: 51.6 us -> 58.4 us
    all_gather x1, waiting for transfers between devices: 56.2 us -> 0.01 us  [shards(): w_in = lax.all_gather(quad[:, :3 * HALF], 'z', axis=0, tiled=True)]
    unnamed x74 -> x10, local copies, waits for them, and re-layouts: 27.6 us -> 0.02 us
    ppermute x18, waiting for transfers between devices: 42.7 us -> 62.3 us  [send(): return lax.ppermute(x, AXES, pairs)]
    ppermute x18, starting transfers between devices: 23.6 us -> 38.4 us  [send(): return lax.ppermute(x, AXES, pairs)]
    pallas_call x2, Pallas kernels: 14.9 us -> 20.4 us  [attend(): pl.pallas_call(attend_kernel, out_shape=jax.ShapeDtypeStruct((2, rows, HA...]
  transfers between devices with their start and end apart: 20 -> 20, of which waited for: 9 -> 10; matrix products, arithmetic and copies ran while one was open for 2% -> 4% of each run, Pallas kernels for 21% -> 30%
where the time goes in v3:
time: 184 us; the launch traced here: 183 us
  waiting for transfers between devices  62.4 us (34%)
  Pallas kernels  58.4 us (32%)
  starting transfers between devices  38.4 us (21%)
  between operations  13.5 us (7%)
  local copies, waits for them, and re-layouts  10.3 us (6%)
    ppermute x18, waiting for transfers between devices, send(): return lax.ppermute(x, AXES, pairs)  62.3 us
    ppermute x18, starting transfers between devices, send(): return lax.ppermute(x, AXES, pairs)  38.4 us
    pallas_call x2, Pallas kernels, project_in(): pl.pallas_call(functools.partial(qkv_kernel, n, m), out_shape=[jax.ShapeD...  30.2 us
    pallas_call x2, Pallas kernels, attend(): pl.pallas_call(attend_kernel, out_shape=jax.ShapeDtypeStruct((2, rows, HA...  20.4 us
    pallas_call x1, Pallas kernels, project_out(): pl.pallas_call(project_kernel, out_shape=jax.ShapeDtypeStruct((rows, 4 *...  3.99 us
    pallas_call x1, Pallas kernels, modulate(): pl.pallas_call(modulate_kernel, out_shape=jax.ShapeDtypeStruct((rows, wid...  3.73 us
  transfers between devices with their start and end apart: 20, of which 10 were waited for; matrix products, arithmetic and copies ran while one was open for 4% of the time, Pallas kernels for 30%

profile of v3, /device:TPU:1, one launch (start us, length us, event | category | flops | bytes accessed | tf_op | source)
XLA Modules:
  0.0 183.3 jit_solution(10782996160687807889)
XLA Ops:
  6.5 0.0 all-gather.3.cloned.1.call-start
  6.5 1.0 constant_dynamic-slice_fusion.4
  7.5 0.9 constant_dynamic-slice_fusion.7
  8.4 3.3 %collective-permute-start = (bf16[48,1920]{1,0:T(8,128)(2,1)S(1)}, bf16[48,1920]{1,0:T(8,128)(2,1)S(1)}, u32[]{:S(2)}, u32[]{:S(2)}) collective-permute-start(bf16[48,1920]{1,0:T(8,128)(2,1)S(1)} %pad_maximum_fusion), channel_id=1, source_target_pairs={{0,1},{1,0},{2,3},{3,2},{4,5},{5,4},{6,7},{7,6},{8,9},{9,8},{10,11... | collective-permute-start | bytes 552968 | tf_op jit(solution)/shard_map/ppermute | solution.py:56
  11.8 1.1 collective-permute-done
  12.8 0.1 maximum_select_fusion.1
  12.9 1.1 collective-permute-start.1
  14.0 0.0 copy-done.2
  14.0 0.6 reshape.26.scale_ref
  14.6 0.6 reshape.27.shift_ref
  15.2 3.7 %modulate.1.refs_4_ = bf16[256,1536]{1,0:T(8,128)(2,1)} custom-call(bf16[256,1536]{1,0:T(8,128)(2,1)} %bitcast.25, f32[1,1536]{1,0:T(1,128)} %reshape.26.scale_ref, f32[1,1536]{1,0:T(1,128)} %reshape.27.shift_ref), custom_call_target="tpu_custom_call" | custom-call | flops 3145728 | bytes 1572864 | tf_op jit(solution)/shard_map/modulate/pallas_call | solution.py:75
  18.9 5.1 %collective-permute-done.1 = bf16[96,1920]{1,0:T(8,128)(2,1)S(1)} collective-permute-done((bf16[96,1920]{1,0:T(8,128)(2,1)S(1)}, bf16[96,1920]{1,0:T(8,128)(2,1)S(1)}, u32[]{:S(2)}, u32[]{:S(2)}) %collective-permute-start.1) | collective-permute-done | bytes 368672 | tf_op jit(solution)/shard_map/ppermute | solution.py:56
  24.0 0.1 maximum_select_fusion
  24.1 0.8 slice.32
  24.9 0.0 all-gather.3.cloned.1.call-update
  25.0 0.0 all-gather.5.cloned.1.call-start
  25.0 0.7 slice.35
  25.8 0.0 all-gather.5.cloned.1.call-update
  25.8 2.2 %collective-permute-start.2 = (bf16[256,1536]{1,0:T(8,128)(2,1)}, bf16[256,1536]{1,0:T(8,128)(2,1)}, u32[]{:S(2)}, u32[]{:S(2)}) collective-permute-start(bf16[256,1536]{1,0:T(8,128)(2,1)} %modulate.1.refs_4_), channel_id=1, source_target_pairs={{0,63},{1,34},{2,33},{3,36},{4,35},{5,38},{6,37},{7,40},{8,39},{9,... | collective-permute-start | bytes 2359304 | tf_op jit(solution)/shard_map/ppermute | solution.py:56
  27.9 0.0 collective-permute-start.3
  27.9 3.4 %collective-permute-start.4 = (bf16[256,1536]{1,0:T(8,128)(2,1)}, bf16[256,1536]{1,0:T(8,128)(2,1)}, u32[]{:S(2)}, u32[]{:S(2)}) collective-permute-start(bf16[256,1536]{1,0:T(8,128)(2,1)} %modulate.1.refs_4_), channel_id=1, source_target_pairs={{0,255},{1,226},{2,225},{3,228},{4,227},{5,230},{6,229},{7,232},{8... | collective-permute-start | bytes 2359304 | tf_op jit(solution)/shard_map/ppermute | solution.py:56
  31.4 0.0 collective-permute-start.5
  31.4 3.6 %collective-permute-start.6 = (bf16[256,1536]{1,0:T(8,128)(2,1)}, bf16[256,1536]{1,0:T(8,128)(2,1)}, u32[]{:S(2)}, u32[]{:S(2)}) collective-permute-start(bf16[256,1536]{1,0:T(8,128)(2,1)} %modulate.1.refs_4_), channel_id=1, source_target_pairs={{0,224},{1,225},{2,226},{3,227},{4,228},{5,229},{6,230},{7,231},{8... | collective-permute-start | bytes 2359304 | tf_op jit(solution)/shard_map/ppermute | solution.py:56
  34.9 33.3 %collective-permute-done.2.refs_0_ = bf16[256,1536]{1,0:T(8,128)(2,1)} collective-permute-done((bf16[256,1536]{1,0:T(8,128)(2,1)}, bf16[256,1536]{1,0:T(8,128)(2,1)}, u32[]{:S(2)}, u32[]{:S(2)}) %collective-permute-start.2) | collective-permute-done | bytes 786464 | tf_op jit(solution)/shard_map/ppermute | solution.py:56
  68.2 0.0 collective-permute-start.8
  68.2 8.0 %collective-permute-done.3.refs_1_ = bf16[256,1536]{1,0:T(8,128)(2,1)} collective-permute-done((bf16[256,1536]{1,0:T(8,128)(2,1)}, bf16[256,1536]{1,0:T(8,128)(2,1)}, u32[]{:S(2)}, u32[]{:S(2)}) %collective-permute-start.3) | collective-permute-done | bytes 786464 | tf_op jit(solution)/shard_map/ppermute | solution.py:56
  76.2 2.3 %collective-permute-start.10 = (bf16[256,1536]{1,0:T(8,128)(2,1)}, bf16[256,1536]{1,0:T(8,128)(2,1)}, u32[]{:S(2)}, u32[]{:S(2)}) collective-permute-start(bf16[256,1536]{1,0:T(8,128)(2,1)} %collective-permute-done.2.refs_0_), channel_id=1, source_target_pairs={{0,1},{1,0},{2,3},{3,2},{4,5},{5,4},{6,7},{7,6},{8,9},{9,8},{10,11... | collective-permute-start | bytes 2359304 | tf_op jit(solution)/shard_map/ppermute | solution.py:56
  78.5 0.0 collective-permute-done.4.refs_2_
  78.5 17.6 %collective-permute-start.11 = (bf16[256,1536]{1,0:T(8,128)(2,1)}, bf16[256,1536]{1,0:T(8,128)(2,1)}, u32[]{:S(2)}, u32[]{:S(2)}) collective-permute-start(bf16[256,1536]{1,0:T(8,128)(2,1)} %collective-permute-done.3.refs_1_), channel_id=1, source_target_pairs={{0,1},{1,0},{2,3},{3,2},{4,5},{5,4},{6,7},{7,6},{8,9},{9,8},{10,11... | collective-permute-start | bytes 2359304 | tf_op jit(solution)/shard_map/ppermute | solution.py:56
  96.1 2.3 %fusion = (bf16[768,1152]{1,0:T(8,128)(2,1)S(1)}, bf16[768,1152]{1,0:T(8,128)(2,1)S(1)}) fusion(bf16[1536,1152]{1,0:T(8,128)(2,1)} %all-gather.3.cloned.1.call-done.refs_12_), kind=kLoop, calls=%fused_computation.16 | loop fusion | bytes 7077888 | tf_op jit(solution)/shard_map/slice | solution.py:273
  98.3 0.0 collective-permute-done.5.refs_3_
  98.3 2.2 %collective-permute-start.13 = (bf16[768,1152]{1,0:T(8,128)(2,1)S(1)}, bf16[768,1152]{1,0:T(8,128)(2,1)}, u32[]{:S(2)}, u32[]{:S(2)}) collective-permute-start(bf16[768,1152]{1,0:T(8,128)(2,1)S(1)} %get-tuple-element.36), channel_id=1, source_target_pairs={{0,192},{1,193},{2,194},{3,195},{4,196},{5,197},{6,198},{7,199},{8... | collective-permute-start | bytes 5308424 | tf_op jit(solution)/shard_map/ppermute | solution.py:56
  100.6 0.0 collective-permute-done.6.refs_5_
  100.6 0.0 collective-permute-start.14
  100.6 0.0 collective-permute-done.8.refs_7_
  100.6 0.4 collective-permute-start.12
  100.9 0.0 collective-permute-done.10.refs_9_
  100.9 0.2 collective-permute-start.7
  101.2 0.0 collective-permute-done.11.refs_10_
  101.2 0.3 collective-permute-start.9
  101.5 0.6 stack.59.far_ref
  102.1 1.2 collective-permute-done.12.refs_11_
  103.3 1.1 collective-permute-done.7.refs_6_
  104.4 1.1 collective-permute-done.9.refs_8_
  105.5 0.6 iota.8.order_ref
  106.1 15.1 %project_in.2 = (bf16[2,3,256,128]{3,2,1,0:T(8,128)(2,1)}, bf16[3,3072,128]{2,1,0:T(8,128)(2,1)}, bf16[3,3072,128]{2,1,0:T(8,128)(2,1)}) custom-call(s32[12]{0:T(128)} %iota.8.order_ref, s32[1]{0:T(128)} %constant.51.clone.1.at_ref, bf16[256,1536]{1,0:T(8,128)(2,1)} %collective-permute-done.2.refs_0_, bf16[256,1536]{1,0:T(8,128)(2,1)} %collective-permute-done.3.refs_1_, ...), custom_call_target="tpu_custom_call" | custom-call | flops 7851737088 | bytes 17694720 | tf_op jit(solution)/shard_map/project_in/pallas_call | solution.py:153
  121.2 10.2 %attend.2 = bf16[2,256,384]{2,1,0:T(8,128)(2,1)} custom-call(f32[12]{0:T(128)} %stack.59.far_ref, bf16[2,3,256,128]{3,2,1,0:T(8,128)(2,1)} %get-tuple-element.24.q_ref, bf16[3,3072,128]{2,1,0:T(8,128)(2,1)} %get-tuple-element.25.k_ref, bf16[3,3072,128]{2,1,0:T(8,128)(2,1)} %get-tuple-element.26.v_ref), custom_call_target="tpu_custom_call" | custom-call | flops 1811939328 | bytes 9437184 | tf_op jit(solution)/shard_map/attend/pallas_call | solution.py:205
  131.4 7.4 %collective-permute-done.13.refs_12_ = bf16[768,1152]{1,0:T(8,128)(2,1)} collective-permute-done((bf16[768,1152]{1,0:T(8,128)(2,1)S(1)}, bf16[768,1152]{1,0:T(8,128)(2,1)}, u32[]{:S(2)}, u32[]{:S(2)}) %collective-permute-start.13) | collective-permute-done | bytes 1769504 | tf_op jit(solution)/shard_map/ppermute | solution.py:56
  138.8 3.0 %collective-permute-done.14.refs_13_ = bf16[768,1152]{1,0:T(8,128)(2,1)} collective-permute-done((bf16[768,1152]{1,0:T(8,128)(2,1)S(1)}, bf16[768,1152]{1,0:T(8,128)(2,1)}, u32[]{:S(2)}, u32[]{:S(2)}) %collective-permute-start.14) | collective-permute-done | bytes 1769504 | tf_op jit(solution)/shard_map/ppermute | solution.py:56
  141.8 0.6 iota.10.at_ref
  142.4 0.5 iota.9.order_ref
  142.9 15.1 %project_in.3 = (bf16[2,3,256,128]{3,2,1,0:T(8,128)(2,1)}, bf16[3,3072,128]{2,1,0:T(8,128)(2,1)}, bf16[3,3072,128]{2,1,0:T(8,128)(2,1)}) custom-call(s32[12]{0:T(128)} %iota.9.order_ref, s32[2]{0:T(128)} %iota.10.at_ref, bf16[256,1536]{1,0:T(8,128)(2,1)} %collective-permute-done.2.refs_0_, bf16[256,1536]{1,0:T(8,128)(2,1)} %collective-permute-done.3.refs_1_, ...), custom_call_target="tpu_custom_call" | custom-call | flops 7851737088 | bytes 17694720 | tf_op jit(solution)/shard_map/project_in/pallas_call | solution.py:153
  158.0 0.0 all-gather.5.cloned.1.call-done.w0
  158.1 1.2 collective-permute-start.17
  159.3 0.1 pad_add_fusion.at_ref
  159.4 0.0 copy-done.1
  159.4 0.1 collective-permute-start.15
  159.5 10.3 %attend.3 = bf16[2,256,384]{2,1,0:T(8,128)(2,1)} custom-call(f32[12]{0:T(128)} %stack.59.far_ref, bf16[2,3,256,128]{3,2,1,0:T(8,128)(2,1)} %get-tuple-element.31.q_ref, bf16[3,3072,128]{2,1,0:T(8,128)(2,1)} %get-tuple-element.32.k_ref, bf16[3,3072,128]{2,1,0:T(8,128)(2,1)} %get-tuple-element.33.v_ref), custom_call_target="tpu_custom_call" | custom-call | flops 1811939328 | bytes 9437184 | tf_op jit(solution)/shard_map/attend/pallas_call | solution.py:205
  169.8 1.1 slice_bitcast_fusion
  170.8 0.6 collective-permute-start.16
  171.4 0.0 collective-permute-done.15.a2
  171.4 1.0 collective-permute-done.16.a3
  172.5 0.0 collective-permute-done.17.w1
  172.5 4.0 %project_out.1 = bf16[256,1536]{1,0:T(8,128)(2,1)} custom-call(s32[1]{0:T(128)} %bitcast.c_ref, s32[4]{0:T(128)S(1)} %pad_add_fusion.at_ref, bf16[256,384]{1,0:T(8,128)(2,1)S(1)} %slice_bitcast_fusion.3.a0, bf16[256,384]{1,0:T(8,128)(2,1)S(1)} %get-tuple-element.44.a1, bf16[256,384]{1,0:T(8,128)(2,1)S(1)} %collective-permute-done.15.a2, ...), custom_call_target="tpu_custom_call" | custom-call | flops 1207959552 | bytes 6291456 | tf_op jit(solution)/shard_map/project_out/pallas_call | solution.py:238
  (13 shorter events, 0.1 us)
Async XLA Ops:
  6.5 7.4 %copy-start.2 = (f32[1536]{0:T(1024)S(1)}, f32[1536]{0:T(1024)}, u32[]{:S(2)}) copy-start(f32[1536]{0:T(1024)} %param.10) | copy-start | bytes 18436
  6.5 8.0 %copy-start.3 = (f32[1536]{0:T(1024)S(1)}, f32[1536]{0:T(1024)}, u32[]{:S(2)}) copy-start(f32[1536]{0:T(1024)} %param.9) | copy-start | bytes 18436
  6.5 89.5 %all-gather.3.cloned.1.call-start = ((), (), s32[]{:S(2)}) async-start(), calls=%async_computation | async-start | bytes 3981312 | tf_op jit(solution)/shard_map/all_gather | solution.py:271
  8.4 4.4 %collective-permute-start = (bf16[48,1920]{1,0:T(8,128)(2,1)S(1)}, bf16[48,1920]{1,0:T(8,128)(2,1)S(1)}, u32[]{:S(2)}, u32[]{:S(2)}) collective-permute-start(bf16[48,1920]{1,0:T(8,128)(2,1)S(1)} %pad_maximum_fusion), channel_id=1, source_target_pairs={{0,1},{1,0},{2,3},{3,2},{4,5},{5,4},{6,7},{7,6},{8,9},{9,8},{10,11... | collective-permute-start | bytes 552968 | tf_op jit(solution)/shard_map/ppermute | solution.py:56
  12.9 11.1 %collective-permute-start.1 = (bf16[96,1920]{1,0:T(8,128)(2,1)S(1)}, bf16[96,1920]{1,0:T(8,128)(2,1)S(1)}, u32[]{:S(2)}, u32[]{:S(2)}) collective-permute-start(bf16[96,1920]{1,0:T(8,128)(2,1)S(1)} %maximum_select_fusion.1), channel_id=1, source_target_pairs={{0,34},{1,35},{2,32},{3,33},{4,38},{5,39},{6,36},{7,37},{8,42},{9,... | collective-permute-start | bytes 1105928 | tf_op jit(solution)/shard_map/ppermute | solution.py:56
  25.0 133.1 %all-gather.5.cloned.1.call-start = ((), (), s32[]{:S(2)}) async-start(), calls=%async_computation.1 | async-start | bytes 2654208 | tf_op jit(solution)/shard_map/all_gather | solution.py:272
  25.8 42.5 %collective-permute-start.2 = (bf16[256,1536]{1,0:T(8,128)(2,1)}, bf16[256,1536]{1,0:T(8,128)(2,1)}, u32[]{:S(2)}, u32[]{:S(2)}) collective-permute-start(bf16[256,1536]{1,0:T(8,128)(2,1)} %modulate.1.refs_4_), channel_id=1, source_target_pairs={{0,63},{1,34},{2,33},{3,36},{4,35},{5,38},{6,37},{7,40},{8,39},{9,... | collective-permute-start | bytes 2359304 | tf_op jit(solution)/shard_map/ppermute | solution.py:56
  27.9 48.3 %collective-permute-start.3 = (bf16[256,1536]{1,0:T(8,128)(2,1)}, bf16[256,1536]{1,0:T(8,128)(2,1)}, u32[]{:S(2)}, u32[]{:S(2)}) collective-permute-start(bf16[256,1536]{1,0:T(8,128)(2,1)} %modulate.1.refs_4_), channel_id=1, source_target_pairs={{0,31},{1,2},{2,1},{3,4},{4,3},{5,6},{6,5},{7,8},{8,7},{9,10},{10,... | collective-permute-start | bytes 2359304 | tf_op jit(solution)/shard_map/ppermute | solution.py:56
  27.9 50.5 %collective-permute-start.4 = (bf16[256,1536]{1,0:T(8,128)(2,1)}, bf16[256,1536]{1,0:T(8,128)(2,1)}, u32[]{:S(2)}, u32[]{:S(2)}) collective-permute-start(bf16[256,1536]{1,0:T(8,128)(2,1)} %modulate.1.refs_4_), channel_id=1, source_target_pairs={{0,255},{1,226},{2,225},{3,228},{4,227},{5,230},{6,229},{7,232},{8... | collective-permute-start | bytes 2359304 | tf_op jit(solution)/shard_map/ppermute | solution.py:56
  31.4 67.0 %collective-permute-start.5 = (bf16[256,1536]{1,0:T(8,128)(2,1)}, bf16[256,1536]{1,0:T(8,128)(2,1)}, u32[]{:S(2)}, u32[]{:S(2)}) collective-permute-start(bf16[256,1536]{1,0:T(8,128)(2,1)} %modulate.1.refs_4_), channel_id=1, source_target_pairs={{0,32},{1,33},{2,34},{3,35},{4,36},{5,37},{6,38},{7,39},{8,40},{9,... | collective-permute-start | bytes 2359304 | tf_op jit(solution)/shard_map/ppermute | solution.py:56
  31.4 69.2 %collective-permute-start.6 = (bf16[256,1536]{1,0:T(8,128)(2,1)}, bf16[256,1536]{1,0:T(8,128)(2,1)}, u32[]{:S(2)}, u32[]{:S(2)}) collective-permute-start(bf16[256,1536]{1,0:T(8,128)(2,1)} %modulate.1.refs_4_), channel_id=1, source_target_pairs={{0,224},{1,225},{2,226},{3,227},{4,228},{5,229},{6,230},{7,231},{8... | collective-permute-start | bytes 2359304 | tf_op jit(solution)/shard_map/ppermute | solution.py:56
  68.2 32.3 %collective-permute-start.8 = (bf16[256,1536]{1,0:T(8,128)(2,1)}, bf16[256,1536]{1,0:T(8,128)(2,1)}, u32[]{:S(2)}, u32[]{:S(2)}) collective-permute-start(bf16[256,1536]{1,0:T(8,128)(2,1)} %modulate.1.refs_4_), channel_id=1, source_target_pairs={{0,1},{1,0},{2,3},{3,2},{4,5},{5,4},{6,7},{7,6},{8,9},{9,8},{10,11... | collective-permute-start | bytes 2359304 | tf_op jit(solution)/shard_map/ppermute | solution.py:56
  76.2 24.7 %collective-permute-start.10 = (bf16[256,1536]{1,0:T(8,128)(2,1)}, bf16[256,1536]{1,0:T(8,128)(2,1)}, u32[]{:S(2)}, u32[]{:S(2)}) collective-permute-start(bf16[256,1536]{1,0:T(8,128)(2,1)} %collective-permute-done.2.refs_0_), channel_id=1, source_target_pairs={{0,1},{1,0},{2,3},{3,2},{4,5},{5,4},{6,7},{7,6},{8,9},{9,8},{10,11... | collective-permute-start | bytes 2359304 | tf_op jit(solution)/shard_map/ppermute | solution.py:56
  78.5 22.7 %collective-permute-start.11 = (bf16[256,1536]{1,0:T(8,128)(2,1)}, bf16[256,1536]{1,0:T(8,128)(2,1)}, u32[]{:S(2)}, u32[]{:S(2)}) collective-permute-start(bf16[256,1536]{1,0:T(8,128)(2,1)} %collective-permute-done.3.refs_1_), channel_id=1, source_target_pairs={{0,1},{1,0},{2,3},{3,2},{4,5},{5,4},{6,7},{7,6},{8,9},{9,8},{10,11... | collective-permute-start | bytes 2359304 | tf_op jit(solution)/shard_map/ppermute | solution.py:56
  98.3 40.4 %collective-permute-start.13 = (bf16[768,1152]{1,0:T(8,128)(2,1)S(1)}, bf16[768,1152]{1,0:T(8,128)(2,1)}, u32[]{:S(2)}, u32[]{:S(2)}) collective-permute-start(bf16[768,1152]{1,0:T(8,128)(2,1)S(1)} %get-tuple-element.36), channel_id=1, source_target_pairs={{0,192},{1,193},{2,194},{3,195},{4,196},{5,197},{6,198},{7,199},{8... | collective-permute-start | bytes 5308424 | tf_op jit(solution)/shard_map/ppermute | solution.py:56
  100.6 41.2 %collective-permute-start.14 = (bf16[768,1152]{1,0:T(8,128)(2,1)S(1)}, bf16[768,1152]{1,0:T(8,128)(2,1)}, u32[]{:S(2)}, u32[]{:S(2)}) collective-permute-start(bf16[768,1152]{1,0:T(8,128)(2,1)S(1)} %get-tuple-element.35), channel_id=1, source_target_pairs={{0,64},{1,65},{2,66},{3,67},{4,68},{5,69},{6,70},{7,71},{8,72},{9,... | collective-permute-start | bytes 5308424 | tf_op jit(solution)/shard_map/ppermute | solution.py:56
  100.6 2.7 %collective-permute-start.12 = (bf16[256,1536]{1,0:T(8,128)(2,1)}, bf16[256,1536]{1,0:T(8,128)(2,1)}, u32[]{:S(2)}, u32[]{:S(2)}) collective-permute-start(bf16[256,1536]{1,0:T(8,128)(2,1)} %collective-permute-done.4.refs_2_), channel_id=1, source_target_pairs={{0,1},{1,0},{2,3},{3,2},{4,5},{5,4},{6,7},{7,6},{8,9},{9,8},{10,11... | collective-permute-start | bytes 2359304 | tf_op jit(solution)/shard_map/ppermute | solution.py:56
  100.9 3.5 %collective-permute-start.7 = (bf16[256,1536]{1,0:T(8,128)(2,1)}, bf16[256,1536]{1,0:T(8,128)(2,1)}, u32[]{:S(2)}, u32[]{:S(2)}) collective-permute-start(bf16[256,1536]{1,0:T(8,128)(2,1)} %collective-permute-done.5.refs_3_), channel_id=1, source_target_pairs={{0,1},{1,0},{2,3},{3,2},{4,5},{5,4},{6,7},{7,6},{8,9},{9,8},{10,11... | collective-permute-start | bytes 2359304 | tf_op jit(solution)/shard_map/ppermute | solution.py:56
  101.2 4.4 %collective-permute-start.9 = (bf16[256,1536]{1,0:T(8,128)(2,1)}, bf16[256,1536]{1,0:T(8,128)(2,1)}, u32[]{:S(2)}, u32[]{:S(2)}) collective-permute-start(bf16[256,1536]{1,0:T(8,128)(2,1)} %collective-permute-done.6.refs_5_), channel_id=1, source_target_pairs={{0,1},{1,0},{2,3},{3,2},{4,5},{5,4},{6,7},{7,6},{8,9},{9,8},{10,11... | collective-permute-start | bytes 2359304 | tf_op jit(solution)/shard_map/ppermute | solution.py:56
  142.9 16.4 %copy-start.4 = (f32[1536]{0:T(1024)S(1)}, f32[1536]{0:T(1024)}, u32[]{:S(2)}) copy-start(f32[1536]{0:T(1024)} %param.11) | copy-start | bytes 18436
  142.9 16.5 %copy-start.1 = (bf16[2,256,384]{2,1,0:T(8,128)(2,1)S(1)}, bf16[2,256,384]{2,1,0:T(8,128)(2,1)}, u32[]{:S(2)}) copy-start(bf16[2,256,384]{2,1,0:T(8,128)(2,1)} %attend.2) | copy-start | bytes 1179652
  158.1 14.4 %collective-permute-start.17 = (bf16[1536,768]{1,0:T(8,128)(2,1)}, bf16[1536,768]{1,0:T(8,128)(2,1)}, u32[]{:S(2)}, u32[]{:S(2)}) collective-permute-start(bf16[1536,768]{1,0:T(8,128)(2,1)} %all-gather.5.cloned.1.call-done.w0), channel_id=1, source_target_pairs={{0,1},{1,0},{2,3},{3,2},{4,5},{5,4},{6,7},{7,6},{8,9},{9,8},{10,11... | collective-permute-start | bytes 7077896 | tf_op jit(solution)/shard_map/ppermute | solution.py:56
  159.4 12.0 %collective-permute-start.15 = (bf16[256,384]{1,0:T(8,128)(2,1)S(1)}, bf16[256,384]{1,0:T(8,128)(2,1)S(1)}, u32[]{:S(2)}, u32[]{:S(2)}) collective-permute-start(bf16[256,384]{1,0:T(8,128)(2,1)S(1)} %slice_bitcast_fusion.1), channel_id=1, source_target_pairs={{0,1},{1,0},{2,3},{3,2},{4,5},{5,4},{6,7},{7,6},{8,9},{9,8},{10,11... | collective-permute-start | bytes 589832 | tf_op jit(solution)/shard_map/ppermute | solution.py:56
  159.5 12.9 %copy-start = (bf16[1536,768]{1,0:T(8,128)(2,1)S(1)}, bf16[1536,768]{1,0:T(8,128)(2,1)}, u32[]{:S(2)}) copy-start(bf16[1536,768]{1,0:T(8,128)(2,1)} %all-gather.5.cloned.1.call-done.w0) | copy-start | bytes 7077892
  170.8 1.6 collective-permute-start.16
Sparse Core Ops, SparseCore 0:
  25.1 65.9 all-gather.2
  92.8 39.6 all-gather.4

commit v4 on v2

v4 whole, which is shorter than its diff:
```python
import functools
import itertools

import jax
import jax.numpy as jnp
from jax import lax
from jax.experimental import pallas as pl
from jax.experimental.pallas import tpu as pltpu
from jax.sharding import Mesh
from jax.sharding import PartitionSpec as P

HEADS = 12
HD = 128
TILE_T = 4
EPS = 1e-06
HALF = 3 * HD
AXES = ("x", "l", "z", "u", "c")
SIZES = (4, 2, 8, 2, 2)
FAR = 1e30
BF = jnp.bfloat16
F32 = jnp.float32


def hops(move):
    pairs = []
    for x, l, z, u, c in itertools.product(*map(range, SIZES)):
        x2, y2, z2, c2 = move(x, u * 2 + l, z, c)
        to = (x2 % 4, y2 % 2, z2 % 8, y2 // 2, c2)
        rank = [functools.reduce(lambda r, d: r * d[0] + d[1], zip(SIZES, at), 0) for at in ((x, l, z, u, c), to)]
        pairs.append(tuple(rank))
    return pairs


def tile_hop(down, across):
    def move(x, y, z, c):
        h, w = ((x * 2 + y % 2 + down) % 8, (z * 2 + y // 2 + across[c]) % 16)
        return h // 2, w % 2 * 2 + h % 2, w // 2, c

    return hops(move)


SIBLING = hops(lambda x, y, z, c: (x, y, z, 1 - c))
Y_FLIP = hops(lambda x, y, z, c: (x, 3 - y, z, c))
X_A = hops(lambda x, y, z, c: (x + 1 - 2 * c, y, z, c))
X_B = hops(lambda x, y, z, c: (x - 1 + 2 * c, y, z, c))
Z_A = hops(lambda x, y, z, c: (x, y, z + 1 - 2 * c, c))
Z_B = hops(lambda x, y, z, c: (x, y, z - 1 + 2 * c, c))
Z_A2 = hops(lambda x, y, z, c: (x, y, z + 2 - 4 * c, c))
Z_B2 = hops(lambda x, y, z, c: (x, y, z - 2 + 4 * c, c))
TOKENS = (
    tile_hop(1, (0, 1)),
    tile_hop(1, (-1, 0)),
    tile_hop(-1, (0, 1)),
    tile_hop(-1, (-1, 0)),
    tile_hop(0, (-1, 1)),
)
ORDER = ((7, 11, 9, 1, 0, 3, 8, 6, 10, 2, 5, 4), (8, 11, 10, 2, 0, 4, 7, 6, 9, 1, 5, 3))
RING = (0, -1, 1, -2, 2, -3, 3, -4)


def send(x, pairs):
    return lax.ppermute(x, AXES, pairs)


def together(*values):
    return lax.optimization_barrier(values)


def cost(flops, nbytes, trans=0):
    return pl.CostEstimate(flops=int(flops), bytes_accessed=int(nbytes), transcendentals=int(trans))


def modulate_kernel(x_ref, scale_ref, shift_ref, o_ref):
    x = x_ref[...].astype(F32)
    mean = jnp.mean(x, axis=-1, keepdims=True)
    centred = x - mean
    var = jnp.mean(centred * centred, axis=-1, keepdims=True)
    normed = centred * lax.rsqrt(var + EPS)
    o_ref[...] = (normed * (1.0 + scale_ref[...]) + shift_ref[...]).astype(BF)


def modulate(x, scale, shift):
    rows, width = x.shape
    step = 64
    return pl.pallas_call(
        modulate_kernel,
        out_shape=jax.ShapeDtypeStruct((rows, width), BF),
        grid=(rows // step,),
        in_specs=[
            pl.BlockSpec((step, width), lambda i: (i, 0)),
            pl.BlockSpec((1, width), lambda i: (0, 0)),
            pl.BlockSpec((1, width), lambda i: (0, 0)),
        ],
        out_specs=pl.BlockSpec((step, width), lambda i: (i, 0)),
        cost_estimate=cost(rows * width * 8, rows * width * 4),
        name="modulate",
    )(x, scale.reshape(1, -1), shift.reshape(1, -1))


def head_norm(raw, gain):
    return (raw * lax.rsqrt(jnp.mean(raw * raw, axis=-1, keepdims=True) + EPS) * gain).astype(BF)


def heads_kernel(n, m, order_ref, at_ref, far_ref, *refs):
    tiles, blocks = (refs[:n], refs[n : n + m])
    qg_ref, kg_ref, mine_ref, theirs_ref, buf, weight, q_ref, k_ref, v_ref, sem, wsem = refs[n + m :]
    i = pl.program_id(0)
    deep = weight.shape[0] // m
    rows = buf.shape[1]
    steps = n

    def copies():
        for j, block in enumerate(blocks):
            to = pl.ds(pl.multiple_of(at_ref[j] * deep, deep), deep)
            yield pltpu.make_async_copy(block, weight.at[to], wsem.at[j])

    def fetch(step, slot):
        which = order_ref[step]
        for t in range(n):

            @pl.when(which == t)
            def _():
                pltpu.make_async_copy(tiles[t], buf.at[slot], sem.at[slot]).start()

    @pl.when(i == 0)
    def _():
        fetch(i, 0)
        for copy in copies():
            copy.start()
        for copy in copies():
            copy.wait()

    slot = lax.rem(i, 2)

    @pl.when(i + 1 < steps)
    def _():
        fetch(i + 1, 1 - slot)

    @pl.when(i < steps)
    def _():
        pltpu.make_async_copy(tiles[0], buf.at[slot], sem.at[slot]).wait()
        raw = jnp.dot(buf[slot], weight[:, : 2 * HALF], preferred_element_type=F32)
        at = pl.ds(pl.multiple_of(i * rows, rows), rows)
        for h in range(3):
            k_ref[h, at] = head_norm(raw[:, h * HD : (h + 1) * HD], kg_ref[...])
            v_ref[h, at] = raw[:, HALF + h * HD : HALF + (h + 1) * HD].astype(BF)

    @pl.when(jnp.logical_or(i == 4, i == 7))
    def _():
        t = jnp.where(i == 4, 0, 1)
        raw = jnp.dot(buf[slot], weight[:, 2 * HALF :], preferred_element_type=F32)
        for h in range(3):
            q_ref[t, h] = head_norm(raw[:, h * HD : (h + 1) * HD], qg_ref[...])

    @pl.when(i >= steps)
    def _():
        h, t = ((i - steps) // 2, lax.rem(i - steps, 2))
        q = q_ref[t, h]
        factor = 1.4426950408889634 / jnp.sqrt(F32(HD))
        scores, top = ([], None)
        for j in range(9):
            at = pl.multiple_of((t * 3 + j) * rows, rows)
            k = k_ref[h, pl.ds(at, rows), :]
            s = lax.dot_general(q, k, (((1,), (1,)), ((), ())), preferred_element_type=F32)
            scores.append(s)
            most = jnp.max(s, axis=-1, keepdims=True) - far_ref[t * 3 + j]
            top = most if top is None else jnp.maximum(top, most)
        total = jnp.zeros((rows, 1), F32)
        acc = jnp.zeros((rows, HD), F32)
        for j in range(9):
            at = pl.multiple_of((t * 3 + j) * rows, rows)
            v = v_ref[h, pl.ds(at, rows), :]
            expo = jnp.exp2((scores[j] - (top + far_ref[t * 3 + j])) * factor)
            total += jnp.sum(expo, axis=-1, keepdims=True)
            acc += jnp.dot(expo.astype(BF), v, preferred_element_type=F32)
        result = (acc / total).astype(BF)
        cols = pl.ds(pl.multiple_of(h * HD, HD), HD)

        @pl.when(t == 0)
        def _():
            mine_ref[:, cols] = result

        @pl.when(t == 1)
        def _():
            theirs_ref[:, cols] = result


def three_heads(order, at, far, tiles, blocks, q_gain, k_gain):
    n, m = (len(tiles), len(blocks))
    rows, width = tiles[0].shape
    hbm = pl.BlockSpec(memory_space=pltpu.HBM)
    return pl.pallas_call(
        functools.partial(heads_kernel, n, m),
        out_shape=[jax.ShapeDtypeStruct((rows, HALF), BF)] * 2,
        grid=(n + 6,),
        in_specs=[pl.BlockSpec(memory_space=pltpu.SMEM)] * 3
        + [hbm] * (n + m)
        + [pl.BlockSpec((1, HD), lambda i: (0, 0))] * 2,
        out_specs=[pl.BlockSpec((rows, HALF), lambda i: (0, 0))] * 2,
        scratch_shapes=[
            pltpu.VMEM((2, rows, width), BF),
            pltpu.VMEM((width, 3 * HALF), BF),
            pltpu.VMEM((2, 3, rows, HD), BF),
            pltpu.VMEM((3, n * rows, HD), BF),
            pltpu.VMEM((3, n * rows, HD), BF),
            pltpu.SemaphoreType.DMA((2,)),
            pltpu.SemaphoreType.DMA((m,)),
        ],
        compiler_params=pltpu.CompilerParams(vmem_limit_bytes=60 << 20),
        cost_estimate=cost(
            2 * (n * 2 + 2) * rows * width * HALF + 6 * rows * 9 * rows * HD * 4,
            (n * rows * width + width * 3 * HALF) * 2,
            6 * rows * 9 * rows,
        ),
        name="three_heads",
    )(order, at, far, *tiles, *blocks, q_gain, k_gain)


def stack_kernel(m, *refs):
    blocks, (o_ref, sem) = (refs[:m], refs[m:])
    deep = o_ref.shape[0] // m
    copies = [
        pltpu.make_async_copy(block, o_ref.at[pl.ds(j * deep, deep)], sem.at[j])
        for j, block in enumerate(blocks)
    ]
    for copy in copies:
        copy.start()
    for copy in copies:
        copy.wait()


def stack(blocks):
    m = len(blocks)
    deep, cols = blocks[0].shape
    hbm = pl.BlockSpec(memory_space=pltpu.HBM)
    return pl.pallas_call(
        functools.partial(stack_kernel, m),
        out_shape=jax.ShapeDtypeStruct((m * deep, cols), BF),
        in_specs=[hbm] * m,
        out_specs=hbm,
        scratch_shapes=[pltpu.SemaphoreType.DMA((m,))],
        compiler_params=pltpu.CompilerParams(vmem_limit_bytes=60 << 20),
        cost_estimate=cost(0, m * deep * cols * 4),
        name="stack",
    )(*blocks)


def project_kernel(c_ref, at_ref, mine_ref, theirs_ref, a0, a1, a2, a3, gate_ref, *refs):
    m = len(RING)
    blocks, theirs, (o_ref, left, weight, sem) = (refs[:m], refs[m : m + 4], refs[m + 4 :])
    deep = weight.shape[1] // m
    sources = [(0, mine_ref[j], blocks[j]) for j in range(m)]
    sources += [(1, theirs_ref[j], theirs[0].at[pl.ds(j * deep, deep)]) for j in range(m - 3)]
    sources += [(1, theirs_ref[m - 3 + j], theirs[1 + j]) for j in range(3)]
    copies = [
        pltpu.make_async_copy(ref, weight.at[side, pl.ds(pl.multiple_of(row * deep, deep), deep)], sem.at[j])
        for j, (side, row, ref) in enumerate(sources)
    ]
    for copy in copies:
        copy.start()
    for j, a in enumerate((a0, a1, a2, a3)):
        left[:, pl.ds(pl.multiple_of(at_ref[j] * HALF, HD), HALF)] = a[...]
    for side in range(2):
        for copy in copies[side * m : (side + 1) * m]:
            copy.wait()
        core = c_ref[0] if side == 0 else 1 - c_ref[0]
        cols = pl.ds(pl.multiple_of(core * 2 * HALF, HD), 2 * HALF)
        out = jnp.dot(left[...], weight[side], preferred_element_type=F32)
        o_ref[:, cols] = (gate_ref[:, cols] * out).astype(BF)


def project_out(c, at, rows_at, attended, blocks, theirs, gate):
    rows = attended[0].shape[0]
    width = 4 * HALF
    vmem = pl.BlockSpec(memory_space=pltpu.VMEM)
    smem = pl.BlockSpec(memory_space=pltpu.SMEM)
    hbm = pl.BlockSpec(memory_space=pltpu.HBM)
    return pl.pallas_call(
        project_kernel,
        out_shape=jax.ShapeDtypeStruct((rows, width), BF),
        in_specs=[smem] * 4 + [vmem] * 5 + [hbm] * (len(blocks) + len(theirs)),
        out_specs=vmem,
        scratch_shapes=[
            pltpu.VMEM((rows, width), BF),
            pltpu.VMEM((2, width, 2 * HALF), BF),
            pltpu.SemaphoreType.DMA((2 * len(RING),)),
        ],
        compiler_params=pltpu.CompilerParams(vmem_limit_bytes=60 << 20),
        cost_estimate=cost(2 * rows * width * width, width * width * 2 + rows * width * 4),
        name="project_out",
    )(c, at, *rows_at, *attended, gate.reshape(1, -1), *blocks, *theirs)


def shards(tokens, shift, scale, gate, qkv_weight, out_weight, q_gain, k_gain):
    frames, tile_h, tile_w, width = tokens.shape
    count = frames * tile_h * tile_w
    x, l, z, u, c = (lax.axis_index(a) for a in AXES)
    parity = lax.rem(x, 2)
    h = x * 2 + l
    w = z * 2 + u

    def columns(core):
        at = (core * 2 + parity) * HALF
        parts = [lax.dynamic_slice_in_dim(qkv_weight, i * width + at, HALF, 1) for i in (1, 2, 0)]
        parts.append(lax.dynamic_slice_in_dim(out_weight, core * 2 * HALF, 2 * HALF, 1))
        return jnp.concatenate(parts, axis=1)

    mine, other = columns(c), send(columns(1 - c), SIBLING)
    own = modulate(tokens.reshape(count, width), scale, shift)
    own, other = together(own, other)
    pair = jnp.where(c == 0, jnp.concatenate([mine, other]), jnp.concatenate([other, mine]))
    other, t1, own2, own = together(send(pair, Y_FLIP), send(own, TOKENS[0]), send(own, SIBLING), own)
    first = jnp.where(u == 0, pair, other)
    last = jnp.where(u == 0, other, pair)
    cut = 3 * HALF
    block = jnp.concatenate([first[:, :cut], last[:, :cut]])
    out0 = jnp.concatenate([first[:, cut:], last[:, cut:]])

    a1, b1, x0, t2, s1, own = together(
        send(block, Z_A), send(block, Z_B), send(block, X_B), send(own, TOKENS[1]), send(t1, SIBLING), own
    )
    a2, b2, xa1, xb1, t3, own, t2 = together(
        send(a1, Z_A), send(b1, Z_B), send(a1, X_A), send(b1, X_B), send(own, TOKENS[2]), own, t2
    )
    a3, b3, xa2, xb2, t4, own, t2 = together(
        send(a2, Z_A), send(b2, Z_B), send(a2, X_A), send(b2, X_B), send(own, TOKENS[3]), own, t2
    )
    a4, xa3, xb3, t5, s2, own, t3, t4 = together(
        send(a3, Z_A), send(a3, X_A), send(b3, X_B), send(own, TOKENS[4]), send(t2, SIBLING), own, t3, t4
    )
    s3, s4, s5, a4 = together(send(t3, SIBLING), send(t4, SIBLING), send(t5, SIBLING), a4)
    tiles = [own, t1, t2, t3, t4, t5, own2, s1, s2, s3, s4, s5]
    blocks = [block, a1, b1, a2, b2, a3, b3, a4]

    col_ok = [jnp.where(c == 0, w > 0, w < 15), True, True, jnp.where(c == 0, w < 15, w > 0)]
    row_ok = [h > 0, True, h < 7]
    far = jnp.stack([jnp.where(jnp.logical_and(a, b), 0.0, FAR).astype(F32) for a in col_ok for b in row_ok])
    order = jnp.where(c == 0, jnp.array(ORDER[0], jnp.int32), jnp.array(ORDER[1], jnp.int32))
    ring = jnp.array(RING, jnp.int32)
    rows_at = [(z + (1 - 2 * c) * ring) % 8, (z - (1 - 2 * c) * ring) % 8]
    gains = (q_gain.reshape(1, HD), k_gain.reshape(1, HD))

    a4, out0, own = together(a4, out0, own)
    xa4, oa1, ob1 = send(a4, X_A), send(out0, Z_A), send(out0, Z_B)
    oa2, ob2 = send(out0, Z_A2), send(out0, Z_B2)
    mine1, theirs1 = three_heads(order, rows_at[0], far, tiles, blocks, *gains)
    mine1, theirs1, xa4, oa1, ob1, oa2, ob2 = together(mine1, theirs1, xa4, oa1, ob1, oa2, ob2)

    blocks = [x0, xa1, xb1, xa2, xb2, xa3, xb3, xa4]
    oa3, ob3, oa4 = send(oa2, Z_A), send(ob2, Z_B), send(oa2, Z_A2)
    near = send(stack([out0, oa1, ob1, oa2, ob2]), SIBLING)
    mine3 = send(theirs1, SIBLING)
    mine2, theirs2 = three_heads(order, rows_at[0], far, tiles, blocks, *gains)
    theirs2, mine3, near, oa3, ob3, oa4 = together(theirs2, mine3, near, oa3, ob3, oa4)
    mine4 = send(theirs2, SIBLING)
    others = [near, send(oa3, SIBLING), send(ob3, SIBLING), send(oa4, SIBLING)]

    at = jnp.stack([c * 2 + parity, c * 2 + 1 - parity, (1 - c) * 2 + parity, (1 - c) * 2 + 1 - parity])
    out = project_out(
        c.reshape(1),
        at.astype(jnp.int32),
        rows_at,
        [mine1, mine2, mine3, mine4],
        [out0, oa1, ob1, oa2, ob2, oa3, ob3, oa4],
        others,
        gate,
    )
    return out.reshape(frames, tile_h, tile_w, width)


def solution(mesh):
    fine = Mesh(mesh.devices.reshape(SIZES), AXES)
    tile = P(None, ("x", "l"), ("z", "u", "c"), None)
    rows = P(("z", "u", "c"), None)
    return jax.shard_map(
        shards,
        mesh=fine,
        in_specs=(tile, P(), P(), P(), rows, rows, P(), P()),
        out_specs=tile,
        check_vma=False,
    )
```

time: 224 us -> 261 us (1.17)
  Pallas kernels: 51.6 us -> 105 us
  starting transfers between devices: 23.7 us -> 71.6 us
  waiting for transfers between devices: 98.9 us -> 71.9 us
  local copies, waits for them, and re-layouts: 34.7 us -> 8.48 us
  between operations: 13.7 us -> 0.83 us
    all_gather x2 -> x0, waiting for transfers between devices: 56.2 us -> none  [the longest x1 56.2 us: shards(): w_in = lax.all_gather(quad[:, :3 * HALF], 'z', axis=0, tiled=True)]
    pallas_call x5 -> x4, Pallas kernels: 47.9 us -> 101 us  [the longest x2 49.5 us: three_heads(): pl.pallas_call(functools.partial(heads_kernel, n, m), out_shape=[jax.Shap...]
    ppermute x18 -> x41, starting transfers between devices: 23.6 us -> 71.6 us  [send(): return lax.ppermute(x, AXES, pairs)]
    ppermute x18 -> x41, waiting for transfers between devices: 42.7 us -> 71.9 us  [send(): return lax.ppermute(x, AXES, pairs)]
    unnamed x74 -> x82, local copies, waits for them, and re-layouts: 27.6 us -> 2.73 us
    slice x3 -> x4, local copies, waits for them, and re-layouts: 3.81 us -> 0.06 us  [the longest x2 0.04 us: shards(): block = jnp.concatenate([first[:, :cut], last[:, :cut]])]
  transfers between devices with their start and end apart: 20 -> 41, of which waited for: 9 -> 13; matrix products, arithmetic and copies ran while one was open for 2% -> 2% of each run, Pallas kernels for 21% -> 21%
where the time goes in v4:
time: 261 us; the launch traced here: 260 us
  Pallas kernels  105 us (40%)
  waiting for transfers between devices  71.9 us (28%)
  starting transfers between devices  71.6 us (27%)
  local copies, waits for them, and re-layouts  8.48 us (3%)
    ppermute x41, waiting for transfers between devices, send(): return lax.ppermute(x, AXES, pairs)  71.9 us
    ppermute x41, starting transfers between devices, send(): return lax.ppermute(x, AXES, pairs)  71.6 us
    pallas_call x2, Pallas kernels, three_heads(): pl.pallas_call(functools.partial(heads_kernel, n, m), out_shape=[jax.Shap...  49.5 us
    pallas_call x1, Pallas kernels, stack(): pl.pallas_call(functools.partial(stack_kernel, m), out_shape=jax.ShapeDty...  45.8 us
    pallas_call x1, Pallas kernels, project_out(): pl.pallas_call(project_kernel, out_shape=jax.ShapeDtypeStruct((rows, widt...  5.81 us
  transfers between devices with their start and end apart: 41, of which 13 were waited for; matrix products, arithmetic and copies ran while one was open for 2% of the time, Pallas kernels for 21%

profile of v4, /device:TPU:1, one launch (start us, length us, event | category | flops | bytes accessed | tf_op | source)
XLA Modules:
  0.0 259.6 jit_solution(16554468746175333191)
XLA Ops:
  0.0 0.9 constant_dynamic-slice_fusion.4
  0.9 0.9 constant_dynamic-slice_fusion.7
  1.9 3.3 %collective-permute-start = (bf16[48,1920]{1,0:T(8,128)(2,1)S(1)}, bf16[48,1920]{1,0:T(8,128)(2,1)S(1)}, u32[]{:S(2)}, u32[]{:S(2)}) collective-permute-start(bf16[48,1920]{1,0:T(8,128)(2,1)S(1)} %pad_maximum_fusion.2), channel_id=1, source_target_pairs={{0,1},{1,0},{2,3},{3,2},{4,5},{5,4},{6,7},{7,6},{8,9},{9,8},{10,11... | collective-permute-start | bytes 552968 | tf_op jit(solution)/shard_map/ppermute | solution.py:62
  5.2 1.3 reshape.27.shift_ref
  6.5 1.3 reshape.26.scale_ref
  7.8 3.7 %modulate.1.refs_0_ = bf16[256,1536]{1,0:T(8,128)(2,1)} custom-call(bf16[256,1536]{1,0:T(8,128)(2,1)} %bitcast.17, f32[1,1536]{1,0:T(1,128)} %reshape.26.scale_ref, f32[1,1536]{1,0:T(1,128)} %reshape.27.shift_ref), custom_call_target="tpu_custom_call" | custom-call | flops 3145728 | bytes 1572864 | tf_op jit(solution)/shard_map/modulate/pallas_call | solution.py:85
  11.5 1.1 collective-permute-start.2
  12.7 2.3 collective-permute-start.1
  15.0 18.0 %collective-permute-done.1 = bf16[96,1920]{1,0:T(8,128)(2,1)S(1)} collective-permute-done((bf16[96,1920]{1,0:T(8,128)(2,1)S(1)}, bf16[96,1920]{1,0:T(8,128)(2,1)S(1)}, u32[]{:S(2)}, u32[]{:S(2)}) %collective-permute-start.1) | collective-permute-done | bytes 368672 | tf_op jit(solution)/shard_map/ppermute | solution.py:62
  33.1 4.9 %collective-permute-start.8 = (bf16[256,1536]{1,0:T(8,128)(2,1)}, bf16[256,1536]{1,0:T(8,128)(2,1)S(1)}, u32[]{:S(2)}, u32[]{:S(2)}) collective-permute-start(bf16[256,1536]{1,0:T(8,128)(2,1)} %collective-permute-done.2.refs_1_), channel_id=1, source_target_pairs={{0,1},{1,0},{2,3},{3,2},{4,5},{5,4},{6,7},{7,6},{8,9},{9,8},{10,11... | collective-permute-start | bytes 2359304 | tf_op jit(solution)/shard_map/ppermute | solution.py:62
  38.2 1.3 collective-permute-start.6
  39.5 2.7 %collective-permute-start.4 = (bf16[192,1152]{1,0:T(8,128)(2,1)S(1)}, bf16[192,1152]{1,0:T(8,128)(2,1)S(1)}, u32[]{:S(2)}, u32[]{:S(2)}) collective-permute-start(bf16[192,1152]{1,0:T(8,128)(2,1)S(1)} %pad_maximum_fusion.refs_12_), channel_id=1, source_target_pairs={{0,4},{1,29},{2,6},{3,31},{4,8},{5,1},{6,10},{7,3},{8,12},{9,5},{1... | collective-permute-start | bytes 1327112 | tf_op jit(solution)/shard_map/ppermute | solution.py:62
  42.2 4.8 %collective-permute-done.6.refs_12_ = bf16[192,1152]{1,0:T(8,128)(2,1)S(1)} collective-permute-done((bf16[192,1152]{1,0:T(8,128)(2,1)S(1)}, bf16[192,1152]{1,0:T(8,128)(2,1)S(1)}, u32[]{:S(2)}, u32[]{:S(2)}) %collective-permute-start.6) | collective-permute-done | bytes 442400 | tf_op jit(solution)/shard_map/ppermute | solution.py:62
  46.9 3.0 %collective-permute-done.5.refs_14_ = bf16[192,1152]{1,0:T(8,128)(2,1)S(1)} collective-permute-done((bf16[192,1152]{1,0:T(8,128)(2,1)S(1)}, bf16[192,1152]{1,0:T(8,128)(2,1)S(1)}, u32[]{:S(2)}, u32[]{:S(2)}) %collective-permute-start.5) | collective-permute-done | bytes 442400 | tf_op jit(solution)/shard_map/ppermute | solution.py:62
  49.9 2.3 collective-permute-done.4.refs_13_
  52.2 2.7 %collective-permute-done.7.refs_2_ = bf16[256,1536]{1,0:T(8,128)(2,1)S(1)} collective-permute-done((bf16[256,1536]{1,0:T(8,128)(2,1)}, bf16[256,1536]{1,0:T(8,128)(2,1)S(1)}, u32[]{:S(2)}, u32[]{:S(2)}) %collective-permute-start.7) | collective-permute-done | bytes 786464 | tf_op jit(solution)/shard_map/ppermute | solution.py:62
  55.0 4.9 %collective-permute-start.13 = (bf16[256,1536]{1,0:T(8,128)(2,1)S(1)}, bf16[256,1536]{1,0:T(8,128)(2,1)S(1)}, u32[]{:S(2)}, u32[]{:S(2)}) collective-permute-start(bf16[256,1536]{1,0:T(8,128)(2,1)S(1)} %copy-done.6), channel_id=1, source_target_pairs={{0,224},{1,227},{2,226},{3,229},{4,228},{5,231},{6,230},{7,233},{8... | collective-permute-start | bytes 2359304 | tf_op jit(solution)/shard_map/ppermute | solution.py:62
  59.9 0.5 collective-permute-start.11
  60.4 5.6 %collective-permute-start.9 = (bf16[192,1152]{1,0:T(8,128)(2,1)S(1)}, bf16[192,1152]{1,0:T(8,128)(2,1)S(1)}, u32[]{:S(2)}, u32[]{:S(2)}) collective-permute-start(bf16[192,1152]{1,0:T(8,128)(2,1)S(1)} %collective-permute-done.4.refs_13_), channel_id=1, source_target_pairs={{0,4},{1,29},{2,6},{3,31},{4,8},{5,1},{6,10},{7,3},{8,12},{9,5},{1... | collective-permute-start | bytes 1327112 | tf_op jit(solution)/shard_map/ppermute | solution.py:62
  66.0 1.0 collective-permute-start.12
  67.0 18.9 %collective-permute-done.11.refs_13_ = bf16[192,1152]{1,0:T(8,128)(2,1)S(1)} collective-permute-done((bf16[192,1152]{1,0:T(8,128)(2,1)S(1)}, bf16[192,1152]{1,0:T(8,128)(2,1)S(1)}, u32[]{:S(2)}, u32[]{:S(2)}) %collective-permute-start.11) | collective-permute-done | bytes 442400 | tf_op jit(solution)/shard_map/ppermute | solution.py:62
  86.1 1.4 collective-permute-start.16
  87.4 14.4 %collective-permute-start.14 = (bf16[192,1152]{1,0:T(8,128)(2,1)S(1)}, bf16[192,1152]{1,0:T(8,128)(2,1)S(1)}, u32[]{:S(2)}, u32[]{:S(2)}) collective-permute-start(bf16[192,1152]{1,0:T(8,128)(2,1)S(1)} %collective-permute-done.9.refs_15_), channel_id=1, source_target_pairs={{0,4},{1,29},{2,6},{3,31},{4,8},{5,1},{6,10},{7,3},{8,12},{9,5},{1... | collective-permute-start | bytes 1327112 | tf_op jit(solution)/shard_map/ppermute | solution.py:62
  101.9 1.2 collective-permute-start.17
  103.1 10.5 %collective-permute-done.16.refs_15_ = bf16[192,1152]{1,0:T(8,128)(2,1)S(1)} collective-permute-done((bf16[192,1152]{1,0:T(8,128)(2,1)S(1)}, bf16[192,1152]{1,0:T(8,128)(2,1)S(1)}, u32[]{:S(2)}, u32[]{:S(2)}) %collective-permute-start.16) | collective-permute-done | bytes 442400 | tf_op jit(solution)/shard_map/ppermute | solution.py:62
  113.7 4.0 %collective-permute-start.23 = (bf16[256,1536]{1,0:T(8,128)(2,1)S(1)}, bf16[256,1536]{1,0:T(8,128)(2,1)S(1)}, u32[]{:S(2)}, u32[]{:S(2)}) collective-permute-start(bf16[256,1536]{1,0:T(8,128)(2,1)S(1)} %collective-permute-done.7.refs_2_), channel_id=1, source_target_pairs={{0,1},{1,0},{2,3},{3,2},{4,5},{5,4},{6,7},{7,6},{8,9},{9,8},{10,11... | collective-permute-start | bytes 2359304 | tf_op jit(solution)/shard_map/ppermute | solution.py:62
  117.7 1.1 collective-permute-start.21
  118.8 1.9 collective-permute-start.20
  120.7 1.5 collective-permute-start.19
  122.2 5.8 %collective-permute-done.21.refs_18_ = bf16[192,1152]{1,0:T(8,128)(2,1)S(1)} collective-permute-done((bf16[192,1152]{1,0:T(8,128)(2,1)S(1)}, bf16[192,1152]{1,0:T(8,128)(2,1)S(1)}, u32[]{:S(2)}, u32[]{:S(2)}) %collective-permute-start.21) | collective-permute-done | bytes 442400 | tf_op jit(solution)/shard_map/ppermute | solution.py:62
  128.0 2.4 collective-permute-done.20.refs_17_
  130.5 1.1 collective-permute-done.19.refs_19_
  131.6 0.3 collective-permute-start.24
  131.9 0.7 copy-done.23
  132.6 0.2 collective-permute-start.25
  132.9 0.4 collective-permute-start.26
  133.3 0.7 stack.60.far_ref
  134.0 0.5 and_select_fusion
  134.5 0.6 broadcast_select_fusion.2.order_ref
  135.2 0.3 collective-permute-done.25.refs_10_
  135.5 1.1 collective-permute-done.26.refs_11_
  136.6 4.0 %collective-permute-start.31 = (bf16[192,768]{1,0:T(8,128)(2,1)S(1)}, bf16[192,768]{1,0:T(8,128)(2,1)S(1)}, u32[]{:S(2)}, u32[]{:S(2)}) collective-permute-start(bf16[192,768]{1,0:T(8,128)(2,1)S(1)} %pad_maximum_fusion.1.refs_0_), channel_id=1, source_target_pairs={{0,24},{1,9},{2,26},{3,11},{4,28},{5,13},{6,30},{7,15},{8,0},{9,17... | collective-permute-start | bytes 884744 | tf_op jit(solution)/shard_map/ppermute | solution.py:62
  140.6 3.1 %collective-permute-start.30 = (bf16[192,768]{1,0:T(8,128)(2,1)S(1)}, bf16[192,768]{1,0:T(8,128)(2,1)S(1)}, u32[]{:S(2)}, u32[]{:S(2)}) collective-permute-start(bf16[192,768]{1,0:T(8,128)(2,1)S(1)} %pad_maximum_fusion.1.refs_0_), channel_id=1, source_target_pairs={{0,8},{1,25},{2,10},{3,27},{4,12},{5,29},{6,14},{7,31},{8,16},{9,1... | collective-permute-start | bytes 884744 | tf_op jit(solution)/shard_map/ppermute | solution.py:62
  143.8 2.7 %collective-permute-start.28 = (bf16[192,768]{1,0:T(8,128)(2,1)S(1)}, bf16[192,768]{1,0:T(8,128)(2,1)S(1)}, u32[]{:S(2)}, u32[]{:S(2)}) collective-permute-start(bf16[192,768]{1,0:T(8,128)(2,1)S(1)} %pad_maximum_fusion.1.refs_0_), channel_id=1, source_target_pairs={{0,4},{1,29},{2,6},{3,31},{4,8},{5,1},{6,10},{7,3},{8,12},{9,5},{1... | collective-permute-start | bytes 884744 | tf_op jit(solution)/shard_map/ppermute | solution.py:62
  146.4 1.5 collective-permute-start.27
  147.9 24.7 %three_heads.2 = (bf16[256,384]{1,0:T(8,128)(2,1)}, bf16[256,384]{1,0:T(8,128)(2,1)}) custom-call(s32[12]{0:T(128)} %broadcast_select_fusion.2.order_ref, s32[8]{0:T(128)} %get-tuple-element.130.at_ref.mine_ref, f32[12]{0:T(128)} %stack.60.far_ref, bf16[256,1536]{1,0:T(8,128)(2,1)} %modulate.1.refs_0_, bf16[256,1536]{1,0:T(8,128)(2,1)} %collective-permute-done.2.refs_1_, ...), custom_call_target="tpu_custom_call" | custom-call | flops 9663676416 | bytes 12976128 | tf_op jit(solution)/shard_map/three_heads/pallas_call | solution.py:192
  172.8 0.6 copy-done.2
  173.4 0.1 copy-done.3
  173.5 0.1 copy-done.4
  173.7 0.2 copy-done.39
  173.9 45.8 %stack.61 = bf16[960,768]{1,0:T(8,128)(2,1)} custom-call(bf16[192,768]{1,0:T(8,128)(2,1)} %copy-done, bf16[192,768]{1,0:T(8,128)(2,1)} %copy-done.5, bf16[192,768]{1,0:T(8,128)(2,1)} %copy-done.4, bf16[192,768]{1,0:T(8,128)(2,1)} %copy-done.3, bf16[192,768]{1,0:T(8,128)(2,1)} %copy-done.2), custom_call_target="tpu_custom_call" | custom-call | bytes 2949120 | tf_op jit(solution)/shard_map/stack/pallas_call | solution.py:236
  219.9 3.5 %collective-permute-start.36 = (bf16[192,768]{1,0:T(8,128)(2,1)}, bf16[192,768]{1,0:T(8,128)(2,1)S(1)}, u32[]{:S(2)}, u32[]{:S(2)}) collective-permute-start(bf16[192,768]{1,0:T(8,128)(2,1)} %copy-done.3), channel_id=1, source_target_pairs={{0,8},{1,25},{2,10},{3,27},{4,12},{5,29},{6,14},{7,31},{8,16},{9,1... | collective-permute-start | bytes 884744 | tf_op jit(solution)/shard_map/ppermute | solution.py:62
  223.4 1.2 collective-permute-start.34
  224.6 24.8 %three_heads.3 = (bf16[256,384]{1,0:T(8,128)(2,1)}, bf16[256,384]{1,0:T(8,128)(2,1)}) custom-call(s32[12]{0:T(128)} %broadcast_select_fusion.2.order_ref, s32[8]{0:T(128)} %get-tuple-element.130.at_ref.mine_ref, f32[12]{0:T(128)} %stack.60.far_ref, bf16[256,1536]{1,0:T(8,128)(2,1)} %modulate.1.refs_0_, bf16[256,1536]{1,0:T(8,128)(2,1)} %collective-permute-done.2.refs_1_, ...), custom_call_target="tpu_custom_call" | custom-call | flops 9663676416 | bytes 12976128 | tf_op jit(solution)/shard_map/three_heads/pallas_call | solution.py:192
  249.5 0.6 collective-permute-start.38
  250.1 0.1 collective-permute-start.39
  250.2 0.4 collective-permute-start.40
  250.6 0.1 collective-permute-start.37
  250.7 0.6 reshape.30.gate_ref
  251.3 0.6 pad_add_fusion.at_ref
  251.9 0.8 collective-permute-done.37.a3
  252.8 0.6 copy-done.11
  253.5 0.1 copy-done.13
  253.6 5.8 %project_out.1 = bf16[256,1536]{1,0:T(8,128)(2,1)} custom-call(s32[1]{0:T(128)} %bitcast.c_ref, s32[4]{0:T(128)} %pad_add_fusion.at_ref, s32[8]{0:T(128)} %get-tuple-element.130.at_ref.mine_ref, s32[8]{0:T(128)} %get-tuple-element.129.theirs_ref, bf16[256,384]{1,0:T(8,128)(2,1)} %get-tuple-element.97.a0, bf16[256,384]{1,0:T(8,128)(2,1)} %get-tuple-element.106.a1, ...), custom_call_target="tpu_custom_call" | custom-call | flops 1207959552 | bytes 6291456 | tf_op jit(solution)/shard_map/project_out/pallas_call | solution.py:278
  (123 shorter events, 1.1 us)
Async XLA Ops:
  1.9 9.6 %collective-permute-start = (bf16[48,1920]{1,0:T(8,128)(2,1)S(1)}, bf16[48,1920]{1,0:T(8,128)(2,1)S(1)}, u32[]{:S(2)}, u32[]{:S(2)}) collective-permute-start(bf16[48,1920]{1,0:T(8,128)(2,1)S(1)} %pad_maximum_fusion.2), channel_id=1, source_target_pairs={{0,1},{1,0},{2,3},{3,2},{4,5},{5,4},{6,7},{7,6},{8,9},{9,8},{10,11... | collective-permute-start | bytes 552968 | tf_op jit(solution)/shard_map/ppermute | solution.py:62
  11.5 21.5 %collective-permute-start.3 = (bf16[256,1536]{1,0:T(8,128)(2,1)}, bf16[256,1536]{1,0:T(8,128)(2,1)S(1)}, u32[]{:S(2)}, u32[]{:S(2)}) collective-permute-start(bf16[256,1536]{1,0:T(8,128)(2,1)} %modulate.1.refs_0_), channel_id=1, source_target_pairs={{0,1},{1,0},{2,3},{3,2},{4,5},{5,4},{6,7},{7,6},{8,9},{9,8},{10,11... | collective-permute-start | bytes 2359304 | tf_op jit(solution)/shard_map/ppermute | solution.py:62
  11.5 21.5 %collective-permute-start.2 = (bf16[256,1536]{1,0:T(8,128)(2,1)}, bf16[256,1536]{1,0:T(8,128)(2,1)}, u32[]{:S(2)}, u32[]{:S(2)}) collective-permute-start(bf16[256,1536]{1,0:T(8,128)(2,1)} %modulate.1.refs_0_), channel_id=1, source_target_pairs={{0,32},{1,35},{2,34},{3,37},{4,36},{5,39},{6,38},{7,41},{8,40},{9,... | collective-permute-start | bytes 2359304 | tf_op jit(solution)/shard_map/ppermute | solution.py:62
  12.7 20.3 %collective-permute-start.1 = (bf16[96,1920]{1,0:T(8,128)(2,1)S(1)}, bf16[96,1920]{1,0:T(8,128)(2,1)S(1)}, u32[]{:S(2)}, u32[]{:S(2)}) collective-permute-start(bf16[96,1920]{1,0:T(8,128)(2,1)S(1)} %maximum_select_fusion), channel_id=1, source_target_pairs={{0,34},{1,35},{2,32},{3,33},{4,38},{5,39},{6,36},{7,37},{8,42},{9,... | collective-permute-start | bytes 1105928 | tf_op jit(solution)/shard_map/ppermute | solution.py:62
  15.0 40.0 %copy-start.6 = (bf16[256,1536]{1,0:T(8,128)(2,1)S(1)}, bf16[256,1536]{1,0:T(8,128)(2,1)}, u32[]{:S(2)}) copy-start(bf16[256,1536]{1,0:T(8,128)(2,1)} %modulate.1.refs_0_) | copy-start | bytes 2359300
  15.0 119.0 %copy-start.16 = (s32[8]{0:T(128)S(1)}, s32[8]{0:T(128)}, u32[]{:S(2)}) copy-start(s32[8]{0:T(128)} %constant.83.clone) | copy-start | bytes 100
  15.0 119.5 %copy-start.17 = (s32[12]{0:T(128)S(1)}, s32[12]{0:T(128)}, u32[]{:S(2)}) copy-start(s32[12]{0:T(128)} %constant.82.clone) | copy-start | bytes 148
  15.0 119.5 %copy-start.18 = (s32[12]{0:T(128)S(1)}, s32[12]{0:T(128)}, u32[]{:S(2)}) copy-start(s32[12]{0:T(128)} %constant.81.clone) | copy-start | bytes 148
  33.0 22.0 %collective-permute-start.7 = (bf16[256,1536]{1,0:T(8,128)(2,1)}, bf16[256,1536]{1,0:T(8,128)(2,1)S(1)}, u32[]{:S(2)}, u32[]{:S(2)}) collective-permute-start(bf16[256,1536]{1,0:T(8,128)(2,1)} %modulate.1.refs_0_), channel_id=1, source_target_pairs={{0,62},{1,33},{2,32},{3,35},{4,34},{5,37},{6,36},{7,39},{8,38},{9,... | collective-permute-start | bytes 2359304 | tf_op jit(solution)/shard_map/ppermute | solution.py:62
  33.1 21.9 %collective-permute-start.8 = (bf16[256,1536]{1,0:T(8,128)(2,1)}, bf16[256,1536]{1,0:T(8,128)(2,1)S(1)}, u32[]{:S(2)}, u32[]{:S(2)}) collective-permute-start(bf16[256,1536]{1,0:T(8,128)(2,1)} %collective-permute-done.2.refs_1_), channel_id=1, source_target_pairs={{0,1},{1,0},{2,3},{3,2},{4,5},{5,4},{6,7},{7,6},{8,9},{9,8},{10,11... | collective-permute-start | bytes 2359304 | tf_op jit(solution)/shard_map/ppermute | solution.py:62
  38.2 97.3 %copy-start.7 = (bf16[192,1152]{1,0:T(8,128)(2,1)}, bf16[192,1152]{1,0:T(8,128)(2,1)S(1)}, u32[]{:S(2)}) copy-start(bf16[192,1152]{1,0:T(8,128)(2,1)S(1)} %pad_maximum_fusion.refs_12_) | copy-start | bytes 1327108
  38.2 8.7 %collective-permute-start.6 = (bf16[192,1152]{1,0:T(8,128)(2,1)S(1)}, bf16[192,1152]{1,0:T(8,128)(2,1)S(1)}, u32[]{:S(2)}, u32[]{:S(2)}) collective-permute-start(bf16[192,1152]{1,0:T(8,128)(2,1)S(1)} %pad_maximum_fusion.refs_12_), channel_id=1, source_target_pairs={{0,192},{1,65},{2,194},{3,67},{4,196},{5,69},{6,198},{7,71},{8,200... | collective-permute-start | bytes 1327112 | tf_op jit(solution)/shard_map/ppermute | solution.py:62
  39.5 10.4 %collective-permute-start.5 = (bf16[192,1152]{1,0:T(8,128)(2,1)S(1)}, bf16[192,1152]{1,0:T(8,128)(2,1)S(1)}, u32[]{:S(2)}, u32[]{:S(2)}) collective-permute-start(bf16[192,1152]{1,0:T(8,128)(2,1)S(1)} %pad_maximum_fusion.refs_12_), channel_id=1, source_target_pairs={{0,28},{1,5},{2,30},{3,7},{4,0},{5,9},{6,2},{7,11},{8,4},{9,13},{1... | collective-permute-start | bytes 1327112 | tf_op jit(solution)/shard_map/ppermute | solution.py:62
  39.5 12.7 %collective-permute-start.4 = (bf16[192,1152]{1,0:T(8,128)(2,1)S(1)}, bf16[192,1152]{1,0:T(8,128)(2,1)S(1)}, u32[]{:S(2)}, u32[]{:S(2)}) collective-permute-start(bf16[192,1152]{1,0:T(8,128)(2,1)S(1)} %pad_maximum_fusion.refs_12_), channel_id=1, source_target_pairs={{0,4},{1,29},{2,6},{3,31},{4,8},{5,1},{6,10},{7,3},{8,12},{9,5},{1... | collective-permute-start | bytes 1327112 | tf_op jit(solution)/shard_map/ppermute | solution.py:62
  46.9 66.7 %copy-start.25 = (bf16[192,1152]{1,0:T(8,128)(2,1)}, bf16[192,1152]{1,0:T(8,128)(2,1)S(1)}, u32[]{:S(2)}) copy-start(bf16[192,1152]{1,0:T(8,128)(2,1)S(1)} %collective-permute-done.6.refs_12_) | copy-start | bytes 1327108
  49.9 82.9 %copy-start.28 = (bf16[192,1152]{1,0:T(8,128)(2,1)}, bf16[192,1152]{1,0:T(8,128)(2,1)S(1)}, u32[]{:S(2)}) copy-start(bf16[192,1152]{1,0:T(8,128)(2,1)S(1)} %collective-permute-done.5.refs_14_) | copy-start | bytes 1327108
  52.2 80.6 %copy-start.29 = (bf16[192,1152]{1,0:T(8,128)(2,1)}, bf16[192,1152]{1,0:T(8,128)(2,1)S(1)}, u32[]{:S(2)}) copy-start(bf16[192,1152]{1,0:T(8,128)(2,1)S(1)} %collective-permute-done.4.refs_13_) | copy-start | bytes 1327108
  54.9 76.7 %copy-start.20 = (bf16[256,1536]{1,0:T(8,128)(2,1)}, bf16[256,1536]{1,0:T(8,128)(2,1)S(1)}, u32[]{:S(2)}) copy-start(bf16[256,1536]{1,0:T(8,128)(2,1)S(1)} %collective-permute-done.7.refs_2_) | copy-start | bytes 2359300
  55.0 76.7 %copy-start.21 = (bf16[256,1536]{1,0:T(8,128)(2,1)}, bf16[256,1536]{1,0:T(8,128)(2,1)S(1)}, u32[]{:S(2)}) copy-start(bf16[256,1536]{1,0:T(8,128)(2,1)S(1)} %collective-permute-done.8.refs_7_) | copy-start | bytes 2359300
  55.0 31.0 %collective-permute-start.13 = (bf16[256,1536]{1,0:T(8,128)(2,1)S(1)}, bf16[256,1536]{1,0:T(8,128)(2,1)S(1)}, u32[]{:S(2)}, u32[]{:S(2)}) collective-permute-start(bf16[256,1536]{1,0:T(8,128)(2,1)S(1)} %copy-done.6), channel_id=1, source_target_pairs={{0,224},{1,227},{2,226},{3,229},{4,228},{5,231},{6,230},{7,233},{8... | collective-permute-start | bytes 2359304 | tf_op jit(solution)/shard_map/ppermute | solution.py:62
  59.9 26.0 %collective-permute-start.11 = (bf16[192,1152]{1,0:T(8,128)(2,1)S(1)}, bf16[192,1152]{1,0:T(8,128)(2,1)S(1)}, u32[]{:S(2)}, u32[]{:S(2)}) collective-permute-start(bf16[192,1152]{1,0:T(8,128)(2,1)S(1)} %collective-permute-done.4.refs_13_), channel_id=1, source_target_pairs={{0,64},{1,193},{2,66},{3,195},{4,68},{5,197},{6,70},{7,199},{8,72}... | collective-permute-start | bytes 1327112 | tf_op jit(solution)/shard_map/ppermute | solution.py:62
  60.4 25.5 %collective-permute-start.9 = (bf16[192,1152]{1,0:T(8,128)(2,1)S(1)}, bf16[192,1152]{1,0:T(8,128)(2,1)S(1)}, u32[]{:S(2)}, u32[]{:S(2)}) collective-permute-start(bf16[192,1152]{1,0:T(8,128)(2,1)S(1)} %collective-permute-done.4.refs_13_), channel_id=1, source_target_pairs={{0,4},{1,29},{2,6},{3,31},{4,8},{5,1},{6,10},{7,3},{8,12},{9,5},{1... | collective-permute-start | bytes 1327112 | tf_op jit(solution)/shard_map/ppermute | solution.py:62
  66.0 19.9 %collective-permute-start.12 = (bf16[192,1152]{1,0:T(8,128)(2,1)S(1)}, bf16[192,1152]{1,0:T(8,128)(2,1)S(1)}, u32[]{:S(2)}, u32[]{:S(2)}) collective-permute-start(bf16[192,1152]{1,0:T(8,128)(2,1)S(1)} %collective-permute-done.5.refs_14_), channel_id=1, source_target_pairs={{0,192},{1,65},{2,194},{3,67},{4,196},{5,69},{6,198},{7,71},{8,200... | collective-permute-start | bytes 1327112 | tf_op jit(solution)/shard_map/ppermute | solution.py:62
  67.0 18.9 %collective-permute-start.10 = (bf16[192,1152]{1,0:T(8,128)(2,1)S(1)}, bf16[192,1152]{1,0:T(8,128)(2,1)S(1)}, u32[]{:S(2)}, u32[]{:S(2)}) collective-permute-start(bf16[192,1152]{1,0:T(8,128)(2,1)S(1)} %collective-permute-done.5.refs_14_), channel_id=1, source_target_pairs={{0,28},{1,5},{2,30},{3,7},{4,0},{5,9},{6,2},{7,11},{8,4},{9,13},{1... | collective-permute-start | bytes 1327112 | tf_op jit(solution)/shard_map/ppermute | solution.py:62
  85.9 27.7 %copy-start.26 = (bf16[192,1152]{1,0:T(8,128)(2,1)}, bf16[192,1152]{1,0:T(8,128)(2,1)S(1)}, u32[]{:S(2)}) copy-start(bf16[192,1152]{1,0:T(8,128)(2,1)S(1)} %collective-permute-done.11.refs_13_) | copy-start | bytes 1327108
  85.9 46.9 %copy-start.32 = (bf16[192,1152]{1,0:T(8,128)(2,1)}, bf16[192,1152]{1,0:T(8,128)(2,1)S(1)}, u32[]{:S(2)}) copy-start(bf16[192,1152]{1,0:T(8,128)(2,1)S(1)} %collective-permute-done.9.refs_15_) | copy-start | bytes 1327108
  85.9 46.9 %copy-start.27 = (bf16[192,1152]{1,0:T(8,128)(2,1)}, bf16[192,1152]{1,0:T(8,128)(2,1)S(1)}, u32[]{:S(2)}) copy-start(bf16[192,1152]{1,0:T(8,128)(2,1)S(1)} %collective-permute-done.12.refs_14_) | copy-start | bytes 1327108
  85.9 46.9 %copy-start.33 = (bf16[192,1152]{1,0:T(8,128)(2,1)}, bf16[192,1152]{1,0:T(8,128)(2,1)S(1)}, u32[]{:S(2)}) copy-start(bf16[192,1152]{1,0:T(8,128)(2,1)S(1)} %collective-permute-done.10.refs_16_) | copy-start | bytes 1327108
  86.0 49.5 %copy-start.22 = (bf16[256,1536]{1,0:T(8,128)(2,1)}, bf16[256,1536]{1,0:T(8,128)(2,1)S(1)}, u32[]{:S(2)}) copy-start(bf16[256,1536]{1,0:T(8,128)(2,1)S(1)} %collective-permute-done.13.refs_3_) | copy-start | bytes 2359300
  86.0 27.6 %collective-permute-start.18 = (bf16[256,1536]{1,0:T(8,128)(2,1)S(1)}, bf16[256,1536]{1,0:T(8,128)(2,1)}, u32[]{:S(2)}, u32[]{:S(2)}) collective-permute-start(bf16[256,1536]{1,0:T(8,128)(2,1)S(1)} %copy-done.6), channel_id=1, source_target_pairs={{0,254},{1,225},{2,224},{3,227},{4,226},{5,229},{6,228},{7,231},{8... | collective-permute-start | bytes 2359304 | tf_op jit(solution)/shard_map/ppermute | solution.py:62
  86.1 27.5 %collective-permute-start.16 = (bf16[192,1152]{1,0:T(8,128)(2,1)S(1)}, bf16[192,1152]{1,0:T(8,128)(2,1)S(1)}, u32[]{:S(2)}, u32[]{:S(2)}) collective-permute-start(bf16[192,1152]{1,0:T(8,128)(2,1)S(1)} %collective-permute-done.9.refs_15_), channel_id=1, source_target_pairs={{0,64},{1,193},{2,66},{3,195},{4,68},{5,197},{6,70},{7,199},{8,72}... | collective-permute-start | bytes 1327112 | tf_op jit(solution)/shard_map/ppermute | solution.py:62
  87.4 26.1 %collective-permute-start.14 = (bf16[192,1152]{1,0:T(8,128)(2,1)S(1)}, bf16[192,1152]{1,0:T(8,128)(2,1)S(1)}, u32[]{:S(2)}, u32[]{:S(2)}) collective-permute-start(bf16[192,1152]{1,0:T(8,128)(2,1)S(1)} %collective-permute-done.9.refs_15_), channel_id=1, source_target_pairs={{0,4},{1,29},{2,6},{3,31},{4,8},{5,1},{6,10},{7,3},{8,12},{9,5},{1... | collective-permute-start | bytes 1327112 | tf_op jit(solution)/shard_map/ppermute | solution.py:62
  101.9 11.7 %collective-permute-start.17 = (bf16[192,1152]{1,0:T(8,128)(2,1)S(1)}, bf16[192,1152]{1,0:T(8,128)(2,1)S(1)}, u32[]{:S(2)}, u32[]{:S(2)}) collective-permute-start(bf16[192,1152]{1,0:T(8,128)(2,1)S(1)} %collective-permute-done.10.refs_16_), channel_id=1, source_target_pairs={{0,192},{1,65},{2,194},{3,67},{4,196},{5,69},{6,198},{7,71},{8,200... | collective-permute-start | bytes 1327112 | tf_op jit(solution)/shard_map/ppermute | solution.py:62
  103.1 10.5 %collective-permute-start.15 = (bf16[192,1152]{1,0:T(8,128)(2,1)S(1)}, bf16[192,1152]{1,0:T(8,128)(2,1)S(1)}, u32[]{:S(2)}, u32[]{:S(2)}) collective-permute-start(bf16[192,1152]{1,0:T(8,128)(2,1)S(1)} %collective-permute-done.10.refs_16_), channel_id=1, source_target_pairs={{0,28},{1,5},{2,30},{3,7},{4,0},{5,9},{6,2},{7,11},{8,4},{9,13},{1... | collective-permute-start | bytes 1327112 | tf_op jit(solution)/shard_map/ppermute | solution.py:62
  113.6 19.3 %copy-start.30 = (bf16[192,1152]{1,0:T(8,128)(2,1)}, bf16[192,1152]{1,0:T(8,128)(2,1)S(1)}, u32[]{:S(2)}) copy-start(bf16[192,1152]{1,0:T(8,128)(2,1)S(1)} %collective-permute-done.16.refs_15_) | copy-start | bytes 1327108
  113.6 19.3 %copy-start.36 = (bf16[192,1152]{1,0:T(8,128)(2,1)}, bf16[192,1152]{1,0:T(8,128)(2,1)S(1)}, u32[]{:S(2)}) copy-start(bf16[192,1152]{1,0:T(8,128)(2,1)S(1)} %collective-permute-done.14.refs_17_) | copy-start | bytes 1327108
  113.6 19.3 %copy-start.31 = (bf16[192,1152]{1,0:T(8,128)(2,1)}, bf16[192,1152]{1,0:T(8,128)(2,1)S(1)}, u32[]{:S(2)}) copy-start(bf16[192,1152]{1,0:T(8,128)(2,1)S(1)} %collective-permute-done.17.refs_16_) | copy-start | bytes 1327108
  113.6 19.3 %copy-start.37 = (bf16[192,1152]{1,0:T(8,128)(2,1)}, bf16[192,1152]{1,0:T(8,128)(2,1)S(1)}, u32[]{:S(2)}) copy-start(bf16[192,1152]{1,0:T(8,128)(2,1)S(1)} %collective-permute-done.15.refs_18_) | copy-start | bytes 1327108
  113.7 18.0 %collective-permute-start.22 = (bf16[256,1536]{1,0:T(8,128)(2,1)S(1)}, bf16[256,1536]{1,0:T(8,128)(2,1)}, u32[]{:S(2)}, u32[]{:S(2)}) collective-permute-start(bf16[256,1536]{1,0:T(8,128)(2,1)S(1)} %copy-done.6), channel_id=1, source_target_pairs={{0,30},{1,3},{2,0},{3,5},{4,2},{5,7},{6,4},{7,9},{8,6},{9,11},{10,... | collective-permute-start | bytes 2359304 | tf_op jit(solution)/shard_map/ppermute | solution.py:62
  113.7 17.9 %collective-permute-start.23 = (bf16[256,1536]{1,0:T(8,128)(2,1)S(1)}, bf16[256,1536]{1,0:T(8,128)(2,1)S(1)}, u32[]{:S(2)}, u32[]{:S(2)}) collective-permute-start(bf16[256,1536]{1,0:T(8,128)(2,1)S(1)} %collective-permute-done.7.refs_2_), channel_id=1, source_target_pairs={{0,1},{1,0},{2,3},{3,2},{4,5},{5,4},{6,7},{7,6},{8,9},{9,8},{10,11... | collective-permute-start | bytes 2359304 | tf_op jit(solution)/shard_map/ppermute | solution.py:62
  117.7 10.3 %collective-permute-start.21 = (bf16[192,1152]{1,0:T(8,128)(2,1)S(1)}, bf16[192,1152]{1,0:T(8,128)(2,1)S(1)}, u32[]{:S(2)}, u32[]{:S(2)}) collective-permute-start(bf16[192,1152]{1,0:T(8,128)(2,1)S(1)} %collective-permute-done.15.refs_18_), channel_id=1, source_target_pairs={{0,192},{1,65},{2,194},{3,67},{4,196},{5,69},{6,198},{7,71},{8,200... | collective-permute-start | bytes 1327112 | tf_op jit(solution)/shard_map/ppermute | solution.py:62
  118.8 11.6 %collective-permute-start.20 = (bf16[192,1152]{1,0:T(8,128)(2,1)S(1)}, bf16[192,1152]{1,0:T(8,128)(2,1)S(1)}, u32[]{:S(2)}, u32[]{:S(2)}) collective-permute-start(bf16[192,1152]{1,0:T(8,128)(2,1)S(1)} %collective-permute-done.14.refs_17_), channel_id=1, source_target_pairs={{0,64},{1,193},{2,66},{3,195},{4,68},{5,197},{6,70},{7,199},{8,72}... | collective-permute-start | bytes 1327112 | tf_op jit(solution)/shard_map/ppermute | solution.py:62
  120.7 10.9 %collective-permute-start.19 = (bf16[192,1152]{1,0:T(8,128)(2,1)S(1)}, bf16[192,1152]{1,0:T(8,128)(2,1)S(1)}, u32[]{:S(2)}, u32[]{:S(2)}) collective-permute-start(bf16[192,1152]{1,0:T(8,128)(2,1)S(1)} %collective-permute-done.14.refs_17_), channel_id=1, source_target_pairs={{0,4},{1,29},{2,6},{3,31},{4,8},{5,1},{6,10},{7,3},{8,12},{9,5},{1... | collective-permute-start | bytes 1327112 | tf_op jit(solution)/shard_map/ppermute | solution.py:62
  131.6 16.3 %copy-start.38 = (bf16[192,1152]{1,0:T(8,128)(2,1)}, bf16[192,1152]{1,0:T(8,128)(2,1)S(1)}, u32[]{:S(2)}) copy-start(bf16[192,1152]{1,0:T(8,128)(2,1)S(1)} %collective-permute-done.19.refs_19_) | copy-start | bytes 1327108
  131.6 3.5 %collective-permute-start.24 = (bf16[256,1536]{1,0:T(8,128)(2,1)S(1)}, bf16[256,1536]{1,0:T(8,128)(2,1)S(1)}, u32[]{:S(2)}, u32[]{:S(2)}) collective-permute-start(bf16[256,1536]{1,0:T(8,128)(2,1)S(1)} %collective-permute-done.13.refs_3_), channel_id=1, source_target_pairs={{0,1},{1,0},{2,3},{3,2},{4,5},{5,4},{6,7},{7,6},{8,9},{9,8},{10,11... | collective-permute-start | bytes 2359304 | tf_op jit(solution)/shard_map/ppermute | solution.py:62
  132.6 2.9 %collective-permute-start.25 = (bf16[256,1536]{1,0:T(8,128)(2,1)}, bf16[256,1536]{1,0:T(8,128)(2,1)}, u32[]{:S(2)}, u32[]{:S(2)}) collective-permute-start(bf16[256,1536]{1,0:T(8,128)(2,1)} %collective-permute-done.18.refs_4_), channel_id=1, source_target_pairs={{0,1},{1,0},{2,3},{3,2},{4,5},{5,4},{6,7},{7,6},{8,9},{9,8},{10,11... | collective-permute-start | bytes 2359304 | tf_op jit(solution)/shard_map/ppermute | solution.py:62
  132.9 3.7 %collective-permute-start.26 = (bf16[256,1536]{1,0:T(8,128)(2,1)}, bf16[256,1536]{1,0:T(8,128)(2,1)}, u32[]{:S(2)}, u32[]{:S(2)}) collective-permute-start(bf16[256,1536]{1,0:T(8,128)(2,1)} %collective-permute-done.22.refs_5_), channel_id=1, source_target_pairs={{0,1},{1,0},{2,3},{3,2},{4,5},{5,4},{6,7},{7,6},{8,9},{9,8},{10,11... | collective-permute-start | bytes 2359304 | tf_op jit(solution)/shard_map/ppermute | solution.py:62
  135.2 37.5 %copy-start = (bf16[192,768]{1,0:T(8,128)(2,1)}, bf16[192,768]{1,0:T(8,128)(2,1)S(1)}, u32[]{:S(2)}) copy-start(bf16[192,768]{1,0:T(8,128)(2,1)S(1)} %pad_maximum_fusion.1.refs_0_) | copy-start | bytes 884740
  136.6 36.1 %collective-permute-start.31 = (bf16[192,768]{1,0:T(8,128)(2,1)S(1)}, bf16[192,768]{1,0:T(8,128)(2,1)S(1)}, u32[]{:S(2)}, u32[]{:S(2)}) collective-permute-start(bf16[192,768]{1,0:T(8,128)(2,1)S(1)} %pad_maximum_fusion.1.refs_0_), channel_id=1, source_target_pairs={{0,24},{1,9},{2,26},{3,11},{4,28},{5,13},{6,30},{7,15},{8,0},{9,17... | collective-permute-start | bytes 884744 | tf_op jit(solution)/shard_map/ppermute | solution.py:62
  140.6 32.1 %collective-permute-start.30 = (bf16[192,768]{1,0:T(8,128)(2,1)S(1)}, bf16[192,768]{1,0:T(8,128)(2,1)S(1)}, u32[]{:S(2)}, u32[]{:S(2)}) collective-permute-start(bf16[192,768]{1,0:T(8,128)(2,1)S(1)} %pad_maximum_fusion.1.refs_0_), channel_id=1, source_target_pairs={{0,8},{1,25},{2,10},{3,27},{4,12},{5,29},{6,14},{7,31},{8,16},{9,1... | collective-permute-start | bytes 884744 | tf_op jit(solution)/shard_map/ppermute | solution.py:62
  143.7 29.0 %collective-permute-start.29 = (bf16[192,768]{1,0:T(8,128)(2,1)S(1)}, bf16[192,768]{1,0:T(8,128)(2,1)S(1)}, u32[]{:S(2)}, u32[]{:S(2)}) collective-permute-start(bf16[192,768]{1,0:T(8,128)(2,1)S(1)} %pad_maximum_fusion.1.refs_0_), channel_id=1, source_target_pairs={{0,28},{1,5},{2,30},{3,7},{4,0},{5,9},{6,2},{7,11},{8,4},{9,13},{1... | collective-permute-start | bytes 884744 | tf_op jit(solution)/shard_map/ppermute | solution.py:62
  143.8 29.0 %collective-permute-start.28 = (bf16[192,768]{1,0:T(8,128)(2,1)S(1)}, bf16[192,768]{1,0:T(8,128)(2,1)S(1)}, u32[]{:S(2)}, u32[]{:S(2)}) collective-permute-start(bf16[192,768]{1,0:T(8,128)(2,1)S(1)} %pad_maximum_fusion.1.refs_0_), channel_id=1, source_target_pairs={{0,4},{1,29},{2,6},{3,31},{4,8},{5,1},{6,10},{7,3},{8,12},{9,5},{1... | collective-permute-start | bytes 884744 | tf_op jit(solution)/shard_map/ppermute | solution.py:62
  146.4 26.4 %collective-permute-start.27 = (bf16[192,1152]{1,0:T(8,128)(2,1)S(1)}, bf16[192,1152]{1,0:T(8,128)(2,1)S(1)}, u32[]{:S(2)}, u32[]{:S(2)}) collective-permute-start(bf16[192,1152]{1,0:T(8,128)(2,1)S(1)} %collective-permute-done.19.refs_19_), channel_id=1, source_target_pairs={{0,64},{1,193},{2,66},{3,195},{4,68},{5,197},{6,70},{7,199},{8,72}... | collective-permute-start | bytes 1327112 | tf_op jit(solution)/shard_map/ppermute | solution.py:62
  173.9 50.7 %copy-start.40 = (bf16[256,384]{1,0:T(8,128)(2,1)S(1)}, bf16[256,384]{1,0:T(8,128)(2,1)}, u32[]{:S(2)}) copy-start(bf16[256,384]{1,0:T(8,128)(2,1)} %get-tuple-element.108) | copy-start | bytes 589828
  219.7 31.0 %copy-start.15 = (f32[1536]{0:T(1024)S(1)}, f32[1536]{0:T(1024)}, u32[]{:S(2)}) copy-start(f32[1536]{0:T(1024)} %param.14) | copy-start | bytes 18436
  219.7 29.8 %collective-permute-start.33 = (bf16[960,768]{1,0:T(8,128)(2,1)}, bf16[960,768]{1,0:T(8,128)(2,1)S(1)}, u32[]{:S(2)}, u32[]{:S(2)}) collective-permute-start(bf16[960,768]{1,0:T(8,128)(2,1)} %stack.61), channel_id=1, source_target_pairs={{0,1},{1,0},{2,3},{3,2},{4,5},{5,4},{6,7},{7,6},{8,9},{9,8},{10,11... | collective-permute-start | bytes 4423688 | tf_op jit(solution)/shard_map/ppermute | solution.py:62
  219.8 29.6 %collective-permute-start.35 = (bf16[192,768]{1,0:T(8,128)(2,1)}, bf16[192,768]{1,0:T(8,128)(2,1)S(1)}, u32[]{:S(2)}, u32[]{:S(2)}) collective-permute-start(bf16[192,768]{1,0:T(8,128)(2,1)} %copy-done.2), channel_id=1, source_target_pairs={{0,28},{1,5},{2,30},{3,7},{4,0},{5,9},{6,2},{7,11},{8,4},{9,13},{1... | collective-permute-start | bytes 884744 | tf_op jit(solution)/shard_map/ppermute | solution.py:62
  219.9 29.5 %collective-permute-start.36 = (bf16[192,768]{1,0:T(8,128)(2,1)}, bf16[192,768]{1,0:T(8,128)(2,1)S(1)}, u32[]{:S(2)}, u32[]{:S(2)}) collective-permute-start(bf16[192,768]{1,0:T(8,128)(2,1)} %copy-done.3), channel_id=1, source_target_pairs={{0,8},{1,25},{2,10},{3,27},{4,12},{5,29},{6,14},{7,31},{8,16},{9,1... | collective-permute-start | bytes 884744 | tf_op jit(solution)/shard_map/ppermute | solution.py:62
  223.4 26.1 %collective-permute-start.34 = (bf16[192,768]{1,0:T(8,128)(2,1)}, bf16[192,768]{1,0:T(8,128)(2,1)S(1)}, u32[]{:S(2)}, u32[]{:S(2)}) collective-permute-start(bf16[192,768]{1,0:T(8,128)(2,1)} %copy-done.3), channel_id=1, source_target_pairs={{0,4},{1,29},{2,6},{3,31},{4,8},{5,1},{6,10},{7,3},{8,12},{9,5},{1... | collective-permute-start | bytes 884744 | tf_op jit(solution)/shard_map/ppermute | solution.py:62
  224.6 24.8 %collective-permute-start.32 = (bf16[256,384]{1,0:T(8,128)(2,1)S(1)}, bf16[256,384]{1,0:T(8,128)(2,1)S(1)}, u32[]{:S(2)}, u32[]{:S(2)}) collective-permute-start(bf16[256,384]{1,0:T(8,128)(2,1)S(1)} %copy-done.40), channel_id=1, source_target_pairs={{0,1},{1,0},{2,3},{3,2},{4,5},{5,4},{6,7},{7,6},{8,9},{9,8},{10,11... | collective-permute-start | bytes 589832 | tf_op jit(solution)/shard_map/ppermute | solution.py:62
  249.5 3.2 %collective-permute-start.38 = (bf16[192,768]{1,0:T(8,128)(2,1)S(1)}, bf16[192,768]{1,0:T(8,128)(2,1)S(1)}, u32[]{:S(2)}, u32[]{:S(2)}) collective-permute-start(bf16[192,768]{1,0:T(8,128)(2,1)S(1)} %collective-permute-done.34.refs_5_), channel_id=1, source_target_pairs={{0,1},{1,0},{2,3},{3,2},{4,5},{5,4},{6,7},{7,6},{8,9},{9,8},{10,11... | collective-permute-start | bytes 884744 | tf_op jit(solution)/shard_map/ppermute | solution.py:62
  250.1 2.6 %collective-permute-start.39 = (bf16[192,768]{1,0:T(8,128)(2,1)S(1)}, bf16[192,768]{1,0:T(8,128)(2,1)S(1)}, u32[]{:S(2)}, u32[]{:S(2)}) collective-permute-start(bf16[192,768]{1,0:T(8,128)(2,1)S(1)} %collective-permute-done.35.refs_6_), channel_id=1, source_target_pairs={{0,1},{1,0},{2,3},{3,2},{4,5},{5,4},{6,7},{7,6},{8,9},{9,8},{10,11... | collective-permute-start | bytes 884744 | tf_op jit(solution)/shard_map/ppermute | solution.py:62
  250.2 2.6 collective-permute-start.40
  250.6 2.1 collective-permute-start.37
  (18 other events, 49.7 us)

commit v5 on v4

v5 whole, which is shorter than its diff:
```python
import functools
import itertools

import jax
import jax.numpy as jnp
from jax import lax
from jax.experimental import pallas as pl
from jax.experimental.pallas import tpu as pltpu
from jax.sharding import Mesh
from jax.sharding import PartitionSpec as P

HEADS = 12
HD = 128
TILE_T = 4
EPS = 1e-06
HALF = 3 * HD
AXES = ("x", "l", "z", "u", "c")
SIZES = (4, 2, 8, 2, 2)
FAR = 1e30
BF = jnp.bfloat16
F32 = jnp.float32


def hops(move):
    pairs = []
    for x, l, z, u, c in itertools.product(*map(range, SIZES)):
        x2, y2, z2, c2 = move(x, u * 2 + l, z, c)
        to = (x2 % 4, y2 % 2, z2 % 8, y2 % 4 // 2, c2)
        rank = [functools.reduce(lambda r, d: r * d[0] + d[1], zip(SIZES, at), 0) for at in ((x, l, z, u, c), to)]
        pairs.append(tuple(rank))
    return pairs


def tile_hop(down, across):
    def move(x, y, z, c):
        h, w = ((x * 2 + y % 2 + down) % 8, (z * 2 + y // 2 + across[c]) % 16)
        return h // 2, w % 2 * 2 + h % 2, w // 2, c

    return hops(move)


SIBLING = hops(lambda x, y, z, c: (x, y, z, 1 - c))
U_FLIP = hops(lambda x, y, z, c: (x, y + 2, z, c))
NEAR = (
    hops(lambda x, y, z, c: (x + 1, y, z, c)),
    hops(lambda x, y, z, c: (x - 1, y, z, c)),
    hops(lambda x, y, z, c: (x, y + 1, z, c)),
    hops(lambda x, y, z, c: (x, y - 1, z, c)),
)
TOKENS = (
    tile_hop(1, (0, 1)),
    tile_hop(1, (-1, 0)),
    tile_hop(-1, (0, 1)),
    tile_hop(-1, (-1, 0)),
    tile_hop(0, (-1, 1)),
)
ORDER = ((7, 11, 9, 1, 0, 3, 8, 6, 10, 2, 5, 4), (8, 11, 10, 2, 0, 4, 7, 6, 9, 1, 5, 3))

def send(x, pairs):
    return lax.ppermute(x, AXES, pairs)


def together(*values):
    return lax.optimization_barrier(values)


def cost(flops, nbytes, trans=0):
    return pl.CostEstimate(flops=int(flops), bytes_accessed=int(nbytes), transcendentals=int(trans))


def modulate_kernel(x_ref, scale_ref, shift_ref, o_ref):
    x = x_ref[...].astype(F32)
    mean = jnp.mean(x, axis=-1, keepdims=True)
    centred = x - mean
    var = jnp.mean(centred * centred, axis=-1, keepdims=True)
    normed = centred * lax.rsqrt(var + EPS)
    o_ref[...] = (normed * (1.0 + scale_ref[...]) + shift_ref[...]).astype(BF)


def modulate(x, scale, shift):
    rows, width = x.shape
    step = 64
    return pl.pallas_call(
        modulate_kernel,
        out_shape=jax.ShapeDtypeStruct((rows, width), BF),
        grid=(rows // step,),
        in_specs=[
            pl.BlockSpec((step, width), lambda i: (i, 0)),
            pl.BlockSpec((1, width), lambda i: (0, 0)),
            pl.BlockSpec((1, width), lambda i: (0, 0)),
        ],
        out_specs=pl.BlockSpec((step, width), lambda i: (i, 0)),
        cost_estimate=cost(rows * width * 8, rows * width * 4),
        name="modulate",
    )(x, scale.reshape(1, -1), shift.reshape(1, -1))


def head_norm(raw, gain):
    return (raw * lax.rsqrt(jnp.mean(raw * raw, axis=-1, keepdims=True) + EPS) * gain).astype(BF)


def heads_kernel(n, m, order_ref, far_ref, *refs):
    tiles, blocks = (refs[:n], refs[n : n + m])
    qg_ref, kg_ref, mine_ref, theirs_ref, buf, weight, q_ref, k_ref, v_ref, sem, wsem = refs[n + m :]
    i = pl.program_id(0)
    parts = wsem.shape[0]
    deep = weight.shape[0] // parts
    rows = buf.shape[1]
    steps = n

    def copies():
        for j in range(parts):
            each = parts // m
            block = blocks[j // each].at[pl.ds(j % each * deep, deep)]
            yield pltpu.make_async_copy(block, weight.at[pl.ds(j * deep, deep)], wsem.at[j])

    def fetch(j, _):
        for t in range(n):

            @pl.when(order_ref[j] == t)
            def _():
                pltpu.make_async_copy(tiles[t], buf.at[j], sem.at[j]).start()

        return 0

    @pl.when(i == 0)
    def _():
        for copy in copies():
            copy.start()
        lax.fori_loop(0, n, fetch, 0)
        for copy in copies():
            copy.wait()

    @pl.when(i < steps)
    def _():
        pltpu.make_async_copy(tiles[0], buf.at[i], sem.at[i]).wait()
        raw = jnp.dot(buf[i], weight[:, : 2 * HALF], preferred_element_type=F32)
        at = pl.ds(pl.multiple_of(i * rows, rows), rows)
        for h in range(3):
            k_ref[h, at] = head_norm(raw[:, h * HD : (h + 1) * HD], kg_ref[...])
            v_ref[h, at] = raw[:, HALF + h * HD : HALF + (h + 1) * HD].astype(BF)

    @pl.when(jnp.logical_or(i == 4, i == 7))
    def _():
        t = jnp.where(i == 4, 0, 1)
        raw = jnp.dot(buf[i], weight[:, 2 * HALF :], preferred_element_type=F32)
        for h in range(3):
            q_ref[t, h] = head_norm(raw[:, h * HD : (h + 1) * HD], qg_ref[...])

    @pl.when(i >= steps)
    def _():
        h, t = ((i - steps) // 2, lax.rem(i - steps, 2))
        q = q_ref[t, h]
        factor = 1.4426950408889634 / jnp.sqrt(F32(HD))
        scores, top = ([], None)
        for j in range(9):
            at = pl.multiple_of((t * 3 + j) * rows, rows)
            k = k_ref[h, pl.ds(at, rows), :]
            s = lax.dot_general(q, k, (((1,), (1,)), ((), ())), preferred_element_type=F32)
            scores.append(s)
            most = jnp.max(s, axis=-1, keepdims=True) - far_ref[t * 3 + j]
            top = most if top is None else jnp.maximum(top, most)
        total = jnp.zeros((rows, 1), F32)
        acc = jnp.zeros((rows, HD), F32)
        for j in range(9):
            at = pl.multiple_of((t * 3 + j) * rows, rows)
            v = v_ref[h, pl.ds(at, rows), :]
            expo = jnp.exp2((scores[j] - (top + far_ref[t * 3 + j])) * factor)
            total += jnp.sum(expo, axis=-1, keepdims=True)
            acc += jnp.dot(expo.astype(BF), v, preferred_element_type=F32)
        result = (acc / total).astype(BF)
        cols = pl.ds(pl.multiple_of(h * HD, HD), HD)

        @pl.when(t == 0)
        def _():
            mine_ref[:, cols] = result

        @pl.when(t == 1)
        def _():
            theirs_ref[:, cols] = result


def three_heads(order, far, tiles, blocks, q_gain, k_gain):
    n, m = (len(tiles), len(blocks))
    rows, width = tiles[0].shape
    hbm = pl.BlockSpec(memory_space=pltpu.HBM)
    return pl.pallas_call(
        functools.partial(heads_kernel, n, m),
        out_shape=[jax.ShapeDtypeStruct((rows, HALF), BF)] * 2,
        grid=(n + 6,),
        in_specs=[pl.BlockSpec(memory_space=pltpu.SMEM)] * 2
        + [hbm] * (n + m)
        + [pl.BlockSpec((1, HD), lambda i: (0, 0))] * 2,
        out_specs=[pl.BlockSpec((rows, HALF), lambda i: (0, 0))] * 2,
        scratch_shapes=[
            pltpu.VMEM((n, rows, width), BF),
            pltpu.VMEM((width, 3 * HALF), BF),
            pltpu.VMEM((2, 3, rows, HD), BF),
            pltpu.VMEM((3, n * rows, HD), BF),
            pltpu.VMEM((3, n * rows, HD), BF),
            pltpu.SemaphoreType.DMA((n,)),
            pltpu.SemaphoreType.DMA((4,)),
        ],
        compiler_params=pltpu.CompilerParams(vmem_limit_bytes=60 << 20),
        cost_estimate=cost(
            2 * (n * 2 + 2) * rows * width * HALF + 6 * rows * 9 * rows * HD * 4,
            (n * rows * width + width * 3 * HALF) * 2,
            6 * rows * 9 * rows,
        ),
        name="three_heads",
    )(order, far, *tiles, *blocks, q_gain, k_gain)


def project_kernel(c_ref, at_ref, a0, a1, a2, a3, w0, w1, gate_ref, o_ref, left):
    for j, a in enumerate((a0, a1, a2, a3)):
        left[:, pl.ds(pl.multiple_of(at_ref[j] * HALF, HD), HALF)] = a[...]
    for j, w in enumerate((w0, w1)):
        side = c_ref[0] if j == 0 else 1 - c_ref[0]
        cols = pl.ds(pl.multiple_of(side * 2 * HALF, HD), 2 * HALF)
        out = jnp.dot(left[...], w[...], preferred_element_type=F32)
        o_ref[:, cols] = (gate_ref[:, cols] * out).astype(BF)


def project_out(c, at, attended, pieces, gate):
    rows = attended[0].shape[0]
    width = pieces[0].shape[0]
    vmem = pl.BlockSpec(memory_space=pltpu.VMEM)
    return pl.pallas_call(
        project_kernel,
        out_shape=jax.ShapeDtypeStruct((rows, 4 * HALF), BF),
        in_specs=[pl.BlockSpec(memory_space=pltpu.SMEM)] * 2 + [vmem] * 7,
        out_specs=vmem,
        scratch_shapes=[pltpu.VMEM((rows, width), BF)],
        compiler_params=pltpu.CompilerParams(vmem_limit_bytes=16 << 20),
        cost_estimate=cost(2 * rows * width * 4 * HALF, width * 4 * HALF * 2 + rows * width * 4),
        name="project_out",
    )(c, at, *attended, *pieces, gate.reshape(1, -1))


def shards(tokens, shift, scale, gate, qkv_weight, out_weight, q_gain, k_gain):
    frames, tile_h, tile_w, width = tokens.shape
    count = frames * tile_h * tile_w
    x, l, z, u, c = (lax.axis_index(a) for a in AXES)
    parity = lax.rem(x + l, 2)
    h = x * 2 + l
    w = z * 2 + u

    def columns(core):
        at = (core * 2 + parity) * HALF
        parts = [lax.dynamic_slice_in_dim(qkv_weight, i * width + at, HALF, 1) for i in (1, 2, 0)]
        parts.append(lax.dynamic_slice_in_dim(out_weight, core * 2 * HALF, 2 * HALF, 1))
        return jnp.concatenate(parts, axis=1)

    mine, other = columns(c), send(columns(1 - c), SIBLING)
    pair = jnp.where(c == 0, jnp.concatenate([mine, other]), jnp.concatenate([other, mine]))
    other = send(pair, U_FLIP)
    flat, pair = together(tokens.reshape(count, width), pair)
    own = modulate(flat, scale, shift)
    own, other = together(own, other)
    quad = jnp.where(u == 0, jnp.concatenate([pair, other]), jnp.concatenate([other, pair]))
    w_in = lax.all_gather(quad[:, : 3 * HALF], "z", axis=0, tiled=True)
    w_out = lax.all_gather(quad[:, 3 * HALF :], "z", axis=0, tiled=True)
    quarter = width // 4
    w_in2 = [send(w_in[i * quarter : (i + 1) * quarter], pairs) for i, pairs in enumerate(NEAR)]

    arrived = [send(own, pairs) for pairs in TOKENS]
    tiles = [own] + arrived
    tiles += [send(t, SIBLING) for t in tiles]

    col_ok = [jnp.where(c == 0, w > 0, w < 15), True, True, jnp.where(c == 0, w < 15, w > 0)]
    row_ok = [h > 0, True, h < 7]
    far = jnp.stack([jnp.where(jnp.logical_and(a, b), 0.0, FAR).astype(F32) for a in col_ok for b in row_ok])
    order = jnp.where(c == 0, jnp.array(ORDER[0], jnp.int32), jnp.array(ORDER[1], jnp.int32))
    gains = (q_gain.reshape(1, HD), k_gain.reshape(1, HD))

    mine1, theirs1 = three_heads(order, far, tiles, [w_in], *gains)
    mine1, theirs1, *w_in2 = together(mine1, theirs1, *w_in2)
    mine3 = send(theirs1, SIBLING)
    mine2, theirs2 = three_heads(order, far, tiles, w_in2, *gains)
    mine2, theirs2, w_out = together(mine2, theirs2, w_out)
    mine4, w_out2 = send(theirs2, SIBLING), send(w_out, SIBLING)

    at = jnp.stack([c * 2 + parity, c * 2 + 1 - parity, (1 - c) * 2 + parity, (1 - c) * 2 + 1 - parity])
    attended = [mine1, mine2, mine3, mine4]
    out = project_out(c.reshape(1), at.astype(jnp.int32), attended, [w_out, w_out2], gate)
    return out.reshape(frames, tile_h, tile_w, width)


def solution(mesh):
    fine = Mesh(mesh.devices.reshape(SIZES), AXES)
    tile = P(None, ("x", "l"), ("z", "u", "c"), None)
    rows = P(("z", "u", "c"), None)
    return jax.shard_map(
        shards,
        mesh=fine,
        in_specs=(tile, P(), P(), P(), rows, rows, P(), P()),
        out_specs=tile,
        check_vma=False,
    )
```

time: 261 us -> 169 us (0.65)
  Pallas kernels: 105 us -> 53 us
  waiting for transfers between devices: 71.9 us -> 33.8 us
  starting transfers between devices: 71.6 us -> 57.3 us
  between operations: 0.83 us -> 13.6 us
    pallas_call x2 -> x1, Pallas kernels: 51.6 us -> 2.88 us  [project_out(): pl.pallas_call(project_kernel, out_shape=jax.ShapeDtypeStruct((rows, 4 *...]
    ppermute x41 -> x20, waiting for transfers between devices: 71.9 us -> 33.8 us  [send(): return lax.ppermute(x, AXES, pairs)]
    ppermute x41 -> x20, starting transfers between devices: 71.6 us -> 57.3 us  [send(): return lax.ppermute(x, AXES, pairs)]
    slice x4 -> x3, local copies, waits for them, and re-layouts: 0.06 us -> 3.78 us  [the longest x1 2.24 us: shards(): w_in[i * quarter:(i + 1) * quarter]]
    pallas_call x2, Pallas kernels: 49.5 us -> 46.4 us  [three_heads(): pl.pallas_call(functools.partial(heads_kernel, n, m), out_shape=[jax.Shap...]
  transfers between devices with their start and end apart: 41 -> 22, of which waited for: 13 -> 6; matrix products, arithmetic and copies ran while one was open for 2% -> 3% of each run, Pallas kernels for 21% -> 30%
where the time goes in v5:
time: 169 us
  starting transfers between devices  57.3 us (34%)
  Pallas kernels  53 us (31%)
  waiting for transfers between devices  33.8 us (20%)
  between operations  13.6 us (8%)
  local copies, waits for them, and re-layouts  10.4 us (6%)
    ppermute x20, starting transfers between devices, send(): return lax.ppermute(x, AXES, pairs)  57.3 us
    pallas_call x2, Pallas kernels, three_heads(): pl.pallas_call(functools.partial(heads_kernel, n, m), out_shape=[jax.Shap...  46.4 us
    ppermute x20, waiting for transfers between devices, send(): return lax.ppermute(x, AXES, pairs)  33.8 us
    pallas_call x1, Pallas kernels, modulate(): pl.pallas_call(modulate_kernel, out_shape=jax.ShapeDtypeStruct((rows, wid...  3.73 us
  transfers between devices with their start and end apart: 22, of which 6 were waited for; matrix products, arithmetic and copies ran while one was open for 3% of the time, Pallas kernels for 30%

profile of v5, /device:TPU:1, one launch (start us, length us, event | category | flops | bytes accessed | tf_op | source)
XLA Modules:
  0.0 168.9 jit_solution(1209186399031441076)
XLA Ops:
  6.5 1.0 constant_dynamic-slice_fusion.4
  7.5 0.9 constant_dynamic-slice_fusion.7
  8.4 3.3 %collective-permute-start = (bf16[48,1920]{1,0:T(8,128)(2,1)S(1)}, bf16[48,1920]{1,0:T(8,128)(2,1)S(1)}, u32[]{:S(2)}, u32[]{:S(2)}) collective-permute-start(bf16[48,1920]{1,0:T(8,128)(2,1)S(1)} %pad_maximum_fusion), channel_id=1, source_target_pairs={{0,1},{1,0},{2,3},{3,2},{4,5},{5,4},{6,7},{7,6},{8,9},{9,8},{10,11... | collective-permute-start | bytes 552968 | tf_op jit(solution)/shard_map/ppermute | solution.py:60
  11.8 1.1 collective-permute-done
  12.8 0.1 maximum_select_fusion.1
  12.9 1.3 collective-permute-start.1
  14.2 0.6 reshape.26.scale_ref
  14.7 0.6 reshape.27.shift_ref
  15.3 3.7 %modulate.1.refs_0_ = bf16[256,1536]{1,0:T(8,128)(2,1)} custom-call(bf16[256,1536]{1,0:T(8,128)(2,1)} %bitcast.17, f32[1,1536]{1,0:T(1,128)} %reshape.26.scale_ref, f32[1,1536]{1,0:T(1,128)} %reshape.27.shift_ref), custom_call_target="tpu_custom_call" | custom-call | flops 3145728 | bytes 1572864 | tf_op jit(solution)/shard_map/modulate/pallas_call | solution.py:83
  19.1 5.2 %collective-permute-done.1 = bf16[96,1920]{1,0:T(8,128)(2,1)S(1)} collective-permute-done((bf16[96,1920]{1,0:T(8,128)(2,1)S(1)}, bf16[96,1920]{1,0:T(8,128)(2,1)S(1)}, u32[]{:S(2)}, u32[]{:S(2)}) %collective-permute-start.1) | collective-permute-done | bytes 368672 | tf_op jit(solution)/shard_map/ppermute | solution.py:60
  24.3 0.1 maximum_select_fusion
  24.4 0.0 copy-start.7
  24.4 0.0 copy-start.8
  24.4 0.8 slice.24
  25.2 0.0 all-gather.3.cloned.1.call-update
  25.3 0.0 all-gather.5.cloned.1.call-start
  25.3 1.1 collective-permute-start.2
  26.4 0.7 slice.29
  27.1 0.0 all-gather.5.cloned.1.call-update
  27.2 0.9 collective-permute-start.3
  28.0 3.3 %collective-permute-start.4 = (bf16[256,1536]{1,0:T(8,128)(2,1)S(1)}, bf16[256,1536]{1,0:T(8,128)(2,1)}, u32[]{:S(2)}, u32[]{:S(2)}) collective-permute-start(bf16[256,1536]{1,0:T(8,128)(2,1)S(1)} %copy-done.3), channel_id=1, source_target_pairs={{0,224},{1,227},{2,226},{3,229},{4,228},{5,231},{6,230},{7,233},{8... | collective-permute-start | bytes 2359304 | tf_op jit(solution)/shard_map/ppermute | solution.py:60
  31.3 0.2 collective-permute-start.5
  31.5 3.2 %collective-permute-start.6 = (bf16[256,1536]{1,0:T(8,128)(2,1)S(1)}, bf16[256,1536]{1,0:T(8,128)(2,1)}, u32[]{:S(2)}, u32[]{:S(2)}) collective-permute-start(bf16[256,1536]{1,0:T(8,128)(2,1)S(1)} %copy-done.3), channel_id=1, source_target_pairs={{0,30},{1,3},{2,0},{3,5},{4,2},{5,7},{6,4},{7,9},{8,6},{9,11},{10,... | collective-permute-start | bytes 2359304 | tf_op jit(solution)/shard_map/ppermute | solution.py:60
  34.7 18.2 %collective-permute-done.2.refs_1_ = bf16[256,1536]{1,0:T(8,128)(2,1)} collective-permute-done((bf16[256,1536]{1,0:T(8,128)(2,1)S(1)}, bf16[256,1536]{1,0:T(8,128)(2,1)}, u32[]{:S(2)}, u32[]{:S(2)}) %collective-permute-start.2) | collective-permute-done | bytes 786464 | tf_op jit(solution)/shard_map/ppermute | solution.py:60
  52.9 4.9 %collective-permute-start.7 = (bf16[256,1536]{1,0:T(8,128)(2,1)S(1)}, bf16[256,1536]{1,0:T(8,128)(2,1)S(1)}, u32[]{:S(2)}, u32[]{:S(2)}) collective-permute-start(bf16[256,1536]{1,0:T(8,128)(2,1)S(1)} %copy-done.3), channel_id=1, source_target_pairs={{0,1},{1,0},{2,3},{3,2},{4,5},{5,4},{6,7},{7,6},{8,9},{9,8},{10,11... | collective-permute-start | bytes 2359304 | tf_op jit(solution)/shard_map/ppermute | solution.py:60
  57.8 0.7 stack.59.far_ref
  58.5 5.0 %collective-permute-done.3.refs_2_ = bf16[256,1536]{1,0:T(8,128)(2,1)} collective-permute-done((bf16[256,1536]{1,0:T(8,128)(2,1)S(1)}, bf16[256,1536]{1,0:T(8,128)(2,1)}, u32[]{:S(2)}, u32[]{:S(2)}) %collective-permute-start.3) | collective-permute-done | bytes 786464 | tf_op jit(solution)/shard_map/ppermute | solution.py:60
  63.5 7.1 %collective-permute-start.8 = (bf16[256,1536]{1,0:T(8,128)(2,1)}, bf16[256,1536]{1,0:T(8,128)(2,1)}, u32[]{:S(2)}, u32[]{:S(2)}) collective-permute-start(bf16[256,1536]{1,0:T(8,128)(2,1)} %collective-permute-done.2.refs_1_), channel_id=1, source_target_pairs={{0,1},{1,0},{2,3},{3,2},{4,5},{5,4},{6,7},{7,6},{8,9},{9,8},{10,11... | collective-permute-start | bytes 2359304 | tf_op jit(solution)/shard_map/ppermute | solution.py:60
  70.6 0.0 collective-permute-done.4.refs_3_
  70.6 3.6 %collective-permute-start.9 = (bf16[256,1536]{1,0:T(8,128)(2,1)}, bf16[256,1536]{1,0:T(8,128)(2,1)}, u32[]{:S(2)}, u32[]{:S(2)}) collective-permute-start(bf16[256,1536]{1,0:T(8,128)(2,1)} %collective-permute-done.3.refs_2_), channel_id=1, source_target_pairs={{0,1},{1,0},{2,3},{3,2},{4,5},{5,4},{6,7},{7,6},{8,9},{9,8},{10,11... | collective-permute-start | bytes 2359304 | tf_op jit(solution)/shard_map/ppermute | solution.py:60
  74.1 0.0 collective-permute-done.5.refs_4_
  74.2 12.2 %collective-permute-start.10 = (bf16[256,1536]{1,0:T(8,128)(2,1)}, bf16[256,1536]{1,0:T(8,128)(2,1)}, u32[]{:S(2)}, u32[]{:S(2)}) collective-permute-start(bf16[256,1536]{1,0:T(8,128)(2,1)} %collective-permute-done.4.refs_3_), channel_id=1, source_target_pairs={{0,1},{1,0},{2,3},{3,2},{4,5},{5,4},{6,7},{7,6},{8,9},{9,8},{10,11... | collective-permute-start | bytes 2359304 | tf_op jit(solution)/shard_map/ppermute | solution.py:60
  86.3 0.0 collective-permute-done.6.refs_5_
  86.3 8.9 %collective-permute-start.11 = (bf16[256,1536]{1,0:T(8,128)(2,1)}, bf16[256,1536]{1,0:T(8,128)(2,1)}, u32[]{:S(2)}, u32[]{:S(2)}) collective-permute-start(bf16[256,1536]{1,0:T(8,128)(2,1)} %collective-permute-done.5.refs_4_), channel_id=1, source_target_pairs={{0,1},{1,0},{2,3},{3,2},{4,5},{5,4},{6,7},{7,6},{8,9},{9,8},{10,11... | collective-permute-start | bytes 2359304 | tf_op jit(solution)/shard_map/ppermute | solution.py:60
  95.2 0.0 collective-permute-done.7.refs_6_
  95.2 0.1 collective-permute-start.12
  95.3 0.6 broadcast_select_fusion.order_ref
  95.9 0.2 copy-done.9
  96.1 2.2 %fusion = (bf16[384,1152]{1,0:T(8,128)(2,1)S(1)}, bf16[384,1152]{1,0:T(8,128)(2,1)S(1)}, bf16[384,1152]{1,0:T(8,128)(2,1)S(1)}, bf16[384,1152]{1,0:T(8,128)(2,1)S(1)}) fusion(bf16[1536,1152]{1,0:T(8,128)(2,1)} %all-gather.3.cloned.1.call-done.refs_12_), kind=kLoop, calls=%fused_computation.13 | loop fusion | bytes 7077888 | tf_op jit(solution)/shard_map/slice | solution.py:264
  98.4 0.0 collective-permute-done.8.refs_7_
  98.4 1.3 collective-permute-start.13
  99.7 0.0 collective-permute-done.9.refs_8_
  99.7 1.4 collective-permute-start.14
  101.2 0.0 collective-permute-done.10.refs_9_
  101.2 0.4 collective-permute-start.15
  101.6 0.0 collective-permute-done.11.refs_10_
  101.6 2.2 %collective-permute-start.16 = (bf16[384,1152]{1,0:T(8,128)(2,1)S(1)}, bf16[384,1152]{1,0:T(8,128)(2,1)}, u32[]{:S(2)}, u32[]{:S(2)}) collective-permute-start(bf16[384,1152]{1,0:T(8,128)(2,1)S(1)} %get-tuple-element.39), channel_id=1, source_target_pairs={{0,34},{1,35},{2,32},{3,33},{4,38},{5,39},{6,36},{7,37},{8,42},{9,... | collective-permute-start | bytes 2654216 | tf_op jit(solution)/shard_map/ppermute | solution.py:60
  103.9 0.0 collective-permute-done.12.refs_11_
  103.9 23.1 %three_heads.2 = (bf16[256,384]{1,0:T(8,128)(2,1)}, bf16[256,384]{1,0:T(8,128)(2,1)}) custom-call(s32[12]{0:T(128)} %broadcast_select_fusion.order_ref, f32[12]{0:T(128)} %stack.59.far_ref, bf16[256,1536]{1,0:T(8,128)(2,1)} %modulate.1.refs_0_, bf16[256,1536]{1,0:T(8,128)(2,1)} %collective-permute-done.2.refs_1_, ...), custom_call_target="tpu_custom_call" | custom-call | flops 9663676416 | bytes 12976128 | tf_op jit(solution)/shard_map/three_heads/pallas_call | solution.py:187
  127.0 0.0 collective-permute-done.13.refs_12_
  127.0 0.0 collective-permute-done.14.refs_13_
  127.0 0.0 collective-permute-done.16.refs_15_
  127.0 0.0 copy-start.6
  127.1 23.3 %three_heads.3 = (bf16[256,384]{1,0:T(8,128)(2,1)}, bf16[256,384]{1,0:T(8,128)(2,1)}) custom-call(s32[12]{0:T(128)} %broadcast_select_fusion.order_ref, f32[12]{0:T(128)} %stack.59.far_ref, bf16[256,1536]{1,0:T(8,128)(2,1)} %modulate.1.refs_0_, bf16[256,1536]{1,0:T(8,128)(2,1)} %collective-permute-done.2.refs_1_, ...), custom_call_target="tpu_custom_call" | custom-call | flops 9663676416 | bytes 12976128 | tf_op jit(solution)/shard_map/three_heads/pallas_call | solution.py:187
  150.3 0.0 all-gather.5.cloned.1.call-done.w0
  150.4 1.3 collective-permute-start.19
  151.7 0.1 collective-permute-start.17
  151.8 0.4 collective-permute-start.18
  152.2 0.1 pad_add_fusion.at_ref
  152.3 4.0 %collective-permute-done.17.a2 = bf16[256,384]{1,0:T(8,128)(2,1)S(1)} collective-permute-done((bf16[256,384]{1,0:T(8,128)(2,1)S(1)}, bf16[256,384]{1,0:T(8,128)(2,1)S(1)}, u32[]{:S(2)}, u32[]{:S(2)}) %collective-permute-start.17) | collective-permute-done | bytes 196640 | tf_op jit(solution)/shard_map/ppermute | solution.py:60
  156.3 0.3 collective-permute-done.18.a3
  156.6 1.7 copy-done
  158.3 0.9 copy-done.2
  159.2 2.9 %project_out.1 = bf16[256,1536]{1,0:T(8,128)(2,1)} custom-call(s32[1]{0:T(128)} %bitcast.c_ref, s32[4]{0:T(128)S(1)} %pad_add_fusion.at_ref, bf16[256,384]{1,0:T(8,128)(2,1)S(1)} %copy-done.1, bf16[256,384]{1,0:T(8,128)(2,1)S(1)} %copy-done.2, bf16[256,384]{1,0:T(8,128)(2,1)S(1)} %collective-permute-done.17.a2, ...), custom_call_target="tpu_custom_call" | custom-call | flops 1207959552 | bytes 6291456 | tf_op jit(solution)/shard_map/project_out/pallas_call | solution.py:228
  (22 shorter events, 0.1 us)
Async XLA Ops:
  6.5 7.6 %copy-start.4 = (f32[1536]{0:T(1024)S(1)}, f32[1536]{0:T(1024)}, u32[]{:S(2)}) copy-start(f32[1536]{0:T(1024)} %param.12) | copy-start | bytes 18436
  6.5 8.2 %copy-start.5 = (f32[1536]{0:T(1024)S(1)}, f32[1536]{0:T(1024)}, u32[]{:S(2)}) copy-start(f32[1536]{0:T(1024)} %param.11) | copy-start | bytes 18436
  6.5 89.6 %all-gather.3.cloned.1.call-start = ((), (), s32[]{:S(2)}) async-start(), calls=%async_computation | async-start | bytes 3981312 | tf_op jit(solution)/shard_map/all_gather | solution.py:261
  8.4 4.4 %collective-permute-start = (bf16[48,1920]{1,0:T(8,128)(2,1)S(1)}, bf16[48,1920]{1,0:T(8,128)(2,1)S(1)}, u32[]{:S(2)}, u32[]{:S(2)}) collective-permute-start(bf16[48,1920]{1,0:T(8,128)(2,1)S(1)} %pad_maximum_fusion), channel_id=1, source_target_pairs={{0,1},{1,0},{2,3},{3,2},{4,5},{5,4},{6,7},{7,6},{8,9},{9,8},{10,11... | collective-permute-start | bytes 552968 | tf_op jit(solution)/shard_map/ppermute | solution.py:60
  12.9 11.4 %collective-permute-start.1 = (bf16[96,1920]{1,0:T(8,128)(2,1)S(1)}, bf16[96,1920]{1,0:T(8,128)(2,1)S(1)}, u32[]{:S(2)}, u32[]{:S(2)}) collective-permute-start(bf16[96,1920]{1,0:T(8,128)(2,1)S(1)} %maximum_select_fusion.1), channel_id=1, source_target_pairs={{0,2},{1,3},{2,0},{3,1},{4,6},{5,7},{6,4},{7,5},{8,10},{9,11},{10,... | collective-permute-start | bytes 1105928 | tf_op jit(solution)/shard_map/ppermute | solution.py:60
  19.1 6.3 %copy-start.3 = (bf16[256,1536]{1,0:T(8,128)(2,1)S(1)}, bf16[256,1536]{1,0:T(8,128)(2,1)}, u32[]{:S(2)}) copy-start(bf16[256,1536]{1,0:T(8,128)(2,1)} %modulate.1.refs_0_) | copy-start | bytes 2359300
  24.4 70.9 %copy-start.7 = (s32[12]{0:T(128)S(1)}, s32[12]{0:T(128)}, u32[]{:S(2)}) copy-start(s32[12]{0:T(128)} %constant.61.clone) | copy-start | bytes 148
  24.4 70.9 %copy-start.8 = (s32[12]{0:T(128)S(1)}, s32[12]{0:T(128)}, u32[]{:S(2)}) copy-start(s32[12]{0:T(128)} %constant.62.clone) | copy-start | bytes 148
  25.3 125.1 %all-gather.5.cloned.1.call-start = ((), (), s32[]{:S(2)}) async-start(), calls=%async_computation.1 | async-start | bytes 2654208 | tf_op jit(solution)/shard_map/all_gather | solution.py:262
  25.3 27.6 %collective-permute-start.2 = (bf16[256,1536]{1,0:T(8,128)(2,1)S(1)}, bf16[256,1536]{1,0:T(8,128)(2,1)}, u32[]{:S(2)}, u32[]{:S(2)}) collective-permute-start(bf16[256,1536]{1,0:T(8,128)(2,1)S(1)} %copy-done.3), channel_id=1, source_target_pairs={{0,32},{1,35},{2,34},{3,37},{4,36},{5,39},{6,38},{7,41},{8,40},{9,... | collective-permute-start | bytes 2359304 | tf_op jit(solution)/shard_map/ppermute | solution.py:60
  27.2 36.3 %collective-permute-start.3 = (bf16[256,1536]{1,0:T(8,128)(2,1)S(1)}, bf16[256,1536]{1,0:T(8,128)(2,1)}, u32[]{:S(2)}, u32[]{:S(2)}) collective-permute-start(bf16[256,1536]{1,0:T(8,128)(2,1)S(1)} %copy-done.3), channel_id=1, source_target_pairs={{0,62},{1,33},{2,32},{3,35},{4,34},{5,37},{6,36},{7,39},{8,38},{9,... | collective-permute-start | bytes 2359304 | tf_op jit(solution)/shard_map/ppermute | solution.py:60
  28.0 42.6 %collective-permute-start.4 = (bf16[256,1536]{1,0:T(8,128)(2,1)S(1)}, bf16[256,1536]{1,0:T(8,128)(2,1)}, u32[]{:S(2)}, u32[]{:S(2)}) collective-permute-start(bf16[256,1536]{1,0:T(8,128)(2,1)S(1)} %copy-done.3), channel_id=1, source_target_pairs={{0,224},{1,227},{2,226},{3,229},{4,228},{5,231},{6,230},{7,233},{8... | collective-permute-start | bytes 2359304 | tf_op jit(solution)/shard_map/ppermute | solution.py:60
  31.3 42.8 %collective-permute-start.5 = (bf16[256,1536]{1,0:T(8,128)(2,1)S(1)}, bf16[256,1536]{1,0:T(8,128)(2,1)}, u32[]{:S(2)}, u32[]{:S(2)}) collective-permute-start(bf16[256,1536]{1,0:T(8,128)(2,1)S(1)} %copy-done.3), channel_id=1, source_target_pairs={{0,254},{1,225},{2,224},{3,227},{4,226},{5,229},{6,228},{7,231},{8... | collective-permute-start | bytes 2359304 | tf_op jit(solution)/shard_map/ppermute | solution.py:60
  31.5 54.8 %collective-permute-start.6 = (bf16[256,1536]{1,0:T(8,128)(2,1)S(1)}, bf16[256,1536]{1,0:T(8,128)(2,1)}, u32[]{:S(2)}, u32[]{:S(2)}) collective-permute-start(bf16[256,1536]{1,0:T(8,128)(2,1)S(1)} %copy-done.3), channel_id=1, source_target_pairs={{0,30},{1,3},{2,0},{3,5},{4,2},{5,7},{6,4},{7,9},{8,6},{9,11},{10,... | collective-permute-start | bytes 2359304 | tf_op jit(solution)/shard_map/ppermute | solution.py:60
  52.9 42.3 %collective-permute-start.7 = (bf16[256,1536]{1,0:T(8,128)(2,1)S(1)}, bf16[256,1536]{1,0:T(8,128)(2,1)S(1)}, u32[]{:S(2)}, u32[]{:S(2)}) collective-permute-start(bf16[256,1536]{1,0:T(8,128)(2,1)S(1)} %copy-done.3), channel_id=1, source_target_pairs={{0,1},{1,0},{2,3},{3,2},{4,5},{5,4},{6,7},{7,6},{8,9},{9,8},{10,11... | collective-permute-start | bytes 2359304 | tf_op jit(solution)/shard_map/ppermute | solution.py:60
  63.5 34.9 %collective-permute-start.8 = (bf16[256,1536]{1,0:T(8,128)(2,1)}, bf16[256,1536]{1,0:T(8,128)(2,1)}, u32[]{:S(2)}, u32[]{:S(2)}) collective-permute-start(bf16[256,1536]{1,0:T(8,128)(2,1)} %collective-permute-done.2.refs_1_), channel_id=1, source_target_pairs={{0,1},{1,0},{2,3},{3,2},{4,5},{5,4},{6,7},{7,6},{8,9},{9,8},{10,11... | collective-permute-start | bytes 2359304 | tf_op jit(solution)/shard_map/ppermute | solution.py:60
  70.6 29.1 %collective-permute-start.9 = (bf16[256,1536]{1,0:T(8,128)(2,1)}, bf16[256,1536]{1,0:T(8,128)(2,1)}, u32[]{:S(2)}, u32[]{:S(2)}) collective-permute-start(bf16[256,1536]{1,0:T(8,128)(2,1)} %collective-permute-done.3.refs_2_), channel_id=1, source_target_pairs={{0,1},{1,0},{2,3},{3,2},{4,5},{5,4},{6,7},{7,6},{8,9},{9,8},{10,11... | collective-permute-start | bytes 2359304 | tf_op jit(solution)/shard_map/ppermute | solution.py:60
  74.2 27.0 %collective-permute-start.10 = (bf16[256,1536]{1,0:T(8,128)(2,1)}, bf16[256,1536]{1,0:T(8,128)(2,1)}, u32[]{:S(2)}, u32[]{:S(2)}) collective-permute-start(bf16[256,1536]{1,0:T(8,128)(2,1)} %collective-permute-done.4.refs_3_), channel_id=1, source_target_pairs={{0,1},{1,0},{2,3},{3,2},{4,5},{5,4},{6,7},{7,6},{8,9},{9,8},{10,11... | collective-permute-start | bytes 2359304 | tf_op jit(solution)/shard_map/ppermute | solution.py:60
  86.3 15.3 %collective-permute-start.11 = (bf16[256,1536]{1,0:T(8,128)(2,1)}, bf16[256,1536]{1,0:T(8,128)(2,1)}, u32[]{:S(2)}, u32[]{:S(2)}) collective-permute-start(bf16[256,1536]{1,0:T(8,128)(2,1)} %collective-permute-done.5.refs_4_), channel_id=1, source_target_pairs={{0,1},{1,0},{2,3},{3,2},{4,5},{5,4},{6,7},{7,6},{8,9},{9,8},{10,11... | collective-permute-start | bytes 2359304 | tf_op jit(solution)/shard_map/ppermute | solution.py:60
  95.2 0.9 copy-start.9
  95.2 8.6 %collective-permute-start.12 = (bf16[256,1536]{1,0:T(8,128)(2,1)}, bf16[256,1536]{1,0:T(8,128)(2,1)}, u32[]{:S(2)}, u32[]{:S(2)}) collective-permute-start(bf16[256,1536]{1,0:T(8,128)(2,1)} %collective-permute-done.6.refs_5_), channel_id=1, source_target_pairs={{0,1},{1,0},{2,3},{3,2},{4,5},{5,4},{6,7},{7,6},{8,9},{9,8},{10,11... | collective-permute-start | bytes 2359304 | tf_op jit(solution)/shard_map/ppermute | solution.py:60
  98.4 28.6 %collective-permute-start.13 = (bf16[384,1152]{1,0:T(8,128)(2,1)S(1)}, bf16[384,1152]{1,0:T(8,128)(2,1)}, u32[]{:S(2)}, u32[]{:S(2)}) collective-permute-start(bf16[384,1152]{1,0:T(8,128)(2,1)S(1)} %get-tuple-element.42), channel_id=1, source_target_pairs={{0,64},{1,65},{2,66},{3,67},{4,68},{5,69},{6,70},{7,71},{8,72},{9,... | collective-permute-start | bytes 2654216 | tf_op jit(solution)/shard_map/ppermute | solution.py:60
  99.7 27.3 %collective-permute-start.14 = (bf16[384,1152]{1,0:T(8,128)(2,1)S(1)}, bf16[384,1152]{1,0:T(8,128)(2,1)}, u32[]{:S(2)}, u32[]{:S(2)}) collective-permute-start(bf16[384,1152]{1,0:T(8,128)(2,1)S(1)} %get-tuple-element.41), channel_id=1, source_target_pairs={{0,192},{1,193},{2,194},{3,195},{4,196},{5,197},{6,198},{7,199},{8... | collective-permute-start | bytes 2654216 | tf_op jit(solution)/shard_map/ppermute | solution.py:60
  101.2 25.8 %collective-permute-start.15 = (bf16[384,1152]{1,0:T(8,128)(2,1)S(1)}, bf16[384,1152]{1,0:T(8,128)(2,1)}, u32[]{:S(2)}, u32[]{:S(2)}) collective-permute-start(bf16[384,1152]{1,0:T(8,128)(2,1)S(1)} %get-tuple-element.40), channel_id=1, source_target_pairs={{0,32},{1,33},{2,34},{3,35},{4,36},{5,37},{6,38},{7,39},{8,40},{9,... | collective-permute-start | bytes 2654216 | tf_op jit(solution)/shard_map/ppermute | solution.py:60
  101.6 25.4 %collective-permute-start.16 = (bf16[384,1152]{1,0:T(8,128)(2,1)S(1)}, bf16[384,1152]{1,0:T(8,128)(2,1)}, u32[]{:S(2)}, u32[]{:S(2)}) collective-permute-start(bf16[384,1152]{1,0:T(8,128)(2,1)S(1)} %get-tuple-element.39), channel_id=1, source_target_pairs={{0,34},{1,35},{2,32},{3,33},{4,38},{5,39},{6,36},{7,37},{8,42},{9,... | collective-permute-start | bytes 2654216 | tf_op jit(solution)/shard_map/ppermute | solution.py:60
  127.0 24.7 %copy-start.10 = (bf16[256,384]{1,0:T(8,128)(2,1)S(1)}, bf16[256,384]{1,0:T(8,128)(2,1)}, u32[]{:S(2)}) copy-start(bf16[256,384]{1,0:T(8,128)(2,1)} %get-tuple-element.36) | copy-start | bytes 589828
  127.0 25.2 %copy-start.6 = (f32[1536]{0:T(1024)S(1)}, f32[1536]{0:T(1024)}, u32[]{:S(2)}) copy-start(f32[1536]{0:T(1024)} %param.13) | copy-start | bytes 18436
  127.0 29.6 %copy-start.1 = (bf16[256,384]{1,0:T(8,128)(2,1)S(1)}, bf16[256,384]{1,0:T(8,128)(2,1)}, u32[]{:S(2)}) copy-start(bf16[256,384]{1,0:T(8,128)(2,1)} %get-tuple-element.28.a0) | copy-start | bytes 589828
  150.4 6.3 %collective-permute-start.19 = (bf16[1536,768]{1,0:T(8,128)(2,1)}, bf16[1536,768]{1,0:T(8,128)(2,1)S(1)}, u32[]{:S(2)}, u32[]{:S(2)}) collective-permute-start(bf16[1536,768]{1,0:T(8,128)(2,1)} %all-gather.5.cloned.1.call-done.w0), channel_id=1, source_target_pairs={{0,1},{1,0},{2,3},{3,2},{4,5},{5,4},{6,7},{7,6},{8,9},{9,8},{10,11... | collective-permute-start | bytes 7077896 | tf_op jit(solution)/shard_map/ppermute | solution.py:60
  151.7 4.6 %collective-permute-start.17 = (bf16[256,384]{1,0:T(8,128)(2,1)S(1)}, bf16[256,384]{1,0:T(8,128)(2,1)S(1)}, u32[]{:S(2)}, u32[]{:S(2)}) collective-permute-start(bf16[256,384]{1,0:T(8,128)(2,1)S(1)} %copy-done.10), channel_id=1, source_target_pairs={{0,1},{1,0},{2,3},{3,2},{4,5},{5,4},{6,7},{7,6},{8,9},{9,8},{10,11... | collective-permute-start | bytes 589832 | tf_op jit(solution)/shard_map/ppermute | solution.py:60
  151.8 4.8 %collective-permute-start.18 = (bf16[256,384]{1,0:T(8,128)(2,1)}, bf16[256,384]{1,0:T(8,128)(2,1)S(1)}, u32[]{:S(2)}, u32[]{:S(2)}) collective-permute-start(bf16[256,384]{1,0:T(8,128)(2,1)} %get-tuple-element.37), channel_id=1, source_target_pairs={{0,1},{1,0},{2,3},{3,2},{4,5},{5,4},{6,7},{7,6},{8,9},{9,8},{10,11... | collective-permute-start | bytes 589832 | tf_op jit(solution)/shard_map/ppermute | solution.py:60
  156.6 1.7 copy-start
  158.3 0.9 copy-start.2
Sparse Core Ops, SparseCore 0:
  25.4 65.5 all-gather.2
  92.8 37.4 all-gather.4

commit v6 on v5

--- a/solution.py
+++ b/solution.py
@@ -17,6 +17,7 @@
 AXES = ("x", "l", "z", "u", "c")
 SIZES = (4, 2, 8, 2, 2)
 FAR = 1e30
+GROUP = 2
 BF = jnp.bfloat16
 F32 = jnp.float32
 
@@ -105,8 +106,9 @@
     i = pl.program_id(0)
     parts = wsem.shape[0]
     deep = weight.shape[0] // parts
-    rows = buf.shape[1]
-    steps = n
+    rows = buf.shape[0] // n
+    steps = n // GROUP
+    wide = GROUP * rows
 
     def copies():
         for j in range(parts):
@@ -114,12 +116,15 @@
             block = blocks[j // each].at[pl.ds(j % each * deep, deep)]
             yield pltpu.make_async_copy(block, weight.at[pl.ds(j * deep, deep)], wsem.at[j])
 
+    def place(j):
+        return buf.at[pl.ds(pl.multiple_of(j * rows, rows), rows)]
+
     def fetch(j, _):
         for t in range(n):
 
             @pl.when(order_ref[j] == t)
             def _():
-                pltpu.make_async_copy(tiles[t], buf.at[j], sem.at[j]).start()
+                pltpu.make_async_copy(tiles[t], place(j), sem.at[j]).start()
 
         return 0
 
@@ -133,29 +138,29 @@
 
     @pl.when(i < steps)
     def _():
-        pltpu.make_async_copy(tiles[0], buf.at[i], sem.at[i]).wait()
-        raw = jnp.dot(buf[i], weight[:, : 2 * HALF], preferred_element_type=F32)
-        at = pl.ds(pl.multiple_of(i * rows, rows), rows)
-        for h in range(3):
-            k_ref[h, at] = head_norm(raw[:, h * HD : (h + 1) * HD], kg_ref[...])
-            v_ref[h, at] = raw[:, HALF + h * HD : HALF + (h + 1) * HD].astype(BF)
-
-    @pl.when(jnp.logical_or(i == 4, i == 7))
+        for j in range(GROUP):
+            pltpu.make_async_copy(tiles[0], place(i * GROUP + j), sem.at[i * GROUP + j]).wait()
+        for j in range(GROUP):
+            at = pl.ds(pl.multiple_of(i * wide + j * rows, rows), rows)
+            raw = jnp.dot(buf[at], weight[:, : 2 * HALF], preferred_element_type=F32)
+            for h in range(3):
+                k_ref[h, at] = head_norm(raw[:, h * HD : (h + 1) * HD], kg_ref[...])
+                v_ref[h, at] = raw[:, HALF + h * HD : HALF + (h + 1) * HD].astype(BF)
+
+    @pl.when(i == steps - 1)
     def _():
-        t = jnp.where(i == 4, 0, 1)
-        raw = jnp.dot(buf[i], weight[:, 2 * HALF :], preferred_element_type=F32)
-        for h in range(3):
-            q_ref[t, h] = head_norm(raw[:, h * HD : (h + 1) * HD], qg_ref[...])
-
-    @pl.when(i >= steps)
-    def _():
-        h, t = ((i - steps) // 2, lax.rem(i - steps, 2))
+        for t, own in enumerate((4, 7)):
+            x = buf[pl.ds(own * rows, rows)]
+            raw = jnp.dot(x, weight[:, 2 * HALF :], preferred_element_type=F32)
+            for h in range(3):
+                q_ref[t, h] = head_norm(raw[:, h * HD : (h + 1) * HD], qg_ref[...])
+
+    def attend(h, t):
         q = q_ref[t, h]
         factor = 1.4426950408889634 / jnp.sqrt(F32(HD))
         scores, top = ([], None)
         for j in range(9):
-            at = pl.multiple_of((t * 3 + j) * rows, rows)
-            k = k_ref[h, pl.ds(at, rows), :]
+            k = k_ref[h, pl.ds((t * 3 + j) * rows, rows), :]
             s = lax.dot_general(q, k, (((1,), (1,)), ((), ())), preferred_element_type=F32)
             scores.append(s)
             most = jnp.max(s, axis=-1, keepdims=True) - far_ref[t * 3 + j]
@@ -163,21 +168,18 @@
         total = jnp.zeros((rows, 1), F32)
         acc = jnp.zeros((rows, HD), F32)
         for j in range(9):
-            at = pl.multiple_of((t * 3 + j) * rows, rows)
-            v = v_ref[h, pl.ds(at, rows), :]
+            v = v_ref[h, pl.ds((t * 3 + j) * rows, rows), :]
             expo = jnp.exp2((scores[j] - (top + far_ref[t * 3 + j])) * factor)
             total += jnp.sum(expo, axis=-1, keepdims=True)
             acc += jnp.dot(expo.astype(BF), v, preferred_element_type=F32)
-        result = (acc / total).astype(BF)
+        return (acc / total).astype(BF)
+
+    @pl.when(i >= steps)
+    def _():
+        h = i - steps
         cols = pl.ds(pl.multiple_of(h * HD, HD), HD)
-
-        @pl.when(t == 0)
-        def _():
-            mine_ref[:, cols] = result
-
-        @pl.when(t == 1)
-        def _():
-            theirs_ref[:, cols] = result
+        mine_ref[:, cols] = attend(h, 0)
+        theirs_ref[:, cols] = attend(h, 1)
 
 
 def three_heads(order, far, tiles, blocks, q_gain, k_gain):
@@ -187,13 +189,13 @@
     return pl.pallas_call(
         functools.partial(heads_kernel, n, m),
         out_shape=[jax.ShapeDtypeStruct((rows, HALF), BF)] * 2,
-        grid=(n + 6,),
+        grid=(n // GROUP + 3,),
         in_specs=[pl.BlockSpec(memory_space=pltpu.SMEM)] * 2
         + [hbm] * (n + m)
         + [pl.BlockSpec((1, HD), lambda i: (0, 0))] * 2,
         out_specs=[pl.BlockSpec((rows, HALF), lambda i: (0, 0))] * 2,
         scratch_shapes=[
-            pltpu.VMEM((n, rows, width), BF),
+            pltpu.VMEM((n * rows, width), BF),
             pltpu.VMEM((width, 3 * HALF), BF),
             pltpu.VMEM((2, 3, rows, HD), BF),
             pltpu.VMEM((3, n * rows, HD), BF),
@@ -211,30 +213,51 @@
     )(order, far, *tiles, *blocks, q_gain, k_gain)
 
 
-def project_kernel(c_ref, at_ref, a0, a1, a2, a3, w0, w1, gate_ref, o_ref, left):
-    for j, a in enumerate((a0, a1, a2, a3)):
-        left[:, pl.ds(pl.multiple_of(at_ref[j] * HALF, HD), HALF)] = a[...]
-    for j, w in enumerate((w0, w1)):
-        side = c_ref[0] if j == 0 else 1 - c_ref[0]
-        cols = pl.ds(pl.multiple_of(side * 2 * HALF, HD), 2 * HALF)
-        out = jnp.dot(left[...], w[...], preferred_element_type=F32)
+def project_kernel(c_ref, at_ref, a0, a1, a2, a3, w0, w1, gate_ref, o_ref, left, weight, asem, wsem):
+    parts = wsem.shape[1]
+    deep = weight.shape[1] // parts
+    weights = [
+        [pltpu.make_async_copy(w.at[rows], weight.at[i, rows], wsem.at[i, j]) for j, rows in enumerate(chunks)]
+        for i, (w, chunks) in enumerate((w, [pl.ds(j * deep, deep) for j in range(parts)]) for w in (w0, w1))
+    ]
+    pieces = [
+        pltpu.make_async_copy(a, left.at[:, pl.ds(pl.multiple_of(at_ref[j] * HALF, HD), HALF)], asem.at[j])
+        for j, a in enumerate((a0, a1, a2, a3))
+    ]
+    for copy in pieces + weights[0] + weights[1]:
+        copy.start()
+    for copy in pieces:
+        copy.wait()
+    for side in range(2):
+        for copy in weights[side]:
+            copy.wait()
+        core = c_ref[0] if side == 0 else 1 - c_ref[0]
+        cols = pl.ds(pl.multiple_of(core * 2 * HALF, HD), 2 * HALF)
+        out = jnp.dot(left[...], weight[side], preferred_element_type=F32)
         o_ref[:, cols] = (gate_ref[:, cols] * out).astype(BF)
 
 
-def project_out(c, at, attended, pieces, gate):
+def project_out(c, at, attended, halves, gate):
     rows = attended[0].shape[0]
-    width = pieces[0].shape[0]
+    width = halves[0].shape[0]
     vmem = pl.BlockSpec(memory_space=pltpu.VMEM)
+    smem = pl.BlockSpec(memory_space=pltpu.SMEM)
+    held = pl.BlockSpec(memory_space=pl.ANY)
     return pl.pallas_call(
         project_kernel,
         out_shape=jax.ShapeDtypeStruct((rows, 4 * HALF), BF),
-        in_specs=[pl.BlockSpec(memory_space=pltpu.SMEM)] * 2 + [vmem] * 7,
+        in_specs=[smem] * 2 + [held] * 6 + [vmem],
         out_specs=vmem,
-        scratch_shapes=[pltpu.VMEM((rows, width), BF)],
-        compiler_params=pltpu.CompilerParams(vmem_limit_bytes=16 << 20),
+        scratch_shapes=[
+            pltpu.VMEM((rows, width), BF),
+            pltpu.VMEM((2, width, 2 * HALF), BF),
+            pltpu.SemaphoreType.DMA((4,)),
+            pltpu.SemaphoreType.DMA((2, 4)),
+        ],
+        compiler_params=pltpu.CompilerParams(vmem_limit_bytes=20 << 20),
         cost_estimate=cost(2 * rows * width * 4 * HALF, width * 4 * HALF * 2 + rows * width * 4),
         name="project_out",
-    )(c, at, *attended, *pieces, gate.reshape(1, -1))
+    )(c, at, *attended, *halves, gate.reshape(1, -1))
 
 
 def shards(tokens, shift, scale, gate, qkv_weight, out_weight, q_gain, k_gain):

time: 169 us -> 166 us (0.982)
  Pallas kernels: 53 us -> 49.4 us
    pallas_call x2, Pallas kernels: 46.4 us -> 41.1 us  [three_heads(): pl.pallas_call(functools.partial(heads_kernel, n, m), out_shape=[jax.Shap...]
  transfers between devices with their start and end apart: 22 -> 22, of which waited for: 6 -> 6; matrix products, arithmetic and copies ran while one was open for 3% -> 3% of each run, Pallas kernels for 30% -> 27%
where the time goes in v6:
time: 166 us; the launch traced here: 165 us
  starting transfers between devices  57.3 us (35%)
  Pallas kernels  49.4 us (30%)
  waiting for transfers between devices  33.8 us (20%)
  between operations  13.6 us (8%)
  local copies, waits for them, and re-layouts  10.4 us (6%)
    ppermute x20, starting transfers between devices, send(): return lax.ppermute(x, AXES, pairs)  57.2 us
    pallas_call x2, Pallas kernels, three_heads(): pl.pallas_call(functools.partial(heads_kernel, n, m), out_shape=[jax.Shap...  41.1 us
    ppermute x20, waiting for transfers between devices, send(): return lax.ppermute(x, AXES, pairs)  33.8 us
    pallas_call x1, Pallas kernels, project_out(): pl.pallas_call(project_kernel, out_shape=jax.ShapeDtypeStruct((rows, 4 *...  4.55 us
    pallas_call x1, Pallas kernels, modulate(): pl.pallas_call(modulate_kernel, out_shape=jax.ShapeDtypeStruct((rows, wid...  3.73 us
  transfers between devices with their start and end apart: 22, of which 6 were waited for; matrix products, arithmetic and copies ran while one was open for 3% of the time, Pallas kernels for 27%

profile of v6, /device:TPU:1, one launch (start us, length us, event | category | flops | bytes accessed | tf_op | source)
XLA Modules:
  0.0 165.3 jit_solution(11909082575188372321)
XLA Ops:
  6.5 1.0 constant_dynamic-slice_fusion.4
  7.5 0.9 constant_dynamic-slice_fusion.7
  8.4 3.3 %collective-permute-start = (bf16[48,1920]{1,0:T(8,128)(2,1)S(1)}, bf16[48,1920]{1,0:T(8,128)(2,1)S(1)}, u32[]{:S(2)}, u32[]{:S(2)}) collective-permute-start(bf16[48,1920]{1,0:T(8,128)(2,1)S(1)} %pad_maximum_fusion), channel_id=1, source_target_pairs={{0,1},{1,0},{2,3},{3,2},{4,5},{5,4},{6,7},{7,6},{8,9},{9,8},{10,11... | collective-permute-start | bytes 552968 | tf_op jit(solution)/shard_map/ppermute | solution.py:61
  11.8 1.1 collective-permute-done
  12.8 0.1 maximum_select_fusion.1
  12.9 1.3 collective-permute-start.1
  14.2 0.6 reshape.26.scale_ref
  14.7 0.6 reshape.27.shift_ref
  15.3 3.7 %modulate.1.refs_0_ = bf16[256,1536]{1,0:T(8,128)(2,1)} custom-call(bf16[256,1536]{1,0:T(8,128)(2,1)} %bitcast.17, f32[1,1536]{1,0:T(1,128)} %reshape.26.scale_ref, f32[1,1536]{1,0:T(1,128)} %reshape.27.shift_ref), custom_call_target="tpu_custom_call" | custom-call | flops 3145728 | bytes 1572864 | tf_op jit(solution)/shard_map/modulate/pallas_call | solution.py:84
  19.1 5.2 %collective-permute-done.1 = bf16[96,1920]{1,0:T(8,128)(2,1)S(1)} collective-permute-done((bf16[96,1920]{1,0:T(8,128)(2,1)S(1)}, bf16[96,1920]{1,0:T(8,128)(2,1)S(1)}, u32[]{:S(2)}, u32[]{:S(2)}) %collective-permute-start.1) | collective-permute-done | bytes 368672 | tf_op jit(solution)/shard_map/ppermute | solution.py:61
  24.3 0.1 maximum_select_fusion
  24.4 0.0 copy-start.7
  24.4 0.0 copy-start.8
  24.4 0.8 slice.24
  25.2 0.0 all-gather.3.cloned.1.call-update
  25.3 0.0 all-gather.5.cloned.1.call-start
  25.3 1.1 collective-permute-start.2
  26.4 0.7 slice.29
  27.1 0.0 all-gather.5.cloned.1.call-update
  27.2 0.9 collective-permute-start.3
  28.0 3.3 %collective-permute-start.4 = (bf16[256,1536]{1,0:T(8,128)(2,1)S(1)}, bf16[256,1536]{1,0:T(8,128)(2,1)}, u32[]{:S(2)}, u32[]{:S(2)}) collective-permute-start(bf16[256,1536]{1,0:T(8,128)(2,1)S(1)} %copy-done.3), channel_id=1, source_target_pairs={{0,224},{1,227},{2,226},{3,229},{4,228},{5,231},{6,230},{7,233},{8... | collective-permute-start | bytes 2359304 | tf_op jit(solution)/shard_map/ppermute | solution.py:61
  31.3 0.2 collective-permute-start.5
  31.5 3.2 %collective-permute-start.6 = (bf16[256,1536]{1,0:T(8,128)(2,1)S(1)}, bf16[256,1536]{1,0:T(8,128)(2,1)}, u32[]{:S(2)}, u32[]{:S(2)}) collective-permute-start(bf16[256,1536]{1,0:T(8,128)(2,1)S(1)} %copy-done.3), channel_id=1, source_target_pairs={{0,30},{1,3},{2,0},{3,5},{4,2},{5,7},{6,4},{7,9},{8,6},{9,11},{10,... | collective-permute-start | bytes 2359304 | tf_op jit(solution)/shard_map/ppermute | solution.py:61
  34.7 18.2 %collective-permute-done.2.refs_1_ = bf16[256,1536]{1,0:T(8,128)(2,1)} collective-permute-done((bf16[256,1536]{1,0:T(8,128)(2,1)S(1)}, bf16[256,1536]{1,0:T(8,128)(2,1)}, u32[]{:S(2)}, u32[]{:S(2)}) %collective-permute-start.2) | collective-permute-done | bytes 786464 | tf_op jit(solution)/shard_map/ppermute | solution.py:61
  52.9 4.9 %collective-permute-start.7 = (bf16[256,1536]{1,0:T(8,128)(2,1)S(1)}, bf16[256,1536]{1,0:T(8,128)(2,1)S(1)}, u32[]{:S(2)}, u32[]{:S(2)}) collective-permute-start(bf16[256,1536]{1,0:T(8,128)(2,1)S(1)} %copy-done.3), channel_id=1, source_target_pairs={{0,1},{1,0},{2,3},{3,2},{4,5},{5,4},{6,7},{7,6},{8,9},{9,8},{10,11... | collective-permute-start | bytes 2359304 | tf_op jit(solution)/shard_map/ppermute | solution.py:61
  57.8 0.7 stack.59.far_ref
  58.5 5.0 %collective-permute-done.3.refs_2_ = bf16[256,1536]{1,0:T(8,128)(2,1)} collective-permute-done((bf16[256,1536]{1,0:T(8,128)(2,1)S(1)}, bf16[256,1536]{1,0:T(8,128)(2,1)}, u32[]{:S(2)}, u32[]{:S(2)}) %collective-permute-start.3) | collective-permute-done | bytes 786464 | tf_op jit(solution)/shard_map/ppermute | solution.py:61
  63.5 7.1 %collective-permute-start.8 = (bf16[256,1536]{1,0:T(8,128)(2,1)}, bf16[256,1536]{1,0:T(8,128)(2,1)}, u32[]{:S(2)}, u32[]{:S(2)}) collective-permute-start(bf16[256,1536]{1,0:T(8,128)(2,1)} %collective-permute-done.2.refs_1_), channel_id=1, source_target_pairs={{0,1},{1,0},{2,3},{3,2},{4,5},{5,4},{6,7},{7,6},{8,9},{9,8},{10,11... | collective-permute-start | bytes 2359304 | tf_op jit(solution)/shard_map/ppermute | solution.py:61
  70.6 0.0 collective-permute-done.4.refs_3_
  70.6 3.6 %collective-permute-start.9 = (bf16[256,1536]{1,0:T(8,128)(2,1)}, bf16[256,1536]{1,0:T(8,128)(2,1)}, u32[]{:S(2)}, u32[]{:S(2)}) collective-permute-start(bf16[256,1536]{1,0:T(8,128)(2,1)} %collective-permute-done.3.refs_2_), channel_id=1, source_target_pairs={{0,1},{1,0},{2,3},{3,2},{4,5},{5,4},{6,7},{7,6},{8,9},{9,8},{10,11... | collective-permute-start | bytes 2359304 | tf_op jit(solution)/shard_map/ppermute | solution.py:61
  74.1 0.0 collective-permute-done.5.refs_4_
  74.2 12.2 %collective-permute-start.10 = (bf16[256,1536]{1,0:T(8,128)(2,1)}, bf16[256,1536]{1,0:T(8,128)(2,1)}, u32[]{:S(2)}, u32[]{:S(2)}) collective-permute-start(bf16[256,1536]{1,0:T(8,128)(2,1)} %collective-permute-done.4.refs_3_), channel_id=1, source_target_pairs={{0,1},{1,0},{2,3},{3,2},{4,5},{5,4},{6,7},{7,6},{8,9},{9,8},{10,11... | collective-permute-start | bytes 2359304 | tf_op jit(solution)/shard_map/ppermute | solution.py:61
  86.3 0.0 collective-permute-done.6.refs_5_
  86.3 8.9 %collective-permute-start.11 = (bf16[256,1536]{1,0:T(8,128)(2,1)}, bf16[256,1536]{1,0:T(8,128)(2,1)}, u32[]{:S(2)}, u32[]{:S(2)}) collective-permute-start(bf16[256,1536]{1,0:T(8,128)(2,1)} %collective-permute-done.5.refs_4_), channel_id=1, source_target_pairs={{0,1},{1,0},{2,3},{3,2},{4,5},{5,4},{6,7},{7,6},{8,9},{9,8},{10,11... | collective-permute-start | bytes 2359304 | tf_op jit(solution)/shard_map/ppermute | solution.py:61
  95.2 0.0 collective-permute-done.7.refs_6_
  95.2 0.1 collective-permute-start.12
  95.3 0.6 broadcast_select_fusion.order_ref
  95.9 0.2 copy-done.9
  96.1 2.2 %fusion = (bf16[384,1152]{1,0:T(8,128)(2,1)S(1)}, bf16[384,1152]{1,0:T(8,128)(2,1)S(1)}, bf16[384,1152]{1,0:T(8,128)(2,1)S(1)}, bf16[384,1152]{1,0:T(8,128)(2,1)S(1)}) fusion(bf16[1536,1152]{1,0:T(8,128)(2,1)} %all-gather.3.cloned.1.call-done.refs_12_), kind=kLoop, calls=%fused_computation.13 | loop fusion | bytes 7077888 | tf_op jit(solution)/shard_map/slice | solution.py:287
  98.4 0.0 collective-permute-done.8.refs_7_
  98.4 1.3 collective-permute-start.13
  99.7 0.0 collective-permute-done.9.refs_8_
  99.7 1.4 collective-permute-start.14
  101.2 0.0 collective-permute-done.10.refs_9_
  101.2 0.4 collective-permute-start.15
  101.6 0.0 collective-permute-done.11.refs_10_
  101.6 2.2 %collective-permute-start.16 = (bf16[384,1152]{1,0:T(8,128)(2,1)S(1)}, bf16[384,1152]{1,0:T(8,128)(2,1)}, u32[]{:S(2)}, u32[]{:S(2)}) collective-permute-start(bf16[384,1152]{1,0:T(8,128)(2,1)S(1)} %get-tuple-element.39), channel_id=1, source_target_pairs={{0,34},{1,35},{2,32},{3,33},{4,38},{5,39},{6,36},{7,37},{8,42},{9,... | collective-permute-start | bytes 2654216 | tf_op jit(solution)/shard_map/ppermute | solution.py:61
  103.9 0.0 collective-permute-done.12.refs_11_
  103.9 20.5 %three_heads.2 = (bf16[256,384]{1,0:T(8,128)(2,1)}, bf16[256,384]{1,0:T(8,128)(2,1)}) custom-call(s32[12]{0:T(128)} %broadcast_select_fusion.order_ref, f32[12]{0:T(128)} %stack.59.far_ref, bf16[256,1536]{1,0:T(8,128)(2,1)} %modulate.1.refs_0_, bf16[256,1536]{1,0:T(8,128)(2,1)} %collective-permute-done.2.refs_1_, ...), custom_call_target="tpu_custom_call" | custom-call | flops 9663676416 | bytes 12976128 | tf_op jit(solution)/shard_map/three_heads/pallas_call | solution.py:189
  124.3 0.0 collective-permute-done.14.refs_13_
  124.3 0.0 collective-permute-done.15.refs_14_
  124.4 0.0 copy-start.6
  124.4 20.7 %three_heads.3 = (bf16[256,384]{1,0:T(8,128)(2,1)}, bf16[256,384]{1,0:T(8,128)(2,1)}) custom-call(s32[12]{0:T(128)} %broadcast_select_fusion.order_ref, f32[12]{0:T(128)} %stack.59.far_ref, bf16[256,1536]{1,0:T(8,128)(2,1)} %modulate.1.refs_0_, bf16[256,1536]{1,0:T(8,128)(2,1)} %collective-permute-done.2.refs_1_, ...), custom_call_target="tpu_custom_call" | custom-call | flops 9663676416 | bytes 12976128 | tf_op jit(solution)/shard_map/three_heads/pallas_call | solution.py:189
  145.1 0.0 all-gather.5.cloned.1.call-done.w0
  145.1 1.3 collective-permute-start.19
  146.4 0.1 collective-permute-start.17
  146.5 0.4 collective-permute-start.18
  146.9 0.1 pad_add_fusion.at_ref
  147.0 4.0 %collective-permute-done.17.a2 = bf16[256,384]{1,0:T(8,128)(2,1)S(1)} collective-permute-done((bf16[256,384]{1,0:T(8,128)(2,1)S(1)}, bf16[256,384]{1,0:T(8,128)(2,1)S(1)}, u32[]{:S(2)}, u32[]{:S(2)}) %collective-permute-start.17) | collective-permute-done | bytes 196640 | tf_op jit(solution)/shard_map/ppermute | solution.py:61
  151.0 0.3 collective-permute-done.18.a3
  151.3 0.0 collective-permute-done.19.w1
  151.3 1.7 %copy-done = bf16[1536,768]{1,0:T(8,128)(2,1)S(1)} copy-done((bf16[1536,768]{1,0:T(8,128)(2,1)S(1)}, bf16[1536,768]{1,0:T(8,128)(2,1)}, u32[]{:S(2)}) %copy-start) | copy-done | bytes 2359320
  153.0 0.9 copy-done.2
  153.9 4.5 %project_out.1 = bf16[256,1536]{1,0:T(8,128)(2,1)} custom-call(s32[1]{0:T(128)} %bitcast.c_ref, s32[4]{0:T(128)S(1)} %pad_add_fusion.at_ref, bf16[256,384]{1,0:T(8,128)(2,1)S(1)} %copy-done.1, bf16[256,384]{1,0:T(8,128)(2,1)S(1)} %copy-done.2, bf16[256,384]{1,0:T(8,128)(2,1)S(1)} %collective-permute-done.17.a2, ...), custom_call_target="tpu_custom_call" | custom-call | flops 1207959552 | bytes 6291456 | tf_op jit(solution)/shard_map/project_out/pallas_call | solution.py:246
  (22 shorter events, 0.1 us)
Async XLA Ops:
  6.5 7.6 %copy-start.4 = (f32[1536]{0:T(1024)S(1)}, f32[1536]{0:T(1024)}, u32[]{:S(2)}) copy-start(f32[1536]{0:T(1024)} %param.12) | copy-start | bytes 18436
  6.5 8.2 %copy-start.5 = (f32[1536]{0:T(1024)S(1)}, f32[1536]{0:T(1024)}, u32[]{:S(2)}) copy-start(f32[1536]{0:T(1024)} %param.11) | copy-start | bytes 18436
  6.5 89.6 %all-gather.3.cloned.1.call-start = ((), (), s32[]{:S(2)}) async-start(), calls=%async_computation | async-start | bytes 3981312 | tf_op jit(solution)/shard_map/all_gather | solution.py:284
  8.4 4.4 %collective-permute-start = (bf16[48,1920]{1,0:T(8,128)(2,1)S(1)}, bf16[48,1920]{1,0:T(8,128)(2,1)S(1)}, u32[]{:S(2)}, u32[]{:S(2)}) collective-permute-start(bf16[48,1920]{1,0:T(8,128)(2,1)S(1)} %pad_maximum_fusion), channel_id=1, source_target_pairs={{0,1},{1,0},{2,3},{3,2},{4,5},{5,4},{6,7},{7,6},{8,9},{9,8},{10,11... | collective-permute-start | bytes 552968 | tf_op jit(solution)/shard_map/ppermute | solution.py:61
  12.9 11.4 %collective-permute-start.1 = (bf16[96,1920]{1,0:T(8,128)(2,1)S(1)}, bf16[96,1920]{1,0:T(8,128)(2,1)S(1)}, u32[]{:S(2)}, u32[]{:S(2)}) collective-permute-start(bf16[96,1920]{1,0:T(8,128)(2,1)S(1)} %maximum_select_fusion.1), channel_id=1, source_target_pairs={{0,2},{1,3},{2,0},{3,1},{4,6},{5,7},{6,4},{7,5},{8,10},{9,11},{10,... | collective-permute-start | bytes 1105928 | tf_op jit(solution)/shard_map/ppermute | solution.py:61
  19.1 6.3 %copy-start.3 = (bf16[256,1536]{1,0:T(8,128)(2,1)S(1)}, bf16[256,1536]{1,0:T(8,128)(2,1)}, u32[]{:S(2)}) copy-start(bf16[256,1536]{1,0:T(8,128)(2,1)} %modulate.1.refs_0_) | copy-start | bytes 2359300
  24.4 70.9 %copy-start.7 = (s32[12]{0:T(128)S(1)}, s32[12]{0:T(128)}, u32[]{:S(2)}) copy-start(s32[12]{0:T(128)} %constant.61.clone) | copy-start | bytes 148
  24.4 70.9 %copy-start.8 = (s32[12]{0:T(128)S(1)}, s32[12]{0:T(128)}, u32[]{:S(2)}) copy-start(s32[12]{0:T(128)} %constant.62.clone) | copy-start | bytes 148
  25.3 119.8 %all-gather.5.cloned.1.call-start = ((), (), s32[]{:S(2)}) async-start(), calls=%async_computation.1 | async-start | bytes 2654208 | tf_op jit(solution)/shard_map/all_gather | solution.py:285
  25.3 27.6 %collective-permute-start.2 = (bf16[256,1536]{1,0:T(8,128)(2,1)S(1)}, bf16[256,1536]{1,0:T(8,128)(2,1)}, u32[]{:S(2)}, u32[]{:S(2)}) collective-permute-start(bf16[256,1536]{1,0:T(8,128)(2,1)S(1)} %copy-done.3), channel_id=1, source_target_pairs={{0,32},{1,35},{2,34},{3,37},{4,36},{5,39},{6,38},{7,41},{8,40},{9,... | collective-permute-start | bytes 2359304 | tf_op jit(solution)/shard_map/ppermute | solution.py:61
  27.2 36.3 %collective-permute-start.3 = (bf16[256,1536]{1,0:T(8,128)(2,1)S(1)}, bf16[256,1536]{1,0:T(8,128)(2,1)}, u32[]{:S(2)}, u32[]{:S(2)}) collective-permute-start(bf16[256,1536]{1,0:T(8,128)(2,1)S(1)} %copy-done.3), channel_id=1, source_target_pairs={{0,62},{1,33},{2,32},{3,35},{4,34},{5,37},{6,36},{7,39},{8,38},{9,... | collective-permute-start | bytes 2359304 | tf_op jit(solution)/shard_map/ppermute | solution.py:61
  28.0 42.6 %collective-permute-start.4 = (bf16[256,1536]{1,0:T(8,128)(2,1)S(1)}, bf16[256,1536]{1,0:T(8,128)(2,1)}, u32[]{:S(2)}, u32[]{:S(2)}) collective-permute-start(bf16[256,1536]{1,0:T(8,128)(2,1)S(1)} %copy-done.3), channel_id=1, source_target_pairs={{0,224},{1,227},{2,226},{3,229},{4,228},{5,231},{6,230},{7,233},{8... | collective-permute-start | bytes 2359304 | tf_op jit(solution)/shard_map/ppermute | solution.py:61
  31.3 42.8 %collective-permute-start.5 = (bf16[256,1536]{1,0:T(8,128)(2,1)S(1)}, bf16[256,1536]{1,0:T(8,128)(2,1)}, u32[]{:S(2)}, u32[]{:S(2)}) collective-permute-start(bf16[256,1536]{1,0:T(8,128)(2,1)S(1)} %copy-done.3), channel_id=1, source_target_pairs={{0,254},{1,225},{2,224},{3,227},{4,226},{5,229},{6,228},{7,231},{8... | collective-permute-start | bytes 2359304 | tf_op jit(solution)/shard_map/ppermute | solution.py:61
  31.5 54.8 %collective-permute-start.6 = (bf16[256,1536]{1,0:T(8,128)(2,1)S(1)}, bf16[256,1536]{1,0:T(8,128)(2,1)}, u32[]{:S(2)}, u32[]{:S(2)}) collective-permute-start(bf16[256,1536]{1,0:T(8,128)(2,1)S(1)} %copy-done.3), channel_id=1, source_target_pairs={{0,30},{1,3},{2,0},{3,5},{4,2},{5,7},{6,4},{7,9},{8,6},{9,11},{10,... | collective-permute-start | bytes 2359304 | tf_op jit(solution)/shard_map/ppermute | solution.py:61
  52.9 42.3 %collective-permute-start.7 = (bf16[256,1536]{1,0:T(8,128)(2,1)S(1)}, bf16[256,1536]{1,0:T(8,128)(2,1)S(1)}, u32[]{:S(2)}, u32[]{:S(2)}) collective-permute-start(bf16[256,1536]{1,0:T(8,128)(2,1)S(1)} %copy-done.3), channel_id=1, source_target_pairs={{0,1},{1,0},{2,3},{3,2},{4,5},{5,4},{6,7},{7,6},{8,9},{9,8},{10,11... | collective-permute-start | bytes 2359304 | tf_op jit(solution)/shard_map/ppermute | solution.py:61
  63.5 34.9 %collective-permute-start.8 = (bf16[256,1536]{1,0:T(8,128)(2,1)}, bf16[256,1536]{1,0:T(8,128)(2,1)}, u32[]{:S(2)}, u32[]{:S(2)}) collective-permute-start(bf16[256,1536]{1,0:T(8,128)(2,1)} %collective-permute-done.2.refs_1_), channel_id=1, source_target_pairs={{0,1},{1,0},{2,3},{3,2},{4,5},{5,4},{6,7},{7,6},{8,9},{9,8},{10,11... | collective-permute-start | bytes 2359304 | tf_op jit(solution)/shard_map/ppermute | solution.py:61
  70.6 29.1 %collective-permute-start.9 = (bf16[256,1536]{1,0:T(8,128)(2,1)}, bf16[256,1536]{1,0:T(8,128)(2,1)}, u32[]{:S(2)}, u32[]{:S(2)}) collective-permute-start(bf16[256,1536]{1,0:T(8,128)(2,1)} %collective-permute-done.3.refs_2_), channel_id=1, source_target_pairs={{0,1},{1,0},{2,3},{3,2},{4,5},{5,4},{6,7},{7,6},{8,9},{9,8},{10,11... | collective-permute-start | bytes 2359304 | tf_op jit(solution)/shard_map/ppermute | solution.py:61
  74.2 27.0 %collective-permute-start.10 = (bf16[256,1536]{1,0:T(8,128)(2,1)}, bf16[256,1536]{1,0:T(8,128)(2,1)}, u32[]{:S(2)}, u32[]{:S(2)}) collective-permute-start(bf16[256,1536]{1,0:T(8,128)(2,1)} %collective-permute-done.4.refs_3_), channel_id=1, source_target_pairs={{0,1},{1,0},{2,3},{3,2},{4,5},{5,4},{6,7},{7,6},{8,9},{9,8},{10,11... | collective-permute-start | bytes 2359304 | tf_op jit(solution)/shard_map/ppermute | solution.py:61
  86.3 15.3 %collective-permute-start.11 = (bf16[256,1536]{1,0:T(8,128)(2,1)}, bf16[256,1536]{1,0:T(8,128)(2,1)}, u32[]{:S(2)}, u32[]{:S(2)}) collective-permute-start(bf16[256,1536]{1,0:T(8,128)(2,1)} %collective-permute-done.5.refs_4_), channel_id=1, source_target_pairs={{0,1},{1,0},{2,3},{3,2},{4,5},{5,4},{6,7},{7,6},{8,9},{9,8},{10,11... | collective-permute-start | bytes 2359304 | tf_op jit(solution)/shard_map/ppermute | solution.py:61
  95.2 0.9 copy-start.9
  95.2 8.6 %collective-permute-start.12 = (bf16[256,1536]{1,0:T(8,128)(2,1)}, bf16[256,1536]{1,0:T(8,128)(2,1)}, u32[]{:S(2)}, u32[]{:S(2)}) collective-permute-start(bf16[256,1536]{1,0:T(8,128)(2,1)} %collective-permute-done.6.refs_5_), channel_id=1, source_target_pairs={{0,1},{1,0},{2,3},{3,2},{4,5},{5,4},{6,7},{7,6},{8,9},{9,8},{10,11... | collective-permute-start | bytes 2359304 | tf_op jit(solution)/shard_map/ppermute | solution.py:61
  98.4 26.0 %collective-permute-start.13 = (bf16[384,1152]{1,0:T(8,128)(2,1)S(1)}, bf16[384,1152]{1,0:T(8,128)(2,1)}, u32[]{:S(2)}, u32[]{:S(2)}) collective-permute-start(bf16[384,1152]{1,0:T(8,128)(2,1)S(1)} %get-tuple-element.42), channel_id=1, source_target_pairs={{0,64},{1,65},{2,66},{3,67},{4,68},{5,69},{6,70},{7,71},{8,72},{9,... | collective-permute-start | bytes 2654216 | tf_op jit(solution)/shard_map/ppermute | solution.py:61
  99.7 24.6 %collective-permute-start.14 = (bf16[384,1152]{1,0:T(8,128)(2,1)S(1)}, bf16[384,1152]{1,0:T(8,128)(2,1)}, u32[]{:S(2)}, u32[]{:S(2)}) collective-permute-start(bf16[384,1152]{1,0:T(8,128)(2,1)S(1)} %get-tuple-element.41), channel_id=1, source_target_pairs={{0,192},{1,193},{2,194},{3,195},{4,196},{5,197},{6,198},{7,199},{8... | collective-permute-start | bytes 2654216 | tf_op jit(solution)/shard_map/ppermute | solution.py:61
  101.2 23.2 %collective-permute-start.15 = (bf16[384,1152]{1,0:T(8,128)(2,1)S(1)}, bf16[384,1152]{1,0:T(8,128)(2,1)}, u32[]{:S(2)}, u32[]{:S(2)}) collective-permute-start(bf16[384,1152]{1,0:T(8,128)(2,1)S(1)} %get-tuple-element.40), channel_id=1, source_target_pairs={{0,32},{1,33},{2,34},{3,35},{4,36},{5,37},{6,38},{7,39},{8,40},{9,... | collective-permute-start | bytes 2654216 | tf_op jit(solution)/shard_map/ppermute | solution.py:61
  101.6 22.7 %collective-permute-start.16 = (bf16[384,1152]{1,0:T(8,128)(2,1)S(1)}, bf16[384,1152]{1,0:T(8,128)(2,1)}, u32[]{:S(2)}, u32[]{:S(2)}) collective-permute-start(bf16[384,1152]{1,0:T(8,128)(2,1)S(1)} %get-tuple-element.39), channel_id=1, source_target_pairs={{0,34},{1,35},{2,32},{3,33},{4,38},{5,39},{6,36},{7,37},{8,42},{9,... | collective-permute-start | bytes 2654216 | tf_op jit(solution)/shard_map/ppermute | solution.py:61
  124.4 22.0 %copy-start.10 = (bf16[256,384]{1,0:T(8,128)(2,1)S(1)}, bf16[256,384]{1,0:T(8,128)(2,1)}, u32[]{:S(2)}) copy-start(bf16[256,384]{1,0:T(8,128)(2,1)} %get-tuple-element.36) | copy-start | bytes 589828
  124.4 22.5 %copy-start.6 = (f32[1536]{0:T(1024)S(1)}, f32[1536]{0:T(1024)}, u32[]{:S(2)}) copy-start(f32[1536]{0:T(1024)} %param.13) | copy-start | bytes 18436
  124.4 26.9 %copy-start.1 = (bf16[256,384]{1,0:T(8,128)(2,1)S(1)}, bf16[256,384]{1,0:T(8,128)(2,1)}, u32[]{:S(2)}) copy-start(bf16[256,384]{1,0:T(8,128)(2,1)} %get-tuple-element.28.a0) | copy-start | bytes 589828
  145.1 6.2 %collective-permute-start.19 = (bf16[1536,768]{1,0:T(8,128)(2,1)}, bf16[1536,768]{1,0:T(8,128)(2,1)S(1)}, u32[]{:S(2)}, u32[]{:S(2)}) collective-permute-start(bf16[1536,768]{1,0:T(8,128)(2,1)} %all-gather.5.cloned.1.call-done.w0), channel_id=1, source_target_pairs={{0,1},{1,0},{2,3},{3,2},{4,5},{5,4},{6,7},{7,6},{8,9},{9,8},{10,11... | collective-permute-start | bytes 7077896 | tf_op jit(solution)/shard_map/ppermute | solution.py:61
  146.4 4.6 %collective-permute-start.17 = (bf16[256,384]{1,0:T(8,128)(2,1)S(1)}, bf16[256,384]{1,0:T(8,128)(2,1)S(1)}, u32[]{:S(2)}, u32[]{:S(2)}) collective-permute-start(bf16[256,384]{1,0:T(8,128)(2,1)S(1)} %copy-done.10), channel_id=1, source_target_pairs={{0,1},{1,0},{2,3},{3,2},{4,5},{5,4},{6,7},{7,6},{8,9},{9,8},{10,11... | collective-permute-start | bytes 589832 | tf_op jit(solution)/shard_map/ppermute | solution.py:61
  146.5 4.8 %collective-permute-start.18 = (bf16[256,384]{1,0:T(8,128)(2,1)}, bf16[256,384]{1,0:T(8,128)(2,1)S(1)}, u32[]{:S(2)}, u32[]{:S(2)}) collective-permute-start(bf16[256,384]{1,0:T(8,128)(2,1)} %get-tuple-element.37), channel_id=1, source_target_pairs={{0,1},{1,0},{2,3},{3,2},{4,5},{5,4},{6,7},{7,6},{8,9},{9,8},{10,11... | collective-permute-start | bytes 589832 | tf_op jit(solution)/shard_map/ppermute | solution.py:61
  151.3 1.7 %copy-start = (bf16[1536,768]{1,0:T(8,128)(2,1)S(1)}, bf16[1536,768]{1,0:T(8,128)(2,1)}, u32[]{:S(2)}) copy-start(bf16[1536,768]{1,0:T(8,128)(2,1)} %all-gather.5.cloned.1.call-done.w0) | copy-start | bytes 7077892
  153.0 0.9 copy-start.2
Sparse Core Ops, SparseCore 0:
  25.4 65.5 all-gather.2
  92.8 37.3 all-gather.4

commit v7 on v6

--- a/solution.py
+++ b/solution.py
@@ -213,51 +213,58 @@
     )(order, far, *tiles, *blocks, q_gain, k_gain)
 
 
-def project_kernel(c_ref, at_ref, a0, a1, a2, a3, w0, w1, gate_ref, o_ref, left, weight, asem, wsem):
-    parts = wsem.shape[1]
-    deep = weight.shape[1] // parts
-    weights = [
-        [pltpu.make_async_copy(w.at[rows], weight.at[i, rows], wsem.at[i, j]) for j, rows in enumerate(chunks)]
-        for i, (w, chunks) in enumerate((w, [pl.ds(j * deep, deep) for j in range(parts)]) for w in (w0, w1))
-    ]
-    pieces = [
+def columns_kernel(own, c_ref, at_ref, a0, a1, a2, a3, w_ref, gate_ref, *refs):
+    before, (o_ref, left, weight, asem, wsem) = (refs[:-5], refs[-5:])
+    parts = wsem.shape[0]
+    deep = weight.shape[0] // parts
+    copies = [
         pltpu.make_async_copy(a, left.at[:, pl.ds(pl.multiple_of(at_ref[j] * HALF, HD), HALF)], asem.at[j])
         for j, a in enumerate((a0, a1, a2, a3))
     ]
-    for copy in pieces + weights[0] + weights[1]:
+    for j in range(parts):
+        rows = pl.ds(j * deep, deep)
+        copies.append(pltpu.make_async_copy(w_ref.at[rows], weight.at[rows], wsem.at[j]))
+    for copy in copies:
         copy.start()
-    for copy in pieces:
+
+    def span(core):
+        return pl.ds(pl.multiple_of(core * 2 * HALF, HD), 2 * HALF)
+
+    cols = span(c_ref[0] if own else 1 - c_ref[0])
+    for copy in copies:
         copy.wait()
-    for side in range(2):
-        for copy in weights[side]:
-            copy.wait()
-        core = c_ref[0] if side == 0 else 1 - c_ref[0]
-        cols = pl.ds(pl.multiple_of(core * 2 * HALF, HD), 2 * HALF)
-        out = jnp.dot(left[...], weight[side], preferred_element_type=F32)
-        o_ref[:, cols] = (gate_ref[:, cols] * out).astype(BF)
-
-
-def project_out(c, at, attended, halves, gate):
+    out = jnp.dot(left[...], weight[...], preferred_element_type=F32)
+    out = (gate_ref[:, cols] * out).astype(BF)
+    if own:
+        o_ref[...] = out
+    else:
+        o_ref[:, cols] = out
+        o_ref[:, span(c_ref[0])] = before[0][...]
+
+
+def out_columns(c, at, attended, w, gate, *before):
+    own = not before
     rows = attended[0].shape[0]
-    width = halves[0].shape[0]
+    width = w.shape[0]
     vmem = pl.BlockSpec(memory_space=pltpu.VMEM)
     smem = pl.BlockSpec(memory_space=pltpu.SMEM)
+    hbm = pl.BlockSpec(memory_space=pltpu.HBM)
     held = pl.BlockSpec(memory_space=pl.ANY)
     return pl.pallas_call(
-        project_kernel,
-        out_shape=jax.ShapeDtypeStruct((rows, 4 * HALF), BF),
-        in_specs=[smem] * 2 + [held] * 6 + [vmem],
+        functools.partial(columns_kernel, own),
+        out_shape=jax.ShapeDtypeStruct((rows, 2 * HALF if own else 4 * HALF), BF),
+        in_specs=[smem] * 2 + [hbm] * 2 + [held] * 2 + [hbm if own else held] + [vmem] * (1 + len(before)),
         out_specs=vmem,
         scratch_shapes=[
             pltpu.VMEM((rows, width), BF),
-            pltpu.VMEM((2, width, 2 * HALF), BF),
+            pltpu.VMEM((width, 2 * HALF), BF),
             pltpu.SemaphoreType.DMA((4,)),
-            pltpu.SemaphoreType.DMA((2, 4)),
+            pltpu.SemaphoreType.DMA((4,)),
         ],
-        compiler_params=pltpu.CompilerParams(vmem_limit_bytes=20 << 20),
-        cost_estimate=cost(2 * rows * width * 4 * HALF, width * 4 * HALF * 2 + rows * width * 4),
-        name="project_out",
-    )(c, at, *attended, *halves, gate.reshape(1, -1))
+        compiler_params=pltpu.CompilerParams(vmem_limit_bytes=(60 if own else 20) << 20),
+        cost_estimate=cost(2 * rows * width * 2 * HALF, width * 2 * HALF * 2 + rows * width * 3),
+        name="out_columns",
+    )(c, at, *attended, w, gate.reshape(1, -1), *before)
 
 
 def shards(tokens, shift, scale, gate, qkv_weight, out_weight, q_gain, k_gain):
@@ -300,12 +307,15 @@
     mine1, theirs1, *w_in2 = together(mine1, theirs1, *w_in2)
     mine3 = send(theirs1, SIBLING)
     mine2, theirs2 = three_heads(order, far, tiles, w_in2, *gains)
-    mine2, theirs2, w_out = together(mine2, theirs2, w_out)
-    mine4, w_out2 = send(theirs2, SIBLING), send(w_out, SIBLING)
+    mine3, mine4, w_out = together(mine3, send(theirs2, SIBLING), w_out)
+    w_out2 = send(w_out, SIBLING)
 
     at = jnp.stack([c * 2 + parity, c * 2 + 1 - parity, (1 - c) * 2 + parity, (1 - c) * 2 + 1 - parity])
+    at, core = (at.astype(jnp.int32), c.reshape(1))
     attended = [mine1, mine2, mine3, mine4]
-    out = project_out(c.reshape(1), at.astype(jnp.int32), attended, [w_out, w_out2], gate)
+    columns_own = out_columns(core, at, attended, w_out, gate)
+    columns_own, w_out2 = together(columns_own, w_out2)
+    out = out_columns(core, at, attended, w_out2, gate, columns_own)
     return out.reshape(frames, tile_h, tile_w, width)
 
 

time: 166 us -> 167 us (level)
  waiting for transfers between devices: 33.8 us -> 31 us
  Pallas kernels: 49.4 us -> 51.9 us
    ppermute x20, waiting for transfers between devices: 33.8 us -> 31 us  [send(): return lax.ppermute(x, AXES, pairs)]
    pallas_call x1 -> x2, Pallas kernels: 4.55 us -> 7.1 us  [out_columns(): pl.pallas_call(functools.partial(columns_kernel, own), out_shape=jax.Shap...]
  transfers between devices with their start and end apart: 22 -> 22, of which waited for: 6 -> 5; matrix products, arithmetic and copies ran while one was open for 3% -> 4% of each run, Pallas kernels for 27% -> 29%
where the time goes in v7:
time: 167 us; the launch traced here: 166 us
  starting transfers between devices  57.3 us (34%)
  Pallas kernels  51.9 us (31%)
  waiting for transfers between devices  31 us (19%)
  between operations  13.6 us (8%)
  local copies, waits for them, and re-layouts  11.2 us (7%)
    ppermute x20, starting transfers between devices, send(): return lax.ppermute(x, AXES, pairs)  57.2 us
    pallas_call x2, Pallas kernels, three_heads(): pl.pallas_call(functools.partial(heads_kernel, n, m), out_shape=[jax.Shap...  41.1 us
    ppermute x20, waiting for transfers between devices, send(): return lax.ppermute(x, AXES, pairs)  31 us
    pallas_call x2, Pallas kernels, out_columns(): pl.pallas_call(functools.partial(columns_kernel, own), out_shape=jax.Shap...  7.1 us
    pallas_call x1, Pallas kernels, modulate(): pl.pallas_call(modulate_kernel, out_shape=jax.ShapeDtypeStruct((rows, wid...  3.73 us
  transfers between devices with their start and end apart: 22, of which 5 were waited for; matrix products, arithmetic and copies ran while one was open for 4% of the time, Pallas kernels for 29%

profile of v7, /device:TPU:1, one launch (start us, length us, event | category | flops | bytes accessed | tf_op | source)
XLA Modules:
  0.0 166.4 jit_solution(1842572964532674672)
XLA Ops:
  6.5 1.0 constant_dynamic-slice_fusion.4
  7.5 0.9 constant_dynamic-slice_fusion.7
  8.4 3.3 %collective-permute-start = (bf16[48,1920]{1,0:T(8,128)(2,1)S(1)}, bf16[48,1920]{1,0:T(8,128)(2,1)S(1)}, u32[]{:S(2)}, u32[]{:S(2)}) collective-permute-start(bf16[48,1920]{1,0:T(8,128)(2,1)S(1)} %pad_maximum_fusion), channel_id=1, source_target_pairs={{0,1},{1,0},{2,3},{3,2},{4,5},{5,4},{6,7},{7,6},{8,9},{9,8},{10,11... | collective-permute-start | bytes 552968 | tf_op jit(solution)/shard_map/ppermute | solution.py:61
  11.8 1.1 collective-permute-done
  12.8 0.1 maximum_select_fusion.1
  12.9 1.3 collective-permute-start.1
  14.2 0.6 reshape.27.scale_ref
  14.8 0.6 reshape.28.shift_ref
  15.4 3.7 %modulate.1.refs_0_ = bf16[256,1536]{1,0:T(8,128)(2,1)} custom-call(bf16[256,1536]{1,0:T(8,128)(2,1)} %bitcast.17, f32[1,1536]{1,0:T(1,128)} %reshape.27.scale_ref, f32[1,1536]{1,0:T(1,128)} %reshape.28.shift_ref), custom_call_target="tpu_custom_call" | custom-call | flops 3145728 | bytes 1572864 | tf_op jit(solution)/shard_map/modulate/pallas_call | solution.py:84
  19.1 5.2 %collective-permute-done.1 = bf16[96,1920]{1,0:T(8,128)(2,1)S(1)} collective-permute-done((bf16[96,1920]{1,0:T(8,128)(2,1)S(1)}, bf16[96,1920]{1,0:T(8,128)(2,1)S(1)}, u32[]{:S(2)}, u32[]{:S(2)}) %collective-permute-start.1) | collective-permute-done | bytes 368672 | tf_op jit(solution)/shard_map/ppermute | solution.py:61
  24.3 0.1 maximum_select_fusion
  24.4 0.0 copy-start.13
  24.4 0.0 copy-start.14
  24.4 0.8 slice.24
  25.3 0.0 all-gather.3.cloned.1.call-update
  25.3 0.0 all-gather.5.cloned.1.call-start
  25.3 1.1 collective-permute-start.2
  26.4 0.8 slice.29
  27.2 0.0 all-gather.5.cloned.1.call-update
  27.2 0.9 collective-permute-start.3
  28.1 3.3 %collective-permute-start.4 = (bf16[256,1536]{1,0:T(8,128)(2,1)S(1)}, bf16[256,1536]{1,0:T(8,128)(2,1)}, u32[]{:S(2)}, u32[]{:S(2)}) collective-permute-start(bf16[256,1536]{1,0:T(8,128)(2,1)S(1)} %copy-done.9), channel_id=1, source_target_pairs={{0,224},{1,227},{2,226},{3,229},{4,228},{5,231},{6,230},{7,233},{8... | collective-permute-start | bytes 2359304 | tf_op jit(solution)/shard_map/ppermute | solution.py:61
  31.4 0.2 collective-permute-start.5
  31.5 3.2 %collective-permute-start.6 = (bf16[256,1536]{1,0:T(8,128)(2,1)S(1)}, bf16[256,1536]{1,0:T(8,128)(2,1)}, u32[]{:S(2)}, u32[]{:S(2)}) collective-permute-start(bf16[256,1536]{1,0:T(8,128)(2,1)S(1)} %copy-done.9), channel_id=1, source_target_pairs={{0,30},{1,3},{2,0},{3,5},{4,2},{5,7},{6,4},{7,9},{8,6},{9,11},{10,... | collective-permute-start | bytes 2359304 | tf_op jit(solution)/shard_map/ppermute | solution.py:61
  34.8 18.1 %collective-permute-done.2.refs_1_ = bf16[256,1536]{1,0:T(8,128)(2,1)} collective-permute-done((bf16[256,1536]{1,0:T(8,128)(2,1)S(1)}, bf16[256,1536]{1,0:T(8,128)(2,1)}, u32[]{:S(2)}, u32[]{:S(2)}) %collective-permute-start.2) | collective-permute-done | bytes 786464 | tf_op jit(solution)/shard_map/ppermute | solution.py:61
  52.9 4.9 %collective-permute-start.7 = (bf16[256,1536]{1,0:T(8,128)(2,1)S(1)}, bf16[256,1536]{1,0:T(8,128)(2,1)S(1)}, u32[]{:S(2)}, u32[]{:S(2)}) collective-permute-start(bf16[256,1536]{1,0:T(8,128)(2,1)S(1)} %copy-done.9), channel_id=1, source_target_pairs={{0,1},{1,0},{2,3},{3,2},{4,5},{5,4},{6,7},{7,6},{8,9},{9,8},{10,11... | collective-permute-start | bytes 2359304 | tf_op jit(solution)/shard_map/ppermute | solution.py:61
  57.8 0.7 stack.59.far_ref
  58.5 5.0 %collective-permute-done.3.refs_2_ = bf16[256,1536]{1,0:T(8,128)(2,1)} collective-permute-done((bf16[256,1536]{1,0:T(8,128)(2,1)S(1)}, bf16[256,1536]{1,0:T(8,128)(2,1)}, u32[]{:S(2)}, u32[]{:S(2)}) %collective-permute-start.3) | collective-permute-done | bytes 786464 | tf_op jit(solution)/shard_map/ppermute | solution.py:61
  63.5 7.1 %collective-permute-start.8 = (bf16[256,1536]{1,0:T(8,128)(2,1)}, bf16[256,1536]{1,0:T(8,128)(2,1)}, u32[]{:S(2)}, u32[]{:S(2)}) collective-permute-start(bf16[256,1536]{1,0:T(8,128)(2,1)} %collective-permute-done.2.refs_1_), channel_id=1, source_target_pairs={{0,1},{1,0},{2,3},{3,2},{4,5},{5,4},{6,7},{7,6},{8,9},{9,8},{10,11... | collective-permute-start | bytes 2359304 | tf_op jit(solution)/shard_map/ppermute | solution.py:61
  70.6 0.0 collective-permute-done.4.refs_3_
  70.6 3.5 %collective-permute-start.9 = (bf16[256,1536]{1,0:T(8,128)(2,1)}, bf16[256,1536]{1,0:T(8,128)(2,1)}, u32[]{:S(2)}, u32[]{:S(2)}) collective-permute-start(bf16[256,1536]{1,0:T(8,128)(2,1)} %collective-permute-done.3.refs_2_), channel_id=1, source_target_pairs={{0,1},{1,0},{2,3},{3,2},{4,5},{5,4},{6,7},{7,6},{8,9},{9,8},{10,11... | collective-permute-start | bytes 2359304 | tf_op jit(solution)/shard_map/ppermute | solution.py:61
  74.1 0.0 collective-permute-done.5.refs_4_
  74.1 12.2 %collective-permute-start.10 = (bf16[256,1536]{1,0:T(8,128)(2,1)}, bf16[256,1536]{1,0:T(8,128)(2,1)}, u32[]{:S(2)}, u32[]{:S(2)}) collective-permute-start(bf16[256,1536]{1,0:T(8,128)(2,1)} %collective-permute-done.4.refs_3_), channel_id=1, source_target_pairs={{0,1},{1,0},{2,3},{3,2},{4,5},{5,4},{6,7},{7,6},{8,9},{9,8},{10,11... | collective-permute-start | bytes 2359304 | tf_op jit(solution)/shard_map/ppermute | solution.py:61
  86.3 0.0 collective-permute-done.6.refs_5_
  86.3 9.0 %collective-permute-start.11 = (bf16[256,1536]{1,0:T(8,128)(2,1)}, bf16[256,1536]{1,0:T(8,128)(2,1)}, u32[]{:S(2)}, u32[]{:S(2)}) collective-permute-start(bf16[256,1536]{1,0:T(8,128)(2,1)} %collective-permute-done.5.refs_4_), channel_id=1, source_target_pairs={{0,1},{1,0},{2,3},{3,2},{4,5},{5,4},{6,7},{7,6},{8,9},{9,8},{10,11... | collective-permute-start | bytes 2359304 | tf_op jit(solution)/shard_map/ppermute | solution.py:61
  95.3 0.0 collective-permute-done.7.refs_6_
  95.3 0.1 collective-permute-start.12
  95.4 0.7 broadcast_select_fusion.order_ref
  96.0 0.1 copy-done.15
  96.1 2.2 %fusion = (bf16[384,1152]{1,0:T(8,128)(2,1)S(1)}, bf16[384,1152]{1,0:T(8,128)(2,1)S(1)}, bf16[384,1152]{1,0:T(8,128)(2,1)S(1)}, bf16[384,1152]{1,0:T(8,128)(2,1)S(1)}) fusion(bf16[1536,1152]{1,0:T(8,128)(2,1)} %all-gather.3.cloned.1.call-done.refs_12_), kind=kLoop, calls=%fused_computation.13 | loop fusion | bytes 7077888 | tf_op jit(solution)/shard_map/slice | solution.py:294
  98.4 1.3 collective-permute-start.13
  99.7 0.0 collective-permute-done.9.refs_8_
  99.7 1.5 collective-permute-start.14
  101.2 0.4 collective-permute-start.15
  101.6 0.0 collective-permute-done.11.refs_10_
  101.6 2.2 %collective-permute-start.16 = (bf16[384,1152]{1,0:T(8,128)(2,1)S(1)}, bf16[384,1152]{1,0:T(8,128)(2,1)}, u32[]{:S(2)}, u32[]{:S(2)}) collective-permute-start(bf16[384,1152]{1,0:T(8,128)(2,1)S(1)} %get-tuple-element.43), channel_id=1, source_target_pairs={{0,34},{1,35},{2,32},{3,33},{4,38},{5,39},{6,36},{7,37},{8,42},{9,... | collective-permute-start | bytes 2654216 | tf_op jit(solution)/shard_map/ppermute | solution.py:61
  103.8 0.0 collective-permute-done.12.refs_11_
  103.8 20.5 %three_heads.2 = (bf16[256,384]{1,0:T(8,128)(2,1)}, bf16[256,384]{1,0:T(8,128)(2,1)}) custom-call(s32[12]{0:T(128)} %broadcast_select_fusion.order_ref, f32[12]{0:T(128)} %stack.59.far_ref, bf16[256,1536]{1,0:T(8,128)(2,1)} %modulate.1.refs_0_, bf16[256,1536]{1,0:T(8,128)(2,1)} %collective-permute-done.2.refs_1_, ...), custom_call_target="tpu_custom_call" | custom-call | flops 9663676416 | bytes 12976128 | tf_op jit(solution)/shard_map/three_heads/pallas_call | solution.py:189
  124.3 0.0 collective-permute-done.13.refs_12_
  124.3 0.0 collective-permute-done.16.refs_15_
  124.4 0.0 copy-start.12
  124.4 1.5 collective-permute-start.17
  125.8 20.6 %three_heads.3 = (bf16[256,384]{1,0:T(8,128)(2,1)}, bf16[256,384]{1,0:T(8,128)(2,1)}) custom-call(s32[12]{0:T(128)} %broadcast_select_fusion.order_ref, f32[12]{0:T(128)} %stack.59.far_ref, bf16[256,1536]{1,0:T(8,128)(2,1)} %modulate.1.refs_0_, bf16[256,1536]{1,0:T(8,128)(2,1)} %collective-permute-done.2.refs_1_, ...), custom_call_target="tpu_custom_call" | custom-call | flops 9663676416 | bytes 12976128 | tf_op jit(solution)/shard_map/three_heads/pallas_call | solution.py:189
  146.4 0.1 collective-permute-start.18
  146.6 0.0 collective-permute-done.17.a2
  146.6 1.6 collective-permute-done.18.a3
  148.2 0.1 collective-permute-start.19
  148.3 0.6 reshape.31.gate_ref
  148.9 0.6 pad_add_fusion.at_ref
  149.6 4.2 %out_columns.2.refs_0_ = bf16[256,768]{1,0:T(8,128)(2,1)} custom-call(s32[1]{0:T(128)} %bitcast.c_ref, s32[4]{0:T(128)} %pad_add_fusion.at_ref, bf16[256,384]{1,0:T(8,128)(2,1)} %get-tuple-element.30.a0, bf16[256,384]{1,0:T(8,128)(2,1)} %get-tuple-element.35.a1, bf16[256,384]{1,0:T(8,128)(2,1)} %copy-done.2, bf16[256,384]{1,0:T(8,128)(2,1)} %copy-done.5, ...), custom_call_target="tpu_custom_call" | custom-call | flops 603979776 | bytes 3538944 | tf_op jit(solution)/shard_map/out_columns/pallas_call | solution.py:253
  153.8 0.0 copy-start
  153.8 1.0 copy-done
  154.8 0.9 copy-done.3
  155.8 0.9 copy-done.6
  156.7 2.9 %out_columns.3 = bf16[256,1536]{1,0:T(8,128)(2,1)} custom-call(s32[1]{0:T(128)} %bitcast.c_ref, s32[4]{0:T(128)S(1)} %copy-done.8, bf16[256,384]{1,0:T(8,128)(2,1)S(1)} %copy-done.1, bf16[256,384]{1,0:T(8,128)(2,1)S(1)} %copy-done.4, bf16[256,384]{1,0:T(8,128)(2,1)S(1)} %copy-done.3, bf16[256,384]{1,0:T(8,128)(2,1)S(1)} %copy-done.6, ...), custom_call_target="tpu_custom_call" | custom-call | flops 603979776 | bytes 3538944 | tf_op jit(solution)/shard_map/out_columns/pallas_call | solution.py:253
  (33 shorter events, 0.1 us)
Async XLA Ops:
  6.5 7.6 %copy-start.10 = (f32[1536]{0:T(1024)S(1)}, f32[1536]{0:T(1024)}, u32[]{:S(2)}) copy-start(f32[1536]{0:T(1024)} %param.12) | copy-start | bytes 18436
  6.5 8.2 %copy-start.11 = (f32[1536]{0:T(1024)S(1)}, f32[1536]{0:T(1024)}, u32[]{:S(2)}) copy-start(f32[1536]{0:T(1024)} %param.11) | copy-start | bytes 18436
  6.5 89.6 %all-gather.3.cloned.1.call-start = ((), (), s32[]{:S(2)}) async-start(), calls=%async_computation | async-start | bytes 3981312 | tf_op jit(solution)/shard_map/all_gather | solution.py:291
  8.4 4.4 %collective-permute-start = (bf16[48,1920]{1,0:T(8,128)(2,1)S(1)}, bf16[48,1920]{1,0:T(8,128)(2,1)S(1)}, u32[]{:S(2)}, u32[]{:S(2)}) collective-permute-start(bf16[48,1920]{1,0:T(8,128)(2,1)S(1)} %pad_maximum_fusion), channel_id=1, source_target_pairs={{0,1},{1,0},{2,3},{3,2},{4,5},{5,4},{6,7},{7,6},{8,9},{9,8},{10,11... | collective-permute-start | bytes 552968 | tf_op jit(solution)/shard_map/ppermute | solution.py:61
  12.9 11.4 %collective-permute-start.1 = (bf16[96,1920]{1,0:T(8,128)(2,1)S(1)}, bf16[96,1920]{1,0:T(8,128)(2,1)S(1)}, u32[]{:S(2)}, u32[]{:S(2)}) collective-permute-start(bf16[96,1920]{1,0:T(8,128)(2,1)S(1)} %maximum_select_fusion.1), channel_id=1, source_target_pairs={{0,2},{1,3},{2,0},{3,1},{4,6},{5,7},{6,4},{7,5},{8,10},{9,11},{10,... | collective-permute-start | bytes 1105928 | tf_op jit(solution)/shard_map/ppermute | solution.py:61
  19.1 6.2 %copy-start.9 = (bf16[256,1536]{1,0:T(8,128)(2,1)S(1)}, bf16[256,1536]{1,0:T(8,128)(2,1)}, u32[]{:S(2)}) copy-start(bf16[256,1536]{1,0:T(8,128)(2,1)} %modulate.1.refs_0_) | copy-start | bytes 2359300
  24.4 70.9 %copy-start.13 = (s32[12]{0:T(128)S(1)}, s32[12]{0:T(128)}, u32[]{:S(2)}) copy-start(s32[12]{0:T(128)} %constant.61.clone) | copy-start | bytes 148
  24.4 70.9 %copy-start.14 = (s32[12]{0:T(128)S(1)}, s32[12]{0:T(128)}, u32[]{:S(2)}) copy-start(s32[12]{0:T(128)} %constant.62.clone) | copy-start | bytes 148
  25.3 121.3 %all-gather.5.cloned.1.call-start = ((), (), s32[]{:S(2)}) async-start(), calls=%async_computation.1 | async-start | bytes 2654208 | tf_op jit(solution)/shard_map/all_gather | solution.py:292
  25.3 27.6 %collective-permute-start.2 = (bf16[256,1536]{1,0:T(8,128)(2,1)S(1)}, bf16[256,1536]{1,0:T(8,128)(2,1)}, u32[]{:S(2)}, u32[]{:S(2)}) collective-permute-start(bf16[256,1536]{1,0:T(8,128)(2,1)S(1)} %copy-done.9), channel_id=1, source_target_pairs={{0,32},{1,35},{2,34},{3,37},{4,36},{5,39},{6,38},{7,41},{8,40},{9,... | collective-permute-start | bytes 2359304 | tf_op jit(solution)/shard_map/ppermute | solution.py:61
  27.2 36.3 %collective-permute-start.3 = (bf16[256,1536]{1,0:T(8,128)(2,1)S(1)}, bf16[256,1536]{1,0:T(8,128)(2,1)}, u32[]{:S(2)}, u32[]{:S(2)}) collective-permute-start(bf16[256,1536]{1,0:T(8,128)(2,1)S(1)} %copy-done.9), channel_id=1, source_target_pairs={{0,62},{1,33},{2,32},{3,35},{4,34},{5,37},{6,36},{7,39},{8,38},{9,... | collective-permute-start | bytes 2359304 | tf_op jit(solution)/shard_map/ppermute | solution.py:61
  28.1 42.5 %collective-permute-start.4 = (bf16[256,1536]{1,0:T(8,128)(2,1)S(1)}, bf16[256,1536]{1,0:T(8,128)(2,1)}, u32[]{:S(2)}, u32[]{:S(2)}) collective-permute-start(bf16[256,1536]{1,0:T(8,128)(2,1)S(1)} %copy-done.9), channel_id=1, source_target_pairs={{0,224},{1,227},{2,226},{3,229},{4,228},{5,231},{6,230},{7,233},{8... | collective-permute-start | bytes 2359304 | tf_op jit(solution)/shard_map/ppermute | solution.py:61
  31.4 42.8 %collective-permute-start.5 = (bf16[256,1536]{1,0:T(8,128)(2,1)S(1)}, bf16[256,1536]{1,0:T(8,128)(2,1)}, u32[]{:S(2)}, u32[]{:S(2)}) collective-permute-start(bf16[256,1536]{1,0:T(8,128)(2,1)S(1)} %copy-done.9), channel_id=1, source_target_pairs={{0,254},{1,225},{2,224},{3,227},{4,226},{5,229},{6,228},{7,231},{8... | collective-permute-start | bytes 2359304 | tf_op jit(solution)/shard_map/ppermute | solution.py:61
  31.5 54.8 %collective-permute-start.6 = (bf16[256,1536]{1,0:T(8,128)(2,1)S(1)}, bf16[256,1536]{1,0:T(8,128)(2,1)}, u32[]{:S(2)}, u32[]{:S(2)}) collective-permute-start(bf16[256,1536]{1,0:T(8,128)(2,1)S(1)} %copy-done.9), channel_id=1, source_target_pairs={{0,30},{1,3},{2,0},{3,5},{4,2},{5,7},{6,4},{7,9},{8,6},{9,11},{10,... | collective-permute-start | bytes 2359304 | tf_op jit(solution)/shard_map/ppermute | solution.py:61
  52.9 42.4 %collective-permute-start.7 = (bf16[256,1536]{1,0:T(8,128)(2,1)S(1)}, bf16[256,1536]{1,0:T(8,128)(2,1)S(1)}, u32[]{:S(2)}, u32[]{:S(2)}) collective-permute-start(bf16[256,1536]{1,0:T(8,128)(2,1)S(1)} %copy-done.9), channel_id=1, source_target_pairs={{0,1},{1,0},{2,3},{3,2},{4,5},{5,4},{6,7},{7,6},{8,9},{9,8},{10,11... | collective-permute-start | bytes 2359304 | tf_op jit(solution)/shard_map/ppermute | solution.py:61
  63.5 34.9 %collective-permute-start.8 = (bf16[256,1536]{1,0:T(8,128)(2,1)}, bf16[256,1536]{1,0:T(8,128)(2,1)}, u32[]{:S(2)}, u32[]{:S(2)}) collective-permute-start(bf16[256,1536]{1,0:T(8,128)(2,1)} %collective-permute-done.2.refs_1_), channel_id=1, source_target_pairs={{0,1},{1,0},{2,3},{3,2},{4,5},{5,4},{6,7},{7,6},{8,9},{9,8},{10,11... | collective-permute-start | bytes 2359304 | tf_op jit(solution)/shard_map/ppermute | solution.py:61
  70.6 29.1 %collective-permute-start.9 = (bf16[256,1536]{1,0:T(8,128)(2,1)}, bf16[256,1536]{1,0:T(8,128)(2,1)}, u32[]{:S(2)}, u32[]{:S(2)}) collective-permute-start(bf16[256,1536]{1,0:T(8,128)(2,1)} %collective-permute-done.3.refs_2_), channel_id=1, source_target_pairs={{0,1},{1,0},{2,3},{3,2},{4,5},{5,4},{6,7},{7,6},{8,9},{9,8},{10,11... | collective-permute-start | bytes 2359304 | tf_op jit(solution)/shard_map/ppermute | solution.py:61
  74.1 27.0 %collective-permute-start.10 = (bf16[256,1536]{1,0:T(8,128)(2,1)}, bf16[256,1536]{1,0:T(8,128)(2,1)}, u32[]{:S(2)}, u32[]{:S(2)}) collective-permute-start(bf16[256,1536]{1,0:T(8,128)(2,1)} %collective-permute-done.4.refs_3_), channel_id=1, source_target_pairs={{0,1},{1,0},{2,3},{3,2},{4,5},{5,4},{6,7},{7,6},{8,9},{9,8},{10,11... | collective-permute-start | bytes 2359304 | tf_op jit(solution)/shard_map/ppermute | solution.py:61
  86.3 15.3 %collective-permute-start.11 = (bf16[256,1536]{1,0:T(8,128)(2,1)}, bf16[256,1536]{1,0:T(8,128)(2,1)}, u32[]{:S(2)}, u32[]{:S(2)}) collective-permute-start(bf16[256,1536]{1,0:T(8,128)(2,1)} %collective-permute-done.5.refs_4_), channel_id=1, source_target_pairs={{0,1},{1,0},{2,3},{3,2},{4,5},{5,4},{6,7},{7,6},{8,9},{9,8},{10,11... | collective-permute-start | bytes 2359304 | tf_op jit(solution)/shard_map/ppermute | solution.py:61
  95.3 0.9 copy-start.15
  95.3 8.6 %collective-permute-start.12 = (bf16[256,1536]{1,0:T(8,128)(2,1)}, bf16[256,1536]{1,0:T(8,128)(2,1)}, u32[]{:S(2)}, u32[]{:S(2)}) collective-permute-start(bf16[256,1536]{1,0:T(8,128)(2,1)} %collective-permute-done.6.refs_5_), channel_id=1, source_target_pairs={{0,1},{1,0},{2,3},{3,2},{4,5},{5,4},{6,7},{7,6},{8,9},{9,8},{10,11... | collective-permute-start | bytes 2359304 | tf_op jit(solution)/shard_map/ppermute | solution.py:61
  98.4 25.9 %collective-permute-start.13 = (bf16[384,1152]{1,0:T(8,128)(2,1)S(1)}, bf16[384,1152]{1,0:T(8,128)(2,1)}, u32[]{:S(2)}, u32[]{:S(2)}) collective-permute-start(bf16[384,1152]{1,0:T(8,128)(2,1)S(1)} %get-tuple-element.46), channel_id=1, source_target_pairs={{0,64},{1,65},{2,66},{3,67},{4,68},{5,69},{6,70},{7,71},{8,72},{9,... | collective-permute-start | bytes 2654216 | tf_op jit(solution)/shard_map/ppermute | solution.py:61
  99.7 24.6 %collective-permute-start.14 = (bf16[384,1152]{1,0:T(8,128)(2,1)S(1)}, bf16[384,1152]{1,0:T(8,128)(2,1)}, u32[]{:S(2)}, u32[]{:S(2)}) collective-permute-start(bf16[384,1152]{1,0:T(8,128)(2,1)S(1)} %get-tuple-element.45), channel_id=1, source_target_pairs={{0,192},{1,193},{2,194},{3,195},{4,196},{5,197},{6,198},{7,199},{8... | collective-permute-start | bytes 2654216 | tf_op jit(solution)/shard_map/ppermute | solution.py:61
  101.2 23.2 %collective-permute-start.15 = (bf16[384,1152]{1,0:T(8,128)(2,1)S(1)}, bf16[384,1152]{1,0:T(8,128)(2,1)}, u32[]{:S(2)}, u32[]{:S(2)}) collective-permute-start(bf16[384,1152]{1,0:T(8,128)(2,1)S(1)} %get-tuple-element.44), channel_id=1, source_target_pairs={{0,32},{1,33},{2,34},{3,35},{4,36},{5,37},{6,38},{7,39},{8,40},{9,... | collective-permute-start | bytes 2654216 | tf_op jit(solution)/shard_map/ppermute | solution.py:61
  101.6 22.7 %collective-permute-start.16 = (bf16[384,1152]{1,0:T(8,128)(2,1)S(1)}, bf16[384,1152]{1,0:T(8,128)(2,1)}, u32[]{:S(2)}, u32[]{:S(2)}) collective-permute-start(bf16[384,1152]{1,0:T(8,128)(2,1)S(1)} %get-tuple-element.43), channel_id=1, source_target_pairs={{0,34},{1,35},{2,32},{3,33},{4,38},{5,39},{6,36},{7,37},{8,42},{9,... | collective-permute-start | bytes 2654216 | tf_op jit(solution)/shard_map/ppermute | solution.py:61
  124.4 24.0 %copy-start.12 = (f32[1536]{0:T(1024)S(1)}, f32[1536]{0:T(1024)}, u32[]{:S(2)}) copy-start(f32[1536]{0:T(1024)} %param.13) | copy-start | bytes 18436
  124.4 22.2 %collective-permute-start.17 = (bf16[256,384]{1,0:T(8,128)(2,1)}, bf16[256,384]{1,0:T(8,128)(2,1)S(1)}, u32[]{:S(2)}, u32[]{:S(2)}) collective-permute-start(bf16[256,384]{1,0:T(8,128)(2,1)} %get-tuple-element.36), channel_id=1, source_target_pairs={{0,1},{1,0},{2,3},{3,2},{4,5},{5,4},{6,7},{7,6},{8,9},{9,8},{10,11... | collective-permute-start | bytes 589832 | tf_op jit(solution)/shard_map/ppermute | solution.py:61
  146.4 1.7 %collective-permute-start.18 = (bf16[256,384]{1,0:T(8,128)(2,1)}, bf16[256,384]{1,0:T(8,128)(2,1)S(1)}, u32[]{:S(2)}, u32[]{:S(2)}) collective-permute-start(bf16[256,384]{1,0:T(8,128)(2,1)} %get-tuple-element.37), channel_id=1, source_target_pairs={{0,1},{1,0},{2,3},{3,2},{4,5},{5,4},{6,7},{7,6},{8,9},{9,8},{10,11... | collective-permute-start | bytes 589832 | tf_op jit(solution)/shard_map/ppermute | solution.py:61
  146.6 3.0 %copy-start.2 = (bf16[256,384]{1,0:T(8,128)(2,1)}, bf16[256,384]{1,0:T(8,128)(2,1)S(1)}, u32[]{:S(2)}) copy-start(bf16[256,384]{1,0:T(8,128)(2,1)S(1)} %collective-permute-done.17.a2) | copy-start | bytes 589828
  148.2 1.4 copy-start.5
  148.2 5.6 %collective-permute-start.19 = (bf16[1536,768]{1,0:T(8,128)(2,1)}, bf16[1536,768]{1,0:T(8,128)(2,1)S(1)}, u32[]{:S(2)}, u32[]{:S(2)}) collective-permute-start(bf16[1536,768]{1,0:T(8,128)(2,1)} %all-gather.5.cloned.1.call-done.w_ref), channel_id=1, source_target_pairs={{0,1},{1,0},{2,3},{3,2},{4,5},{5,4},{6,7},{7,6},{8,9},{9,8},{10,11... | collective-permute-start | bytes 7077896 | tf_op jit(solution)/shard_map/ppermute | solution.py:61
  149.5 4.3 %copy-start.1 = (bf16[256,384]{1,0:T(8,128)(2,1)S(1)}, bf16[256,384]{1,0:T(8,128)(2,1)}, u32[]{:S(2)}) copy-start(bf16[256,384]{1,0:T(8,128)(2,1)} %get-tuple-element.30.a0) | copy-start | bytes 589828
  149.5 4.3 %copy-start.4 = (bf16[256,384]{1,0:T(8,128)(2,1)S(1)}, bf16[256,384]{1,0:T(8,128)(2,1)}, u32[]{:S(2)}) copy-start(bf16[256,384]{1,0:T(8,128)(2,1)} %get-tuple-element.35.a1) | copy-start | bytes 589828
  149.5 4.3 %copy-start.7 = (f32[1,1536]{1,0:T(1,128)S(1)}, f32[1,1536]{1,0:T(1,128)}, u32[]{:S(2)}) copy-start(f32[1,1536]{1,0:T(1,128)} %reshape.31.gate_ref) | copy-start | bytes 18436
  149.6 4.3 %copy-start.8 = (s32[4]{0:T(128)S(1)}, s32[4]{0:T(128)}, u32[]{:S(2)}) copy-start(s32[4]{0:T(128)} %pad_add_fusion.at_ref) | copy-start | bytes 52
  153.8 1.0 copy-start
  154.8 0.9 copy-start.3
  155.8 0.9 copy-start.6
Sparse Core Ops, SparseCore 0:
  25.4 65.5 all-gather.2
  92.8 37.3 all-gather.4

commit v8 on v7

--- a/solution.py
+++ b/solution.py
@@ -42,6 +42,7 @@
 
 SIBLING = hops(lambda x, y, z, c: (x, y, z, 1 - c))
 U_FLIP = hops(lambda x, y, z, c: (x, y + 2, z, c))
+U_CROSS = hops(lambda x, y, z, c: (x, y + 2, z, 1 - c))
 NEAR = (
     hops(lambda x, y, z, c: (x + 1, y, z, c)),
     hops(lambda x, y, z, c: (x - 1, y, z, c)),
@@ -261,7 +262,7 @@
             pltpu.SemaphoreType.DMA((4,)),
             pltpu.SemaphoreType.DMA((4,)),
         ],
-        compiler_params=pltpu.CompilerParams(vmem_limit_bytes=(60 if own else 20) << 20),
+        compiler_params=pltpu.CompilerParams(vmem_limit_bytes=62 << 20),
         cost_estimate=cost(2 * rows * width * 2 * HALF, width * 2 * HALF * 2 + rows * width * 3),
         name="out_columns",
     )(c, at, *attended, w, gate.reshape(1, -1), *before)
@@ -281,13 +282,17 @@
         parts.append(lax.dynamic_slice_in_dim(out_weight, core * 2 * HALF, 2 * HALF, 1))
         return jnp.concatenate(parts, axis=1)
 
-    mine, other = columns(c), send(columns(1 - c), SIBLING)
-    pair = jnp.where(c == 0, jnp.concatenate([mine, other]), jnp.concatenate([other, mine]))
-    other = send(pair, U_FLIP)
-    flat, pair = together(tokens.reshape(count, width), pair)
+    mine, theirs = columns(c), columns(1 - c)
+    sibling, same, cross = send(theirs, SIBLING), send(mine, U_FLIP), send(theirs, U_CROSS)
+    flat, mine = together(tokens.reshape(count, width), mine)
     own = modulate(flat, scale, shift)
-    own, other = together(own, other)
-    quad = jnp.where(u == 0, jnp.concatenate([pair, other]), jnp.concatenate([other, pair]))
+    own, sibling, same, cross = together(own, sibling, same, cross)
+
+    def pair(first, second):
+        return jnp.where(c == 0, jnp.concatenate([first, second]), jnp.concatenate([second, first]))
+
+    near, away = pair(mine, sibling), pair(same, cross)
+    quad = jnp.where(u == 0, jnp.concatenate([near, away]), jnp.concatenate([away, near]))
     w_in = lax.all_gather(quad[:, : 3 * HALF], "z", axis=0, tiled=True)
     w_out = lax.all_gather(quad[:, 3 * HALF :], "z", axis=0, tiled=True)
     quarter = width // 4

time: 167 us -> 164 us (0.982)
  local copies, waits for them, and re-layouts: 11.2 us -> 8.5 us
  starting transfers between devices: 57.3 us -> 54.7 us
  Pallas kernels: 51.9 us -> 53.6 us
    unnamed x32 -> x18, local copies, waits for them, and re-layouts: 3.02 us -> 0.4 us
    ppermute x20 -> x21, starting transfers between devices: 57.2 us -> 54.6 us  [send(): return lax.ppermute(x, AXES, pairs)]
    ppermute x20 -> x21, waiting for transfers between devices: 31 us -> 31.9 us  [send(): return lax.ppermute(x, AXES, pairs)]
  transfers between devices with their start and end apart: 22 -> 23, of which waited for: 5 -> 5; matrix products, arithmetic and copies ran while one was open for 4% -> 4% of each run, Pallas kernels for 29% -> 30%
where the time goes in v8:
time: 164 us
  starting transfers between devices  54.7 us (33%)
  Pallas kernels  53.6 us (33%)
  waiting for transfers between devices  31.9 us (19%)
  between operations  13.6 us (8%)
  local copies, waits for them, and re-layouts  8.5 us (5%)
    ppermute x21, starting transfers between devices, send(): return lax.ppermute(x, AXES, pairs)  54.6 us
    pallas_call x2, Pallas kernels, three_heads(): pl.pallas_call(functools.partial(heads_kernel, n, m), out_shape=[jax.Shap...  41.1 us
    ppermute x21, waiting for transfers between devices, send(): return lax.ppermute(x, AXES, pairs)  31.9 us
    pallas_call x2, Pallas kernels, out_columns(): pl.pallas_call(functools.partial(columns_kernel, own), out_shape=jax.Shap...  8.74 us
    pallas_call x1, Pallas kernels, modulate(): pl.pallas_call(modulate_kernel, out_shape=jax.ShapeDtypeStruct((rows, wid...  3.73 us
  transfers between devices with their start and end apart: 23, of which 5 were waited for; matrix products, arithmetic and copies ran while one was open for 4% of the time, Pallas kernels for 30%

profile of v8, /device:TPU:1, one launch (start us, length us, event | category | flops | bytes accessed | tf_op | source)
XLA Modules:
  0.0 163.7 jit_solution(7480327170298281507)
XLA Ops:
  6.5 1.0 constant_dynamic-slice_fusion
  7.5 0.9 constant_dynamic-slice_fusion.3
  8.4 3.3 %collective-permute-start = (bf16[48,1920]{1,0:T(8,128)(2,1)S(1)}, bf16[48,1920]{1,0:T(8,128)(2,1)S(1)}, u32[]{:S(2)}, u32[]{:S(2)}) collective-permute-start(bf16[48,1920]{1,0:T(8,128)(2,1)S(1)} %pad_maximum_fusion.1), channel_id=1, source_target_pairs={{0,1},{1,0},{2,3},{3,2},{4,5},{5,4},{6,7},{7,6},{8,9},{9,8},{10,11... | collective-permute-start | bytes 552968 | tf_op jit(solution)/shard_map/ppermute | solution.py:62
  11.8 1.3 collective-permute-start.1
  13.0 2.0 %collective-permute-start.2 = (bf16[48,1920]{1,0:T(8,128)(2,1)S(1)}, bf16[48,1920]{1,0:T(8,128)(2,1)S(1)}, u32[]{:S(2)}, u32[]{:S(2)}) collective-permute-start(bf16[48,1920]{1,0:T(8,128)(2,1)S(1)} %pad_maximum_fusion.1), channel_id=1, source_target_pairs={{0,3},{1,2},{2,1},{3,0},{4,7},{5,6},{6,5},{7,4},{8,11},{9,10},{10,... | collective-permute-start | bytes 552968 | tf_op jit(solution)/shard_map/ppermute | solution.py:62
  15.0 0.6 reshape.27.scale_ref
  15.6 0.6 reshape.28.shift_ref
  16.2 3.7 %modulate.1.refs_0_ = bf16[256,1536]{1,0:T(8,128)(2,1)} custom-call(bf16[256,1536]{1,0:T(8,128)(2,1)} %bitcast.17, f32[1,1536]{1,0:T(1,128)} %reshape.27.scale_ref, f32[1,1536]{1,0:T(1,128)} %reshape.28.shift_ref), custom_call_target="tpu_custom_call" | custom-call | flops 3145728 | bytes 1572864 | tf_op jit(solution)/shard_map/modulate/pallas_call | solution.py:85
  19.9 0.0 collective-permute-done
  19.9 0.0 collective-permute-done.1
  20.0 3.7 %collective-permute-done.2 = bf16[48,1920]{1,0:T(8,128)(2,1)S(1)} collective-permute-done((bf16[48,1920]{1,0:T(8,128)(2,1)S(1)}, bf16[48,1920]{1,0:T(8,128)(2,1)S(1)}, u32[]{:S(2)}, u32[]{:S(2)}) %collective-permute-start.2) | collective-permute-done | bytes 184352 | tf_op jit(solution)/shard_map/ppermute | solution.py:62
  23.7 0.1 maximum_select_fusion.1
  23.8 0.0 copy-start.2
  23.8 0.1 maximum_select_fusion
  24.0 0.0 copy-start.6
  24.0 0.0 copy-start.7
  24.0 0.8 slice.24
  24.8 0.0 all-gather.3.cloned.1.call-update
  24.8 0.0 all-gather.5.cloned.1.call-start
  24.9 0.1 copy-done.2
  25.0 1.0 collective-permute-start.3
  26.0 0.7 slice.29
  26.7 0.0 all-gather.5.cloned.1.call-update
  26.8 0.9 collective-permute-start.4
  27.6 3.3 %collective-permute-start.5 = (bf16[256,1536]{1,0:T(8,128)(2,1)S(1)}, bf16[256,1536]{1,0:T(8,128)(2,1)}, u32[]{:S(2)}, u32[]{:S(2)}) collective-permute-start(bf16[256,1536]{1,0:T(8,128)(2,1)S(1)} %copy-done.2), channel_id=1, source_target_pairs={{0,224},{1,227},{2,226},{3,229},{4,228},{5,231},{6,230},{7,233},{8... | collective-permute-start | bytes 2359304 | tf_op jit(solution)/shard_map/ppermute | solution.py:62
  30.9 0.2 collective-permute-start.6
  31.1 3.2 %collective-permute-start.7 = (bf16[256,1536]{1,0:T(8,128)(2,1)S(1)}, bf16[256,1536]{1,0:T(8,128)(2,1)}, u32[]{:S(2)}, u32[]{:S(2)}) collective-permute-start(bf16[256,1536]{1,0:T(8,128)(2,1)S(1)} %copy-done.2), channel_id=1, source_target_pairs={{0,30},{1,3},{2,0},{3,5},{4,2},{5,7},{6,4},{7,9},{8,6},{9,11},{10,... | collective-permute-start | bytes 2359304 | tf_op jit(solution)/shard_map/ppermute | solution.py:62
  34.3 18.5 %collective-permute-done.3.refs_1_ = bf16[256,1536]{1,0:T(8,128)(2,1)} collective-permute-done((bf16[256,1536]{1,0:T(8,128)(2,1)S(1)}, bf16[256,1536]{1,0:T(8,128)(2,1)}, u32[]{:S(2)}, u32[]{:S(2)}) %collective-permute-start.3) | collective-permute-done | bytes 786464 | tf_op jit(solution)/shard_map/ppermute | solution.py:62
  52.8 3.7 %collective-permute-start.8 = (bf16[256,1536]{1,0:T(8,128)(2,1)S(1)}, bf16[256,1536]{1,0:T(8,128)(2,1)S(1)}, u32[]{:S(2)}, u32[]{:S(2)}) collective-permute-start(bf16[256,1536]{1,0:T(8,128)(2,1)S(1)} %copy-done.2), channel_id=1, source_target_pairs={{0,1},{1,0},{2,3},{3,2},{4,5},{5,4},{6,7},{7,6},{8,9},{9,8},{10,11... | collective-permute-start | bytes 2359304 | tf_op jit(solution)/shard_map/ppermute | solution.py:62
  56.5 0.7 stack.59.far_ref
  57.2 5.9 %collective-permute-done.4.refs_2_ = bf16[256,1536]{1,0:T(8,128)(2,1)} collective-permute-done((bf16[256,1536]{1,0:T(8,128)(2,1)S(1)}, bf16[256,1536]{1,0:T(8,128)(2,1)}, u32[]{:S(2)}, u32[]{:S(2)}) %collective-permute-start.4) | collective-permute-done | bytes 786464 | tf_op jit(solution)/shard_map/ppermute | solution.py:62
  63.1 5.8 %collective-permute-start.9 = (bf16[256,1536]{1,0:T(8,128)(2,1)}, bf16[256,1536]{1,0:T(8,128)(2,1)}, u32[]{:S(2)}, u32[]{:S(2)}) collective-permute-start(bf16[256,1536]{1,0:T(8,128)(2,1)} %collective-permute-done.3.refs_1_), channel_id=1, source_target_pairs={{0,1},{1,0},{2,3},{3,2},{4,5},{5,4},{6,7},{7,6},{8,9},{9,8},{10,11... | collective-permute-start | bytes 2359304 | tf_op jit(solution)/shard_map/ppermute | solution.py:62
  68.9 0.0 collective-permute-done.5.refs_3_
  68.9 3.9 %collective-permute-start.10 = (bf16[256,1536]{1,0:T(8,128)(2,1)}, bf16[256,1536]{1,0:T(8,128)(2,1)}, u32[]{:S(2)}, u32[]{:S(2)}) collective-permute-start(bf16[256,1536]{1,0:T(8,128)(2,1)} %collective-permute-done.4.refs_2_), channel_id=1, source_target_pairs={{0,1},{1,0},{2,3},{3,2},{4,5},{5,4},{6,7},{7,6},{8,9},{9,8},{10,11... | collective-permute-start | bytes 2359304 | tf_op jit(solution)/shard_map/ppermute | solution.py:62
  72.8 0.0 collective-permute-done.6.refs_4_
  72.8 12.2 %collective-permute-start.11 = (bf16[256,1536]{1,0:T(8,128)(2,1)}, bf16[256,1536]{1,0:T(8,128)(2,1)}, u32[]{:S(2)}, u32[]{:S(2)}) collective-permute-start(bf16[256,1536]{1,0:T(8,128)(2,1)} %collective-permute-done.5.refs_3_), channel_id=1, source_target_pairs={{0,1},{1,0},{2,3},{3,2},{4,5},{5,4},{6,7},{7,6},{8,9},{9,8},{10,11... | collective-permute-start | bytes 2359304 | tf_op jit(solution)/shard_map/ppermute | solution.py:62
  84.9 2.1 %collective-permute-done.7.refs_5_ = bf16[256,1536]{1,0:T(8,128)(2,1)} collective-permute-done((bf16[256,1536]{1,0:T(8,128)(2,1)S(1)}, bf16[256,1536]{1,0:T(8,128)(2,1)}, u32[]{:S(2)}, u32[]{:S(2)}) %collective-permute-start.7) | collective-permute-done | bytes 786464 | tf_op jit(solution)/shard_map/ppermute | solution.py:62
  87.1 6.8 %collective-permute-start.12 = (bf16[256,1536]{1,0:T(8,128)(2,1)}, bf16[256,1536]{1,0:T(8,128)(2,1)}, u32[]{:S(2)}, u32[]{:S(2)}) collective-permute-start(bf16[256,1536]{1,0:T(8,128)(2,1)} %collective-permute-done.6.refs_4_), channel_id=1, source_target_pairs={{0,1},{1,0},{2,3},{3,2},{4,5},{5,4},{6,7},{7,6},{8,9},{9,8},{10,11... | collective-permute-start | bytes 2359304 | tf_op jit(solution)/shard_map/ppermute | solution.py:62
  93.9 0.0 collective-permute-done.8.refs_6_
  93.9 0.1 collective-permute-start.13
  94.0 0.6 broadcast_select_fusion.order_ref
  94.6 0.2 copy-done.8
  94.8 2.2 %fusion = (bf16[384,1152]{1,0:T(8,128)(2,1)S(1)}, bf16[384,1152]{1,0:T(8,128)(2,1)S(1)}, bf16[384,1152]{1,0:T(8,128)(2,1)S(1)}, bf16[384,1152]{1,0:T(8,128)(2,1)S(1)}) fusion(bf16[1536,1152]{1,0:T(8,128)(2,1)} %all-gather.3.cloned.1.call-done.refs_12_), kind=kLoop, calls=%fused_computation.15 | loop fusion | bytes 7077888 | tf_op jit(solution)/shard_map/slice | solution.py:299
  97.1 1.3 collective-permute-start.14
  98.4 0.0 collective-permute-done.10.refs_8_
  98.4 1.5 collective-permute-start.15
  99.8 0.4 collective-permute-start.16
  100.3 0.0 collective-permute-done.12.refs_10_
  100.3 2.2 %collective-permute-start.17 = (bf16[384,1152]{1,0:T(8,128)(2,1)S(1)}, bf16[384,1152]{1,0:T(8,128)(2,1)}, u32[]{:S(2)}, u32[]{:S(2)}) collective-permute-start(bf16[384,1152]{1,0:T(8,128)(2,1)S(1)} %get-tuple-element.47), channel_id=1, source_target_pairs={{0,34},{1,35},{2,32},{3,33},{4,38},{5,39},{6,36},{7,37},{8,42},{9,... | collective-permute-start | bytes 2654216 | tf_op jit(solution)/shard_map/ppermute | solution.py:62
  102.5 0.0 collective-permute-done.13.refs_11_
  102.5 20.5 %three_heads.2 = (bf16[256,384]{1,0:T(8,128)(2,1)}, bf16[256,384]{1,0:T(8,128)(2,1)}) custom-call(s32[12]{0:T(128)} %broadcast_select_fusion.order_ref, f32[12]{0:T(128)} %stack.59.far_ref, bf16[256,1536]{1,0:T(8,128)(2,1)} %modulate.1.refs_0_, bf16[256,1536]{1,0:T(8,128)(2,1)} %collective-permute-done.3.refs_1_, ...), custom_call_target="tpu_custom_call" | custom-call | flops 9663676416 | bytes 12976128 | tf_op jit(solution)/shard_map/three_heads/pallas_call | solution.py:190
  123.0 0.0 collective-permute-done.15.refs_13_
  123.0 0.0 collective-permute-done.16.refs_14_
  123.0 0.0 copy-start.5
  123.0 1.3 collective-permute-start.18
  124.3 20.6 %three_heads.3 = (bf16[256,384]{1,0:T(8,128)(2,1)}, bf16[256,384]{1,0:T(8,128)(2,1)}) custom-call(s32[12]{0:T(128)} %broadcast_select_fusion.order_ref, f32[12]{0:T(128)} %stack.59.far_ref, bf16[256,1536]{1,0:T(8,128)(2,1)} %modulate.1.refs_0_, bf16[256,1536]{1,0:T(8,128)(2,1)} %collective-permute-done.3.refs_1_, ...), custom_call_target="tpu_custom_call" | custom-call | flops 9663676416 | bytes 12976128 | tf_op jit(solution)/shard_map/three_heads/pallas_call | solution.py:190
  145.0 0.1 collective-permute-start.19
  145.1 1.6 collective-permute-done.19.a3
  146.7 0.1 collective-permute-start.20
  146.9 0.6 reshape.31.gate_ref
  147.5 0.6 pad_add_fusion.at_ref
  148.1 4.1 %out_columns.2.refs_0_ = bf16[256,768]{1,0:T(8,128)(2,1)} custom-call(s32[1]{0:T(128)} %bitcast.c_ref, s32[4]{0:T(128)} %pad_add_fusion.at_ref, bf16[256,384]{1,0:T(8,128)(2,1)} %get-tuple-element.34.a0, bf16[256,384]{1,0:T(8,128)(2,1)} %get-tuple-element.39.a1, bf16[256,384]{1,0:T(8,128)(2,1)} %copy-done, bf16[256,384]{1,0:T(8,128)(2,1)} %copy-done.1, ...), custom_call_target="tpu_custom_call" | custom-call | flops 603979776 | bytes 3538944 | tf_op jit(solution)/shard_map/out_columns/pallas_call | solution.py:254
  152.3 0.0 collective-permute-done.20.w_ref
  152.3 4.6 %out_columns.3 = bf16[256,1536]{1,0:T(8,128)(2,1)} custom-call(s32[1]{0:T(128)} %bitcast.c_ref, s32[4]{0:T(128)} %pad_add_fusion.at_ref, bf16[256,384]{1,0:T(8,128)(2,1)} %get-tuple-element.34.a0, bf16[256,384]{1,0:T(8,128)(2,1)} %get-tuple-element.39.a1, bf16[256,384]{1,0:T(8,128)(2,1)} %copy-done, bf16[256,384]{1,0:T(8,128)(2,1)} %copy-done.1, ...), custom_call_target="tpu_custom_call" | custom-call | flops 603979776 | bytes 3538944 | tf_op jit(solution)/shard_map/out_columns/pallas_call | solution.py:254
  (22 shorter events, 0.1 us)
Async XLA Ops:
  6.5 8.5 %copy-start.3 = (f32[1536]{0:T(1024)S(1)}, f32[1536]{0:T(1024)}, u32[]{:S(2)}) copy-start(f32[1536]{0:T(1024)} %param.12) | copy-start | bytes 18436
  6.5 9.1 %copy-start.4 = (f32[1536]{0:T(1024)S(1)}, f32[1536]{0:T(1024)}, u32[]{:S(2)}) copy-start(f32[1536]{0:T(1024)} %param.11) | copy-start | bytes 18436
  6.5 88.3 %all-gather.3.cloned.1.call-start = ((), (), s32[]{:S(2)}) async-start(), calls=%async_computation | async-start | bytes 3981312 | tf_op jit(solution)/shard_map/all_gather | solution.py:296
  8.4 11.5 %collective-permute-start = (bf16[48,1920]{1,0:T(8,128)(2,1)S(1)}, bf16[48,1920]{1,0:T(8,128)(2,1)S(1)}, u32[]{:S(2)}, u32[]{:S(2)}) collective-permute-start(bf16[48,1920]{1,0:T(8,128)(2,1)S(1)} %pad_maximum_fusion.1), channel_id=1, source_target_pairs={{0,1},{1,0},{2,3},{3,2},{4,5},{5,4},{6,7},{7,6},{8,9},{9,8},{10,11... | collective-permute-start | bytes 552968 | tf_op jit(solution)/shard_map/ppermute | solution.py:62
  11.8 8.2 %collective-permute-start.1 = (bf16[48,1920]{1,0:T(8,128)(2,1)S(1)}, bf16[48,1920]{1,0:T(8,128)(2,1)S(1)}, u32[]{:S(2)}, u32[]{:S(2)}) collective-permute-start(bf16[48,1920]{1,0:T(8,128)(2,1)S(1)} %pad_maximum_fusion), channel_id=1, source_target_pairs={{0,2},{1,3},{2,0},{3,1},{4,6},{5,7},{6,4},{7,5},{8,10},{9,11},{10,... | collective-permute-start | bytes 552968 | tf_op jit(solution)/shard_map/ppermute | solution.py:62
  13.0 10.6 %collective-permute-start.2 = (bf16[48,1920]{1,0:T(8,128)(2,1)S(1)}, bf16[48,1920]{1,0:T(8,128)(2,1)S(1)}, u32[]{:S(2)}, u32[]{:S(2)}) collective-permute-start(bf16[48,1920]{1,0:T(8,128)(2,1)S(1)} %pad_maximum_fusion.1), channel_id=1, source_target_pairs={{0,3},{1,2},{2,1},{3,0},{4,7},{5,6},{6,5},{7,4},{8,11},{9,10},{10,... | collective-permute-start | bytes 552968 | tf_op jit(solution)/shard_map/ppermute | solution.py:62
  23.8 1.2 copy-start.2
  24.0 70.0 %copy-start.6 = (s32[12]{0:T(128)S(1)}, s32[12]{0:T(128)}, u32[]{:S(2)}) copy-start(s32[12]{0:T(128)} %constant.61.clone) | copy-start | bytes 148
  24.0 70.0 %copy-start.7 = (s32[12]{0:T(128)S(1)}, s32[12]{0:T(128)}, u32[]{:S(2)}) copy-start(s32[12]{0:T(128)} %constant.62.clone) | copy-start | bytes 148
  24.8 120.3 %all-gather.5.cloned.1.call-start = ((), (), s32[]{:S(2)}) async-start(), calls=%async_computation.1 | async-start | bytes 2654208 | tf_op jit(solution)/shard_map/all_gather | solution.py:297
  25.0 27.8 %collective-permute-start.3 = (bf16[256,1536]{1,0:T(8,128)(2,1)S(1)}, bf16[256,1536]{1,0:T(8,128)(2,1)}, u32[]{:S(2)}, u32[]{:S(2)}) collective-permute-start(bf16[256,1536]{1,0:T(8,128)(2,1)S(1)} %copy-done.2), channel_id=1, source_target_pairs={{0,32},{1,35},{2,34},{3,37},{4,36},{5,39},{6,38},{7,41},{8,40},{9,... | collective-permute-start | bytes 2359304 | tf_op jit(solution)/shard_map/ppermute | solution.py:62
  26.8 36.3 %collective-permute-start.4 = (bf16[256,1536]{1,0:T(8,128)(2,1)S(1)}, bf16[256,1536]{1,0:T(8,128)(2,1)}, u32[]{:S(2)}, u32[]{:S(2)}) collective-permute-start(bf16[256,1536]{1,0:T(8,128)(2,1)S(1)} %copy-done.2), channel_id=1, source_target_pairs={{0,62},{1,33},{2,32},{3,35},{4,34},{5,37},{6,36},{7,39},{8,38},{9,... | collective-permute-start | bytes 2359304 | tf_op jit(solution)/shard_map/ppermute | solution.py:62
  27.6 41.3 %collective-permute-start.5 = (bf16[256,1536]{1,0:T(8,128)(2,1)S(1)}, bf16[256,1536]{1,0:T(8,128)(2,1)}, u32[]{:S(2)}, u32[]{:S(2)}) collective-permute-start(bf16[256,1536]{1,0:T(8,128)(2,1)S(1)} %copy-done.2), channel_id=1, source_target_pairs={{0,224},{1,227},{2,226},{3,229},{4,228},{5,231},{6,230},{7,233},{8... | collective-permute-start | bytes 2359304 | tf_op jit(solution)/shard_map/ppermute | solution.py:62
  30.9 41.8 %collective-permute-start.6 = (bf16[256,1536]{1,0:T(8,128)(2,1)S(1)}, bf16[256,1536]{1,0:T(8,128)(2,1)}, u32[]{:S(2)}, u32[]{:S(2)}) collective-permute-start(bf16[256,1536]{1,0:T(8,128)(2,1)S(1)} %copy-done.2), channel_id=1, source_target_pairs={{0,254},{1,225},{2,224},{3,227},{4,226},{5,229},{6,228},{7,231},{8... | collective-permute-start | bytes 2359304 | tf_op jit(solution)/shard_map/ppermute | solution.py:62
  31.1 56.0 %collective-permute-start.7 = (bf16[256,1536]{1,0:T(8,128)(2,1)S(1)}, bf16[256,1536]{1,0:T(8,128)(2,1)}, u32[]{:S(2)}, u32[]{:S(2)}) collective-permute-start(bf16[256,1536]{1,0:T(8,128)(2,1)S(1)} %copy-done.2), channel_id=1, source_target_pairs={{0,30},{1,3},{2,0},{3,5},{4,2},{5,7},{6,4},{7,9},{8,6},{9,11},{10,... | collective-permute-start | bytes 2359304 | tf_op jit(solution)/shard_map/ppermute | solution.py:62
  52.8 41.1 %collective-permute-start.8 = (bf16[256,1536]{1,0:T(8,128)(2,1)S(1)}, bf16[256,1536]{1,0:T(8,128)(2,1)S(1)}, u32[]{:S(2)}, u32[]{:S(2)}) collective-permute-start(bf16[256,1536]{1,0:T(8,128)(2,1)S(1)} %copy-done.2), channel_id=1, source_target_pairs={{0,1},{1,0},{2,3},{3,2},{4,5},{5,4},{6,7},{7,6},{8,9},{9,8},{10,11... | collective-permute-start | bytes 2359304 | tf_op jit(solution)/shard_map/ppermute | solution.py:62
  63.1 34.0 %collective-permute-start.9 = (bf16[256,1536]{1,0:T(8,128)(2,1)}, bf16[256,1536]{1,0:T(8,128)(2,1)}, u32[]{:S(2)}, u32[]{:S(2)}) collective-permute-start(bf16[256,1536]{1,0:T(8,128)(2,1)} %collective-permute-done.3.refs_1_), channel_id=1, source_target_pairs={{0,1},{1,0},{2,3},{3,2},{4,5},{5,4},{6,7},{7,6},{8,9},{9,8},{10,11... | collective-permute-start | bytes 2359304 | tf_op jit(solution)/shard_map/ppermute | solution.py:62
  68.9 29.5 %collective-permute-start.10 = (bf16[256,1536]{1,0:T(8,128)(2,1)}, bf16[256,1536]{1,0:T(8,128)(2,1)}, u32[]{:S(2)}, u32[]{:S(2)}) collective-permute-start(bf16[256,1536]{1,0:T(8,128)(2,1)} %collective-permute-done.4.refs_2_), channel_id=1, source_target_pairs={{0,1},{1,0},{2,3},{3,2},{4,5},{5,4},{6,7},{7,6},{8,9},{9,8},{10,11... | collective-permute-start | bytes 2359304 | tf_op jit(solution)/shard_map/ppermute | solution.py:62
  72.8 27.1 %collective-permute-start.11 = (bf16[256,1536]{1,0:T(8,128)(2,1)}, bf16[256,1536]{1,0:T(8,128)(2,1)}, u32[]{:S(2)}, u32[]{:S(2)}) collective-permute-start(bf16[256,1536]{1,0:T(8,128)(2,1)} %collective-permute-done.5.refs_3_), channel_id=1, source_target_pairs={{0,1},{1,0},{2,3},{3,2},{4,5},{5,4},{6,7},{7,6},{8,9},{9,8},{10,11... | collective-permute-start | bytes 2359304 | tf_op jit(solution)/shard_map/ppermute | solution.py:62
  87.1 13.2 %collective-permute-start.12 = (bf16[256,1536]{1,0:T(8,128)(2,1)}, bf16[256,1536]{1,0:T(8,128)(2,1)}, u32[]{:S(2)}, u32[]{:S(2)}) collective-permute-start(bf16[256,1536]{1,0:T(8,128)(2,1)} %collective-permute-done.6.refs_4_), channel_id=1, source_target_pairs={{0,1},{1,0},{2,3},{3,2},{4,5},{5,4},{6,7},{7,6},{8,9},{9,8},{10,11... | collective-permute-start | bytes 2359304 | tf_op jit(solution)/shard_map/ppermute | solution.py:62
  93.9 0.9 copy-start.8
  93.9 8.6 %collective-permute-start.13 = (bf16[256,1536]{1,0:T(8,128)(2,1)}, bf16[256,1536]{1,0:T(8,128)(2,1)}, u32[]{:S(2)}, u32[]{:S(2)}) collective-permute-start(bf16[256,1536]{1,0:T(8,128)(2,1)} %collective-permute-done.7.refs_5_), channel_id=1, source_target_pairs={{0,1},{1,0},{2,3},{3,2},{4,5},{5,4},{6,7},{7,6},{8,9},{9,8},{10,11... | collective-permute-start | bytes 2359304 | tf_op jit(solution)/shard_map/ppermute | solution.py:62
  97.1 25.9 %collective-permute-start.14 = (bf16[384,1152]{1,0:T(8,128)(2,1)S(1)}, bf16[384,1152]{1,0:T(8,128)(2,1)}, u32[]{:S(2)}, u32[]{:S(2)}) collective-permute-start(bf16[384,1152]{1,0:T(8,128)(2,1)S(1)} %get-tuple-element.50), channel_id=1, source_target_pairs={{0,64},{1,65},{2,66},{3,67},{4,68},{5,69},{6,70},{7,71},{8,72},{9,... | collective-permute-start | bytes 2654216 | tf_op jit(solution)/shard_map/ppermute | solution.py:62
  98.4 24.6 %collective-permute-start.15 = (bf16[384,1152]{1,0:T(8,128)(2,1)S(1)}, bf16[384,1152]{1,0:T(8,128)(2,1)}, u32[]{:S(2)}, u32[]{:S(2)}) collective-permute-start(bf16[384,1152]{1,0:T(8,128)(2,1)S(1)} %get-tuple-element.49), channel_id=1, source_target_pairs={{0,192},{1,193},{2,194},{3,195},{4,196},{5,197},{6,198},{7,199},{8... | collective-permute-start | bytes 2654216 | tf_op jit(solution)/shard_map/ppermute | solution.py:62
  99.8 23.2 %collective-permute-start.16 = (bf16[384,1152]{1,0:T(8,128)(2,1)S(1)}, bf16[384,1152]{1,0:T(8,128)(2,1)}, u32[]{:S(2)}, u32[]{:S(2)}) collective-permute-start(bf16[384,1152]{1,0:T(8,128)(2,1)S(1)} %get-tuple-element.48), channel_id=1, source_target_pairs={{0,32},{1,33},{2,34},{3,35},{4,36},{5,37},{6,38},{7,39},{8,40},{9,... | collective-permute-start | bytes 2654216 | tf_op jit(solution)/shard_map/ppermute | solution.py:62
  100.3 22.7 %collective-permute-start.17 = (bf16[384,1152]{1,0:T(8,128)(2,1)S(1)}, bf16[384,1152]{1,0:T(8,128)(2,1)}, u32[]{:S(2)}, u32[]{:S(2)}) collective-permute-start(bf16[384,1152]{1,0:T(8,128)(2,1)S(1)} %get-tuple-element.47), channel_id=1, source_target_pairs={{0,34},{1,35},{2,32},{3,33},{4,38},{5,39},{6,36},{7,37},{8,42},{9,... | collective-permute-start | bytes 2654216 | tf_op jit(solution)/shard_map/ppermute | solution.py:62
  123.0 23.8 %copy-start.5 = (f32[1536]{0:T(1024)S(1)}, f32[1536]{0:T(1024)}, u32[]{:S(2)}) copy-start(f32[1536]{0:T(1024)} %param.13) | copy-start | bytes 18436
  123.0 22.1 %collective-permute-start.18 = (bf16[256,384]{1,0:T(8,128)(2,1)}, bf16[256,384]{1,0:T(8,128)(2,1)S(1)}, u32[]{:S(2)}, u32[]{:S(2)}) collective-permute-start(bf16[256,384]{1,0:T(8,128)(2,1)} %get-tuple-element.40), channel_id=1, source_target_pairs={{0,1},{1,0},{2,3},{3,2},{4,5},{5,4},{6,7},{7,6},{8,9},{9,8},{10,11... | collective-permute-start | bytes 589832 | tf_op jit(solution)/shard_map/ppermute | solution.py:62
  145.0 1.7 %collective-permute-start.19 = (bf16[256,384]{1,0:T(8,128)(2,1)}, bf16[256,384]{1,0:T(8,128)(2,1)S(1)}, u32[]{:S(2)}, u32[]{:S(2)}) collective-permute-start(bf16[256,384]{1,0:T(8,128)(2,1)} %get-tuple-element.41), channel_id=1, source_target_pairs={{0,1},{1,0},{2,3},{3,2},{4,5},{5,4},{6,7},{7,6},{8,9},{9,8},{10,11... | collective-permute-start | bytes 589832 | tf_op jit(solution)/shard_map/ppermute | solution.py:62
  145.1 3.0 %copy-start = (bf16[256,384]{1,0:T(8,128)(2,1)}, bf16[256,384]{1,0:T(8,128)(2,1)S(1)}, u32[]{:S(2)}) copy-start(bf16[256,384]{1,0:T(8,128)(2,1)S(1)} %collective-permute-done.18.a2) | copy-start | bytes 589828
  146.7 1.4 copy-start.1
  146.7 5.5 %collective-permute-start.20 = (bf16[1536,768]{1,0:T(8,128)(2,1)}, bf16[1536,768]{1,0:T(8,128)(2,1)}, u32[]{:S(2)}, u32[]{:S(2)}) collective-permute-start(bf16[1536,768]{1,0:T(8,128)(2,1)} %all-gather.5.cloned.1.call-done.w_ref), channel_id=1, source_target_pairs={{0,1},{1,0},{2,3},{3,2},{4,5},{5,4},{6,7},{7,6},{8,9},{9,8},{10,11... | collective-permute-start | bytes 7077896 | tf_op jit(solution)/shard_map/ppermute | solution.py:62
Sparse Core Ops, SparseCore 0:
  24.9 64.6 all-gather.2
  91.4 38.2 all-gather.4

commit v9 on v8

--- a/solution.py
+++ b/solution.py
@@ -17,7 +17,7 @@
 AXES = ("x", "l", "z", "u", "c")
 SIZES = (4, 2, 8, 2, 2)
 FAR = 1e30
-GROUP = 2
+GROUP = 4
 BF = jnp.bfloat16
 F32 = jnp.float32
 
@@ -232,9 +232,13 @@
         return pl.ds(pl.multiple_of(core * 2 * HALF, HD), 2 * HALF)
 
     cols = span(c_ref[0] if own else 1 - c_ref[0])
-    for copy in copies:
+    for copy in copies[:4]:
         copy.wait()
-    out = jnp.dot(left[...], weight[...], preferred_element_type=F32)
+    out = jnp.zeros(gate_ref[:, cols].shape, F32)
+    for j in range(parts):
+        copies[4 + j].wait()
+        rows = pl.ds(j * deep, deep)
+        out += jnp.dot(left[:, rows], weight[rows], preferred_element_type=F32)
     out = (gate_ref[:, cols] * out).astype(BF)
     if own:
         o_ref[...] = out

time: 164 us -> 164 us (level)
  no operation moved by 1% of the time
where the time goes in v9:
time: 164 us
  starting transfers between devices  54.9 us (33%)
  Pallas kernels  53.7 us (33%)
  waiting for transfers between devices  31.9 us (19%)
  between operations  13.6 us (8%)
  local copies, waits for them, and re-layouts  8.5 us (5%)
    ppermute x21, starting transfers between devices, send(): return lax.ppermute(x, AXES, pairs)  54.8 us
    pallas_call x2, Pallas kernels, three_heads(): pl.pallas_call(functools.partial(heads_kernel, n, m), out_shape=[jax.Shap...  40.3 us
    ppermute x21, waiting for transfers between devices, send(): return lax.ppermute(x, AXES, pairs)  31.9 us
    pallas_call x2, Pallas kernels, out_columns(): pl.pallas_call(functools.partial(columns_kernel, own), out_shape=jax.Shap...  9.66 us
    pallas_call x1, Pallas kernels, modulate(): pl.pallas_call(modulate_kernel, out_shape=jax.ShapeDtypeStruct((rows, wid...  3.73 us
  transfers between devices with their start and end apart: 23, of which 5 were waited for; matrix products, arithmetic and copies ran while one was open for 4% of the time, Pallas kernels for 30%

profile of v9, /device:TPU:1, one launch (start us, length us, event | category | flops | bytes accessed | tf_op | source)
XLA Modules:
  0.0 164.0 jit_solution(1932834533867476788)
XLA Ops:
  6.5 1.0 constant_dynamic-slice_fusion
  7.5 0.9 constant_dynamic-slice_fusion.3
  8.4 3.3 %collective-permute-start = (bf16[48,1920]{1,0:T(8,128)(2,1)S(1)}, bf16[48,1920]{1,0:T(8,128)(2,1)S(1)}, u32[]{:S(2)}, u32[]{:S(2)}) collective-permute-start(bf16[48,1920]{1,0:T(8,128)(2,1)S(1)} %pad_maximum_fusion.1), channel_id=1, source_target_pairs={{0,1},{1,0},{2,3},{3,2},{4,5},{5,4},{6,7},{7,6},{8,9},{9,8},{10,11... | collective-permute-start | bytes 552968 | tf_op jit(solution)/shard_map/ppermute | solution.py:62
  11.8 1.3 collective-permute-start.1
  13.0 2.0 %collective-permute-start.2 = (bf16[48,1920]{1,0:T(8,128)(2,1)S(1)}, bf16[48,1920]{1,0:T(8,128)(2,1)S(1)}, u32[]{:S(2)}, u32[]{:S(2)}) collective-permute-start(bf16[48,1920]{1,0:T(8,128)(2,1)S(1)} %pad_maximum_fusion.1), channel_id=1, source_target_pairs={{0,3},{1,2},{2,1},{3,0},{4,7},{5,6},{6,5},{7,4},{8,11},{9,10},{10,... | collective-permute-start | bytes 552968 | tf_op jit(solution)/shard_map/ppermute | solution.py:62
  15.0 0.6 reshape.27.scale_ref
  15.6 0.6 reshape.28.shift_ref
  16.2 3.7 %modulate.1.refs_0_ = bf16[256,1536]{1,0:T(8,128)(2,1)} custom-call(bf16[256,1536]{1,0:T(8,128)(2,1)} %bitcast.17, f32[1,1536]{1,0:T(1,128)} %reshape.27.scale_ref, f32[1,1536]{1,0:T(1,128)} %reshape.28.shift_ref), custom_call_target="tpu_custom_call" | custom-call | flops 3145728 | bytes 1572864 | tf_op jit(solution)/shard_map/modulate/pallas_call | solution.py:85
  19.9 0.0 collective-permute-done
  19.9 0.0 collective-permute-done.1
  20.0 3.7 %collective-permute-done.2 = bf16[48,1920]{1,0:T(8,128)(2,1)S(1)} collective-permute-done((bf16[48,1920]{1,0:T(8,128)(2,1)S(1)}, bf16[48,1920]{1,0:T(8,128)(2,1)S(1)}, u32[]{:S(2)}, u32[]{:S(2)}) %collective-permute-start.2) | collective-permute-done | bytes 184352 | tf_op jit(solution)/shard_map/ppermute | solution.py:62
  23.7 0.1 maximum_select_fusion.1
  23.8 0.0 copy-start.2
  23.8 0.1 maximum_select_fusion
  24.0 0.0 copy-start.6
  24.0 0.0 copy-start.7
  24.0 0.8 slice.24
  24.8 0.0 all-gather.3.cloned.1.call-update
  24.8 0.0 all-gather.5.cloned.1.call-start
  24.9 0.1 copy-done.2
  25.0 1.0 collective-permute-start.3
  26.0 0.7 slice.29
  26.7 0.0 all-gather.5.cloned.1.call-update
  26.8 0.9 collective-permute-start.4
  27.6 3.3 %collective-permute-start.5 = (bf16[256,1536]{1,0:T(8,128)(2,1)S(1)}, bf16[256,1536]{1,0:T(8,128)(2,1)}, u32[]{:S(2)}, u32[]{:S(2)}) collective-permute-start(bf16[256,1536]{1,0:T(8,128)(2,1)S(1)} %copy-done.2), channel_id=1, source_target_pairs={{0,224},{1,227},{2,226},{3,229},{4,228},{5,231},{6,230},{7,233},{8... | collective-permute-start | bytes 2359304 | tf_op jit(solution)/shard_map/ppermute | solution.py:62
  30.9 0.2 collective-permute-start.6
  31.1 3.2 %collective-permute-start.7 = (bf16[256,1536]{1,0:T(8,128)(2,1)S(1)}, bf16[256,1536]{1,0:T(8,128)(2,1)}, u32[]{:S(2)}, u32[]{:S(2)}) collective-permute-start(bf16[256,1536]{1,0:T(8,128)(2,1)S(1)} %copy-done.2), channel_id=1, source_target_pairs={{0,30},{1,3},{2,0},{3,5},{4,2},{5,7},{6,4},{7,9},{8,6},{9,11},{10,... | collective-permute-start | bytes 2359304 | tf_op jit(solution)/shard_map/ppermute | solution.py:62
  34.3 18.5 %collective-permute-done.3.refs_1_ = bf16[256,1536]{1,0:T(8,128)(2,1)} collective-permute-done((bf16[256,1536]{1,0:T(8,128)(2,1)S(1)}, bf16[256,1536]{1,0:T(8,128)(2,1)}, u32[]{:S(2)}, u32[]{:S(2)}) %collective-permute-start.3) | collective-permute-done | bytes 786464 | tf_op jit(solution)/shard_map/ppermute | solution.py:62
  52.8 3.7 %collective-permute-start.8 = (bf16[256,1536]{1,0:T(8,128)(2,1)S(1)}, bf16[256,1536]{1,0:T(8,128)(2,1)S(1)}, u32[]{:S(2)}, u32[]{:S(2)}) collective-permute-start(bf16[256,1536]{1,0:T(8,128)(2,1)S(1)} %copy-done.2), channel_id=1, source_target_pairs={{0,1},{1,0},{2,3},{3,2},{4,5},{5,4},{6,7},{7,6},{8,9},{9,8},{10,11... | collective-permute-start | bytes 2359304 | tf_op jit(solution)/shard_map/ppermute | solution.py:62
  56.5 0.7 stack.59.far_ref
  57.2 5.9 %collective-permute-done.4.refs_2_ = bf16[256,1536]{1,0:T(8,128)(2,1)} collective-permute-done((bf16[256,1536]{1,0:T(8,128)(2,1)S(1)}, bf16[256,1536]{1,0:T(8,128)(2,1)}, u32[]{:S(2)}, u32[]{:S(2)}) %collective-permute-start.4) | collective-permute-done | bytes 786464 | tf_op jit(solution)/shard_map/ppermute | solution.py:62
  63.1 5.8 %collective-permute-start.9 = (bf16[256,1536]{1,0:T(8,128)(2,1)}, bf16[256,1536]{1,0:T(8,128)(2,1)}, u32[]{:S(2)}, u32[]{:S(2)}) collective-permute-start(bf16[256,1536]{1,0:T(8,128)(2,1)} %collective-permute-done.3.refs_1_), channel_id=1, source_target_pairs={{0,1},{1,0},{2,3},{3,2},{4,5},{5,4},{6,7},{7,6},{8,9},{9,8},{10,11... | collective-permute-start | bytes 2359304 | tf_op jit(solution)/shard_map/ppermute | solution.py:62
  68.9 0.0 collective-permute-done.5.refs_3_
  68.9 3.9 %collective-permute-start.10 = (bf16[256,1536]{1,0:T(8,128)(2,1)}, bf16[256,1536]{1,0:T(8,128)(2,1)}, u32[]{:S(2)}, u32[]{:S(2)}) collective-permute-start(bf16[256,1536]{1,0:T(8,128)(2,1)} %collective-permute-done.4.refs_2_), channel_id=1, source_target_pairs={{0,1},{1,0},{2,3},{3,2},{4,5},{5,4},{6,7},{7,6},{8,9},{9,8},{10,11... | collective-permute-start | bytes 2359304 | tf_op jit(solution)/shard_map/ppermute | solution.py:62
  72.8 0.0 collective-permute-done.6.refs_4_
  72.8 12.2 %collective-permute-start.11 = (bf16[256,1536]{1,0:T(8,128)(2,1)}, bf16[256,1536]{1,0:T(8,128)(2,1)}, u32[]{:S(2)}, u32[]{:S(2)}) collective-permute-start(bf16[256,1536]{1,0:T(8,128)(2,1)} %collective-permute-done.5.refs_3_), channel_id=1, source_target_pairs={{0,1},{1,0},{2,3},{3,2},{4,5},{5,4},{6,7},{7,6},{8,9},{9,8},{10,11... | collective-permute-start | bytes 2359304 | tf_op jit(solution)/shard_map/ppermute | solution.py:62
  84.9 2.1 %collective-permute-done.7.refs_5_ = bf16[256,1536]{1,0:T(8,128)(2,1)} collective-permute-done((bf16[256,1536]{1,0:T(8,128)(2,1)S(1)}, bf16[256,1536]{1,0:T(8,128)(2,1)}, u32[]{:S(2)}, u32[]{:S(2)}) %collective-permute-start.7) | collective-permute-done | bytes 786464 | tf_op jit(solution)/shard_map/ppermute | solution.py:62
  87.1 6.8 %collective-permute-start.12 = (bf16[256,1536]{1,0:T(8,128)(2,1)}, bf16[256,1536]{1,0:T(8,128)(2,1)}, u32[]{:S(2)}, u32[]{:S(2)}) collective-permute-start(bf16[256,1536]{1,0:T(8,128)(2,1)} %collective-permute-done.6.refs_4_), channel_id=1, source_target_pairs={{0,1},{1,0},{2,3},{3,2},{4,5},{5,4},{6,7},{7,6},{8,9},{9,8},{10,11... | collective-permute-start | bytes 2359304 | tf_op jit(solution)/shard_map/ppermute | solution.py:62
  93.9 0.0 collective-permute-done.8.refs_6_
  93.9 0.1 collective-permute-start.13
  94.0 0.6 broadcast_select_fusion.order_ref
  94.6 0.2 copy-done.8
  94.8 2.2 %fusion = (bf16[384,1152]{1,0:T(8,128)(2,1)S(1)}, bf16[384,1152]{1,0:T(8,128)(2,1)S(1)}, bf16[384,1152]{1,0:T(8,128)(2,1)S(1)}, bf16[384,1152]{1,0:T(8,128)(2,1)S(1)}) fusion(bf16[1536,1152]{1,0:T(8,128)(2,1)} %all-gather.3.cloned.1.call-done.refs_12_), kind=kLoop, calls=%fused_computation.15 | loop fusion | bytes 7077888 | tf_op jit(solution)/shard_map/slice | solution.py:303
  97.0 0.0 collective-permute-done.9.refs_7_
  97.1 1.3 collective-permute-start.14
  98.4 0.0 collective-permute-done.10.refs_8_
  98.4 1.5 collective-permute-start.15
  99.8 0.4 collective-permute-start.16
  100.3 2.2 %collective-permute-start.17 = (bf16[384,1152]{1,0:T(8,128)(2,1)S(1)}, bf16[384,1152]{1,0:T(8,128)(2,1)}, u32[]{:S(2)}, u32[]{:S(2)}) collective-permute-start(bf16[384,1152]{1,0:T(8,128)(2,1)S(1)} %get-tuple-element.47), channel_id=1, source_target_pairs={{0,34},{1,35},{2,32},{3,33},{4,38},{5,39},{6,36},{7,37},{8,42},{9,... | collective-permute-start | bytes 2654216 | tf_op jit(solution)/shard_map/ppermute | solution.py:62
  102.5 20.0 %three_heads.2 = (bf16[256,384]{1,0:T(8,128)(2,1)}, bf16[256,384]{1,0:T(8,128)(2,1)}) custom-call(s32[12]{0:T(128)} %broadcast_select_fusion.order_ref, f32[12]{0:T(128)} %stack.59.far_ref, bf16[256,1536]{1,0:T(8,128)(2,1)} %modulate.1.refs_0_, bf16[256,1536]{1,0:T(8,128)(2,1)} %collective-permute-done.3.refs_1_, ...), custom_call_target="tpu_custom_call" | custom-call | flops 9663676416 | bytes 12976128 | tf_op jit(solution)/shard_map/three_heads/pallas_call | solution.py:190
  122.6 0.0 collective-permute-done.15.refs_13_
  122.6 0.0 collective-permute-done.16.refs_14_
  122.6 0.0 copy-start.5
  122.6 1.3 collective-permute-start.18
  123.9 20.2 %three_heads.3 = (bf16[256,384]{1,0:T(8,128)(2,1)}, bf16[256,384]{1,0:T(8,128)(2,1)}) custom-call(s32[12]{0:T(128)} %broadcast_select_fusion.order_ref, f32[12]{0:T(128)} %stack.59.far_ref, bf16[256,1536]{1,0:T(8,128)(2,1)} %modulate.1.refs_0_, bf16[256,1536]{1,0:T(8,128)(2,1)} %collective-permute-done.3.refs_1_, ...), custom_call_target="tpu_custom_call" | custom-call | flops 9663676416 | bytes 12976128 | tf_op jit(solution)/shard_map/three_heads/pallas_call | solution.py:190
  144.2 0.4 collective-permute-start.19
  144.5 0.0 collective-permute-done.18.a2
  144.5 1.6 collective-permute-done.19.a3
  146.1 0.1 collective-permute-start.20
  146.3 0.6 reshape.31.gate_ref
  146.9 0.6 pad_add_fusion.at_ref
  147.5 4.6 %out_columns.2.refs_0_ = bf16[256,768]{1,0:T(8,128)(2,1)} custom-call(s32[1]{0:T(128)} %bitcast.c_ref, s32[4]{0:T(128)} %pad_add_fusion.at_ref, bf16[256,384]{1,0:T(8,128)(2,1)} %get-tuple-element.34.a0, bf16[256,384]{1,0:T(8,128)(2,1)} %get-tuple-element.39.a1, bf16[256,384]{1,0:T(8,128)(2,1)} %copy-done, bf16[256,384]{1,0:T(8,128)(2,1)} %copy-done.1, ...), custom_call_target="tpu_custom_call" | custom-call | flops 603979776 | bytes 3538944 | tf_op jit(solution)/shard_map/out_columns/pallas_call | solution.py:258
  152.1 0.0 collective-permute-done.20.w_ref
  152.1 5.1 %out_columns.3 = bf16[256,1536]{1,0:T(8,128)(2,1)} custom-call(s32[1]{0:T(128)} %bitcast.c_ref, s32[4]{0:T(128)} %pad_add_fusion.at_ref, bf16[256,384]{1,0:T(8,128)(2,1)} %get-tuple-element.34.a0, bf16[256,384]{1,0:T(8,128)(2,1)} %get-tuple-element.39.a1, bf16[256,384]{1,0:T(8,128)(2,1)} %copy-done, bf16[256,384]{1,0:T(8,128)(2,1)} %copy-done.1, ...), custom_call_target="tpu_custom_call" | custom-call | flops 603979776 | bytes 3538944 | tf_op jit(solution)/shard_map/out_columns/pallas_call | solution.py:258
  (22 shorter events, 0.1 us)
Async XLA Ops:
  6.5 8.5 %copy-start.3 = (f32[1536]{0:T(1024)S(1)}, f32[1536]{0:T(1024)}, u32[]{:S(2)}) copy-start(f32[1536]{0:T(1024)} %param.12) | copy-start | bytes 18436
  6.5 9.1 %copy-start.4 = (f32[1536]{0:T(1024)S(1)}, f32[1536]{0:T(1024)}, u32[]{:S(2)}) copy-start(f32[1536]{0:T(1024)} %param.11) | copy-start | bytes 18436
  6.5 88.3 %all-gather.3.cloned.1.call-start = ((), (), s32[]{:S(2)}) async-start(), calls=%async_computation | async-start | bytes 3981312 | tf_op jit(solution)/shard_map/all_gather | solution.py:300
  8.4 11.5 %collective-permute-start = (bf16[48,1920]{1,0:T(8,128)(2,1)S(1)}, bf16[48,1920]{1,0:T(8,128)(2,1)S(1)}, u32[]{:S(2)}, u32[]{:S(2)}) collective-permute-start(bf16[48,1920]{1,0:T(8,128)(2,1)S(1)} %pad_maximum_fusion.1), channel_id=1, source_target_pairs={{0,1},{1,0},{2,3},{3,2},{4,5},{5,4},{6,7},{7,6},{8,9},{9,8},{10,11... | collective-permute-start | bytes 552968 | tf_op jit(solution)/shard_map/ppermute | solution.py:62
  11.8 8.2 %collective-permute-start.1 = (bf16[48,1920]{1,0:T(8,128)(2,1)S(1)}, bf16[48,1920]{1,0:T(8,128)(2,1)S(1)}, u32[]{:S(2)}, u32[]{:S(2)}) collective-permute-start(bf16[48,1920]{1,0:T(8,128)(2,1)S(1)} %pad_maximum_fusion), channel_id=1, source_target_pairs={{0,2},{1,3},{2,0},{3,1},{4,6},{5,7},{6,4},{7,5},{8,10},{9,11},{10,... | collective-permute-start | bytes 552968 | tf_op jit(solution)/shard_map/ppermute | solution.py:62
  13.0 10.6 %collective-permute-start.2 = (bf16[48,1920]{1,0:T(8,128)(2,1)S(1)}, bf16[48,1920]{1,0:T(8,128)(2,1)S(1)}, u32[]{:S(2)}, u32[]{:S(2)}) collective-permute-start(bf16[48,1920]{1,0:T(8,128)(2,1)S(1)} %pad_maximum_fusion.1), channel_id=1, source_target_pairs={{0,3},{1,2},{2,1},{3,0},{4,7},{5,6},{6,5},{7,4},{8,11},{9,10},{10,... | collective-permute-start | bytes 552968 | tf_op jit(solution)/shard_map/ppermute | solution.py:62
  23.8 1.2 copy-start.2
  24.0 70.0 %copy-start.6 = (s32[12]{0:T(128)S(1)}, s32[12]{0:T(128)}, u32[]{:S(2)}) copy-start(s32[12]{0:T(128)} %constant.61.clone) | copy-start | bytes 148
  24.0 70.0 %copy-start.7 = (s32[12]{0:T(128)S(1)}, s32[12]{0:T(128)}, u32[]{:S(2)}) copy-start(s32[12]{0:T(128)} %constant.62.clone) | copy-start | bytes 148
  24.8 119.7 %all-gather.5.cloned.1.call-start = ((), (), s32[]{:S(2)}) async-start(), calls=%async_computation.1 | async-start | bytes 2654208 | tf_op jit(solution)/shard_map/all_gather | solution.py:301
  25.0 27.8 %collective-permute-start.3 = (bf16[256,1536]{1,0:T(8,128)(2,1)S(1)}, bf16[256,1536]{1,0:T(8,128)(2,1)}, u32[]{:S(2)}, u32[]{:S(2)}) collective-permute-start(bf16[256,1536]{1,0:T(8,128)(2,1)S(1)} %copy-done.2), channel_id=1, source_target_pairs={{0,32},{1,35},{2,34},{3,37},{4,36},{5,39},{6,38},{7,41},{8,40},{9,... | collective-permute-start | bytes 2359304 | tf_op jit(solution)/shard_map/ppermute | solution.py:62
  26.8 36.3 %collective-permute-start.4 = (bf16[256,1536]{1,0:T(8,128)(2,1)S(1)}, bf16[256,1536]{1,0:T(8,128)(2,1)}, u32[]{:S(2)}, u32[]{:S(2)}) collective-permute-start(bf16[256,1536]{1,0:T(8,128)(2,1)S(1)} %copy-done.2), channel_id=1, source_target_pairs={{0,62},{1,33},{2,32},{3,35},{4,34},{5,37},{6,36},{7,39},{8,38},{9,... | collective-permute-start | bytes 2359304 | tf_op jit(solution)/shard_map/ppermute | solution.py:62
  27.6 41.3 %collective-permute-start.5 = (bf16[256,1536]{1,0:T(8,128)(2,1)S(1)}, bf16[256,1536]{1,0:T(8,128)(2,1)}, u32[]{:S(2)}, u32[]{:S(2)}) collective-permute-start(bf16[256,1536]{1,0:T(8,128)(2,1)S(1)} %copy-done.2), channel_id=1, source_target_pairs={{0,224},{1,227},{2,226},{3,229},{4,228},{5,231},{6,230},{7,233},{8... | collective-permute-start | bytes 2359304 | tf_op jit(solution)/shard_map/ppermute | solution.py:62
  30.9 41.8 %collective-permute-start.6 = (bf16[256,1536]{1,0:T(8,128)(2,1)S(1)}, bf16[256,1536]{1,0:T(8,128)(2,1)}, u32[]{:S(2)}, u32[]{:S(2)}) collective-permute-start(bf16[256,1536]{1,0:T(8,128)(2,1)S(1)} %copy-done.2), channel_id=1, source_target_pairs={{0,254},{1,225},{2,224},{3,227},{4,226},{5,229},{6,228},{7,231},{8... | collective-permute-start | bytes 2359304 | tf_op jit(solution)/shard_map/ppermute | solution.py:62
  31.1 56.0 %collective-permute-start.7 = (bf16[256,1536]{1,0:T(8,128)(2,1)S(1)}, bf16[256,1536]{1,0:T(8,128)(2,1)}, u32[]{:S(2)}, u32[]{:S(2)}) collective-permute-start(bf16[256,1536]{1,0:T(8,128)(2,1)S(1)} %copy-done.2), channel_id=1, source_target_pairs={{0,30},{1,3},{2,0},{3,5},{4,2},{5,7},{6,4},{7,9},{8,6},{9,11},{10,... | collective-permute-start | bytes 2359304 | tf_op jit(solution)/shard_map/ppermute | solution.py:62
  52.8 41.1 %collective-permute-start.8 = (bf16[256,1536]{1,0:T(8,128)(2,1)S(1)}, bf16[256,1536]{1,0:T(8,128)(2,1)S(1)}, u32[]{:S(2)}, u32[]{:S(2)}) collective-permute-start(bf16[256,1536]{1,0:T(8,128)(2,1)S(1)} %copy-done.2), channel_id=1, source_target_pairs={{0,1},{1,0},{2,3},{3,2},{4,5},{5,4},{6,7},{7,6},{8,9},{9,8},{10,11... | collective-permute-start | bytes 2359304 | tf_op jit(solution)/shard_map/ppermute | solution.py:62
  63.1 34.0 %collective-permute-start.9 = (bf16[256,1536]{1,0:T(8,128)(2,1)}, bf16[256,1536]{1,0:T(8,128)(2,1)}, u32[]{:S(2)}, u32[]{:S(2)}) collective-permute-start(bf16[256,1536]{1,0:T(8,128)(2,1)} %collective-permute-done.3.refs_1_), channel_id=1, source_target_pairs={{0,1},{1,0},{2,3},{3,2},{4,5},{5,4},{6,7},{7,6},{8,9},{9,8},{10,11... | collective-permute-start | bytes 2359304 | tf_op jit(solution)/shard_map/ppermute | solution.py:62
  68.9 29.5 %collective-permute-start.10 = (bf16[256,1536]{1,0:T(8,128)(2,1)}, bf16[256,1536]{1,0:T(8,128)(2,1)}, u32[]{:S(2)}, u32[]{:S(2)}) collective-permute-start(bf16[256,1536]{1,0:T(8,128)(2,1)} %collective-permute-done.4.refs_2_), channel_id=1, source_target_pairs={{0,1},{1,0},{2,3},{3,2},{4,5},{5,4},{6,7},{7,6},{8,9},{9,8},{10,11... | collective-permute-start | bytes 2359304 | tf_op jit(solution)/shard_map/ppermute | solution.py:62
  72.8 27.1 %collective-permute-start.11 = (bf16[256,1536]{1,0:T(8,128)(2,1)}, bf16[256,1536]{1,0:T(8,128)(2,1)}, u32[]{:S(2)}, u32[]{:S(2)}) collective-permute-start(bf16[256,1536]{1,0:T(8,128)(2,1)} %collective-permute-done.5.refs_3_), channel_id=1, source_target_pairs={{0,1},{1,0},{2,3},{3,2},{4,5},{5,4},{6,7},{7,6},{8,9},{9,8},{10,11... | collective-permute-start | bytes 2359304 | tf_op jit(solution)/shard_map/ppermute | solution.py:62
  87.1 13.2 %collective-permute-start.12 = (bf16[256,1536]{1,0:T(8,128)(2,1)}, bf16[256,1536]{1,0:T(8,128)(2,1)}, u32[]{:S(2)}, u32[]{:S(2)}) collective-permute-start(bf16[256,1536]{1,0:T(8,128)(2,1)} %collective-permute-done.6.refs_4_), channel_id=1, source_target_pairs={{0,1},{1,0},{2,3},{3,2},{4,5},{5,4},{6,7},{7,6},{8,9},{9,8},{10,11... | collective-permute-start | bytes 2359304 | tf_op jit(solution)/shard_map/ppermute | solution.py:62
  93.9 0.9 copy-start.8
  93.9 8.6 %collective-permute-start.13 = (bf16[256,1536]{1,0:T(8,128)(2,1)}, bf16[256,1536]{1,0:T(8,128)(2,1)}, u32[]{:S(2)}, u32[]{:S(2)}) collective-permute-start(bf16[256,1536]{1,0:T(8,128)(2,1)} %collective-permute-done.7.refs_5_), channel_id=1, source_target_pairs={{0,1},{1,0},{2,3},{3,2},{4,5},{5,4},{6,7},{7,6},{8,9},{9,8},{10,11... | collective-permute-start | bytes 2359304 | tf_op jit(solution)/shard_map/ppermute | solution.py:62
  97.1 25.5 %collective-permute-start.14 = (bf16[384,1152]{1,0:T(8,128)(2,1)S(1)}, bf16[384,1152]{1,0:T(8,128)(2,1)}, u32[]{:S(2)}, u32[]{:S(2)}) collective-permute-start(bf16[384,1152]{1,0:T(8,128)(2,1)S(1)} %get-tuple-element.50), channel_id=1, source_target_pairs={{0,64},{1,65},{2,66},{3,67},{4,68},{5,69},{6,70},{7,71},{8,72},{9,... | collective-permute-start | bytes 2654216 | tf_op jit(solution)/shard_map/ppermute | solution.py:62
  98.4 24.2 %collective-permute-start.15 = (bf16[384,1152]{1,0:T(8,128)(2,1)S(1)}, bf16[384,1152]{1,0:T(8,128)(2,1)}, u32[]{:S(2)}, u32[]{:S(2)}) collective-permute-start(bf16[384,1152]{1,0:T(8,128)(2,1)S(1)} %get-tuple-element.49), channel_id=1, source_target_pairs={{0,192},{1,193},{2,194},{3,195},{4,196},{5,197},{6,198},{7,199},{8... | collective-permute-start | bytes 2654216 | tf_op jit(solution)/shard_map/ppermute | solution.py:62
  99.8 22.8 %collective-permute-start.16 = (bf16[384,1152]{1,0:T(8,128)(2,1)S(1)}, bf16[384,1152]{1,0:T(8,128)(2,1)}, u32[]{:S(2)}, u32[]{:S(2)}) collective-permute-start(bf16[384,1152]{1,0:T(8,128)(2,1)S(1)} %get-tuple-element.48), channel_id=1, source_target_pairs={{0,32},{1,33},{2,34},{3,35},{4,36},{5,37},{6,38},{7,39},{8,40},{9,... | collective-permute-start | bytes 2654216 | tf_op jit(solution)/shard_map/ppermute | solution.py:62
  100.3 22.3 %collective-permute-start.17 = (bf16[384,1152]{1,0:T(8,128)(2,1)S(1)}, bf16[384,1152]{1,0:T(8,128)(2,1)}, u32[]{:S(2)}, u32[]{:S(2)}) collective-permute-start(bf16[384,1152]{1,0:T(8,128)(2,1)S(1)} %get-tuple-element.47), channel_id=1, source_target_pairs={{0,34},{1,35},{2,32},{3,33},{4,38},{5,39},{6,36},{7,37},{8,42},{9,... | collective-permute-start | bytes 2654216 | tf_op jit(solution)/shard_map/ppermute | solution.py:62
  122.6 23.6 %copy-start.5 = (f32[1536]{0:T(1024)S(1)}, f32[1536]{0:T(1024)}, u32[]{:S(2)}) copy-start(f32[1536]{0:T(1024)} %param.13) | copy-start | bytes 18436
  122.6 21.9 %collective-permute-start.18 = (bf16[256,384]{1,0:T(8,128)(2,1)}, bf16[256,384]{1,0:T(8,128)(2,1)S(1)}, u32[]{:S(2)}, u32[]{:S(2)}) collective-permute-start(bf16[256,384]{1,0:T(8,128)(2,1)} %get-tuple-element.40), channel_id=1, source_target_pairs={{0,1},{1,0},{2,3},{3,2},{4,5},{5,4},{6,7},{7,6},{8,9},{9,8},{10,11... | collective-permute-start | bytes 589832 | tf_op jit(solution)/shard_map/ppermute | solution.py:62
  144.2 2.0 %collective-permute-start.19 = (bf16[256,384]{1,0:T(8,128)(2,1)}, bf16[256,384]{1,0:T(8,128)(2,1)S(1)}, u32[]{:S(2)}, u32[]{:S(2)}) collective-permute-start(bf16[256,384]{1,0:T(8,128)(2,1)} %get-tuple-element.41), channel_id=1, source_target_pairs={{0,1},{1,0},{2,3},{3,2},{4,5},{5,4},{6,7},{7,6},{8,9},{9,8},{10,11... | collective-permute-start | bytes 589832 | tf_op jit(solution)/shard_map/ppermute | solution.py:62
  144.5 3.0 %copy-start = (bf16[256,384]{1,0:T(8,128)(2,1)}, bf16[256,384]{1,0:T(8,128)(2,1)S(1)}, u32[]{:S(2)}) copy-start(bf16[256,384]{1,0:T(8,128)(2,1)S(1)} %collective-permute-done.18.a2) | copy-start | bytes 589828
  146.1 1.4 copy-start.1
  146.1 6.0 %collective-permute-start.20 = (bf16[1536,768]{1,0:T(8,128)(2,1)}, bf16[1536,768]{1,0:T(8,128)(2,1)}, u32[]{:S(2)}, u32[]{:S(2)}) collective-permute-start(bf16[1536,768]{1,0:T(8,128)(2,1)} %all-gather.5.cloned.1.call-done.w_ref), channel_id=1, source_target_pairs={{0,1},{1,0},{2,3},{3,2},{4,5},{5,4},{6,7},{7,6},{8,9},{9,8},{10,11... | collective-permute-start | bytes 7077896 | tf_op jit(solution)/shard_map/ppermute | solution.py:62
Sparse Core Ops, SparseCore 0:
  24.9 64.6 all-gather.2
  91.4 38.2 all-gather.4
